TPU v7x, 32 devices: a whole 2x2x4 slice. The times are simulated.
32 devices in a mesh: wide: 16 (over z, x, core), narrow: 2 (over y).
Axes of the slice: x: 2, y: 2, z: 4, core: 2. Of those that a mesh axis runs over, the one named last changes fastest.
Arguments:
- tokens: bfloat16 [6144, 1536], P('wide'), may hold values from -6 to 6
- lengths: int32 [2], replicated, may hold values from 1024 to 3456, as said below
- norm1_gain: bfloat16 [1536], P('wide'), may hold values from 0.5 to 1.5
- w_query: bfloat16 [1536, 1536], P('wide', 'narrow'), may hold values from -0.15625 to 0.15625
- b_query: bfloat16 [12, 128], P('narrow', 'wide'), may hold values from -3 to 3
- key_projection: bfloat16 [1536, 256], P('wide', 'narrow'), may hold values from -0.15625 to 0.15625
- key_bias_vector: bfloat16 [2, 128], P('narrow', 'wide'), may hold values from -3 to 3
- value_projection: bfloat16 [1536, 256], P('wide', 'narrow'), may hold values from -0.15625 to 0.15625
- value_bias_vector: bfloat16 [2, 128], P('narrow', 'wide'), may hold values from -3 to 3
- w_out: bfloat16 [1536, 1536], P('narrow', 'wide'), may hold values from -6 to 6
- norm2_gain: bfloat16 [1536], P('wide'), may hold values from 0.5 to 1.5
- w_gate: bfloat16 [1536, 8960], P('wide', 'narrow'), may hold values from -0.15625 to 0.15625
- w_up: bfloat16 [1536, 8960], P('wide', 'narrow'), may hold values from -0.15625 to 0.15625
- w_down: bfloat16 [8960, 1536], P('narrow', 'wide'), may hold values from -0.0625 to 0.0625
- cotangent: bfloat16 [6144, 1536], P('wide'), may hold values from -6 to 6
Outputs:
- result: bfloat16 [6144, 1536], P('wide')
- grad_tokens: bfloat16 [6144, 1536], P('wide')
- grad_norm1_gain: float32 [1536], P('wide')
- grad_w_query: float32 [1536, 1536], P('wide', 'narrow')
- grad_b_query: float32 [12, 128], P('narrow', 'wide')
- grad_w_key: float32 [1536, 256], P('wide', 'narrow')
- grad_b_key: float32 [2, 128], P('narrow', 'wide')
- grad_w_value: float32 [1536, 256], P('wide', 'narrow')
- grad_b_value: float32 [2, 128], P('narrow', 'wide')
- grad_w_out: float32 [1536, 1536], P('narrow', 'wide')
- grad_norm2_gain: float32 [1536], P('wide')
- grad_w_gate: float32 [1536, 8960], P('wide', 'narrow')
- grad_w_up: float32 [1536, 8960], P('wide', 'narrow')
- grad_w_down: float32 [8960, 1536], P('narrow', 'wide')
Inputs may be any that keep to these rules, and one draw needn't show every extreme that they name: Every sequence has 1024 tokens or more, the lengths add up to 6144, and the longest has exactly 3456 tokens.
All inputs are finite; a program needn't handle non-finite values.
Results may differ from a plain program's by a relative error of at most 0.038.
Values may be sent and summed in bfloat16 or wider, within the bound.
No kernel may reach another device: no remote copies, remote signals or barrier semaphores. Data moves between devices by JAX's collectives and lax.ppermute only.
A program may use at most 256 MiB of HBM per device.

v0:
```python
import math

import jax
import jax.numpy as jnp
from jax import lax
from jax.sharding import PartitionSpec as P

ROPE_BASE = 10000.0
EPSILON = 1e-06


def product(left, right):
    return jnp.dot(left, right, preferred_element_type=jnp.float32)


def product_left(left, right):
    return lax.dot_general(
        left, right, (((0,), (0,)), ((), ())), preferred_element_type=jnp.float32
    )


def product_right(left, right):
    return lax.dot_general(
        left, right, (((1,), (1,)), ((), ())), preferred_element_type=jnp.float32
    )


def rotate_halves(value_rows, cosine_table, sine_table):
    middle_at = value_rows.shape[-1] // 2
    first = value_rows[..., :middle_at]
    second = value_rows[..., middle_at:]
    return jnp.concatenate(
        [first * cosine_table - second * sine_table, second * cosine_table + first * sine_table],
        axis=-1,
    )


def norm_scale(value_rows):
    return lax.rsqrt(jnp.mean(value_rows * value_rows, axis=-1, keepdims=True) + EPSILON)


def norm_back(value_rows, scale, gain, grad):
    normed = value_rows * scale
    inner = grad * gain
    back = scale * (inner - normed * jnp.mean(inner * normed, axis=-1, keepdims=True))
    return (back, jnp.sum(grad * normed, axis=0))


def local(
    tokens,
    lengths,
    norm1_gain,
    w_query,
    b_query,
    key_projection,
    key_bias_vector,
    value_projection,
    value_bias_vector,
    w_out,
    norm2_gain,
    w_gate,
    w_up,
    w_down,
    cotangent,
):
    rows = tokens.shape[0]
    devices = lax.axis_size("wide")
    own_index = lax.axis_index("wide")
    first = own_index * rows
    index = first + jnp.arange(rows, dtype=jnp.int32)
    ends = jnp.cumsum(lengths, dtype=jnp.int32)
    starts = ends - lengths
    seq_start = jnp.max(jnp.where(starts[None, :] <= index[:, None], starts[None, :], 0), axis=1)
    lowest = jnp.min(seq_start)
    highest = first + rows - 1
    head = key_projection.shape[1]
    freq = 1.0 / ROPE_BASE ** (jnp.arange(head // 2, dtype=jnp.float32) * 2.0 / head)
    angle = (index - seq_start).astype(jnp.float32)[:, None] * freq[None, :]
    cosine_table = jnp.cos(angle)[:, None, :]
    sine_table = jnp.sin(angle)[:, None, :]
    factor = 1.0 / math.sqrt(head)
    span = rows * max(1, devices // 16)
    weights = (
        lax.all_gather(norm1_gain, "wide", axis=0, tiled=True),
        lax.all_gather(w_query, "wide", axis=0, tiled=True),
        lax.all_gather(b_query, "wide", axis=1, tiled=True),
        lax.all_gather(key_projection, "wide", axis=0, tiled=True),
        lax.all_gather(key_bias_vector, "wide", axis=1, tiled=True),
        lax.all_gather(value_projection, "wide", axis=0, tiled=True),
        lax.all_gather(value_bias_vector, "wide", axis=1, tiled=True),
        lax.all_gather(w_out, "wide", axis=1, tiled=True),
        lax.all_gather(norm2_gain, "wide", axis=0, tiled=True),
        lax.all_gather(w_gate, "wide", axis=0, tiled=True),
        lax.all_gather(w_up, "wide", axis=0, tiled=True),
        lax.all_gather(w_down, "wide", axis=1, tiled=True),
    )
    inputs = tokens.astype(jnp.float32)
    gain_one = weights[0].astype(jnp.float32)
    scale_one = norm_scale(inputs)
    normed_one = (inputs * scale_one * gain_one).astype(jnp.bfloat16)
    query_pre = product(normed_one, weights[1]) + weights[2].reshape(-1).astype(jnp.float32)
    query_group = query_pre.shape[1] // head
    query_rows = (
        rotate_halves(query_pre.reshape(rows, query_group, head), cosine_table, sine_table)
        .astype(jnp.bfloat16)
        .reshape(rows * query_group, head)
    )
    key_before_rotation = product(normed_one, weights[3]) + weights[4].reshape(-1).astype(
        jnp.float32
    )
    key_rows = (
        rotate_halves(key_before_rotation.reshape(rows, 1, head), cosine_table, sine_table)
        .reshape(rows, head)
        .astype(jnp.bfloat16)
    )
    value_rows = (
        product(normed_one, weights[5]) + weights[6].reshape(-1).astype(jnp.float32)
    ).astype(jnp.bfloat16)

    def exp_scores(key_block, key_begin):
        count = key_block.shape[0]
        key_index = key_begin + jnp.arange(count, dtype=jnp.int32)
        allowed = (key_index[None, :] >= seq_start[:, None]) & (
            key_index[None, :] <= index[:, None]
        )
        scores = product_right(query_rows, key_block) * factor
        exp_weights = jnp.where(
            allowed[:, None, :], jnp.exp(scores.reshape(rows, query_group, count)), 0.0
        )
        return exp_weights.reshape(rows * query_group, count)

    def is_live(key_begin, count):
        return (key_begin + count > lowest) & (key_begin <= highest)

    def add_block(inner, key_block, value_block, key_begin):
        weighted, totals = inner
        exp_weights = exp_scores(key_block, key_begin)
        return (
            weighted + product(exp_weights.astype(jnp.bfloat16), value_block),
            totals + jnp.sum(exp_weights, axis=1),
        )

    initial = (
        jnp.zeros((rows * query_group, head), jnp.float32),
        jnp.zeros((rows * query_group,), jnp.float32),
    )
    whole = (
        lax.all_gather(key_rows, "wide", axis=0, tiled=True),
        lax.all_gather(value_rows, "wide", axis=0, tiled=True),
    )
    forward_key_all, forward_value_all = whole
    count = forward_key_all.shape[0]

    def turn(step, state):
        offset = step * span

        def turn_compute(inner):
            key_block = lax.dynamic_slice_in_dim(forward_key_all, offset, span, 0)
            value_block = lax.dynamic_slice_in_dim(forward_value_all, offset, span, 0)
            return add_block(inner, key_block, value_block, 0 + offset)

        return lax.cond(is_live(0 + offset, span), turn_compute, lambda inner: inner, state)

    weighted, totals = lax.fori_loop(0, count // span, turn, initial)
    attended = weighted / totals[:, None]
    attended_low = attended.reshape(rows, query_group * head).astype(jnp.bfloat16)
    attention = lax.psum(product(attended_low, weights[7]), "narrow")
    middle = inputs + attention
    gain_two = weights[8].astype(jnp.float32)
    scale_two = norm_scale(middle)
    normed_two = (middle * scale_two * gain_two).astype(jnp.bfloat16)
    gate = product(normed_two, weights[9])
    up_part = product(normed_two, weights[10])
    sigmoid_gate = jax.nn.sigmoid(gate)
    silu_gate = gate * sigmoid_gate
    hidden = (silu_gate * up_part).astype(jnp.bfloat16)
    down_part = lax.psum(product(hidden, weights[11]).astype(jnp.bfloat16), "narrow").astype(
        jnp.float32
    )
    result = (middle + down_part).astype(jnp.bfloat16)
    grad_w_down = product_left(hidden, cotangent)
    grad_hidden = product_right(cotangent, weights[11])
    grad_gate = (grad_hidden * up_part * sigmoid_gate * (1.0 + gate * (1.0 - sigmoid_gate))).astype(
        jnp.bfloat16
    )
    grad_up = (grad_hidden * silu_gate).astype(jnp.bfloat16)
    grad_w_gate = product_left(normed_two, grad_gate)
    grad_w_up = product_left(normed_two, grad_up)
    grad_normed_two = lax.psum(
        product_right(grad_gate, weights[9]) + product_right(grad_up, weights[10]), "narrow"
    )
    back_two, grad_gain_two = norm_back(middle, scale_two, gain_two, grad_normed_two)
    grad_middle = cotangent.astype(jnp.float32) + back_two
    grad_att = grad_middle.astype(jnp.bfloat16)
    grad_w_out = product_left(attended_low, grad_att)
    grad_attended = product_right(grad_att, weights[7]).reshape(rows * query_group, head)
    grad_accum = (grad_attended / totals[:, None]).astype(jnp.bfloat16)
    delta = jnp.sum(grad_attended * attended, axis=1) / totals

    def back_block(key_block, value_block, key_begin):
        exp_weights = exp_scores(key_block, key_begin)
        grad_probs = product_right(grad_accum, value_block)
        grad_scores = (exp_weights * (grad_probs - delta[:, None])).astype(jnp.bfloat16)
        query_term = product(grad_scores, key_block)
        grad_keys = product_left(grad_scores, query_rows) * factor
        grad_values = product_left(exp_weights.astype(jnp.bfloat16), grad_accum)
        return (query_term, jnp.concatenate([grad_keys, grad_values], axis=1))

    key_all, value_all = whole
    count_all = key_all.shape[0]

    def back_turn(step, state):
        offset = step * span

        def back_compute(inner):
            grad_queries, buffer = inner
            key_block = lax.dynamic_slice_in_dim(key_all, offset, span, 0)
            value_block = lax.dynamic_slice_in_dim(value_all, offset, span, 0)
            query_term, update = back_block(key_block, value_block, offset)
            return (
                grad_queries + query_term,
                lax.dynamic_update_slice_in_dim(buffer, update, offset, 0),
            )

        return lax.cond(is_live(offset, span), back_compute, lambda inner: inner, state)

    start_state = (
        jnp.zeros((rows * query_group, head), jnp.float32),
        jnp.zeros((count_all, 2 * head), jnp.float32),
    )
    grad_queries, buffer = lax.fori_loop(0, count_all // span, back_turn, start_state)
    key_value_grads = lax.psum_scatter(buffer, "wide", scatter_dimension=0, tiled=True)
    grad_query_pre = (
        rotate_halves(
            (grad_queries * factor).reshape(rows, query_group, head), cosine_table, -sine_table
        )
        .reshape(rows, query_group * head)
        .astype(jnp.bfloat16)
    )
    grad_key_pre = (
        rotate_halves(key_value_grads[:, :head].reshape(rows, 1, head), cosine_table, -sine_table)
        .reshape(rows, head)
        .astype(jnp.bfloat16)
    )
    grad_value_pre = key_value_grads[:, head:].astype(jnp.bfloat16)
    grad_w_query = product_left(normed_one, grad_query_pre)
    grad_w_key = product_left(normed_one, grad_key_pre)
    grad_w_value = product_left(normed_one, grad_value_pre)
    grad_b_query = jnp.sum(grad_query_pre.astype(jnp.float32), axis=0).reshape(query_group, head)
    grad_b_key = jnp.sum(grad_key_pre.astype(jnp.float32), axis=0).reshape(1, head)
    grad_b_value = jnp.sum(grad_value_pre.astype(jnp.float32), axis=0).reshape(1, head)
    grad_normed_one = lax.psum(
        (
            product_right(grad_query_pre, weights[1])
            + product_right(grad_key_pre, weights[3])
            + product_right(grad_value_pre, weights[5])
        ).astype(jnp.bfloat16),
        "narrow",
    ).astype(jnp.float32)
    back_one, grad_gain_one = norm_back(inputs, scale_one, gain_one, grad_normed_one)
    grad_tokens = (grad_middle + back_one).astype(jnp.bfloat16)
    summed = (
        lax.psum_scatter(grad_gain_one, "wide", scatter_dimension=0, tiled=True),
        lax.psum_scatter(grad_w_query, "wide", scatter_dimension=0, tiled=True),
        lax.psum_scatter(grad_b_query, "wide", scatter_dimension=1, tiled=True),
        lax.psum_scatter(grad_w_key, "wide", scatter_dimension=0, tiled=True),
        lax.psum_scatter(grad_b_key, "wide", scatter_dimension=1, tiled=True),
        lax.psum_scatter(grad_w_value, "wide", scatter_dimension=0, tiled=True),
        lax.psum_scatter(grad_b_value, "wide", scatter_dimension=1, tiled=True),
        lax.psum_scatter(grad_w_out, "wide", scatter_dimension=1, tiled=True),
        lax.psum_scatter(grad_gain_two, "wide", scatter_dimension=0, tiled=True),
        lax.psum_scatter(grad_w_gate, "wide", scatter_dimension=0, tiled=True),
        lax.psum_scatter(grad_w_up, "wide", scatter_dimension=0, tiled=True),
        lax.psum_scatter(grad_w_down, "wide", scatter_dimension=1, tiled=True),
    )
    attn_grads = summed[:8]
    mlp_grads = summed[8:]
    return (
        result,
        grad_tokens,
        attn_grads[0],
        attn_grads[1],
        attn_grads[2],
        attn_grads[3],
        attn_grads[4],
        attn_grads[5],
        attn_grads[6],
        attn_grads[7],
        mlp_grads[0],
        mlp_grads[1],
        mlp_grads[2],
        mlp_grads[3],
    )


def solution(mesh):
    placed = (
        P("wide", None),
        P(),
        P("wide"),
        P("wide", "narrow"),
        P("narrow", "wide"),
        P("wide", "narrow"),
        P("narrow", "wide"),
        P("wide", "narrow"),
        P("narrow", "wide"),
        P("narrow", "wide"),
        P("wide"),
        P("wide", "narrow"),
        P("wide", "narrow"),
        P("narrow", "wide"),
        P("wide", None),
    )
    return jax.shard_map(
        local,
        mesh=mesh,
        in_specs=placed,
        out_specs=(
            P("wide", None),
            P("wide", None),
            P("wide"),
            P("wide", "narrow"),
            P("narrow", "wide"),
            P("wide", "narrow"),
            P("narrow", "wide"),
            P("wide", "narrow"),
            P("narrow", "wide"),
            P("narrow", "wide"),
            P("wide"),
            P("wide", "narrow"),
            P("wide", "narrow"),
            P("narrow", "wide"),
        ),
        check_vma=False,
    )
```

profile of v0, /device:TPU:0, one launch (start us, length us, event | category | flops | bytes accessed | tf_op | source)
XLA Modules:
  0.0 2142.1 jit_solution(5908820730716654291)
XLA Ops:
  13.4 36.0 %all-reduce.10 = (bf16[128]{0:T(256)(128)(2,1)S(1)}, bf16[1536]{0:T(1024)(128)(2,1)S(1)}, bf16[128]{0:T(256)(128)(2,1)S(1)}, bf16[1536]{0:T(1024)(128)(2,1)S(1)}) all-reduce(bf16[128]{0:T(256)(128)(2,1)S(1)} %dynamic-update-slice.1, bf16[1536]{0:T(1024)(128)(2,1)S(1)} %dynamic-update-slice, ...), channel_id=1, replica_groups=mesh['wide'=16,'narrow'=2] {'wide'}, use_global_device_ids=true, to_apply=%add.1 | all-reduce | flops 3328 | bytes 13312
  53.3 18.5 all_gather.43
  76.4 20.7 all_gather.48
  99.8 17.9 all_gather.47
  121.5 36.4 %all-gather.9.cloned.1.call-done = bf16[1536,768]{1,0:T(8,128)(2,1)} async-done(((bf16[96,768]{1,0:T(8,128)(2,1)}), bf16[1536,768]{1,0:T(8,128)(2,1)}) %all-gather.9.cloned.1.call-update) | async-done | bytes 2359312 | tf_op jit(solution)/shard_map/all_gather | solution.py:85
  164.1 35.1 %all-gather.11.cloned.1.call-done = bf16[6144,128]{1,0:T(8,128)(2,1)} async-done(((bf16[384,128]{1,0:T(8,128)(2,1)}), bf16[6144,128]{1,0:T(8,128)(2,1)}) %all-gather.11.cloned.1.call-update) | async-done | bytes 1572880 | tf_op jit(solution)/shard_map/all_gather | solution.py:149
  199.2 17.8 while.32
  218.0 24.4 %all-gather.13.cloned.1.call-done = bf16[768,1536]{0,1:T(8,128)(2,1)} async-done(((bf16[768,96]{0,1:T(8,128)(2,1)}), bf16[768,1536]{0,1:T(8,128)(2,1)}) %all-gather.13.cloned.1.call-update) | async-done | bytes 2359312 | tf_op jit(solution)/shard_map/all_gather | solution.py:91
  249.8 90.4 %all-reduce.16.cloned.1.call-done = f32[384,1536]{1,0:T(8,128)} async-done(((f32[384,1536]{1,0:T(8,128)}), f32[384,1536]{1,0:T(8,128)}) %all-reduce.16.cloned.1.call-update) | async-done | bytes 2359312 | tf_op jit(solution)/shard_map/psum | solution.py:167
  344.5 105.6 %all-gather.15.cloned.1.call-done = bf16[1536,4480]{1,0:T(8,128)(2,1)} async-done(((bf16[96,4480]{1,0:T(8,128)(2,1)}), bf16[1536,4480]{1,0:T(8,128)(2,1)}) %all-gather.15.cloned.1.call-update) | async-done | bytes 13762576 | tf_op jit(solution)/shard_map/all_gather | solution.py:93
  450.0 12.8 fusion.82
  462.8 95.4 %all-gather.17.cloned.1.call-done = bf16[1536,4480]{1,0:T(8,128)(2,1)} async-done(((bf16[96,4480]{1,0:T(8,128)(2,1)}), bf16[1536,4480]{1,0:T(8,128)(2,1)}) %all-gather.17.cloned.1.call-update) | async-done | bytes 13762576 | tf_op jit(solution)/shard_map/all_gather | solution.py:94
  558.2 12.8 fusion.83
  571.0 95.4 %all-gather.19.cloned.1.call-done = bf16[4480,1536]{0,1:T(8,128)(2,1)} async-done(((bf16[4480,96]{0,1:T(8,128)(2,1)}), bf16[4480,1536]{0,1:T(8,128)(2,1)}) %all-gather.19.cloned.1.call-update) | async-done | bytes 13762576 | tf_op jit(solution)/shard_map/all_gather | solution.py:95
  666.4 14.8 multiply_convert_fusion
  681.2 10.1 fusion.84
  691.3 10.9 convolution_add_fusion.4
  702.4 66.8 %all-reduce.18.cloned.1.call-done = f32[384,1536]{1,0:T(8,128)} async-done(((f32[384,1536]{1,0:T(8,128)}), f32[384,1536]{1,0:T(8,128)}) %all-reduce.18.cloned.1.call-update) | async-done | bytes 2359312 | tf_op jit(solution)/shard_map/psum | solution.py:189
  783.2 22.4 %while.33 = (s32[]{:T(128)}, f32[2304,128]{1,0:T(8,128)}, f32[6144,256]{0,1:T(8,128)}, s32[]{:T(128)}, s32[]{:T(128)}, /*index=5*/s32[384]{0:T(512)S(1)}, bf16[6...) while((s32[]{:T(128)}, f32[2304,128]{1,0:T(8,128)}, ...), condition=%wide.region_18.19_spmd.clone, body=%wide.region_15.18_spmd.clone.sunk | while | flops 1138656000 | bytes 27742064 | solution.py:231
  783.8 11.1 conditional.7
  807.6 10.1 convolution_convert_fusion
  823.5 153.8 %reduce-scatter.12.cloned.1.call-done = f32[384,256]{0,1:T(8,128)} async-done(((f32[6144,256]{0,1:T(8,128)}), f32[384,256]{0,1:T(8,128)}) %reduce-scatter.12.cloned.1.call-update) | async-done | bytes 393232 | tf_op jit(solution)/shard_map/reduce_scatter | solution.py:232
  997.5 14.5 fusion.85
  1012.0 14.4 fusion.86
  1027.7 14.4 fusion.87
  1053.4 62.1 %all-reduce.9 = (f32[1536]{0:T(1024)}, f32[6,128]{1,0:T(8,128)}, f32[1,128]{1,0:T(1,128)}, f32[1,128]{1,0:T(1,128)}, f32[1536]{0:T(1024)}) all-reduce(f32[1536]{0:T(1024)} %get-tuple-element.634, f32[6,128]{1,0:T(8,128)S(1)} %get-tuple-element.691, f32[1,128]{1,0:T(1,128)} %bitcast.89, ...), channel_id=4, replica_groups=mesh['wide'=16,'narrow'=2] {'wide'}, use_global_device_ids=true, to_apply=%region_23.24.clone | all-reduce | flops 4096 | bytes 32768
  1130.9 79.2 %reduce-scatter.20.cloned.1.call-done = f32[768,96]{0,1:T(8,128)} async-done(((f32[768,1536]{0,1:T(8,128)}), f32[768,96]{0,1:T(8,128)}) %reduce-scatter.20.cloned.1.call-update) | async-done | bytes 294928 | tf_op jit(solution)/shard_map/reduce_scatter | solution.py:270
  1210.2 60.0 %reduce-scatter.16.cloned.1.call-done = f32[96,128]{1,0:T(8,128)} async-done(((f32[1536,128]{1,0:T(8,128)}), f32[96,128]{1,0:T(8,128)}) %reduce-scatter.16.cloned.1.call-update) | async-done | bytes 49168 | tf_op jit(solution)/shard_map/reduce_scatter | solution.py:266
  1270.2 59.8 %reduce-scatter.18.cloned.1.call-done = f32[96,128]{1,0:T(8,128)} async-done(((f32[1536,128]{1,0:T(8,128)}), f32[96,128]{1,0:T(8,128)}) %reduce-scatter.18.cloned.1.call-update) | async-done | bytes 49168 | tf_op jit(solution)/shard_map/reduce_scatter | solution.py:268
  1330.0 268.3 %reduce-scatter.22.cloned.1.call-done = f32[96,4480]{1,0:T(8,128)} async-done(((f32[1536,4480]{1,0:T(8,128)}), f32[96,4480]{1,0:T(8,128)}) %reduce-scatter.22.cloned.1.call-update) | async-done | bytes 1720336 | tf_op jit(solution)/shard_map/reduce_scatter | solution.py:272
  1598.3 268.4 %reduce-scatter.24.cloned.1.call-done = f32[96,4480]{1,0:T(8,128)} async-done(((f32[1536,4480]{1,0:T(8,128)}), f32[96,4480]{1,0:T(8,128)}) %reduce-scatter.24.cloned.1.call-update) | async-done | bytes 1720336 | tf_op jit(solution)/shard_map/reduce_scatter | solution.py:273
  1866.6 268.4 %reduce-scatter.26.cloned.1.call-done = f32[4480,96]{0,1:T(8,128)} async-done(((f32[4480,1536]{0,1:T(8,128)}), f32[4480,96]{0,1:T(8,128)}) %reduce-scatter.26.cloned.1.call-update) | async-done | bytes 1720336 | tf_op jit(solution)/shard_map/reduce_scatter | solution.py:274
  (282 shorter events, 131.3 us)
Async XLA Ops:
  7.2 111.7 %all-gather.21.cloned.1.call-start = ((), (), s32[]{:S(2)}) async-start(), calls=%async_computation.24 | async-start | bytes 1671168 | tf_op jit(solution)/shard_map/all_gather | solution.py:148
  7.3 110.5 %copy-start.37 = (f32[64]{0:T(128)}, f32[64]{0:T(128)S(1)}, u32[]{:S(2)}) copy-start(f32[64]{0:T(128)S(1)} %negate_power_fusion) | copy-start | bytes 772
  49.4 108.6 %copy-start.27 = (f32[1536]{0:T(1024)}, f32[1536]{0:T(1024)S(1)}, u32[]{:S(2)}) copy-start(f32[1536]{0:T(1024)S(1)} %convert_element_type.133) | copy-start | bytes 18436
  49.4 27.0 %copy-start.36 = (bf16[96,128]{1,0:T(8,128)(2,1)S(1)}, bf16[96,128]{1,0:T(8,128)(2,1)}, u32[]{:S(2)}) copy-start(bf16[96,128]{1,0:T(8,128)(2,1)} %param.30) | copy-start | bytes 73732
  49.4 48.5 %copy-start.3 = (bf16[384,1536]{1,0:T(8,128)(2,1)S(1)}, bf16[384,1536]{1,0:T(8,128)(2,1)}, u32[]{:S(2)}) copy-start(bf16[384,1536]{1,0:T(8,128)(2,1)} %param.23) | copy-start | bytes 3538948
  51.1 106.8 %copy-start.31 = (f32[384]{0:T(512)}, f32[384]{0:T(512)S(1)}, u32[]{:S(2)}) copy-start(f32[384]{0:T(512)S(1)} %add_rsqrt_fusion.1) | copy-start | bytes 4612
  53.3 64.5 %copy-start.33 = (f32[384]{0:T(512)}, f32[384]{0:T(512)S(1)}, u32[]{:S(2)}) copy-start(f32[384]{0:T(512)S(1)} %get-tuple-element.721) | copy-start | bytes 4612
  75.6 82.3 %all-gather.9.cloned.1.call-start = ((), (), s32[]{:S(2)}) async-start(), calls=%async_computation.8 | async-start | bytes 2506752 | tf_op jit(solution)/shard_map/all_gather | solution.py:85
  76.3 122.8 %all-gather.11.cloned.1.call-start = ((), (), s32[]{:S(2)}) async-start(), calls=%async_computation.9 | async-start | bytes 1671168 | tf_op jit(solution)/shard_map/all_gather | solution.py:149
  99.1 143.2 %all-gather.13.cloned.1.call-start = ((), (), s32[]{:S(2)}) async-start(), calls=%async_computation.10 | async-start | bytes 2506752 | tf_op jit(solution)/shard_map/all_gather | solution.py:91
  99.7 240.5 %all-reduce.16.cloned.1.call-start = ((), (), s32[]{:S(2)}) async-start(), calls=%async_computation.11 | async-start | bytes 4718592 | tf_op jit(solution)/shard_map/psum | solution.py:167
  118.9 42.2 %copy-start.18 = (f32[384,64]{0,1:T(8,128)}, f32[384,64]{0,1:T(8,128)S(1)}, u32[]{:S(2)}) copy-start(f32[384,64]{0,1:T(8,128)S(1)} %get-tuple-element.720) | copy-start | bytes 294916
  217.9 28.6 %copy-start.11 = (bf16[384,768]{1,0:T(8,128)(2,1)}, bf16[384,768]{1,0:T(8,128)(2,1)S(1)}, u32[]{:S(2)}) copy-start(bf16[384,768]{1,0:T(8,128)(2,1)S(1)} %convert_element_type.141) | copy-start | bytes 1769476
  246.5 203.5 %all-gather.15.cloned.1.call-start = ((), (), s32[]{:S(2)}) async-start(), calls=%async_computation.12 | async-start | bytes 14622720 | tf_op jit(solution)/shard_map/all_gather | solution.py:93
  247.1 311.1 %all-gather.17.cloned.1.call-start = ((), (), s32[]{:S(2)}) async-start(), calls=%async_computation.13 | async-start | bytes 14622720 | tf_op jit(solution)/shard_map/all_gather | solution.py:94
  247.9 418.5 %all-gather.19.cloned.1.call-start = ((), (), s32[]{:S(2)}) async-start(), calls=%async_computation.14 | async-start | bytes 14622720 | tf_op jit(solution)/shard_map/all_gather | solution.py:95
  248.6 520.6 %all-reduce.18.cloned.1.call-start = ((), (), s32[]{:S(2)}) async-start(), calls=%async_computation.15 | async-start | bytes 4718592 | tf_op jit(solution)/shard_map/psum | solution.py:189
  342.5 429.8 %copy-start.1 = (f32[384,1536]{1,0:T(8,128)}, f32[384,1536]{1,0:T(8,128)S(1)}, u32[]{:S(2)}) copy-start(f32[384,1536]{1,0:T(8,128)S(1)} %get-tuple-element.694) | copy-start | bytes 7077892
  702.2 275.0 %reduce-scatter.12.cloned.1.call-start = ((), (), s32[]{:S(2)}) async-start(), calls=%async_computation.16 | async-start | bytes 6684672 | tf_op jit(solution)/shard_map/reduce_scatter | solution.py:232
  805.6 245.1 %all-reduce.20.cloned.1.call-start = ((), (), s32[]{:S(2)}) async-start(), calls=%async_computation.25 | async-start | bytes 4718592 | tf_op jit(solution)/shard_map/psum | solution.py:177
  823.0 155.8 %copy-start.34 = (f32[384]{0:T(512)S(1)}, f32[384]{0:T(512)}, u32[]{:S(2)}) copy-start(f32[384]{0:T(512)} %copy-done.33) | copy-start | bytes 4612
  823.1 155.8 %copy-start.38 = (f32[64]{0:T(128)S(1)}, f32[64]{0:T(128)}, u32[]{:S(2)}) copy-start(f32[64]{0:T(128)} %copy-done.37) | copy-start | bytes 772
  823.1 156.3 %copy-start.15 = (bf16[1536,128]{1,0:T(8,128)(2,1)S(1)}, bf16[1536,128]{1,0:T(8,128)(2,1)}, u32[]{:S(2)}) copy-start(bf16[1536,128]{1,0:T(8,128)(2,1)} %copy-done.14) | copy-start | bytes 1179652
  823.3 156.7 %copy-start.13 = (bf16[1536,768]{1,0:T(8,128)(2,1)S(1)}, bf16[1536,768]{1,0:T(8,128)(2,1)}, u32[]{:S(2)}) copy-start(bf16[1536,768]{1,0:T(8,128)(2,1)} %all-gather.9.cloned.1.call-done) | copy-start | bytes 7077892
  982.7 148.2 %reduce-scatter.14.cloned.1.call-start = ((), (), s32[]{:S(2)}) async-start(), calls=%async_computation.17 | async-start | bytes 5013504 | tf_op jit(solution)/shard_map/reduce_scatter | solution.py:264
  986.5 223.7 %reduce-scatter.20.cloned.1.call-start = ((), (), s32[]{:S(2)}) async-start(), calls=%async_computation.20 | async-start | bytes 5013504 | tf_op jit(solution)/shard_map/reduce_scatter | solution.py:270
  993.1 277.0 %reduce-scatter.16.cloned.1.call-start = ((), (), s32[]{:S(2)}) async-start(), calls=%async_computation.18 | async-start | bytes 835584 | tf_op jit(solution)/shard_map/reduce_scatter | solution.py:266
  995.5 334.5 %reduce-scatter.18.cloned.1.call-start = ((), (), s32[]{:S(2)}) async-start(), calls=%async_computation.19 | async-start | bytes 835584 | tf_op jit(solution)/shard_map/reduce_scatter | solution.py:268
  997.1 601.1 %reduce-scatter.22.cloned.1.call-start = ((), (), s32[]{:S(2)}) async-start(), calls=%async_computation.21 | async-start | bytes 29245440 | tf_op jit(solution)/shard_map/reduce_scatter | solution.py:272
  1012.0 854.7 %reduce-scatter.24.cloned.1.call-start = ((), (), s32[]{:S(2)}) async-start(), calls=%async_computation.22 | async-start | bytes 29245440 | tf_op jit(solution)/shard_map/reduce_scatter | solution.py:273
  1026.4 1108.6 %reduce-scatter.26.cloned.1.call-start = ((), (), s32[]{:S(2)}) async-start(), calls=%async_computation.23 | async-start | bytes 29245440 | tf_op jit(solution)/shard_map/reduce_scatter | solution.py:274
  1042.1 79.2 %copy-start.2 = (f32[384,1536]{1,0:T(8,128)S(1)}, f32[384,1536]{1,0:T(8,128)}, u32[]{:S(2)}) copy-start(f32[384,1536]{1,0:T(8,128)} %copy-done.1) | copy-start | bytes 7077892
  (27 other events, 80.5 us)
Sparse Core Ops, SparseCore 0:
  75.7 38.6 all-gather.20
  116.6 41.2 all-gather.8
  160.8 38.3 all-gather.10
  201.3 41.0 all-gather.12
  246.7 93.4 all-reduce.15
  342.3 107.6 all-gather.14
  452.3 105.8 all-gather.16
  560.5 105.8 all-gather.18
  702.3 66.8 all-reduce.17
  805.7 171.4 reduce-scatter.11
  982.9 67.8 all-reduce.19
  1055.0 75.8 reduce-scatter.13
  1135.4 74.7 reduce-scatter.19
  1214.2 55.9 reduce-scatter.15
  1274.1 55.8 reduce-scatter.17
  1334.5 263.6 reduce-scatter.21
  1602.8 263.7 reduce-scatter.23
  1871.2 263.7 reduce-scatter.25
where the time goes:
time: 2150 us; the launch traced here: 2140 us
  waiting for transfers between devices  1720 us (80%)
  blocking collectives  155 us (7%)
  matrix products  154 us (7%)
  local copies, waits for them, and re-layouts  35.6 us (2%)
  other arithmetic  32.9 us (2%)
  loops' own time  22.7 us (1%)
    reduce_scatter x1, waiting for transfers between devices, local(): lax.psum_scatter(grad_w_down, 'wide', scatter_dimension=1, tiled=True)  268 us
    reduce_scatter x1, waiting for transfers between devices, local(): lax.psum_scatter(grad_w_up, 'wide', scatter_dimension=0, tiled=True)  268 us
    reduce_scatter x1, waiting for transfers between devices, local(): lax.psum_scatter(grad_w_gate, 'wide', scatter_dimension=0, tiled=True)  268 us
    reduce_scatter x1, waiting for transfers between devices, local(): lax.psum_scatter(buffer, 'wide', scatter_dimension=0, tiled=True)  154 us
    all_gather x1, waiting for transfers between devices, local(): lax.all_gather(w_gate, 'wide', axis=0, tiled=True)  106 us
    unnamed x2, blocking collectives  98 us
    all_gather x1, waiting for transfers between devices, local(): lax.all_gather(w_up, 'wide', axis=0, tiled=True)  95.4 us
    all_gather x1, waiting for transfers between devices, local(): lax.all_gather(w_down, 'wide', axis=1, tiled=True)  95.4 us
  transfers between devices with their start and end apart: 18, of which 17 were waited for; matrix products, arithmetic and copies ran while one was open for 6% of the time, Pallas kernels for 0%

commit v1 on v0

v1 whole, which is shorter than its diff:
```python
import math

import jax
import jax.numpy as jnp
from jax import lax
from jax.sharding import Mesh
from jax.sharding import PartitionSpec as P

ROPE_BASE = 10000.0
EPSILON = 1e-06


def product(left, right):
    return jnp.dot(left, right, preferred_element_type=jnp.float32)


def product_left(left, right):
    return lax.dot_general(
        left, right, (((0,), (0,)), ((), ())), preferred_element_type=jnp.float32
    )


def product_right(left, right):
    return lax.dot_general(
        left, right, (((1,), (1,)), ((), ())), preferred_element_type=jnp.float32
    )


def rotate_halves(value_rows, cosine_table, sine_table):
    middle_at = value_rows.shape[-1] // 2
    first = value_rows[..., :middle_at]
    second = value_rows[..., middle_at:]
    return jnp.concatenate(
        [first * cosine_table - second * sine_table, second * cosine_table + first * sine_table],
        axis=-1,
    )


def norm_scale(value_rows):
    return lax.rsqrt(jnp.mean(value_rows * value_rows, axis=-1, keepdims=True) + EPSILON)


def norm_back(value_rows, scale, gain, grad):
    normed = value_rows * scale
    inner = grad * gain
    back = scale * (inner - normed * jnp.mean(inner * normed, axis=-1, keepdims=True))
    return (back, jnp.sum(grad * normed, axis=0))


WIDE = ("z", "x", "c")
GROUP = ("x", "c")


def other(value, axis):
    return lax.ppermute(value, axis, [(0, 1), (1, 0)])


def low(value):
    return value.astype(jnp.bfloat16)


def gather_group(own):
    core = other(own, "c")
    across = other(own, "x")
    far = other(across, "c")
    return jnp.concatenate([own, core, across, far], axis=0)


def scatter_group(partial, rows):
    sent = low(jnp.concatenate([partial[rows : 2 * rows], partial[3 * rows :]], axis=0))
    core = other(sent, "c").astype(jnp.float32)
    across = low(partial[2 * rows : 3 * rows] + core[rows:])
    own = partial[:rows] + core[:rows] + other(across, "x").astype(jnp.float32)
    return sum_narrow(own)


def sum_narrow(partial):
    mine = low(partial)
    return mine.astype(jnp.float32) + other(mine, "y").astype(jnp.float32)


def spread(weight):
    features, hidden = weight.shape
    parts = weight.reshape(features, 4, hidden // 4).transpose(1, 0, 2)
    parts = lax.all_to_all(parts, GROUP, split_axis=0, concat_axis=0, tiled=True)
    return parts.reshape(4 * features, hidden // 4)


def collect(grad):
    summed = lax.psum_scatter(low(grad), "z", scatter_dimension=0, tiled=True)
    features = summed.shape[0] // 4
    parts = summed.reshape(4, features, summed.shape[1])
    parts = lax.all_to_all(parts, GROUP, split_axis=0, concat_axis=0, tiled=True)
    return parts.transpose(1, 0, 2).reshape(features, 4 * summed.shape[1]).astype(jnp.float32)


def local(
    tokens,
    lengths,
    norm1_gain,
    w_query,
    b_query,
    key_projection,
    key_bias_vector,
    value_projection,
    value_bias_vector,
    w_out,
    norm2_gain,
    w_gate,
    w_up,
    w_down,
    cotangent,
):
    rows, width = tokens.shape
    devices = lax.axis_size(WIDE)
    own_index = lax.axis_index(WIDE)
    first = own_index * rows
    index = first + jnp.arange(rows, dtype=jnp.int32)
    ends = jnp.cumsum(lengths, dtype=jnp.int32)
    starts = ends - lengths
    seq_start = jnp.max(jnp.where(starts[None, :] <= index[:, None], starts[None, :], 0), axis=1)
    lowest = jnp.min(seq_start)
    highest = first + rows - 1
    head = key_projection.shape[1]
    freq = 1.0 / ROPE_BASE ** (jnp.arange(head // 2, dtype=jnp.float32) * 2.0 / head)
    angle = (index - seq_start).astype(jnp.float32)[:, None] * freq[None, :]
    cosine_table = jnp.cos(angle)[:, None, :]
    sine_table = jnp.sin(angle)[:, None, :]
    factor = 1.0 / math.sqrt(head)
    span = rows * max(1, devices // 16)
    features = w_query.shape[0]
    heads_width = w_query.shape[1]
    query_group = heads_width // head
    projected = heads_width + 2 * head

    piece = b_query.shape[1]
    small_parts = [norm1_gain, norm2_gain, b_query.reshape(-1), key_bias_vector.reshape(-1),
                   value_bias_vector.reshape(-1)]
    small_sizes = [part.shape[0] for part in small_parts]
    small_rows = -(-sum(small_sizes) // head)
    small = jnp.concatenate(small_parts)
    small = jnp.pad(small, (0, features * head - small.shape[0])).reshape(features, head)
    packed = jnp.concatenate([w_query, key_projection, value_projection, small], axis=1)
    w_project = lax.all_gather(packed, WIDE, axis=0, tiled=True)
    small_all = w_project[:, projected:].reshape(devices, features, head)[:, :small_rows]
    small_all = small_all.reshape(devices, small_rows * head).astype(jnp.float32)
    cuts = [0]
    for size in small_sizes:
        cuts.append(cuts[-1] + size)
    gain_one = small_all[:, cuts[0] : cuts[1]].reshape(-1)
    gain_two = small_all[:, cuts[1] : cuts[2]].reshape(-1)
    bias_query = small_all[:, cuts[2] : cuts[3]].reshape(devices, query_group, piece)
    bias_query = bias_query.transpose(1, 0, 2).reshape(-1)
    bias_key = small_all[:, cuts[3] : cuts[4]].reshape(-1)
    bias_value = small_all[:, cuts[4] : cuts[5]].reshape(-1)

    gate_part = spread(w_gate)
    up_part_weight = spread(w_up)
    down_part_weight = spread(w_down.T)

    inputs = tokens.astype(jnp.float32)
    scale_one = norm_scale(inputs)
    normed_one = low(inputs * scale_one * gain_one)
    projections = product(normed_one, w_project)
    query_pre = projections[:, :heads_width] + bias_query
    query_rows = low(
        rotate_halves(query_pre.reshape(rows, query_group, head), cosine_table, sine_table)
    ).reshape(rows * query_group, head)
    key_pre = projections[:, heads_width : heads_width + head] + bias_key
    key_rows = low(
        rotate_halves(key_pre.reshape(rows, 1, head), cosine_table, sine_table).reshape(rows, head)
    )
    value_rows = low(projections[:, heads_width + head : projected] + bias_value)

    key_value = lax.all_gather(
        jnp.concatenate([key_rows, value_rows], axis=1), WIDE, axis=0, tiled=True
    )
    w_out_all = lax.all_gather(w_out.T, WIDE, axis=0, tiled=True)
    gate_all = lax.all_gather(gate_part, "z", axis=0, tiled=True)
    up_all = lax.all_gather(up_part_weight, "z", axis=0, tiled=True)
    down_all = lax.all_gather(down_part_weight, "z", axis=0, tiled=True)
    count = key_value.shape[0]

    def exp_scores(key_block, key_begin):
        size = key_block.shape[0]
        key_index = key_begin + jnp.arange(size, dtype=jnp.int32)
        allowed = (key_index[None, :] >= seq_start[:, None]) & (
            key_index[None, :] <= index[:, None]
        )
        scores = product_right(query_rows, key_block) * factor
        exp_weights = jnp.where(
            allowed[:, None, :], jnp.exp(scores.reshape(rows, query_group, size)), 0.0
        )
        return exp_weights.reshape(rows * query_group, size)

    def is_live(key_begin, size):
        return (key_begin + size > lowest) & (key_begin <= highest)

    initial = (
        jnp.zeros((rows * query_group, head), jnp.float32),
        jnp.zeros((rows * query_group,), jnp.float32),
    )

    def turn(step, state):
        offset = step * span

        def turn_compute(inner):
            weighted, totals = inner
            block = lax.dynamic_slice_in_dim(key_value, offset, span, 0)
            exp_weights = exp_scores(block[:, :head], offset)
            return (
                weighted + product(low(exp_weights), block[:, head:]),
                totals + jnp.sum(exp_weights, axis=1),
            )

        return lax.cond(is_live(offset, span), turn_compute, lambda inner: inner, state)

    weighted, totals = lax.fori_loop(0, count // span, turn, initial)
    attended = weighted / totals[:, None]
    attended_low = low(attended.reshape(rows, heads_width))
    middle = inputs + sum_narrow(product_right(attended_low, w_out_all))
    scale_two = norm_scale(middle)
    normed_two = low(middle * scale_two * gain_two)

    cotangent_group = gather_group(cotangent)
    normed_group = gather_group(normed_two)
    gate = product(normed_group, gate_all)
    up_part = product(normed_group, up_all)
    sigmoid_gate = jax.nn.sigmoid(gate)
    silu_gate = gate * sigmoid_gate
    hidden = low(silu_gate * up_part)
    result = low(middle + scatter_group(product_right(hidden, down_all), rows))
    grad_down = product_left(cotangent_group, hidden)
    grad_hidden = product(cotangent_group, down_all)
    grad_gate = low(grad_hidden * up_part * sigmoid_gate * (1.0 + gate * (1.0 - sigmoid_gate)))
    grad_up = low(grad_hidden * silu_gate)
    grad_normed_two = scatter_group(
        product_right(grad_gate, gate_all) + product_right(grad_up, up_all), rows
    )
    grad_w_down = collect(grad_down).T
    grad_w_gate = collect(product_left(normed_group, grad_gate))
    grad_w_up = collect(product_left(normed_group, grad_up))

    back_two, grad_gain_two = norm_back(middle, scale_two, gain_two, grad_normed_two)
    grad_middle = cotangent.astype(jnp.float32) + back_two
    grad_att = low(grad_middle)
    grad_w_out = (
        lax.psum_scatter(
            low(product_left(grad_att, attended_low)), WIDE, scatter_dimension=0, tiled=True
        )
        .astype(jnp.float32)
        .T
    )
    grad_attended = product(grad_att, w_out_all).reshape(rows * query_group, head)
    grad_accum = low(grad_attended / totals[:, None])
    delta = jnp.sum(grad_attended * attended, axis=1) / totals

    def back_turn(step, state):
        offset = step * span

        def back_compute(inner):
            grad_queries, buffer = inner
            block = lax.dynamic_slice_in_dim(key_value, offset, span, 0)
            exp_weights = exp_scores(block[:, :head], offset)
            grad_probs = product_right(grad_accum, block[:, head:])
            grad_scores = low(exp_weights * (grad_probs - delta[:, None]))
            grad_keys = product_left(grad_scores, query_rows) * factor
            grad_values = product_left(low(exp_weights), grad_accum)
            update = low(jnp.concatenate([grad_keys, grad_values], axis=1))
            return (
                grad_queries + product(grad_scores, block[:, :head]),
                lax.dynamic_update_slice_in_dim(buffer, update, offset, 0),
            )

        return lax.cond(is_live(offset, span), back_compute, lambda inner: inner, state)

    start_state = (
        jnp.zeros((rows * query_group, head), jnp.float32),
        jnp.zeros((count, 2 * head), jnp.bfloat16),
    )
    grad_queries, buffer = lax.fori_loop(0, count // span, back_turn, start_state)
    key_value_grads = lax.psum_scatter(buffer, WIDE, scatter_dimension=0, tiled=True).astype(
        jnp.float32
    )
    grad_query_pre = low(
        rotate_halves(
            (grad_queries * factor).reshape(rows, query_group, head), cosine_table, -sine_table
        )
    ).reshape(rows, heads_width)
    grad_key_pre = low(
        rotate_halves(key_value_grads[:, :head].reshape(rows, 1, head), cosine_table, -sine_table)
    ).reshape(rows, head)
    grad_value_pre = low(key_value_grads[:, head:])
    grad_project = jnp.concatenate([grad_query_pre, grad_key_pre, grad_value_pre], axis=1)
    grad_bias = jnp.sum(grad_project.astype(jnp.float32), axis=0)
    grad_normed_one = sum_narrow(product_right(grad_project, w_project[:, :projected]))
    back_one, grad_gain_one = norm_back(inputs, scale_one, gain_one, grad_normed_one)
    grad_tokens = low(grad_middle + back_one)

    small_grads = jnp.concatenate(
        [
            grad_gain_one.reshape(devices, -1),
            grad_gain_two.reshape(devices, -1),
            grad_bias[:heads_width]
            .reshape(query_group, devices, piece)
            .transpose(1, 0, 2)
            .reshape(devices, -1),
            grad_bias[heads_width : heads_width + head].reshape(devices, -1),
            grad_bias[heads_width + head :].reshape(devices, -1),
        ],
        axis=1,
    )
    small_grads = jnp.pad(small_grads, ((0, 0), (0, features * head - small_grads.shape[1])))
    packed_grads = low(
        jnp.concatenate(
            [product_left(normed_one, grad_project), small_grads.reshape(devices * features, head)],
            axis=1,
        )
    )
    packed_grads = lax.psum_scatter(packed_grads, WIDE, scatter_dimension=0, tiled=True).astype(
        jnp.float32
    )
    small_own = packed_grads[:, projected:].reshape(-1)
    return (
        result,
        grad_tokens,
        small_own[cuts[0] : cuts[1]],
        packed_grads[:, :heads_width],
        small_own[cuts[2] : cuts[3]].reshape(query_group, piece),
        packed_grads[:, heads_width : heads_width + head],
        small_own[cuts[3] : cuts[4]].reshape(1, piece),
        packed_grads[:, heads_width + head : projected],
        small_own[cuts[4] : cuts[5]].reshape(1, piece),
        grad_w_out,
        small_own[cuts[1] : cuts[2]],
        grad_w_gate,
        grad_w_up,
        grad_w_down,
    )


def solution(mesh):
    wide, narrow = mesh.devices.shape
    grouped = Mesh(mesh.devices.reshape(wide // 4, 2, 2, narrow), WIDE + ("y",))
    rows = P(WIDE, None)
    vector = P(WIDE)
    columns = P(WIDE, "y")
    lines = P("y", WIDE)
    return jax.shard_map(
        local,
        mesh=grouped,
        in_specs=(rows, P(), vector, columns, lines, columns, lines, columns, lines, lines,
                  vector, columns, columns, lines, rows),
        out_specs=(rows, rows, vector, columns, lines, columns, lines, columns, lines, lines,
                   vector, columns, columns, lines),
        check_vma=False,
    )
```

time: 2150 us -> 1090 us (0.51)
  waiting for transfers between devices: 1720 us -> 678 us
  blocking collectives: 155 us -> 40.2 us
  local copies, waits for them, and re-layouts: 35.6 us -> 106 us
  starting transfers between devices: 1.89 us -> 29.8 us
    reduce_scatter x8 -> x6, waiting for transfers between devices: 1160 us -> 366 us  [the longest x3 143 us: collect(): summed = lax.psum_scatter(low(grad), 'z', scatter_dimension=0, tiled=True)]
    all_gather x7 -> x6, waiting for transfers between devices: 392 us -> 176 us  [the longest x1 58.5 us: local(): down_all = lax.all_gather(down_part_weight, 'z', axis=0, tiled=True)]
    psum x3 -> x0, waiting for transfers between devices: 163 us -> none  [the longest x1 90.4 us: local(): attention = lax.psum(product(attended_low, weights[7]), 'narrow')]
    ppermute x0 -> x14, waiting for transfers between devices: none -> 124 us  [other(): return lax.ppermute(value, axis, [(0, 1), (1, 0)])]
    unnamed x2 -> x0, blocking collectives: 98 us -> none
    all_gather x3 -> x0, blocking collectives: 57.1 us -> none  [the longest x1 20.7 us: local(): lax.all_gather(value_projection, 'wide', axis=0, tiled=True)]
    all_to_all x0 -> x2, blocking collectives: none -> 40.2 us  [spread(): lax.all_to_all(parts, GROUP, split_axis=0, concat_axis=0, tiled=True)]
    dot_general x9 -> x7, matrix products: 56.7 us -> 35.8 us  [product_left(): lax.dot_general(left, right, (((0,), (0,)), ((), ())), preferred_element_...]
  transfers between devices with their start and end apart: 18 -> 30, of which waited for: 17 -> 20; matrix products, arithmetic and copies ran while one was open for 6% -> 19% of each run, Pallas kernels for 0% -> 0%
where the time goes in v1:
time: 1090 us; the launch traced here: 1080 us
  waiting for transfers between devices  678 us (62%)
  matrix products  133 us (12%)
  local copies, waits for them, and re-layouts  106 us (10%)
  other arithmetic  52.5 us (5%)
  blocking collectives  40.2 us (4%)
  starting transfers between devices  29.8 us (3%)
  loops' own time  22.9 us (2%)
  between operations  15.3 us (1%)
    reduce_scatter x3, waiting for transfers between devices, collect(): summed = lax.psum_scatter(low(grad), 'z', scatter_dimension=0, tiled=True)  143 us
    ppermute x14, waiting for transfers between devices, other(): return lax.ppermute(value, axis, [(0, 1), (1, 0)])  124 us
    reduce_scatter x1, waiting for transfers between devices, local(): lax.psum_scatter(buffer, WIDE, scatter_dimension=0, tiled=True)  114 us
    reduce_scatter x1, waiting for transfers between devices, local(): lax.psum_scatter(packed_grads, WIDE, scatter_dimension=0, tiled=True)  65.9 us
    all_gather x1, waiting for transfers between devices, local(): down_all = lax.all_gather(down_part_weight, 'z', axis=0, tiled=True)  58.5 us
    dot_general x7, matrix products, product(): return jnp.dot(left, right, preferred_element_type=jnp.float32)  50.1 us
    dot_general x8, matrix products, product_right(): lax.dot_general(left, right, (((1,), (1,)), ((), ())), preferred_element_...  47.2 us
    all_gather x1, waiting for transfers between devices, local(): up_all = lax.all_gather(up_part_weight, 'z', axis=0, tiled=True)  46.6 us
  transfers between devices with their start and end apart: 30, of which 20 were waited for; matrix products, arithmetic and copies ran while one was open for 19% of the time, Pallas kernels for 0%

profile of v1, /device:TPU:0, one launch (start us, length us, event | category | flops | bytes accessed | tf_op | source)
XLA Modules:
  0.0 1078.1 jit_solution(300020334108806881)
XLA Ops:
  16.4 46.1 %all-gather.7.cloned.1.call-done = bf16[1536,1152]{1,0:T(8,128)(2,1)} async-done(((bf16[96,1152]{1,0:T(8,128)(2,1)}), bf16[1536,1152]{1,0:T(8,128)(2,1)}) %all-gather.7.cloned.1.call-update) | async-done | bytes 3538960 | tf_op jit(solution)/shard_map/all_gather | solution.py:144
  73.8 17.6 %all_to_all.30 = bf16[4,96,1120]{2,1,0:T(8,128)(2,1)} all-to-all(bf16[4,96,1120]{2,1,0:T(8,128)(2,1)S(1)} %bitcast.114), channel_id=1, replica_groups=mesh['z'=4,'x'=2,'c'=2,'y'=2] {'x','c'}, dimensions={0} | all-to-all | bytes 1720320 | tf_op jit(solution)/shard_map/all_to_all | solution.py:85
  94.1 22.6 %all_to_all.31 = bf16[4,96,1120]{2,1,0:T(8,128)(2,1)} all-to-all(bf16[4,96,1120]{2,1,0:T(8,128)(2,1)S(1)} %bitcast.115), channel_id=1, replica_groups=mesh['z'=4,'x'=2,'c'=2,'y'=2] {'x','c'}, dimensions={0} | all-to-all | bytes 1720320 | tf_op jit(solution)/shard_map/all_to_all | solution.py:85
  121.7 19.0 %while.32 = (s32[]{:T(128)}, f32[2304,128]{1,0:T(8,128)S(1)}, f32[2304]{0:T(1024)S(1)}, s32[]{:T(128)}, s32[]{:T(128)}, /*index=5*/s32[384]{0:T(512)S(1)}, bf16[...) while((s32[]{:T(128)}, f32[2304,128]{1,0:T(8,128)S(1)}, ...), condition=%wide.region_8.9_spmd.clone, body=%wide.region_4.8_spmd.clone.sunk | while | flops 457261824 | bytes 12335953 | solution.py:218
  122.3 7.6 conditional.6
  141.6 25.0 %all-gather.11.cloned.1.call-done = bf16[1536,768]{1,0:T(8,128)(2,1)} async-done(((bf16[96,768]{1,0:T(8,128)(2,1)}), bf16[1536,768]{1,0:T(8,128)(2,1)}) %all-gather.11.cloned.1.call-update) | async-done | bytes 2359312 | tf_op jit(solution)/shard_map/all_gather | solution.py:178
  180.0 11.2 %all-to-all-done.2 = bf16[4,96,1120]{2,1,0:T(8,128)(2,1)S(1)} async-done(((bf16[4,96,1120]{2,1,0:T(8,128)(2,1)}), bf16[4,96,1120]{2,1,0:T(8,128)(2,1)S(1)}, u32[]{:S(2)}, u32[]{:S(2)}) %all-to-all-start.2) | async-done | bytes 860192 | tf_op jit(solution)/shard_map/all_to_all | solution.py:85
  202.1 14.5 %collective-permute-done.8 = bf16[384,1536]{1,0:T(8,128)(2,1)} collective-permute-done((bf16[384,1536]{1,0:T(8,128)(2,1)}, bf16[384,1536]{1,0:T(8,128)(2,1)}, u32[]{:S(2)}, u32[]{:S(2)}) %collective-permute-start.8) | collective-permute-done | bytes 1179680 | tf_op jit(solution)/shard_map/ppermute | solution.py:55
  217.1 24.2 %collective-permute-done.2 = bf16[384,1536]{1,0:T(8,128)(2,1)} collective-permute-done((bf16[384,1536]{1,0:T(8,128)(2,1)}, bf16[384,1536]{1,0:T(8,128)(2,1)}, u32[]{:S(2)}, u32[]{:S(2)}) %collective-permute-start.2) | collective-permute-done | bytes 1179680 | tf_op jit(solution)/shard_map/ppermute | solution.py:55
  248.3 11.8 %fusion.87 = f32[1536,1120]{0,1:T(8,128)} fusion(bf16[1536,1120]{1,0:T(8,128)(2,1)} %all-gather.13.cloned.1.call-done, bf16[384,1536]{1,0:T(8,128)(2,1)} %collective-permute-done.3, bf16[384,1536]{1,0:T(8,128)(2,1)} %collective-permute-done.2, bf16[384,1536]{1,0:T(8,128)(2,1)} %collective-permute-done.1, bf16[384,1536]{1,0:T(8,128)(2,1)} %multiply_convert_fusion.3), kind=kOutput, calls=%fused_computation.170 | convolution fusion | flops 5303697408 | bytes 15040512 | tf_op jit(solution)/shard_map/dot_general | solution.py:14
  260.0 46.6 %all-gather.15.cloned.1.call-done = bf16[1536,1120]{1,0:T(8,128)(2,1)} async-done(((bf16[384,1120]{1,0:T(8,128)(2,1)}), bf16[1536,1120]{1,0:T(8,128)(2,1)}) %all-gather.15.cloned.1.call-update) | async-done | bytes 3440656 | tf_op jit(solution)/shard_map/all_gather | solution.py:180
  306.6 12.1 %fusion.86 = f32[1536,1120]{0,1:T(8,128)} fusion(bf16[1536,1120]{1,0:T(8,128)(2,1)} %all-gather.15.cloned.1.call-done, bf16[384,1536]{1,0:T(8,128)(2,1)} %collective-permute-done.3, bf16[384,1536]{1,0:T(8,128)(2,1)} %collective-permute-done.2, bf16[384,1536]{1,0:T(8,128)(2,1)} %collective-permute-done.1, bf16[384,1536]{1,0:T(8,128)(2,1)} %multiply_convert_fusion.3), kind=kOutput, calls=%fused_computation.169 | convolution fusion | flops 5303697408 | bytes 15040512 | tf_op jit(solution)/shard_map/dot_general | solution.py:14
  318.7 58.5 %all-gather.17.cloned.1.call-done = bf16[1536,1120]{1,0:T(8,128)(2,1)} async-done(((bf16[384,1120]{1,0:T(8,128)(2,1)}), bf16[1536,1120]{1,0:T(8,128)(2,1)}) %all-gather.17.cloned.1.call-update) | async-done | bytes 3440656 | tf_op jit(solution)/shard_map/all_gather | solution.py:181
  377.2 16.6 %multiply_convert_fusion = (bf16[1536,1120]{0,1:T(8,128)(2,1)}, bf16[1536,1120]{0,1:T(8,128)(2,1)}, bf16[1536,1120]{0,1:T(8,128)(2,1)}) fusion(f32[1536,1120]{0,1:T(8,128)} %fusion.87, f32[1536,1120]{0,1:T(8,128)} %fusion.86, bf16[1536,1536]{1,0:T(8,128)(2,1)} %constant_dynamic-update-slice_fusion, bf16[1536,1120]{1,0:T(8,128)(2,1)} %all-gather.17.cloned.1.call-done), kind=kOutput, calls=%fused_computation.41 | convolution fusion | flops 5310627840 | bytes 32243712 | tf_op jit(solution)/shard_map/dot_general | solution.py:14
  393.8 11.0 %fusion.99 = f32[1536,1536]{1,0:T(8,128)} fusion(bf16[1536,1120]{0,1:T(8,128)(2,1)} %get-tuple-element.577, bf16[1536,1120]{1,0:T(8,128)(2,1)S(1)} %copy-done.27), kind=kOutput, calls=%fused_computation.182 | convolution fusion | flops 5284823040 | bytes 16318464 | tf_op jit(solution)/shard_map/dot_general | solution.py:24
  404.8 10.5 fusion.97
  415.7 11.7 %fusion.98 = (bf16[1536,1536]{1,0:T(8,128)(2,1)S(1)}, f32[1536,1536]{1,0:T(8,128)}) fusion(bf16[1536,1120]{0,1:T(8,128)(2,1)} %get-tuple-element.578, bf16[1536,1120]{1,0:T(8,128)(2,1)} %all-gather.17.cloned.1.call-done), kind=kOutput, calls=%fused_computation.181 | convolution fusion | flops 5287182336 | bytes 21037056 | tf_op jit(solution)/shard_map/dot_general | solution.py:24
  436.6 21.8 %collective-permute-done.11 = bf16[384,1536]{1,0:T(8,128)(2,1)S(1)} collective-permute-done((bf16[384,1536]{1,0:T(8,128)(2,1)S(1)}, bf16[384,1536]{1,0:T(8,128)(2,1)S(1)}, u32[]{:S(2)}, u32[]{:S(2)}) %collective-permute-start.11) | collective-permute-done | bytes 1179680 | tf_op jit(solution)/shard_map/ppermute | solution.py:55
  460.5 22.2 %collective-permute-done.5 = bf16[384,1536]{1,0:T(8,128)(2,1)S(1)} collective-permute-done((bf16[384,1536]{1,0:T(8,128)(2,1)S(1)}, bf16[384,1536]{1,0:T(8,128)(2,1)S(1)}, u32[]{:S(2)}, u32[]{:S(2)}) %collective-permute-start.5) | collective-permute-done | bytes 1179680 | tf_op jit(solution)/shard_map/ppermute | solution.py:55
  487.9 24.2 %collective-permute-done.6 = bf16[384,1536]{1,0:T(8,128)(2,1)S(1)} collective-permute-done((bf16[384,1536]{1,0:T(8,128)(2,1)S(1)}, bf16[384,1536]{1,0:T(8,128)(2,1)S(1)}, u32[]{:S(2)}, u32[]{:S(2)}) %collective-permute-start.6) | collective-permute-done | bytes 1179680 | tf_op jit(solution)/shard_map/ppermute | solution.py:55
  523.2 24.5 %while.33 = (s32[]{:T(128)}, f32[2304,128]{1,0:T(8,128)}, bf16[6144,256]{0,1:T(8,128)(2,1)}, s32[]{:T(128)}, s32[]{:T(128)}, /*index=5*/s32[384]{0:T(512)S(1)}, ...) while((s32[]{:T(128)}, f32[2304,128]{1,0:T(8,128)}, ...), condition=%wide.region_15.16_spmd.clone, body=%wide.region_12.15_spmd.clone.sunk | while | flops 1139049216 | bytes 31870896 | solution.py:281
  524.0 13.1 %conditional.7 = ((f32[2304,128]{1,0:T(8,128)}, bf16[6144,256]{0,1:T(8,128)(2,1)})) conditional(s32[]{:T(128)} %convert_element_type.373, (f32[2304,128]{1,0:T(8,128)}, bf16[6144,256]{0,1:T(8,128)(2,1)}) %tuple.120, (s32[]{:T(128)}, s32[384]{0:T(512)S(1)}, s32[]{:T(128)}, bf16[6144,256]{1,0:T(8,128)(2,1)}, bf16[2304,128]{1,0:T(8,128)(2,1)}, ...), branch_computations={%region_13.13_spmd, %region_14.14_spmd} | conditional | flops 1139049216 | bytes 31869082 | solution.py:275
  552.5 8.5 convolution_convert_fusion.2
  564.9 8.5 convolution_convert_fusion.1
  577.3 8.8 convolution_convert_fusion
  606.5 114.3 %reduce-scatter.15.cloned.1.call-done = bf16[384,256]{1,0:T(8,128)(2,1)} async-done(((bf16[6144,256]{1,0:T(8,128)(2,1)}), bf16[384,256]{1,0:T(8,128)(2,1)}) %reduce-scatter.15.cloned.1.call-update) | async-done | bytes 196624 | tf_op jit(solution)/shard_map/reduce_scatter | solution.py:282
  744.6 10.9 %collective-permute-done.13 = bf16[384,1536]{1,0:T(8,128)(2,1)} collective-permute-done((bf16[384,1536]{1,0:T(8,128)(2,1)}, bf16[384,1536]{1,0:T(8,128)(2,1)}, u32[]{:S(2)}, u32[]{:S(2)}) %collective-permute-start.13) | collective-permute-done | bytes 1179680 | tf_op jit(solution)/shard_map/ppermute | solution.py:55
  774.5 14.0 %reduce-scatter.21.cloned.1.call-done = bf16[384,1120]{1,0:T(8,128)(2,1)} async-done(((bf16[1536,1120]{1,0:T(8,128)(2,1)}), bf16[384,1120]{1,0:T(8,128)(2,1)}) %reduce-scatter.21.cloned.1.call-update) | async-done | bytes 860176 | tf_op jit(solution)/shard_map/reduce_scatter | solution.py:90
  792.7 64.8 %reduce-scatter.23.cloned.1.call-done = bf16[384,1120]{1,0:T(8,128)(2,1)} async-done(((bf16[1536,1120]{1,0:T(8,128)(2,1)}), bf16[384,1120]{1,0:T(8,128)(2,1)}) %reduce-scatter.23.cloned.1.call-update) | async-done | bytes 860176 | tf_op jit(solution)/shard_map/reduce_scatter | solution.py:90
  861.7 64.7 %reduce-scatter.25.cloned.1.call-done = bf16[384,1120]{1,0:T(8,128)(2,1)} async-done(((bf16[1536,1120]{1,0:T(8,128)(2,1)}), bf16[384,1120]{1,0:T(8,128)(2,1)}) %reduce-scatter.25.cloned.1.call-update) | async-done | bytes 860176 | tf_op jit(solution)/shard_map/reduce_scatter | solution.py:90
  951.1 42.5 %reduce-scatter.17.cloned.1.call-done = bf16[96,768]{1,0:T(8,128)(2,1)} async-done(((bf16[1536,768]{1,0:T(8,128)(2,1)}), bf16[96,768]{1,0:T(8,128)(2,1)}) %reduce-scatter.17.cloned.1.call-update) | async-done | bytes 147472 | tf_op jit(solution)/shard_map/reduce_scatter | solution.py:248
  998.7 65.9 %reduce-scatter.19.cloned.1.call-done = bf16[96,1152]{1,0:T(8,128)(2,1)} async-done(((bf16[1536,1152]{1,0:T(8,128)(2,1)}), bf16[96,1152]{1,0:T(8,128)(2,1)}) %reduce-scatter.19.cloned.1.call-update) | async-done | bytes 221200 | tf_op jit(solution)/shard_map/reduce_scatter | solution.py:320
  (329 shorter events, 229.6 us)
Async XLA Ops:
  7.2 55.4 %all-gather.7.cloned.1.call-start = ((), (), s32[]{:S(2)}) async-start(), calls=%async_computation.12 | async-start | bytes 3760128 | tf_op jit(solution)/shard_map/all_gather | solution.py:144
  12.5 109.0 %all-gather.9.cloned.1.call-start = ((), (), s32[]{:S(2)}) async-start(), calls=%async_computation.13 | async-start | bytes 3342336 | tf_op jit(solution)/shard_map/all_gather | solution.py:175
  70.3 96.2 %all-gather.11.cloned.1.call-start = ((), (), s32[]{:S(2)}) async-start(), calls=%async_computation.14 | async-start | bytes 2506752 | tf_op jit(solution)/shard_map/all_gather | solution.py:178
  71.1 177.2 %all-gather.13.cloned.1.call-start = ((), (), s32[]{:S(2)}) async-start(), calls=%async_computation.15 | async-start | bytes 4423680 | tf_op jit(solution)/shard_map/all_gather | solution.py:179
  91.4 215.2 %all-gather.15.cloned.1.call-start = ((), (), s32[]{:S(2)}) async-start(), calls=%async_computation.16 | async-start | bytes 4423680 | tf_op jit(solution)/shard_map/all_gather | solution.py:180
  169.4 28.3 %collective-permute-start = (bf16[384,1536]{1,0:T(8,128)(2,1)S(1)}, bf16[384,1536]{1,0:T(8,128)(2,1)}, u32[]{:S(2)}, u32[]{:S(2)}) collective-permute-start(bf16[384,1536]{1,0:T(8,128)(2,1)S(1)} %convolution_convert_fusion.5), channel_id=1, source_target_pairs={{0,1},{1,0},{2,3},{3,2},{4,5},{5,4},{6,7},{7,6},{8,9},{9,8},{10,11... | collective-permute-start | bytes 3538952 | tf_op jit(solution)/shard_map/ppermute | solution.py:55
  174.5 16.7 %all-to-all-start.2 = ((bf16[4,96,1120]{2,1,0:T(8,128)(2,1)}), bf16[4,96,1120]{2,1,0:T(8,128)(2,1)S(1)}, u32[]{:S(2)}, u32[]{:S(2)}) async-start(bf16[4,96,1120]{2,1,0:T(8,128)(2,1)} %bitcast.106), calls=%async_computation.2 | async-start | bytes 1769472 | tf_op jit(solution)/shard_map/all_to_all | solution.py:85
  178.0 199.2 %all-gather.17.cloned.1.call-start = ((), (), s32[]{:S(2)}) async-start(), calls=%async_computation.17 | async-start | bytes 4423680 | tf_op jit(solution)/shard_map/all_gather | solution.py:181
  178.0 38.5 %collective-permute-start.8 = (bf16[384,1536]{1,0:T(8,128)(2,1)}, bf16[384,1536]{1,0:T(8,128)(2,1)}, u32[]{:S(2)}, u32[]{:S(2)}) collective-permute-start(bf16[384,1536]{1,0:T(8,128)(2,1)} %param.37), channel_id=1, source_target_pairs={{0,4},{4,0},{1,5},{5,1},{2,6},{6,2},{3,7},{7,3},{8,12},{12,8},{9,1... | collective-permute-start | bytes 3538952 | tf_op jit(solution)/shard_map/ppermute | solution.py:55
  192.1 528.7 %reduce-scatter.15.cloned.1.call-start = ((), (), s32[]{:S(2)}) async-start(), calls=%async_computation.18 | async-start | bytes 3342336 | tf_op jit(solution)/shard_map/reduce_scatter | solution.py:282
  201.5 39.7 %collective-permute-start.2 = (bf16[384,1536]{1,0:T(8,128)(2,1)}, bf16[384,1536]{1,0:T(8,128)(2,1)}, u32[]{:S(2)}, u32[]{:S(2)}) collective-permute-start(bf16[384,1536]{1,0:T(8,128)(2,1)} %multiply_convert_fusion.3), channel_id=1, source_target_pairs={{0,4},{4,0},{1,5},{5,1},{2,6},{6,2},{3,7},{7,3},{8,12},{12,8},{9,1... | collective-permute-start | bytes 3538952 | tf_op jit(solution)/shard_map/ppermute | solution.py:55
  202.1 41.6 %collective-permute-start.7 = (bf16[384,1536]{1,0:T(8,128)(2,1)}, bf16[384,1536]{1,0:T(8,128)(2,1)S(1)}, u32[]{:S(2)}, u32[]{:S(2)}) collective-permute-start(bf16[384,1536]{1,0:T(8,128)(2,1)} %param.37), channel_id=1, source_target_pairs={{0,2},{2,0},{1,3},{3,1},{4,6},{6,4},{5,7},{7,5},{8,10},{10,8},{9,1... | collective-permute-start | bytes 3538952 | tf_op jit(solution)/shard_map/ppermute | solution.py:55
  216.6 30.6 %collective-permute-start.9 = (bf16[384,1536]{1,0:T(8,128)(2,1)}, bf16[384,1536]{1,0:T(8,128)(2,1)S(1)}, u32[]{:S(2)}, u32[]{:S(2)}) collective-permute-start(bf16[384,1536]{1,0:T(8,128)(2,1)} %collective-permute-done.8), channel_id=1, source_target_pairs={{0,2},{2,0},{1,3},{3,1},{4,6},{6,4},{5,7},{7,5},{8,10},{10,8},{9,1... | collective-permute-start | bytes 3538952 | tf_op jit(solution)/shard_map/ppermute | solution.py:55
  216.6 31.7 %collective-permute-start.1 = (bf16[384,1536]{1,0:T(8,128)(2,1)}, bf16[384,1536]{1,0:T(8,128)(2,1)}, u32[]{:S(2)}, u32[]{:S(2)}) collective-permute-start(bf16[384,1536]{1,0:T(8,128)(2,1)} %multiply_convert_fusion.3), channel_id=1, source_target_pairs={{0,2},{2,0},{1,3},{3,1},{4,6},{6,4},{5,7},{7,5},{8,10},{10,8},{9,1... | collective-permute-start | bytes 3538952 | tf_op jit(solution)/shard_map/ppermute | solution.py:55
  241.3 7.0 collective-permute-start.3
  415.7 12.6 %collective-permute-start.10 = (bf16[768,1536]{1,0:T(8,128)(2,1)S(1)}, bf16[768,1536]{1,0:T(8,128)(2,1)S(1)}, u32[]{:S(2)}, u32[]{:S(2)}) collective-permute-start(bf16[768,1536]{1,0:T(8,128)(2,1)S(1)} %pad_maximum_fusion.3), channel_id=1, source_target_pairs={{0,2},{2,0},{1,3},{3,1},{4,6},{6,4},{5,7},{7,5},{8,10},{10,8},{9,1... | collective-permute-start | bytes 7077896 | tf_op jit(solution)/shard_map/ppermute | solution.py:55
  427.8 4.7 collective-permute-start.4
  429.4 28.9 %collective-permute-start.11 = (bf16[384,1536]{1,0:T(8,128)(2,1)S(1)}, bf16[384,1536]{1,0:T(8,128)(2,1)S(1)}, u32[]{:S(2)}, u32[]{:S(2)}) collective-permute-start(bf16[384,1536]{1,0:T(8,128)(2,1)S(1)} %fusion.46), channel_id=1, source_target_pairs={{0,4},{4,0},{1,5},{5,1},{2,6},{6,2},{3,7},{7,3},{8,12},{12,8},{9,1... | collective-permute-start | bytes 3538952 | tf_op jit(solution)/shard_map/ppermute | solution.py:55
  435.1 47.6 %collective-permute-start.5 = (bf16[384,1536]{1,0:T(8,128)(2,1)S(1)}, bf16[384,1536]{1,0:T(8,128)(2,1)S(1)}, u32[]{:S(2)}, u32[]{:S(2)}) collective-permute-start(bf16[384,1536]{1,0:T(8,128)(2,1)S(1)} %fusion.49), channel_id=1, source_target_pairs={{0,4},{4,0},{1,5},{5,1},{2,6},{6,2},{3,7},{7,3},{8,12},{12,8},{9,1... | collective-permute-start | bytes 3538952 | tf_op jit(solution)/shard_map/ppermute | solution.py:55
  459.0 27.5 %collective-permute-start.12 = (bf16[384,1536]{1,0:T(8,128)(2,1)S(1)}, bf16[384,1536]{1,0:T(8,128)(2,1)S(1)}, u32[]{:S(2)}, u32[]{:S(2)}) collective-permute-start(bf16[384,1536]{1,0:T(8,128)(2,1)S(1)} %fusion.48), channel_id=1, source_target_pairs={{0,1},{1,0},{2,3},{3,2},{4,5},{5,4},{6,7},{7,6},{8,9},{9,8},{10,11... | collective-permute-start | bytes 3538952 | tf_op jit(solution)/shard_map/ppermute | solution.py:55
  485.0 27.1 %collective-permute-start.6 = (bf16[384,1536]{1,0:T(8,128)(2,1)S(1)}, bf16[384,1536]{1,0:T(8,128)(2,1)S(1)}, u32[]{:S(2)}, u32[]{:S(2)}) collective-permute-start(bf16[384,1536]{1,0:T(8,128)(2,1)S(1)} %fusion.51), channel_id=1, source_target_pairs={{0,1},{1,0},{2,3},{3,2},{4,5},{5,4},{6,7},{7,6},{8,9},{9,8},{10,11... | collective-permute-start | bytes 3538952 | tf_op jit(solution)/shard_map/ppermute | solution.py:55
  552.4 236.1 %reduce-scatter.21.cloned.1.call-start = ((), (), s32[]{:S(2)}) async-start(), calls=%async_computation.21 | async-start | bytes 4423680 | tf_op jit(solution)/shard_map/reduce_scatter | solution.py:90
  564.9 292.6 %reduce-scatter.23.cloned.1.call-start = ((), (), s32[]{:S(2)}) async-start(), calls=%async_computation.22 | async-start | bytes 4423680 | tf_op jit(solution)/shard_map/reduce_scatter | solution.py:90
  577.2 349.1 %reduce-scatter.25.cloned.1.call-start = ((), (), s32[]{:S(2)}) async-start(), calls=%async_computation.23 | async-start | bytes 4423680 | tf_op jit(solution)/shard_map/reduce_scatter | solution.py:90
  590.0 403.6 %reduce-scatter.17.cloned.1.call-start = ((), (), s32[]{:S(2)}) async-start(), calls=%async_computation.19 | async-start | bytes 2506752 | tf_op jit(solution)/shard_map/reduce_scatter | solution.py:248
  596.9 467.7 %reduce-scatter.19.cloned.1.call-start = ((), (), s32[]{:S(2)}) async-start(), calls=%async_computation.20 | async-start | bytes 3760128 | tf_op jit(solution)/shard_map/reduce_scatter | solution.py:320
  604.5 118.0 %copy-start.17 = (f32[384]{0:T(512)S(1)}, f32[384]{0:T(512)}, u32[]{:S(2)}) copy-start(f32[384]{0:T(512)} %copy-done.16) | copy-start | bytes 4612
  604.5 118.0 %copy-start.26 = (f32[64]{0:T(128)S(1)}, f32[64]{0:T(128)}, u32[]{:S(2)}) copy-start(f32[64]{0:T(128)} %copy-done.25) | copy-start | bytes 772
  729.5 25.9 %collective-permute-start.13 = (bf16[384,1536]{1,0:T(8,128)(2,1)}, bf16[384,1536]{1,0:T(8,128)(2,1)}, u32[]{:S(2)}, u32[]{:S(2)}) collective-permute-start(bf16[384,1536]{1,0:T(8,128)(2,1)} %fusion.35), channel_id=1, source_target_pairs={{0,1},{1,0},{2,3},{3,2},{4,5},{5,4},{6,7},{7,6},{8,9},{9,8},{10,11... | collective-permute-start | bytes 3538952 | tf_op jit(solution)/shard_map/ppermute | solution.py:55
  788.5 69.0 %all-to-all-start.3 = ((bf16[4,96,1120]{2,1,0:T(8,128)(2,1)}), bf16[4,96,1120]{2,1,0:T(8,128)(2,1)}, u32[]{:S(2)}, u32[]{:S(2)}) async-start(bf16[4,96,1120]{2,1,0:T(8,128)(2,1)} %bitcast.121), calls=%async_computation.5 | async-start | bytes 1769472 | tf_op jit(solution)/shard_map/all_to_all | solution.py:93
  857.5 68.9 %all-to-all-start.4 = ((bf16[4,96,1120]{2,1,0:T(8,128)(2,1)}), bf16[4,96,1120]{2,1,0:T(8,128)(2,1)}, u32[]{:S(2)}, u32[]{:S(2)}) async-start(bf16[4,96,1120]{2,1,0:T(8,128)(2,1)} %bitcast.122), calls=%async_computation.6 | async-start | bytes 1769472 | tf_op jit(solution)/shard_map/all_to_all | solution.py:93
  926.4 17.9 %all-to-all-start.5 = ((bf16[4,96,1120]{2,1,0:T(8,128)(2,1)}), bf16[4,96,1120]{2,1,0:T(8,128)(2,1)}, u32[]{:S(2)}, u32[]{:S(2)}) async-start(bf16[4,96,1120]{2,1,0:T(8,128)(2,1)} %bitcast.120), calls=%async_computation.7 | async-start | bytes 1769472 | tf_op jit(solution)/shard_map/all_to_all | solution.py:93
  (27 other events, 679.5 us)
Sparse Core Ops, SparseCore 0:
  12.7 49.8 all-gather.6
  70.5 51.0 all-gather.8
  123.9 42.6 all-gather.10
  168.0 68.6 all-gather.12
  238.1 68.5 all-gather.14
  308.6 68.5 all-gather.16
  552.5 168.2 reduce-scatter.14
  723.1 65.3 reduce-scatter.20
  790.8 66.6 reduce-scatter.22
  859.7 66.6 reduce-scatter.24
  930.2 63.3 reduce-scatter.16
  997.3 67.2 reduce-scatter.18

commit v2 on v1

--- a/solution.py
+++ b/solution.py
@@ -3,6 +3,8 @@
 import jax
 import jax.numpy as jnp
 from jax import lax
+from jax.experimental import pallas as pl
+from jax.experimental.pallas import tpu as pltpu
 from jax.sharding import Mesh
 from jax.sharding import PartitionSpec as P
 
@@ -47,8 +49,8 @@
     return (back, jnp.sum(grad * normed, axis=0))
 
 
-WIDE = ("z", "x", "c")
-GROUP = ("x", "c")
+WIDE = ("zh", "zl", "x", "c")
+GROUP = ("zl", "c")
 
 
 def other(value, axis):
@@ -61,7 +63,7 @@
 
 def gather_group(own):
     core = other(own, "c")
-    across = other(own, "x")
+    across = other(own, "zl")
     far = other(across, "c")
     return jnp.concatenate([own, core, across, far], axis=0)
 
@@ -70,7 +72,7 @@
     sent = low(jnp.concatenate([partial[rows : 2 * rows], partial[3 * rows :]], axis=0))
     core = other(sent, "c").astype(jnp.float32)
     across = low(partial[2 * rows : 3 * rows] + core[rows:])
-    own = partial[:rows] + core[:rows] + other(across, "x").astype(jnp.float32)
+    own = partial[:rows] + core[:rows] + other(across, "zl").astype(jnp.float32)
     return sum_narrow(own)
 
 
@@ -83,15 +85,188 @@
     features, hidden = weight.shape
     parts = weight.reshape(features, 4, hidden // 4).transpose(1, 0, 2)
     parts = lax.all_to_all(parts, GROUP, split_axis=0, concat_axis=0, tiled=True)
-    return parts.reshape(4 * features, hidden // 4)
+    own = parts.reshape(1, 2, 1, 2 * features, hidden // 4)
+    high = lax.axis_size("zh")
+    at_x = lax.axis_index("x")
+    if high == 2:
+        at_high = lax.axis_index("zh")
+        far = other(own, "zh")
+        whole = jnp.zeros((high, 2, 2, 2 * features, hidden // 4), jnp.bfloat16)
+        for piece, place in ((own, at_high), (far, 1 - at_high)):
+            whole = lax.dynamic_update_slice(whole, piece, (place, 0, at_x, 0, 0))
+        mine = jnp.concatenate([own, far], axis=0)
+        across = other(mine, "x")
+        for number, place in ((0, at_high), (1, 1 - at_high)):
+            whole = lax.dynamic_update_slice(
+                whole, across[number : number + 1], (place, 0, 1 - at_x, 0, 0)
+            )
+    else:
+        mine = lax.all_gather(own, "zh", axis=0, tiled=True)
+        across = other(mine, "x")
+        whole = jnp.zeros((high, 2, 2, 2 * features, hidden // 4), jnp.bfloat16)
+        whole = lax.dynamic_update_slice(whole, mine, (0, 0, at_x, 0, 0))
+        whole = lax.dynamic_update_slice(whole, across, (0, 0, 1 - at_x, 0, 0))
+    return whole.reshape(high * 8 * features, hidden // 4)
+
+
+def halve(grad, axis, position):
+    at = lax.axis_index(axis)
+    sent = lax.dynamic_slice_in_dim(grad, 1 - at, 1, position)
+    kept = lax.dynamic_slice_in_dim(grad, at, 1, position)
+    return low(kept.astype(jnp.float32) + other(sent, axis).astype(jnp.float32))
 
 
 def collect(grad):
-    summed = lax.psum_scatter(low(grad), "z", scatter_dimension=0, tiled=True)
-    features = summed.shape[0] // 4
-    parts = summed.reshape(4, features, summed.shape[1])
+    high = lax.axis_size("zh")
+    features = grad.shape[0] // (8 * high)
+    hidden = grad.shape[1]
+    summed = halve(grad.reshape(high, 2, 2, 2 * features, hidden), "x", 2)
+    if high == 2:
+        summed = halve(summed, "zh", 0)
+    else:
+        summed = lax.psum_scatter(summed, "zh", scatter_dimension=0, tiled=True)
+    parts = summed.reshape(4, features, hidden)
     parts = lax.all_to_all(parts, GROUP, split_axis=0, concat_axis=0, tiled=True)
-    return parts.transpose(1, 0, 2).reshape(features, 4 * summed.shape[1]).astype(jnp.float32)
+    return parts.transpose(1, 0, 2).reshape(features, 4 * hidden).astype(jnp.float32)
+
+
+def rotate_rows(value_rows, cosine, sine):
+    return value_rows * cosine + pltpu.roll(value_rows, value_rows.shape[1] // 2, 1) * sine
+
+
+def mask_bias(place_ref, begin, span):
+    rows = place_ref.shape[1]
+    key_index = begin + lax.broadcasted_iota(jnp.int32, (span, rows), 0)
+    allowed = (key_index >= place_ref[0:1, :]) & (key_index <= place_ref[1:2, :])
+    return jnp.where(allowed, 0.0, -1e30)
+
+
+def turned(value):
+    return value.astype(jnp.float32).T.astype(value.dtype)
+
+
+def attend_kernel(
+    bounds_ref, query_ref, cosine_ref, sine_ref, place_ref, pair_ref,
+    rotated_ref, attended_ref, totals_ref, sums_ref,
+):
+    rows, wide = query_ref.shape
+    head = cosine_ref.shape[1]
+    factor = math.log2(math.e) / math.sqrt(head)
+    cosine = cosine_ref[...]
+    sine = sine_ref[...]
+    for at in range(0, wide, head):
+        rotated_ref[:, at : at + head] = low(
+            rotate_rows(query_ref[:, at : at + head], cosine, sine)
+        )
+    sums_ref[...] = jnp.zeros_like(sums_ref)
+    totals_ref[...] = jnp.zeros_like(totals_ref)
+
+    def step(number, carry):
+        begin = pl.multiple_of(number * rows, rows)
+        keys = pair_ref[pl.ds(begin, rows), :head]
+        values_turned = turned(pair_ref[pl.ds(begin, rows), head:])
+        bias = mask_bias(place_ref, begin, rows)
+        for order in range(wide // head):
+            at = order * head
+            scores = product_right(keys, rotated_ref[:, at : at + head])
+            weights = jnp.exp2(scores * factor + bias)
+            totals_ref[order : order + 1, :] += jnp.sum(weights, axis=0, keepdims=True)
+            sums_ref[at : at + head, :] += product(values_turned, low(weights))
+        return carry
+
+    lax.fori_loop(bounds_ref[0], bounds_ref[1] + 1, step, 0)
+    for order in range(wide // head):
+        at = order * head
+        attended_ref[:, at : at + head] = (
+            sums_ref[at : at + head, :] / totals_ref[order : order + 1, :]
+        ).T
+
+
+def attend_back_kernel(
+    bounds_ref, rotated_ref, accum_ref, delta_ref, cosine_ref, sine_ref, place_ref, pair_ref,
+    grad_query_ref, grad_pair_ref, sums_ref,
+):
+    rows, wide = rotated_ref.shape
+    head = cosine_ref.shape[1]
+    scale = 1.0 / math.sqrt(head)
+    factor = math.log2(math.e) * scale
+
+    def clear(number, carry):
+        begin = pl.multiple_of(number * rows, rows)
+        grad_pair_ref[pl.ds(begin, rows), :] = jnp.zeros((rows, 2 * head), jnp.bfloat16)
+        return carry
+
+    lax.fori_loop(0, grad_pair_ref.shape[0] // rows, clear, 0)
+    sums_ref[...] = jnp.zeros_like(sums_ref)
+
+    def step(number, carry):
+        begin = pl.multiple_of(number * rows, rows)
+        keys = pair_ref[pl.ds(begin, rows), :head]
+        values = pair_ref[pl.ds(begin, rows), head:]
+        keys_turned = turned(keys)
+        bias = mask_bias(place_ref, begin, rows)
+        grad_keys = jnp.zeros((rows, head), jnp.float32)
+        grad_values = jnp.zeros((rows, head), jnp.float32)
+        for order in range(wide // head):
+            at = order * head
+            query = rotated_ref[:, at : at + head]
+            accum = accum_ref[:, at : at + head]
+            weights = jnp.exp2(product_right(keys, query) * factor + bias)
+            grad_scores = low(
+                weights * (product_right(values, accum) - delta_ref[order : order + 1, :])
+            )
+            grad_values += product(low(weights), accum)
+            grad_keys += product(grad_scores, query)
+            sums_ref[at : at + head, :] += product(keys_turned, grad_scores)
+        grad_pair_ref[pl.ds(begin, rows), :head] = low(grad_keys * scale)
+        grad_pair_ref[pl.ds(begin, rows), head:] = low(grad_values)
+        return carry
+
+    lax.fori_loop(bounds_ref[0], bounds_ref[1] + 1, step, 0)
+    cosine = cosine_ref[...]
+    sine = -sine_ref[...]
+    for order in range(wide // head):
+        at = order * head
+        grad_query_ref[:, at : at + head] = low(
+            rotate_rows(sums_ref[at : at + head, :].T * scale, cosine, sine)
+        )
+
+
+def in_vmem(count):
+    return [pl.BlockSpec(memory_space=pltpu.SMEM)] + [
+        pl.BlockSpec(memory_space=pltpu.VMEM) for _ in range(count)
+    ]
+
+
+def attend(bounds, query_pre, cosine, sine, place, pair):
+    rows, wide = query_pre.shape
+    return pl.pallas_call(
+        attend_kernel,
+        out_shape=(
+            jax.ShapeDtypeStruct((rows, wide), jnp.bfloat16),
+            jax.ShapeDtypeStruct((rows, wide), jnp.float32),
+            jax.ShapeDtypeStruct((8 * -(-wide // cosine.shape[1] // 8), rows), jnp.float32),
+        ),
+        in_specs=in_vmem(5),
+        out_specs=tuple(in_vmem(3)[1:]),
+        scratch_shapes=[pltpu.VMEM((wide, rows), jnp.float32)],
+        name="attend",
+    )(bounds, query_pre, cosine, sine, place, pair)
+
+
+def attend_back(bounds, rotated, accum, delta, cosine, sine, place, pair):
+    rows, wide = rotated.shape
+    return pl.pallas_call(
+        attend_back_kernel,
+        out_shape=(
+            jax.ShapeDtypeStruct((rows, wide), jnp.bfloat16),
+            jax.ShapeDtypeStruct(pair.shape, jnp.bfloat16),
+        ),
+        in_specs=in_vmem(7),
+        out_specs=tuple(in_vmem(2)[1:]),
+        scratch_shapes=[pltpu.VMEM((wide, rows), jnp.float32)],
+        name="attend_back",
+    )(bounds, rotated, accum, delta, cosine, sine, place, pair)
 
 
 def local(
@@ -126,8 +301,10 @@
     angle = (index - seq_start).astype(jnp.float32)[:, None] * freq[None, :]
     cosine_table = jnp.cos(angle)[:, None, :]
     sine_table = jnp.sin(angle)[:, None, :]
-    factor = 1.0 / math.sqrt(head)
-    span = rows * max(1, devices // 16)
+    cosine_head = jnp.concatenate([cosine_table[:, 0], cosine_table[:, 0]], axis=1)
+    sine_head = jnp.concatenate([-sine_table[:, 0], sine_table[:, 0]], axis=1)
+    place = jnp.concatenate([seq_start[None], index[None], jnp.zeros((6, rows), jnp.int32)], axis=0)
+    bounds = jnp.stack([lowest // rows, highest // rows])
     features = w_query.shape[0]
     heads_width = w_query.shape[1]
     query_group = heads_width // head
@@ -154,18 +331,15 @@
     bias_key = small_all[:, cuts[3] : cuts[4]].reshape(-1)
     bias_value = small_all[:, cuts[4] : cuts[5]].reshape(-1)
 
-    gate_part = spread(w_gate)
-    up_part_weight = spread(w_up)
-    down_part_weight = spread(w_down.T)
+    gate_all = spread(w_gate)
+    up_all = spread(w_up)
+    down_all = spread(w_down.T)
 
     inputs = tokens.astype(jnp.float32)
     scale_one = norm_scale(inputs)
     normed_one = low(inputs * scale_one * gain_one)
     projections = product(normed_one, w_project)
     query_pre = projections[:, :heads_width] + bias_query
-    query_rows = low(
-        rotate_halves(query_pre.reshape(rows, query_group, head), cosine_table, sine_table)
-    ).reshape(rows * query_group, head)
     key_pre = projections[:, heads_width : heads_width + head] + bias_key
     key_rows = low(
         rotate_halves(key_pre.reshape(rows, 1, head), cosine_table, sine_table).reshape(rows, head)
@@ -176,48 +350,11 @@
         jnp.concatenate([key_rows, value_rows], axis=1), WIDE, axis=0, tiled=True
     )
     w_out_all = lax.all_gather(w_out.T, WIDE, axis=0, tiled=True)
-    gate_all = lax.all_gather(gate_part, "z", axis=0, tiled=True)
-    up_all = lax.all_gather(up_part_weight, "z", axis=0, tiled=True)
-    down_all = lax.all_gather(down_part_weight, "z", axis=0, tiled=True)
-    count = key_value.shape[0]
-
-    def exp_scores(key_block, key_begin):
-        size = key_block.shape[0]
-        key_index = key_begin + jnp.arange(size, dtype=jnp.int32)
-        allowed = (key_index[None, :] >= seq_start[:, None]) & (
-            key_index[None, :] <= index[:, None]
-        )
-        scores = product_right(query_rows, key_block) * factor
-        exp_weights = jnp.where(
-            allowed[:, None, :], jnp.exp(scores.reshape(rows, query_group, size)), 0.0
-        )
-        return exp_weights.reshape(rows * query_group, size)
-
-    def is_live(key_begin, size):
-        return (key_begin + size > lowest) & (key_begin <= highest)
-
-    initial = (
-        jnp.zeros((rows * query_group, head), jnp.float32),
-        jnp.zeros((rows * query_group,), jnp.float32),
-    )
-
-    def turn(step, state):
-        offset = step * span
-
-        def turn_compute(inner):
-            weighted, totals = inner
-            block = lax.dynamic_slice_in_dim(key_value, offset, span, 0)
-            exp_weights = exp_scores(block[:, :head], offset)
-            return (
-                weighted + product(low(exp_weights), block[:, head:]),
-                totals + jnp.sum(exp_weights, axis=1),
-            )
-
-        return lax.cond(is_live(offset, span), turn_compute, lambda inner: inner, state)
-
-    weighted, totals = lax.fori_loop(0, count // span, turn, initial)
-    attended = weighted / totals[:, None]
-    attended_low = low(attended.reshape(rows, heads_width))
+    query_rows, attended, totals = attend(
+        bounds, query_pre, cosine_head, sine_head, place, key_value
+    )
+    totals = totals[:query_group]
+    attended_low = low(attended)
     middle = inputs + sum_narrow(product_right(attended_low, w_out_all))
     scale_two = norm_scale(middle)
     normed_two = low(middle * scale_two * gain_two)
@@ -230,16 +367,21 @@
     silu_gate = gate * sigmoid_gate
     hidden = low(silu_gate * up_part)
     result = low(middle + scatter_group(product_right(hidden, down_all), rows))
-    grad_down = product_left(cotangent_group, hidden)
+    grad_down = low(product_left(cotangent_group, hidden))
     grad_hidden = product(cotangent_group, down_all)
     grad_gate = low(grad_hidden * up_part * sigmoid_gate * (1.0 + gate * (1.0 - sigmoid_gate)))
     grad_up = low(grad_hidden * silu_gate)
     grad_normed_two = scatter_group(
         product_right(grad_gate, gate_all) + product_right(grad_up, up_all), rows
     )
+    grad_gate_all = low(product_left(normed_group, grad_gate))
+    grad_up_all = low(product_left(normed_group, grad_up))
+    grad_normed_two, grad_gate_all, grad_up_all, grad_down = lax.optimization_barrier(
+        (grad_normed_two, grad_gate_all, grad_up_all, grad_down)
+    )
     grad_w_down = collect(grad_down).T
-    grad_w_gate = collect(product_left(normed_group, grad_gate))
-    grad_w_up = collect(product_left(normed_group, grad_up))
+    grad_w_gate = collect(grad_gate_all)
+    grad_w_up = collect(grad_up_all)
 
     back_two, grad_gain_two = norm_back(middle, scale_two, gain_two, grad_normed_two)
     grad_middle = cotangent.astype(jnp.float32) + back_two
@@ -251,42 +393,17 @@
         .astype(jnp.float32)
         .T
     )
-    grad_attended = product(grad_att, w_out_all).reshape(rows * query_group, head)
-    grad_accum = low(grad_attended / totals[:, None])
-    delta = jnp.sum(grad_attended * attended, axis=1) / totals
-
-    def back_turn(step, state):
-        offset = step * span
-
-        def back_compute(inner):
-            grad_queries, buffer = inner
-            block = lax.dynamic_slice_in_dim(key_value, offset, span, 0)
-            exp_weights = exp_scores(block[:, :head], offset)
-            grad_probs = product_right(grad_accum, block[:, head:])
-            grad_scores = low(exp_weights * (grad_probs - delta[:, None]))
-            grad_keys = product_left(grad_scores, query_rows) * factor
-            grad_values = product_left(low(exp_weights), grad_accum)
-            update = low(jnp.concatenate([grad_keys, grad_values], axis=1))
-            return (
-                grad_queries + product(grad_scores, block[:, :head]),
-                lax.dynamic_update_slice_in_dim(buffer, update, offset, 0),
-            )
-
-        return lax.cond(is_live(offset, span), back_compute, lambda inner: inner, state)
-
-    start_state = (
-        jnp.zeros((rows * query_group, head), jnp.float32),
-        jnp.zeros((count, 2 * head), jnp.bfloat16),
-    )
-    grad_queries, buffer = lax.fori_loop(0, count // span, back_turn, start_state)
+    grad_attended = product(grad_att, w_out_all).reshape(rows, query_group, head)
+    divided = grad_attended / totals.T[:, :, None]
+    grad_accum = low(divided).reshape(rows, heads_width)
+    delta = jnp.sum(divided * attended.reshape(rows, query_group, head), axis=2).T
+    delta = jnp.pad(delta, ((0, -query_group % 8), (0, 0)))
+    grad_query_pre, buffer = attend_back(
+        bounds, query_rows, grad_accum, delta, cosine_head, sine_head, place, key_value
+    )
     key_value_grads = lax.psum_scatter(buffer, WIDE, scatter_dimension=0, tiled=True).astype(
         jnp.float32
     )
-    grad_query_pre = low(
-        rotate_halves(
-            (grad_queries * factor).reshape(rows, query_group, head), cosine_table, -sine_table
-        )
-    ).reshape(rows, heads_width)
     grad_key_pre = low(
         rotate_halves(key_value_grads[:, :head].reshape(rows, 1, head), cosine_table, -sine_table)
     ).reshape(rows, head)
@@ -341,7 +458,7 @@
 
 def solution(mesh):
     wide, narrow = mesh.devices.shape
-    grouped = Mesh(mesh.devices.reshape(wide // 4, 2, 2, narrow), WIDE + ("y",))
+    grouped = Mesh(mesh.devices.reshape(wide // 8, 2, 2, 2, narrow), WIDE + ("y",))
     rows = P(WIDE, None)
     vector = P(WIDE)
     columns = P(WIDE, "y")

time: 1090 us -> 873 us (0.80)
  waiting for transfers between devices: 678 us -> 398 us
  starting transfers between devices: 29.8 us -> 104 us
  blocking collectives: 40.2 us -> 0 us
  local copies, waits for them, and re-layouts: 106 us -> 130 us
  other arithmetic: 52.5 us -> 75.6 us
  loops' own time: 22.9 us -> 0 us
  Pallas kernels: 0 us -> 13.6 us
  matrix products: 133 us -> 122 us
    ppermute x14 -> x26, waiting for transfers between devices: 124 us -> 279 us  [other(): return lax.ppermute(value, axis, [(0, 1), (1, 0)])]
    reduce_scatter x3 -> x0, waiting for transfers between devices: 143 us -> none  [collect(): summed = lax.psum_scatter(low(grad), 'z', scatter_dimension=0, tiled=True)]
    reduce_scatter x1, waiting for transfers between devices: 114 us -> 1.92 us  [local(): lax.psum_scatter(buffer, WIDE, scatter_dimension=0, tiled=True)]
    all_gather x3 -> x0, waiting for transfers between devices: 105 us -> none  [the longest x1 58.5 us: local(): down_all = lax.all_gather(down_part_weight, 'z', axis=0, tiled=True)]
    ppermute x14 -> x26, starting transfers between devices: 12.7 us -> 67.1 us  [other(): return lax.ppermute(value, axis, [(0, 1), (1, 0)])]
    reduce_scatter x1, waiting for transfers between devices: 42.5 us -> 0.02 us  [local(): lax.psum_scatter(low(product_left(grad_att, attended_low)), WIDE, scatter...]
    reduce_scatter x1, waiting for transfers between devices: 65.9 us -> 25.2 us  [local(): lax.psum_scatter(packed_grads, WIDE, scatter_dimension=0, tiled=True)]
    all_to_all x2 -> x0, blocking collectives: 40.2 us -> none  [spread(): lax.all_to_all(parts, GROUP, split_axis=0, concat_axis=0, tiled=True)]
  transfers between devices with their start and end apart: 30 -> 38, of which waited for: 20 -> 20; matrix products, arithmetic and copies ran while one was open for 19% -> 28% of each run, Pallas kernels for 0% -> 1%
where the time goes in v2:
time: 873 us; the launch traced here: 862 us
  waiting for transfers between devices  398 us (46%)
  local copies, waits for them, and re-layouts  130 us (15%)
  matrix products  122 us (14%)
  starting transfers between devices  104 us (12%)
  other arithmetic  75.6 us (9%)
  between operations  17.4 us (2%)
  Pallas kernels  13.6 us (2%)
    ppermute x26, waiting for transfers between devices, other(): return lax.ppermute(value, axis, [(0, 1), (1, 0)])  279 us
    ppermute x26, starting transfers between devices, other(): return lax.ppermute(value, axis, [(0, 1), (1, 0)])  67.1 us
    all_to_all x3, waiting for transfers between devices, spread(): lax.all_to_all(parts, GROUP, split_axis=0, concat_axis=0, tiled=True)  46.2 us
    all_gather x1, waiting for transfers between devices, local(): w_project = lax.all_gather(packed, WIDE, axis=0, tiled=True)  46.1 us
    dot_general x5, matrix products, product(): return jnp.dot(left, right, preferred_element_type=jnp.float32)  45.4 us
    dot_general x5, matrix products, product_right(): lax.dot_general(left, right, (((1,), (1,)), ((), ())), preferred_element_...  40.2 us
    dot_general x5, matrix products, product_left(): lax.dot_general(left, right, (((0,), (0,)), ((), ())), preferred_element_...  36.3 us
    all_to_all x3, starting transfers between devices, collect(): lax.all_to_all(parts, GROUP, split_axis=0, concat_axis=0, tiled=True)  26 us
  transfers between devices with their start and end apart: 38, of which 20 were waited for; matrix products, arithmetic and copies ran while one was open for 28% of the time, Pallas kernels for 1%

profile of v2, /device:TPU:0, one launch (start us, length us, event | category | flops | bytes accessed | tf_op | source)
XLA Modules:
  0.0 861.6 jit_solution(9018766812379321253)
XLA Ops:
  16.4 46.1 %all-gather.4.cloned.1.call-done = bf16[1536,1152]{1,0:T(8,128)(2,1)} async-done(((bf16[96,1152]{1,0:T(8,128)(2,1)}), bf16[1536,1152]{1,0:T(8,128)(2,1)}) %all-gather.4.cloned.1.call-update) | async-done | bytes 3538960 | tf_op jit(solution)/shard_map/all_gather | solution.py:321
  79.5 15.4 %all-to-all-done.2 = bf16[4,96,1120]{2,1,0:T(8,128)(2,1)S(1)} async-done(((bf16[4,96,1120]{2,1,0:T(8,128)(2,1)}), bf16[4,96,1120]{2,1,0:T(8,128)(2,1)S(1)}, u32[]{:S(2)}, u32[]{:S(2)}) %all-to-all-start.2) | async-done | bytes 860192 | tf_op jit(solution)/shard_map/all_to_all | solution.py:87
  106.6 16.3 %all-to-all-done.1 = bf16[4,96,1120]{2,1,0:T(8,128)(2,1)S(1)} async-done(((bf16[4,96,1120]{2,1,0:T(8,128)(2,1)}), bf16[4,96,1120]{2,1,0:T(8,128)(2,1)S(1)}, u32[]{:S(2)}, u32[]{:S(2)}) %all-to-all-start.1) | async-done | bytes 860192 | tf_op jit(solution)/shard_map/all_to_all | solution.py:87
  132.8 20.2 %collective-permute-done.14 = bf16[384,1536]{1,0:T(8,128)(2,1)} collective-permute-done((bf16[384,1536]{1,0:T(8,128)(2,1)}, bf16[384,1536]{1,0:T(8,128)(2,1)}, u32[]{:S(2)}, u32[]{:S(2)}) %collective-permute-start.14) | collective-permute-done | bytes 1179680 | tf_op jit(solution)/shard_map/ppermute | solution.py:57
  160.9 14.4 %all-to-all-done = bf16[4,96,1120]{2,1,0:T(8,128)(2,1)} async-done(((bf16[4,96,1120]{2,1,0:T(8,128)(2,1)}), bf16[4,96,1120]{2,1,0:T(8,128)(2,1)}, u32[]{:S(2)}, u32[]{:S(2)}) %all-to-all-start) | async-done | bytes 860192 | tf_op jit(solution)/shard_map/all_to_all | solution.py:87
  183.6 60.8 %collective-permute-done.6 = bf16[1,2,1,192,1120]{4,3,1,2,0:T(8,128)(2,1)} collective-permute-done((bf16[1,2,1,192,1120]{4,3,1,2,0:T(8,128)(2,1)S(1)}, bf16[1,2,1,192,1120]{4,3,1,2,0:T(8,128)(2,1)}, u32[]{:S(2)}, u32[]{:S(2)}) %collective-permute-start.6) | collective-permute-done | bytes 860192 | tf_op jit(solution)/shard_map/ppermute | solution.py:57
  248.5 14.8 %collective-permute-done.8 = bf16[1,2,1,192,1120]{4,3,1,2,0:T(8,128)(2,1)} collective-permute-done((bf16[1,2,1,192,1120]{4,3,1,2,0:T(8,128)(2,1)S(1)}, bf16[1,2,1,192,1120]{4,3,1,2,0:T(8,128)(2,1)}, u32[]{:S(2)}, u32[]{:S(2)}) %collective-permute-start.8) | collective-permute-done | bytes 860192 | tf_op jit(solution)/shard_map/ppermute | solution.py:57
  267.4 14.3 %collective-permute-done.4 = bf16[1,2,1,192,1120]{4,3,1,2,0:T(8,128)(2,1)S(1)} collective-permute-done((bf16[1,2,1,192,1120]{4,3,1,2,0:T(8,128)(2,1)}, bf16[1,2,1,192,1120]{4,3,1,2,0:T(8,128)(2,1)S(1)}, u32[]{:S(2)}, u32[]{:S(2)}) %collective-permute-start.4) | collective-permute-done | bytes 860192 | tf_op jit(solution)/shard_map/ppermute | solution.py:57
  295.4 6.2 attend.1
  309.7 17.0 %collective-permute-done.9 = bf16[2,2,1,192,1120]{4,3,1,2,0:T(8,128)(2,1)S(1)} collective-permute-done((bf16[2,2,1,192,1120]{4,3,1,2,0:T(8,128)(2,1)}, bf16[2,2,1,192,1120]{4,3,1,2,0:T(8,128)(2,1)S(1)}, u32[]{:S(2)}, u32[]{:S(2)}) %collective-permute-start.9) | collective-permute-done | bytes 1720352 | tf_op jit(solution)/shard_map/ppermute | solution.py:57
  337.5 6.3 collective-permute-start.2
  344.8 18.1 %collective-permute-done.5 = bf16[2,2,1,192,1120]{4,3,1,2,0:T(8,128)(2,1)} collective-permute-done((bf16[2,2,1,192,1120]{4,3,1,2,0:T(8,128)(2,1)}, bf16[2,2,1,192,1120]{4,3,1,2,0:T(8,128)(2,1)}, u32[]{:S(2)}, u32[]{:S(2)}) %collective-permute-start.5) | collective-permute-done | bytes 1720352 | tf_op jit(solution)/shard_map/ppermute | solution.py:57
  370.2 10.3 %fusion.75 = f32[1536,1120]{0,1:T(8,128)} fusion(bf16[1536,1536]{1,0:T(8,128)(2,1)S(1)} %copy-done.29, bf16[1536,1120]{1,0:T(8,128)(2,1)} %bitcast.36), kind=kOutput, calls=%fused_computation.171 | convolution fusion | flops 5284823040 | bytes 15040512 | tf_op jit(solution)/shard_map/dot_general | solution.py:16
  380.6 12.8 %fusion.64 = f32[1536,1120]{0,1:T(8,128)} fusion(bf16[1536,1120]{1,0:T(8,128)(2,1)} %bitcast.28, bf16[384,1536]{1,0:T(8,128)(2,1)S(1)} %collective-permute-done.3, bf16[384,1536]{1,0:T(8,128)(2,1)S(1)} %collective-permute-done.2, bf16[384,1536]{1,0:T(8,128)(2,1)S(1)} %collective-permute-done.1, bf16[384,1536]{1,0:T(8,128)(2,1)S(1)} %multiply_convert_fusion.3), kind=kOutput, calls=%fused_computation.160 | convolution fusion | flops 5303697408 | bytes 15040512 | tf_op jit(solution)/shard_map/dot_general | solution.py:16
  393.4 16.2 %multiply_convert_fusion.1 = (bf16[1536,1120]{0,1:T(8,128)(2,1)}, bf16[1536,1120]{0,1:T(8,128)(2,1)}, bf16[1536,1120]{0,1:T(8,128)(2,1)}) fusion(f32[1536,1120]{0,1:T(8,128)} %fusion.75, f32[1536,1120]{0,1:T(8,128)} %fusion.64, bf16[1536,1120]{1,0:T(8,128)(2,1)S(1)} %bitcast.146, bf16[384,1536]{1,0:T(8,128)(2,1)} %copy-done.51, ...), kind=kOutput, calls=%fused_computation.5 | convolution fusion | flops 5329502208 | bytes 32243712 | tf_op jit(solution)/shard_map/dot_general | solution.py:16
  409.6 9.4 %fusion.76 = f32[1536,1536]{1,0:T(8,128)S(1)} fusion(bf16[1536,1120]{0,1:T(8,128)(2,1)} %get-tuple-element.81, bf16[1536,1120]{1,0:T(8,128)(2,1)} %bitcast.28), kind=kOutput, calls=%fused_computation.172 | convolution fusion | flops 5284823040 | bytes 16318464 | tf_op jit(solution)/shard_map/dot_general | solution.py:26
  419.0 11.3 %fusion.73 = (bf16[1536,1536]{1,0:T(8,128)(2,1)S(1)}, f32[1536,1536]{1,0:T(8,128)}) fusion(f32[1536,1536]{1,0:T(8,128)S(1)} %fusion.76, bf16[1536,1120]{0,1:T(8,128)(2,1)} %get-tuple-element.80, bf16[1536,1120]{1,0:T(8,128)(2,1)S(1)} %bitcast.147), kind=kOutput, calls=%fused_computation.169 | convolution fusion | flops 5289541632 | bytes 30474240 | tf_op jit(solution)/shard_map/dot_general | solution.py:26
  433.3 10.9 %fusion.74 = (bf16[1536,1536]{1,0:T(8,128)(2,1)S(1)}, f32[1536,1536]{1,0:T(8,128)}) fusion(bf16[1536,1120]{0,1:T(8,128)(2,1)S(1)} %copy-done.53, bf16[1536,1120]{1,0:T(8,128)(2,1)} %bitcast.36), kind=kOutput, calls=%fused_computation.170 | convolution fusion | flops 5287182336 | bytes 21037056 | tf_op jit(solution)/shard_map/dot_general | solution.py:26
  448.2 9.9 %convolution_convert_fusion = bf16[1536,1120]{0,1:T(8,128)(2,1)} fusion(bf16[1536,1120]{0,1:T(8,128)(2,1)} %get-tuple-element.82, bf16[1536,1536]{1,0:T(8,128)(2,1)} %constant_dynamic-update-slice_fusion), kind=kOutput, calls=%fused_computation.1 | convolution fusion | flops 5286543360 | bytes 11599872 | tf_op jit(solution)/shard_map/dot_general | solution.py:20
  466.8 9.7 %convolution_convert_fusion.1 = bf16[1536,1120]{0,1:T(8,128)(2,1)} fusion(bf16[1536,1120]{0,1:T(8,128)(2,1)} %get-tuple-element.81, bf16[384,1536]{1,0:T(8,128)(2,1)} %copy-done.51, bf16[384,1536]{1,0:T(8,128)(2,1)} %copy-done.47, bf16[384,1536]{1,0:T(8,128)(2,1)} %copy-done.49, bf16[384,1536]{1,0:T(8,128)(2,1)S(1)} %copy-done.19), kind=kOutput, calls=%fused_computation.2 | convolution fusion | flops 5305417728 | bytes 11599872 | tf_op jit(solution)/shard_map/dot_general | solution.py:20
  476.5 13.5 %collective-permute-done.17 = bf16[384,1536]{1,0:T(8,128)(2,1)} collective-permute-done((bf16[384,1536]{1,0:T(8,128)(2,1)S(1)}, bf16[384,1536]{1,0:T(8,128)(2,1)}, u32[]{:S(2)}, u32[]{:S(2)}) %collective-permute-start.17) | collective-permute-done | bytes 1179680 | tf_op jit(solution)/shard_map/ppermute | solution.py:57
  493.5 21.0 %collective-permute-done.11 = bf16[384,1536]{1,0:T(8,128)(2,1)} collective-permute-done((bf16[384,1536]{1,0:T(8,128)(2,1)}, bf16[384,1536]{1,0:T(8,128)(2,1)}, u32[]{:S(2)}, u32[]{:S(2)}) %collective-permute-start.11) | collective-permute-done | bytes 1179680 | tf_op jit(solution)/shard_map/ppermute | solution.py:57
  517.9 9.0 %convolution_convert_fusion.2 = bf16[1536,1120]{0,1:T(8,128)(2,1)} fusion(bf16[1536,1120]{0,1:T(8,128)(2,1)} %get-tuple-element.80, bf16[384,1536]{1,0:T(8,128)(2,1)S(1)} %copy-done.52, bf16[384,1536]{1,0:T(8,128)(2,1)S(1)} %copy-done.48, bf16[384,1536]{1,0:T(8,128)(2,1)S(1)} %copy-done.50, bf16[384,1536]{1,0:T(8,128)(2,1)S(1)} %copy-done.20), kind=kOutput, calls=%fused_computation.3 | convolution fusion | flops 5305417728 | bytes 11599872 | tf_op jit(solution)/shard_map/dot_general | solution.py:20
  529.3 14.4 %collective-permute-done.12 = bf16[384,1536]{1,0:T(8,128)(2,1)S(1)} collective-permute-done((bf16[384,1536]{1,0:T(8,128)(2,1)S(1)}, bf16[384,1536]{1,0:T(8,128)(2,1)S(1)}, u32[]{:S(2)}, u32[]{:S(2)}) %collective-permute-start.12) | collective-permute-done | bytes 1179680 | tf_op jit(solution)/shard_map/ppermute | solution.py:57
  552.7 7.4 attend_back.1
  596.3 16.5 %collective-permute-done.24 = bf16[2,2,1,192,1120]{4,3,2,1,0:T(8,128)(2,1)} collective-permute-done((bf16[2,2,1,192,1120]{4,3,2,1,0:T(8,128)(2,1)}, bf16[2,2,1,192,1120]{4,3,2,1,0:T(8,128)(2,1)}, u32[]{:S(2)}, u32[]{:S(2)}) %collective-permute-start.24) | collective-permute-done | bytes 1720352 | tf_op jit(solution)/shard_map/ppermute | solution.py:57
  616.7 20.4 %collective-permute-start.25 = (bf16[1,2,1,192,1120]{4,3,2,1,0:T(8,128)(2,1)}, bf16[1,2,1,192,1120]{4,3,2,1,0:T(8,128)(2,1)}, u32[]{:S(2)}, u32[]{:S(2)}) collective-permute-start(bf16[1,2,1,192,1120]{4,3,2,1,0:T(8,128)(2,1)} %constant_dynamic-slice_fusion), channel_id=1, source_target_pairs={{0,16},{16,0},{1,17},{17,1},{2,18},{18,2},{3,19},{19,3},{4,20},{20... | collective-permute-start | bytes 2580488 | tf_op jit(solution)/shard_map/ppermute | solution.py:57
  637.2 24.1 %collective-permute-done.22 = bf16[2,2,1,192,1120]{4,3,2,1,0:T(8,128)(2,1)} collective-permute-done((bf16[2,2,1,192,1120]{4,3,2,1,0:T(8,128)(2,1)}, bf16[2,2,1,192,1120]{4,3,2,1,0:T(8,128)(2,1)}, u32[]{:S(2)}, u32[]{:S(2)}) %collective-permute-start.22) | collective-permute-done | bytes 1720352 | tf_op jit(solution)/shard_map/ppermute | solution.py:57
  665.4 12.6 %collective-permute-start.23 = (bf16[1,2,1,192,1120]{4,3,2,1,0:T(8,128)(2,1)}, bf16[1,2,1,192,1120]{4,3,2,1,0:T(8,128)(2,1)}, u32[]{:S(2)}, u32[]{:S(2)}) collective-permute-start(bf16[1,2,1,192,1120]{4,3,2,1,0:T(8,128)(2,1)} %constant_dynamic-slice_fusion.2), channel_id=1, source_target_pairs={{0,16},{16,0},{1,17},{17,1},{2,18},{18,2},{3,19},{19,3},{4,20},{20... | collective-permute-start | bytes 2580488 | tf_op jit(solution)/shard_map/ppermute | solution.py:57
  690.1 17.2 %all-to-all-start.5 = ((bf16[4,96,1120]{2,1,0:T(8,128)(2,1)}), bf16[4,96,1120]{2,1,0:T(8,128)(2,1)}, u32[]{:S(2)}, u32[]{:S(2)}) async-start(bf16[4,96,1120]{2,1,0:T(8,128)(2,1)} %bitcast.140), calls=%async_computation.7 | async-start | bytes 1769472 | tf_op jit(solution)/shard_map/all_to_all | solution.py:129
  754.1 36.5 %collective-permute-done.21 = bf16[1,2,1,192,1120]{4,3,2,1,0:T(8,128)(2,1)} collective-permute-done((bf16[1,2,1,192,1120]{4,3,2,1,0:T(8,128)(2,1)}, bf16[1,2,1,192,1120]{4,3,2,1,0:T(8,128)(2,1)}, u32[]{:S(2)}, u32[]{:S(2)}) %collective-permute-start.21) | collective-permute-done | bytes 860192 | tf_op jit(solution)/shard_map/ppermute | solution.py:57
  822.9 25.2 %reduce-scatter.10.cloned.1.call-done = bf16[96,1152]{1,0:T(8,128)(2,1)} async-done(((bf16[1536,1152]{1,0:T(8,128)(2,1)}), bf16[96,1152]{1,0:T(8,128)(2,1)}) %reduce-scatter.10.cloned.1.call-update) | async-done | bytes 221200 | tf_op jit(solution)/shard_map/reduce_scatter | solution.py:437
  (335 shorter events, 285.8 us)
Async XLA Ops:
  7.2 55.4 %all-gather.4.cloned.1.call-start = ((), (), s32[]{:S(2)}) async-start(), calls=%async_computation.9 | async-start | bytes 3760128 | tf_op jit(solution)/shard_map/all_gather | solution.py:321
  12.5 282.9 %all-gather.6.cloned.1.call-start = ((), (), s32[]{:S(2)}) async-start(), calls=%async_computation.10 | async-start | bytes 3342336 | tf_op jit(solution)/shard_map/all_gather | solution.py:349
  94.9 28.1 %all-to-all-start.1 = ((bf16[4,96,1120]{2,1,0:T(8,128)(2,1)}), bf16[4,96,1120]{2,1,0:T(8,128)(2,1)S(1)}, u32[]{:S(2)}, u32[]{:S(2)}) async-start(bf16[4,96,1120]{2,1,0:T(8,128)(2,1)} %copy.137), calls=%async_computation.1 | async-start | bytes 1769472 | tf_op jit(solution)/shard_map/all_to_all | solution.py:87
  98.4 203.3 %all-gather.8.cloned.1.call-start = ((), (), s32[]{:S(2)}) async-start(), calls=%async_computation.11 | async-start | bytes 2506752 | tf_op jit(solution)/shard_map/all_gather | solution.py:352
  98.4 54.6 %collective-permute-start.14 = (bf16[384,1536]{1,0:T(8,128)(2,1)}, bf16[384,1536]{1,0:T(8,128)(2,1)}, u32[]{:S(2)}, u32[]{:S(2)}) collective-permute-start(bf16[384,1536]{1,0:T(8,128)(2,1)} %param.29), channel_id=1, source_target_pairs={{0,8},{8,0},{1,9},{9,1},{2,10},{10,2},{3,11},{11,3},{4,12},{12,4},... | collective-permute-start | bytes 3538952 | tf_op jit(solution)/shard_map/ppermute | solution.py:57
  100.4 52.7 %collective-permute-start.13 = (bf16[384,1536]{1,0:T(8,128)(2,1)}, bf16[384,1536]{1,0:T(8,128)(2,1)}, u32[]{:S(2)}, u32[]{:S(2)}) collective-permute-start(bf16[384,1536]{1,0:T(8,128)(2,1)} %param.29), channel_id=1, source_target_pairs={{0,2},{2,0},{1,3},{3,1},{4,6},{6,4},{5,7},{7,5},{8,10},{10,8},{9,1... | collective-permute-start | bytes 3538952 | tf_op jit(solution)/shard_map/ppermute | solution.py:57
  122.9 52.4 %all-to-all-start = ((bf16[4,96,1120]{2,1,0:T(8,128)(2,1)}), bf16[4,96,1120]{2,1,0:T(8,128)(2,1)}, u32[]{:S(2)}, u32[]{:S(2)}) async-start(bf16[4,96,1120]{2,1,0:T(8,128)(2,1)} %copy.132), calls=%async_computation | async-start | bytes 1769472 | tf_op jit(solution)/shard_map/all_to_all | solution.py:87
  127.2 552.7 %reduce-scatter.6.cloned.1.call-start = ((), (), s32[]{:S(2)}) async-start(), calls=%async_computation.12 | async-start | bytes 3342336 | tf_op jit(solution)/shard_map/reduce_scatter | solution.py:404
  153.1 154.2 %collective-permute-start.15 = (bf16[384,1536]{1,0:T(8,128)(2,1)}, bf16[384,1536]{1,0:T(8,128)(2,1)}, u32[]{:S(2)}, u32[]{:S(2)}) collective-permute-start(bf16[384,1536]{1,0:T(8,128)(2,1)} %collective-permute-done.14), channel_id=1, source_target_pairs={{0,2},{2,0},{1,3},{3,1},{4,6},{6,4},{5,7},{7,5},{8,10},{10,8},{9,1... | collective-permute-start | bytes 3538952 | tf_op jit(solution)/shard_map/ppermute | solution.py:57
  154.4 90.0 %collective-permute-start.6 = (bf16[1,2,1,192,1120]{4,3,1,2,0:T(8,128)(2,1)S(1)}, bf16[1,2,1,192,1120]{4,3,1,2,0:T(8,128)(2,1)}, u32[]{:S(2)}, u32[]{:S(2)}) collective-permute-start(bf16[1,2,1,192,1120]{4,3,1,2,0:T(8,128)(2,1)S(1)} %bitcast.134), channel_id=1, source_target_pairs={{0,16},{16,0},{1,17},{17,1},{2,18},{18,2},{3,19},{19,3},{4,20},{20... | collective-permute-start | bytes 2580488 | tf_op jit(solution)/shard_map/ppermute | solution.py:57
  160.4 103.0 %collective-permute-start.8 = (bf16[1,2,1,192,1120]{4,3,1,2,0:T(8,128)(2,1)S(1)}, bf16[1,2,1,192,1120]{4,3,1,2,0:T(8,128)(2,1)}, u32[]{:S(2)}, u32[]{:S(2)}) collective-permute-start(bf16[1,2,1,192,1120]{4,3,1,2,0:T(8,128)(2,1)S(1)} %bitcast.131), channel_id=1, source_target_pairs={{0,16},{16,0},{1,17},{17,1},{2,18},{18,2},{3,19},{19,3},{4,20},{20... | collective-permute-start | bytes 2580488 | tf_op jit(solution)/shard_map/ppermute | solution.py:57
  175.3 106.4 %collective-permute-start.4 = (bf16[1,2,1,192,1120]{4,3,1,2,0:T(8,128)(2,1)}, bf16[1,2,1,192,1120]{4,3,1,2,0:T(8,128)(2,1)S(1)}, u32[]{:S(2)}, u32[]{:S(2)}) collective-permute-start(bf16[1,2,1,192,1120]{4,3,1,2,0:T(8,128)(2,1)} %bitcast.16), channel_id=1, source_target_pairs={{0,16},{16,0},{1,17},{17,1},{2,18},{18,2},{3,19},{19,3},{4,20},{20... | collective-permute-start | bytes 2580488 | tf_op jit(solution)/shard_map/ppermute | solution.py:57
  247.1 62.6 %collective-permute-start.7 = (bf16[2,2,1,192,1120]{4,3,1,2,0:T(8,128)(2,1)}, bf16[2,2,1,192,1120]{4,3,1,2,0:T(8,128)(2,1)}, u32[]{:S(2)}, u32[]{:S(2)}) collective-permute-start(bf16[2,2,1,192,1120]{4,3,1,2,0:T(8,128)(2,1)} %pad_maximum_fusion.5), channel_id=1, source_target_pairs={{0,4},{4,0},{1,5},{5,1},{2,6},{6,2},{3,7},{7,3},{8,12},{12,8},{9,1... | collective-permute-start | bytes 5160968 | tf_op jit(solution)/shard_map/ppermute | solution.py:57
  266.0 60.7 %collective-permute-start.9 = (bf16[2,2,1,192,1120]{4,3,1,2,0:T(8,128)(2,1)}, bf16[2,2,1,192,1120]{4,3,1,2,0:T(8,128)(2,1)S(1)}, u32[]{:S(2)}, u32[]{:S(2)}) collective-permute-start(bf16[2,2,1,192,1120]{4,3,1,2,0:T(8,128)(2,1)} %pad_maximum_fusion.6), channel_id=1, source_target_pairs={{0,4},{4,0},{1,5},{5,1},{2,6},{6,2},{3,7},{7,3},{8,12},{12,8},{9,1... | collective-permute-start | bytes 5160968 | tf_op jit(solution)/shard_map/ppermute | solution.py:57
  284.4 78.5 %collective-permute-start.5 = (bf16[2,2,1,192,1120]{4,3,1,2,0:T(8,128)(2,1)}, bf16[2,2,1,192,1120]{4,3,1,2,0:T(8,128)(2,1)}, u32[]{:S(2)}, u32[]{:S(2)}) collective-permute-start(bf16[2,2,1,192,1120]{4,3,1,2,0:T(8,128)(2,1)} %pad_maximum_fusion.4), channel_id=1, source_target_pairs={{0,4},{4,0},{1,5},{5,1},{2,6},{6,2},{3,7},{7,3},{8,12},{12,8},{9,1... | collective-permute-start | bytes 5160968 | tf_op jit(solution)/shard_map/ppermute | solution.py:57
  305.8 29.0 %collective-permute-start = (bf16[384,1536]{1,0:T(8,128)(2,1)}, bf16[384,1536]{1,0:T(8,128)(2,1)}, u32[]{:S(2)}, u32[]{:S(2)}) collective-permute-start(bf16[384,1536]{1,0:T(8,128)(2,1)} %convolution_convert_fusion.5), channel_id=1, source_target_pairs={{0,1},{1,0},{2,3},{3,2},{4,5},{5,4},{6,7},{7,6},{8,9},{9,8},{10,11... | collective-permute-start | bytes 3538952 | tf_op jit(solution)/shard_map/ppermute | solution.py:57
  337.5 32.7 %collective-permute-start.2 = (bf16[384,1536]{1,0:T(8,128)(2,1)S(1)}, bf16[384,1536]{1,0:T(8,128)(2,1)S(1)}, u32[]{:S(2)}, u32[]{:S(2)}) collective-permute-start(bf16[384,1536]{1,0:T(8,128)(2,1)S(1)} %multiply_convert_fusion.3), channel_id=1, source_target_pairs={{0,8},{8,0},{1,9},{9,1},{2,10},{10,2},{3,11},{11,3},{4,12},{12,4},... | collective-permute-start | bytes 3538952 | tf_op jit(solution)/shard_map/ppermute | solution.py:57
  461.0 29.0 %collective-permute-start.17 = (bf16[384,1536]{1,0:T(8,128)(2,1)S(1)}, bf16[384,1536]{1,0:T(8,128)(2,1)}, u32[]{:S(2)}, u32[]{:S(2)}) collective-permute-start(bf16[384,1536]{1,0:T(8,128)(2,1)S(1)} %fusion.18), channel_id=1, source_target_pairs={{0,8},{8,0},{1,9},{9,1},{2,10},{10,2},{3,11},{11,3},{4,12},{12,4},... | collective-permute-start | bytes 3538952 | tf_op jit(solution)/shard_map/ppermute | solution.py:57
  466.5 48.0 %collective-permute-start.11 = (bf16[384,1536]{1,0:T(8,128)(2,1)}, bf16[384,1536]{1,0:T(8,128)(2,1)}, u32[]{:S(2)}, u32[]{:S(2)}) collective-permute-start(bf16[384,1536]{1,0:T(8,128)(2,1)} %fusion.21), channel_id=1, source_target_pairs={{0,8},{8,0},{1,9},{9,1},{2,10},{10,2},{3,11},{11,3},{4,12},{12,4},... | collective-permute-start | bytes 3538952 | tf_op jit(solution)/shard_map/ppermute | solution.py:57
  491.9 35.0 %collective-permute-start.18 = (bf16[384,1536]{1,0:T(8,128)(2,1)S(1)}, bf16[384,1536]{1,0:T(8,128)(2,1)S(1)}, u32[]{:S(2)}, u32[]{:S(2)}) collective-permute-start(bf16[384,1536]{1,0:T(8,128)(2,1)S(1)} %fusion.20), channel_id=1, source_target_pairs={{0,1},{1,0},{2,3},{3,2},{4,5},{5,4},{6,7},{7,6},{8,9},{9,8},{10,11... | collective-permute-start | bytes 3538952 | tf_op jit(solution)/shard_map/ppermute | solution.py:57
  516.4 27.3 %collective-permute-start.12 = (bf16[384,1536]{1,0:T(8,128)(2,1)S(1)}, bf16[384,1536]{1,0:T(8,128)(2,1)S(1)}, u32[]{:S(2)}, u32[]{:S(2)}) collective-permute-start(bf16[384,1536]{1,0:T(8,128)(2,1)S(1)} %fusion.23), channel_id=1, source_target_pairs={{0,1},{1,0},{2,3},{3,2},{4,5},{5,4},{6,7},{7,6},{8,9},{9,8},{10,11... | collective-permute-start | bytes 3538952 | tf_op jit(solution)/shard_map/ppermute | solution.py:57
  560.1 237.6 %reduce-scatter.8.cloned.1.call-start = ((), (), s32[]{:S(2)}) async-start(), calls=%async_computation.13 | async-start | bytes 2506752 | tf_op jit(solution)/shard_map/reduce_scatter | solution.py:390
  568.7 44.1 %collective-permute-start.24 = (bf16[2,2,1,192,1120]{4,3,2,1,0:T(8,128)(2,1)}, bf16[2,2,1,192,1120]{4,3,2,1,0:T(8,128)(2,1)}, u32[]{:S(2)}, u32[]{:S(2)}) collective-permute-start(bf16[2,2,1,192,1120]{4,3,2,1,0:T(8,128)(2,1)} %constant_dynamic-slice_fusion.1), channel_id=1, source_target_pairs={{0,4},{4,0},{1,5},{5,1},{2,6},{6,2},{3,7},{7,3},{8,12},{12,8},{9,1... | collective-permute-start | bytes 5160968 | tf_op jit(solution)/shard_map/ppermute | solution.py:57
  582.0 79.3 %collective-permute-start.22 = (bf16[2,2,1,192,1120]{4,3,2,1,0:T(8,128)(2,1)}, bf16[2,2,1,192,1120]{4,3,2,1,0:T(8,128)(2,1)}, u32[]{:S(2)}, u32[]{:S(2)}) collective-permute-start(bf16[2,2,1,192,1120]{4,3,2,1,0:T(8,128)(2,1)} %constant_dynamic-slice_fusion.3), channel_id=1, source_target_pairs={{0,4},{4,0},{1,5},{5,1},{2,6},{6,2},{3,7},{7,3},{8,12},{12,8},{9,1... | collective-permute-start | bytes 5160968 | tf_op jit(solution)/shard_map/ppermute | solution.py:57
  590.7 148.7 %collective-permute-start.20 = (bf16[2,2,1,192,1120]{4,3,2,1,0:T(8,128)(2,1)}, bf16[2,2,1,192,1120]{4,3,2,1,0:T(8,128)(2,1)}, u32[]{:S(2)}, u32[]{:S(2)}) collective-permute-start(bf16[2,2,1,192,1120]{4,3,2,1,0:T(8,128)(2,1)} %constant_dynamic-slice_fusion.5), channel_id=1, source_target_pairs={{0,4},{4,0},{1,5},{5,1},{2,6},{6,2},{3,7},{7,3},{8,12},{12,8},{9,1... | collective-permute-start | bytes 5160968 | tf_op jit(solution)/shard_map/ppermute | solution.py:57
  616.7 71.1 %collective-permute-start.25 = (bf16[1,2,1,192,1120]{4,3,2,1,0:T(8,128)(2,1)}, bf16[1,2,1,192,1120]{4,3,2,1,0:T(8,128)(2,1)}, u32[]{:S(2)}, u32[]{:S(2)}) collective-permute-start(bf16[1,2,1,192,1120]{4,3,2,1,0:T(8,128)(2,1)} %constant_dynamic-slice_fusion), channel_id=1, source_target_pairs={{0,16},{16,0},{1,17},{17,1},{2,18},{18,2},{3,19},{19,3},{4,20},{20... | collective-permute-start | bytes 2580488 | tf_op jit(solution)/shard_map/ppermute | solution.py:57
  665.4 82.1 %collective-permute-start.23 = (bf16[1,2,1,192,1120]{4,3,2,1,0:T(8,128)(2,1)}, bf16[1,2,1,192,1120]{4,3,2,1,0:T(8,128)(2,1)}, u32[]{:S(2)}, u32[]{:S(2)}) collective-permute-start(bf16[1,2,1,192,1120]{4,3,2,1,0:T(8,128)(2,1)} %constant_dynamic-slice_fusion.2), channel_id=1, source_target_pairs={{0,16},{16,0},{1,17},{17,1},{2,18},{18,2},{3,19},{19,3},{4,20},{20... | collective-permute-start | bytes 2580488 | tf_op jit(solution)/shard_map/ppermute | solution.py:57
  686.3 34.0 %collective-permute-start.19 = (bf16[384,1536]{1,0:T(8,128)(2,1)}, bf16[384,1536]{1,0:T(8,128)(2,1)}, u32[]{:S(2)}, u32[]{:S(2)}) collective-permute-start(bf16[384,1536]{1,0:T(8,128)(2,1)} %fusion.7), channel_id=1, source_target_pairs={{0,1},{1,0},{2,3},{3,2},{4,5},{5,4},{6,7},{7,6},{8,9},{9,8},{10,11... | collective-permute-start | bytes 3538952 | tf_op jit(solution)/shard_map/ppermute | solution.py:57
  690.1 59.7 %all-to-all-start.5 = ((bf16[4,96,1120]{2,1,0:T(8,128)(2,1)}), bf16[4,96,1120]{2,1,0:T(8,128)(2,1)}, u32[]{:S(2)}, u32[]{:S(2)}) async-start(bf16[4,96,1120]{2,1,0:T(8,128)(2,1)} %bitcast.140), calls=%async_computation.7 | async-start | bytes 1769472 | tf_op jit(solution)/shard_map/all_to_all | solution.py:129
  707.3 140.8 %reduce-scatter.10.cloned.1.call-start = ((), (), s32[]{:S(2)}) async-start(), calls=%async_computation.14 | async-start | bytes 3760128 | tf_op jit(solution)/shard_map/reduce_scatter | solution.py:437
  744.1 46.4 %collective-permute-start.21 = (bf16[1,2,1,192,1120]{4,3,2,1,0:T(8,128)(2,1)}, bf16[1,2,1,192,1120]{4,3,2,1,0:T(8,128)(2,1)}, u32[]{:S(2)}, u32[]{:S(2)}) collective-permute-start(bf16[1,2,1,192,1120]{4,3,2,1,0:T(8,128)(2,1)} %constant_dynamic-slice_fusion.4), channel_id=1, source_target_pairs={{0,16},{16,0},{1,17},{17,1},{2,18},{18,2},{3,19},{19,3},{4,20},{20... | collective-permute-start | bytes 2580488 | tf_op jit(solution)/shard_map/ppermute | solution.py:57
  749.8 43.4 %all-to-all-start.4 = ((bf16[4,96,1120]{2,1,0:T(8,128)(2,1)}), bf16[4,96,1120]{2,1,0:T(8,128)(2,1)}, u32[]{:S(2)}, u32[]{:S(2)}) async-start(bf16[4,96,1120]{2,1,0:T(8,128)(2,1)} %bitcast.142), calls=%async_computation.6 | async-start | bytes 1769472 | tf_op jit(solution)/shard_map/all_to_all | solution.py:129
  (66 other events, 1214.6 us)
Sparse Core Ops, SparseCore 0:
  12.7 49.8 all-gather.3
  70.9 53.0 all-gather.5
  126.2 107.4 all-gather.7
  560.2 119.6 reduce-scatter.5
  683.5 92.3 reduce-scatter.7
  779.6 68.3 reduce-scatter.9

commit v3 on v2

--- a/solution.py
+++ b/solution.py
@@ -61,6 +61,10 @@
     return value.astype(jnp.bfloat16)
 
 
+def after(value, *earlier):
+    return lax.optimization_barrier((value, *earlier))[0]
+
+
 def gather_group(own):
     core = other(own, "c")
     across = other(own, "zl")
@@ -68,12 +72,18 @@
     return jnp.concatenate([own, core, across, far], axis=0)
 
 
-def scatter_group(partial, rows):
+def sum_core(partial, rows):
     sent = low(jnp.concatenate([partial[rows : 2 * rows], partial[3 * rows :]], axis=0))
     core = other(sent, "c").astype(jnp.float32)
-    across = low(partial[2 * rows : 3 * rows] + core[rows:])
-    own = partial[:rows] + core[:rows] + other(across, "zl").astype(jnp.float32)
-    return sum_narrow(own)
+    return partial[:rows] + core[:rows], low(partial[2 * rows : 3 * rows] + core[rows:])
+
+
+def sum_low_z(own, across, *earlier):
+    return low(own + after(other(across, "zl"), *earlier).astype(jnp.float32))
+
+
+def sum_pair(mine, *earlier):
+    return mine.astype(jnp.float32) + after(other(mine, "y"), *earlier).astype(jnp.float32)
 
 
 def sum_narrow(partial):
@@ -81,53 +91,85 @@
     return mine.astype(jnp.float32) + other(mine, "y").astype(jnp.float32)
 
 
-def spread(weight):
+def deal(weight):
     features, hidden = weight.shape
     parts = weight.reshape(features, 4, hidden // 4).transpose(1, 0, 2)
     parts = lax.all_to_all(parts, GROUP, split_axis=0, concat_axis=0, tiled=True)
-    own = parts.reshape(1, 2, 1, 2 * features, hidden // 4)
+    return parts.reshape(1, 2, 1, 2 * features, hidden // 4)
+
+
+def fetch_first(own):
+    if lax.axis_size("zh") == 2:
+        return own, other(own, "zh"), other(own, "x")
+    every = lax.all_gather(own, "zh", axis=0, tiled=True)
+    return every, None, None
+
+
+def fetch_last(pieces, *earlier):
+    own, far, near = pieces
     high = lax.axis_size("zh")
     at_x = lax.axis_index("x")
+    whole = jnp.zeros((high, *own.shape[1:2], 2, *own.shape[3:]), jnp.bfloat16)
     if high == 2:
         at_high = lax.axis_index("zh")
-        far = other(own, "zh")
-        whole = jnp.zeros((high, 2, 2, 2 * features, hidden // 4), jnp.bfloat16)
-        for piece, place in ((own, at_high), (far, 1 - at_high)):
-            whole = lax.dynamic_update_slice(whole, piece, (place, 0, at_x, 0, 0))
-        mine = jnp.concatenate([own, far], axis=0)
-        across = other(mine, "x")
-        for number, place in ((0, at_high), (1, 1 - at_high)):
-            whole = lax.dynamic_update_slice(
-                whole, across[number : number + 1], (place, 0, 1 - at_x, 0, 0)
-            )
+        corner = other(after(far, *earlier), "x")
+        placed = (
+            (own, at_high, at_x),
+            (far, 1 - at_high, at_x),
+            (near, at_high, 1 - at_x),
+            (corner, 1 - at_high, 1 - at_x),
+        )
     else:
-        mine = lax.all_gather(own, "zh", axis=0, tiled=True)
-        across = other(mine, "x")
-        whole = jnp.zeros((high, 2, 2, 2 * features, hidden // 4), jnp.bfloat16)
-        whole = lax.dynamic_update_slice(whole, mine, (0, 0, at_x, 0, 0))
-        whole = lax.dynamic_update_slice(whole, across, (0, 0, 1 - at_x, 0, 0))
-    return whole.reshape(high * 8 * features, hidden // 4)
-
-
-def halve(grad, axis, position):
+        placed = ((own, 0, at_x), (other(own, "x"), 0, 1 - at_x))
+    return whole, placed
+
+
+def assemble(whole_placed, *earlier):
+    whole, placed = whole_placed
+    for piece, high_place, x_place in placed:
+        whole = lax.dynamic_update_slice(
+            whole, after(piece, *earlier), (high_place, 0, x_place, 0, 0)
+        )
+    high, low_z, across, features, hidden = whole.shape
+    return whole.reshape(high * low_z * across * features, hidden)
+
+
+def split_half(grad, axis, position):
     at = lax.axis_index(axis)
     sent = lax.dynamic_slice_in_dim(grad, 1 - at, 1, position)
     kept = lax.dynamic_slice_in_dim(grad, at, 1, position)
-    return low(kept.astype(jnp.float32) + other(sent, axis).astype(jnp.float32))
-
-
-def collect(grad):
+    return kept, other(sent, axis)
+
+
+def add_half(halves, *earlier):
+    kept, came = halves
+    return low(kept.astype(jnp.float32) + after(came, *earlier).astype(jnp.float32))
+
+
+def collect_first(grad):
     high = lax.axis_size("zh")
-    features = grad.shape[0] // (8 * high)
-    hidden = grad.shape[1]
-    summed = halve(grad.reshape(high, 2, 2, 2 * features, hidden), "x", 2)
-    if high == 2:
-        summed = halve(summed, "zh", 0)
-    else:
-        summed = lax.psum_scatter(summed, "zh", scatter_dimension=0, tiled=True)
-    parts = summed.reshape(4, features, hidden)
-    parts = lax.all_to_all(parts, GROUP, split_axis=0, concat_axis=0, tiled=True)
-    return parts.transpose(1, 0, 2).reshape(features, 4 * hidden).astype(jnp.float32)
+    return split_half(grad.reshape(high, 2, 2, grad.shape[0] // (4 * high), grad.shape[1]), "x", 2)
+
+
+def collect_second(halves, *earlier):
+    summed = add_half(halves, *earlier)
+    if lax.axis_size("zh") == 2:
+        return split_half(summed, "zh", 0)
+    return lax.psum_scatter(summed, "zh", scatter_dimension=0, tiled=True)
+
+
+def collect_last(halves, *earlier):
+    if lax.axis_size("zh") == 2:
+        halves = add_half(halves, *earlier)
+    features = halves.shape[3] // 2
+    hidden = halves.shape[4]
+    parts = halves.reshape(4, features, hidden)
+    return lax.all_to_all(parts, GROUP, split_axis=0, concat_axis=0, tiled=True)
+
+
+def collect_end(parts):
+    count, features, hidden = parts.shape
+    return parts.transpose(1, 0, 2).reshape(features, count * hidden).astype(jnp.float32)
 
 
 def rotate_rows(value_rows, cosine, sine):
@@ -183,13 +225,21 @@
 
 
 def attend_back_kernel(
-    bounds_ref, rotated_ref, accum_ref, delta_ref, cosine_ref, sine_ref, place_ref, pair_ref,
-    grad_query_ref, grad_pair_ref, sums_ref,
+    bounds_ref, rotated_ref, grad_ref, attended_ref, totals_ref, cosine_ref, sine_ref, place_ref,
+    pair_ref, grad_query_ref, grad_pair_ref, sums_ref, accum_ref, delta_ref,
 ):
     rows, wide = rotated_ref.shape
     head = cosine_ref.shape[1]
     scale = 1.0 / math.sqrt(head)
     factor = math.log2(math.e) * scale
+    for order in range(wide // head):
+        at = order * head
+        totals = jnp.broadcast_to(totals_ref[order : order + 1, :], (head, rows)).T
+        divided = grad_ref[:, at : at + head] / totals
+        accum_ref[:, at : at + head] = low(divided)
+        delta_ref[order : order + 1, :] = jnp.sum(
+            (divided * attended_ref[:, at : at + head]).T, axis=0, keepdims=True
+        )
 
     def clear(number, carry):
         begin = pl.multiple_of(number * rows, rows)
@@ -250,11 +300,14 @@
         in_specs=in_vmem(5),
         out_specs=tuple(in_vmem(3)[1:]),
         scratch_shapes=[pltpu.VMEM((wide, rows), jnp.float32)],
+        cost_estimate=pl.CostEstimate(
+            flops=4 * 9 * rows * rows * wide, transcendentals=9 * rows * rows * 6, bytes_accessed=20 << 20
+        ),
         name="attend",
     )(bounds, query_pre, cosine, sine, place, pair)
 
 
-def attend_back(bounds, rotated, accum, delta, cosine, sine, place, pair):
+def attend_back(bounds, rotated, grad, attended, totals, cosine, sine, place, pair):
     rows, wide = rotated.shape
     return pl.pallas_call(
         attend_back_kernel,
@@ -262,11 +315,18 @@
             jax.ShapeDtypeStruct((rows, wide), jnp.bfloat16),
             jax.ShapeDtypeStruct(pair.shape, jnp.bfloat16),
         ),
-        in_specs=in_vmem(7),
+        in_specs=in_vmem(8),
         out_specs=tuple(in_vmem(2)[1:]),
-        scratch_shapes=[pltpu.VMEM((wide, rows), jnp.float32)],
+        scratch_shapes=[
+            pltpu.VMEM((wide, rows), jnp.float32),
+            pltpu.VMEM((rows, wide), jnp.bfloat16),
+            pltpu.VMEM(totals.shape, jnp.float32),
+        ],
+        cost_estimate=pl.CostEstimate(
+            flops=10 * 9 * rows * rows * wide, transcendentals=9 * rows * rows * 6, bytes_accessed=30 << 20
+        ),
         name="attend_back",
-    )(bounds, rotated, accum, delta, cosine, sine, place, pair)
+    )(bounds, rotated, grad, attended, totals, cosine, sine, place, pair)
 
 
 def local(
@@ -317,8 +377,12 @@
     small_rows = -(-sum(small_sizes) // head)
     small = jnp.concatenate(small_parts)
     small = jnp.pad(small, (0, features * head - small.shape[0])).reshape(features, head)
-    packed = jnp.concatenate([w_query, key_projection, value_projection, small], axis=1)
-    w_project = lax.all_gather(packed, WIDE, axis=0, tiled=True)
+    packed = jnp.concatenate([w_query, key_projection, value_projection, small, w_out.T], axis=1)
+    gate_own = deal(w_gate)
+    up_own = deal(w_up)
+    w_packed = after(lax.all_gather(packed, WIDE, axis=0, tiled=True), gate_own, up_own)
+    w_project = w_packed[:, : projected + head]
+    w_out_all = w_packed[:, projected + head :]
     small_all = w_project[:, projected:].reshape(devices, features, head)[:, :small_rows]
     small_all = small_all.reshape(devices, small_rows * head).astype(jnp.float32)
     cuts = [0]
@@ -331,9 +395,6 @@
     bias_key = small_all[:, cuts[3] : cuts[4]].reshape(-1)
     bias_value = small_all[:, cuts[4] : cuts[5]].reshape(-1)
 
-    gate_all = spread(w_gate)
-    up_all = spread(w_up)
-    down_all = spread(w_down.T)
 
     inputs = tokens.astype(jnp.float32)
     scale_one = norm_scale(inputs)
@@ -349,66 +410,87 @@
     key_value = lax.all_gather(
         jnp.concatenate([key_rows, value_rows], axis=1), WIDE, axis=0, tiled=True
     )
-    w_out_all = lax.all_gather(w_out.T, WIDE, axis=0, tiled=True)
+    down_own = deal(w_down.T)
+    cotangent_group = gather_group(cotangent)
+    cotangent_turned = cotangent_group.T
+    gate_own, up_own, down_own, key_value, cotangent_group, cotangent_turned = (
+        lax.optimization_barrier(
+            (gate_own, up_own, down_own, key_value, cotangent_group, cotangent_turned)
+        )
+    )
+    gate_pieces = fetch_first(gate_own)
+    up_pieces = fetch_first(up_own)
+    down_pieces = fetch_first(down_own)
     query_rows, attended, totals = attend(
         bounds, query_pre, cosine_head, sine_head, place, key_value
     )
-    totals = totals[:query_group]
     attended_low = low(attended)
-    middle = inputs + sum_narrow(product_right(attended_low, w_out_all))
+    attention = product_right(attended_low, w_out_all)
+    gate_pieces = fetch_last(gate_pieces, attention)
+    middle = inputs + sum_narrow(attention)
     scale_two = norm_scale(middle)
     normed_two = low(middle * scale_two * gain_two)
-
-    cotangent_group = gather_group(cotangent)
+    up_pieces = fetch_last(up_pieces, normed_two)
     normed_group = gather_group(normed_two)
+    normed_turned = lax.optimization_barrier(normed_group.T)
+    gate_all = assemble(gate_pieces, attention)
     gate = product(normed_group, gate_all)
+    up_all = assemble(up_pieces, normed_two)
+    down_pieces = fetch_last(down_pieces, normed_group)
     up_part = product(normed_group, up_all)
     sigmoid_gate = jax.nn.sigmoid(gate)
     silu_gate = gate * sigmoid_gate
     hidden = low(silu_gate * up_part)
-    result = low(middle + scatter_group(product_right(hidden, down_all), rows))
-    grad_down = low(product_left(cotangent_group, hidden))
-    grad_hidden = product(cotangent_group, down_all)
+    grad_down = low(product(cotangent_turned, hidden))
+    down_halves = collect_first(grad_down)
+    down_all = assemble(down_pieces, normed_group)
+    grad_hidden = product(after(cotangent_group, grad_down), down_all)
     grad_gate = low(grad_hidden * up_part * sigmoid_gate * (1.0 + gate * (1.0 - sigmoid_gate)))
     grad_up = low(grad_hidden * silu_gate)
-    grad_normed_two = scatter_group(
-        product_right(grad_gate, gate_all) + product_right(grad_up, up_all), rows
-    )
-    grad_gate_all = low(product_left(normed_group, grad_gate))
-    grad_up_all = low(product_left(normed_group, grad_up))
-    grad_normed_two, grad_gate_all, grad_up_all, grad_down = lax.optimization_barrier(
-        (grad_normed_two, grad_gate_all, grad_up_all, grad_down)
-    )
-    grad_w_down = collect(grad_down).T
-    grad_w_gate = collect(grad_gate_all)
-    grad_w_up = collect(grad_up_all)
+    grad_normed_part = product_right(grad_gate, gate_all) + product_right(grad_up, up_all)
+    grad_normed_own, grad_normed_across = sum_core(grad_normed_part, rows)
+    grad_gate_all = low(
+        product(normed_turned, after(grad_gate, grad_normed_across, down_halves[1]))
+    )
+    down_halves = collect_second(down_halves, grad_normed_across)
+    gate_halves = collect_first(grad_gate_all)
+    grad_up_all = low(product(normed_turned, after(grad_up, grad_gate_all, down_halves[0])))
+    up_halves = collect_first(grad_up_all)
+    grad_normed_mine = sum_low_z(grad_normed_own, grad_normed_across, grad_up_all)
+    down_part = product_right(after(hidden, grad_normed_mine), down_all)
+    down_mine, down_across = sum_core(down_part, rows)
+    grad_normed_two = sum_pair(grad_normed_mine, down_across, gate_halves[1])
+    down_mine = sum_low_z(down_mine, down_across, grad_normed_two)
+    result = low(middle + sum_pair(down_mine))
+    down_parts = collect_last(down_halves, grad_normed_two)
+    gate_halves = collect_second(gate_halves, grad_normed_two)
 
     back_two, grad_gain_two = norm_back(middle, scale_two, gain_two, grad_normed_two)
     grad_middle = cotangent.astype(jnp.float32) + back_two
     grad_att = low(grad_middle)
-    grad_w_out = (
-        lax.psum_scatter(
-            low(product_left(grad_att, attended_low)), WIDE, scatter_dimension=0, tiled=True
-        )
-        .astype(jnp.float32)
-        .T
-    )
-    grad_attended = product(grad_att, w_out_all).reshape(rows, query_group, head)
-    divided = grad_attended / totals.T[:, :, None]
-    grad_accum = low(divided).reshape(rows, heads_width)
-    delta = jnp.sum(divided * attended.reshape(rows, query_group, head), axis=2).T
-    delta = jnp.pad(delta, ((0, -query_group % 8), (0, 0)))
+    grad_out_all = product_left(attended_low, grad_att).T
+    grad_attended = product(grad_att, w_out_all)
+    up_halves = collect_second(up_halves, gate_halves[0])
     grad_query_pre, buffer = attend_back(
-        bounds, query_rows, grad_accum, delta, cosine_head, sine_head, place, key_value
-    )
-    key_value_grads = lax.psum_scatter(buffer, WIDE, scatter_dimension=0, tiled=True).astype(
-        jnp.float32
-    )
+        bounds, query_rows, after(grad_attended, up_halves[0], down_halves[1]), attended, totals,
+        cosine_head, sine_head, place, key_value,
+    )
+    key_value_grads = lax.psum_scatter(buffer, WIDE, scatter_dimension=0, tiled=True)
+    gate_parts = collect_last(gate_halves, buffer)
+    square_grads = low(
+        jnp.concatenate([product_left(grad_query_pre, normed_one).T, grad_out_all], axis=1)
+    )
+    up_parts = collect_last(up_halves, gate_parts)
+    key_value_grads = after(
+        key_value_grads, square_grads, gate_parts, down_parts, up_parts
+    ).astype(jnp.float32)
+    square_grads = lax.psum_scatter(square_grads, WIDE, scatter_dimension=0, tiled=True)
     grad_key_pre = low(
         rotate_halves(key_value_grads[:, :head].reshape(rows, 1, head), cosine_table, -sine_table)
     ).reshape(rows, head)
     grad_value_pre = low(key_value_grads[:, head:])
-    grad_project = jnp.concatenate([grad_query_pre, grad_key_pre, grad_value_pre], axis=1)
+    grad_pair = jnp.concatenate([grad_key_pre, grad_value_pre], axis=1)
+    grad_project = jnp.concatenate([grad_query_pre, grad_pair], axis=1)
     grad_bias = jnp.sum(grad_project.astype(jnp.float32), axis=0)
     grad_normed_one = sum_narrow(product_right(grad_project, w_project[:, :projected]))
     back_one, grad_gain_one = norm_back(inputs, scale_one, gain_one, grad_normed_one)
@@ -430,23 +512,28 @@
     small_grads = jnp.pad(small_grads, ((0, 0), (0, features * head - small_grads.shape[1])))
     packed_grads = low(
         jnp.concatenate(
-            [product_left(normed_one, grad_project), small_grads.reshape(devices * features, head)],
+            [product_left(grad_pair, normed_one).T, small_grads.reshape(devices * features, head)],
             axis=1,
         )
     )
     packed_grads = lax.psum_scatter(packed_grads, WIDE, scatter_dimension=0, tiled=True).astype(
         jnp.float32
     )
-    small_own = packed_grads[:, projected:].reshape(-1)
+    small_own = packed_grads[:, 2 * head :].reshape(-1)
+    square_grads = square_grads.astype(jnp.float32)
+    grad_w_out = square_grads[:, heads_width:].T
+    grad_w_down = collect_end(down_parts).T
+    grad_w_gate = collect_end(gate_parts)
+    grad_w_up = collect_end(up_parts)
     return (
         result,
         grad_tokens,
         small_own[cuts[0] : cuts[1]],
-        packed_grads[:, :heads_width],
+        square_grads[:, :heads_width],
         small_own[cuts[2] : cuts[3]].reshape(query_group, piece),
-        packed_grads[:, heads_width : heads_width + head],
+        packed_grads[:, :head],
         small_own[cuts[3] : cuts[4]].reshape(1, piece),
-        packed_grads[:, heads_width + head : projected],
+        packed_grads[:, head : 2 * head],
         small_own[cuts[4] : cuts[5]].reshape(1, piece),
         grad_w_out,
         small_own[cuts[1] : cuts[2]],

time: 873 us -> 842 us (0.964)
  starting transfers between devices: 104 us -> 78.3 us
  local copies, waits for them, and re-layouts: 130 us -> 105 us
  blocking collectives: 0 us -> 17.1 us
  waiting for transfers between devices: 398 us -> 411 us
    all_gather x2 -> x1, waiting for transfers between devices: 46.1 us -> 12.2 us  [local(): lax.all_gather(packed, WIDE, axis=0, tiled=True)]
    all_to_all x6 -> x5, waiting for transfers between devices: 46.2 us -> 76.8 us  [the longest x3 49.1 us: deal(): lax.all_to_all(parts, GROUP, split_axis=0, concat_axis=0, tiled=True)]
    dot_general x5 -> x3, matrix products: 36.3 us -> 6.71 us  [product_left(): lax.dot_general(left, right, (((0,), (0,)), ((), ())), preferred_element_...]
    dot_general x5 -> x8, matrix products: 45.4 us -> 71 us  [product(): return jnp.dot(left, right, preferred_element_type=jnp.float32)]
    all_to_all x0 -> x1, blocking collectives: none -> 17.1 us  [collect_last(): return lax.all_to_all(parts, GROUP, split_axis=0, concat_axis=0, tiled=True)]
    optimization_barrier x3 -> x0, local copies, waits for them, and re-layouts: 17.1 us -> none  [local(): lax.optimization_barrier((grad_normed_two, grad_gate_all, grad_up_all, gr...]
    all_to_all x6 -> x5, starting transfers between devices: 37.2 us -> 20.5 us  [the longest x3 12 us: deal(): lax.all_to_all(parts, GROUP, split_axis=0, concat_axis=0, tiled=True)]
    reduce_scatter x1, waiting for transfers between devices: 25.2 us -> 41.8 us  [local(): lax.psum_scatter(packed_grads, WIDE, scatter_dimension=0, tiled=True)]
  transfers between devices with their start and end apart: 38 -> 39, of which waited for: 20 -> 21; matrix products, arithmetic and copies ran while one was open for 28% -> 25% of each run, Pallas kernels for 1% -> 1%
where the time goes in v3:
time: 842 us; the launch traced here: 831 us
  waiting for transfers between devices  411 us (49%)
  matrix products  118 us (14%)
  local copies, waits for them, and re-layouts  105 us (12%)
  starting transfers between devices  78.3 us (9%)
  other arithmetic  68.7 us (8%)
  blocking collectives  17.1 us (2%)
  between operations  16.9 us (2%)
  Pallas kernels  15.1 us (2%)
    ppermute x29, waiting for transfers between devices, other(): return lax.ppermute(value, axis, [(0, 1), (1, 0)])  280 us
    dot_general x8, matrix products, product(): return jnp.dot(left, right, preferred_element_type=jnp.float32)  71 us
    ppermute x29, starting transfers between devices, other(): return lax.ppermute(value, axis, [(0, 1), (1, 0)])  57.7 us
    all_to_all x3, waiting for transfers between devices, deal(): lax.all_to_all(parts, GROUP, split_axis=0, concat_axis=0, tiled=True)  49.1 us
    reduce_scatter x1, waiting for transfers between devices, local(): lax.psum_scatter(packed_grads, WIDE, scatter_dimension=0, tiled=True)  41.8 us
    dot_general x5, matrix products, product_right(): lax.dot_general(left, right, (((1,), (1,)), ((), ())), preferred_element_...  40.6 us
    all_to_all x2, waiting for transfers between devices, collect_last(): return lax.all_to_all(parts, GROUP, split_axis=0, concat_axis=0, tiled=True)  27.7 us
    convert_element_type x13, other arithmetic, low(): return value.astype(jnp.bfloat16)  24.3 us
  transfers between devices with their start and end apart: 39, of which 21 were waited for; matrix products, arithmetic and copies ran while one was open for 25% of the time, Pallas kernels for 1%

profile of v3, /device:TPU:0, one launch (start us, length us, event | category | flops | bytes accessed | tf_op | source)
XLA Modules:
  0.0 830.7 jit_solution(4976188027055323558)
XLA Ops:
  26.4 19.0 %all-to-all-done.1 = bf16[4,96,1120]{2,1,0:T(8,128)(2,1)S(1)} async-done(((bf16[4,96,1120]{2,1,0:T(8,128)(2,1)}), bf16[4,96,1120]{2,1,0:T(8,128)(2,1)S(1)}, u32[]{:S(2)}, u32[]{:S(2)}) %all-to-all-start.1) | async-done | bytes 860192 | tf_op jit(solution)/shard_map/all_to_all | solution.py:97
  50.2 24.7 %all-to-all-done = bf16[4,96,1120]{2,1,0:T(8,128)(2,1)S(1)} async-done(((bf16[4,96,1120]{2,1,0:T(8,128)(2,1)}), bf16[4,96,1120]{2,1,0:T(8,128)(2,1)S(1)}, u32[]{:S(2)}, u32[]{:S(2)}) %all-to-all-start) | async-done | bytes 860192 | tf_op jit(solution)/shard_map/all_to_all | solution.py:97
  74.9 12.2 %all-gather.3.cloned.1.call-done = bf16[1536,1920]{1,0:T(8,128)(2,1)} async-done(((bf16[96,1920]{1,0:T(8,128)(2,1)}), bf16[1536,1920]{1,0:T(8,128)(2,1)}) %all-gather.3.cloned.1.call-update) | async-done | bytes 5898256 | tf_op jit(solution)/shard_map/all_gather | solution.py:383
  109.5 27.1 %collective-permute-done.1 = bf16[384,1536]{1,0:T(8,128)(2,1)} collective-permute-done((bf16[384,1536]{1,0:T(8,128)(2,1)S(1)}, bf16[384,1536]{1,0:T(8,128)(2,1)}, u32[]{:S(2)}, u32[]{:S(2)}) %collective-permute-start.1) | collective-permute-done | bytes 1179680 | tf_op jit(solution)/shard_map/ppermute | solution.py:57
  169.6 14.3 %collective-permute-start.10 = (bf16[1,2,1,192,1120]{4,3,1,2,0:T(8,128)(2,1)S(1)}, bf16[1,2,1,192,1120]{4,3,1,2,0:T(8,128)(2,1)S(1)}, u32[]{:S(2)}, u32[]{:S(2)}) collective-permute-start(bf16[1,2,1,192,1120]{4,3,1,2,0:T(8,128)(2,1)S(1)} %bitcast.118), channel_id=1, source_target_pairs={{0,16},{16,0},{1,17},{17,1},{2,18},{18,2},{3,19},{19,3},{4,20},{20... | collective-permute-start | bytes 2580488 | tf_op jit(solution)/shard_map/ppermute | solution.py:57
  184.5 29.9 %collective-permute-done.7 = bf16[1,2,1,192,1120]{4,3,1,2,0:T(8,128)(2,1)} collective-permute-done((bf16[1,2,1,192,1120]{4,3,1,2,0:T(8,128)(2,1)S(1)}, bf16[1,2,1,192,1120]{4,3,1,2,0:T(8,128)(2,1)}, u32[]{:S(2)}, u32[]{:S(2)}) %collective-permute-start.7) | collective-permute-done | bytes 860192 | tf_op jit(solution)/shard_map/ppermute | solution.py:57
  223.5 28.9 %collective-permute-done.10 = bf16[1,2,1,192,1120]{4,3,1,2,0:T(8,128)(2,1)S(1)} collective-permute-done((bf16[1,2,1,192,1120]{4,3,1,2,0:T(8,128)(2,1)S(1)}, bf16[1,2,1,192,1120]{4,3,1,2,0:T(8,128)(2,1)S(1)}, u32[]{:S(2)}, u32[]{:S(2)}) %collective-permute-start.10) | collective-permute-done | bytes 860192 | tf_op jit(solution)/shard_map/ppermute | solution.py:57
  254.6 27.7 %collective-permute-done.5 = bf16[384,1536]{1,0:T(8,128)(2,1)S(1)} collective-permute-done((bf16[384,1536]{1,0:T(8,128)(2,1)S(1)}, bf16[384,1536]{1,0:T(8,128)(2,1)S(1)}, u32[]{:S(2)}, u32[]{:S(2)}) %collective-permute-start.5) | collective-permute-done | bytes 1179680 | tf_op jit(solution)/shard_map/ppermute | solution.py:57
  288.0 17.2 %collective-permute-done.14 = bf16[1,2,1,192,1120]{4,3,1,2,0:T(8,128)(2,1)S(1)} collective-permute-done((bf16[1,2,1,192,1120]{4,3,1,2,0:T(8,128)(2,1)}, bf16[1,2,1,192,1120]{4,3,1,2,0:T(8,128)(2,1)S(1)}, u32[]{:S(2)}, u32[]{:S(2)}) %collective-permute-start.14) | collective-permute-done | bytes 860192 | tf_op jit(solution)/shard_map/ppermute | solution.py:57
  305.2 10.4 %fusion.71 = f32[1536,1120]{0,1:T(8,128)} fusion(bf16[1536,1120]{1,0:T(8,128)(2,1)S(1)} %bitcast.131, bf16[384,1536]{1,0:T(8,128)(2,1)S(1)} %collective-permute-done.6, bf16[384,1536]{1,0:T(8,128)(2,1)S(1)} %collective-permute-done.5, bf16[384,1536]{1,0:T(8,128)(2,1)S(1)} %collective-permute-done.4, bf16[384,1536]{1,0:T(8,128)(2,1)S(1)} %multiply_convert_fusion.3), kind=kOutput, calls=%fused_computation.167 | convolution fusion | flops 5303697408 | bytes 15040512 | tf_op jit(solution)/shard_map/dot_general | solution.py:16
  315.6 13.7 %multiply_convert_fusion.2 = (bf16[1536,1120]{0,1:T(8,128)(2,1)}, f32[1536,1120]{0,1:T(8,128)}) fusion(f32[1536,1120]{0,1:T(8,128)} %fusion.71, bf16[1536,1120]{1,0:T(8,128)(2,1)S(1)} %bitcast.127, bf16[384,1536]{1,0:T(8,128)(2,1)S(1)} %collective-permute-done.6, bf16[384,1536]{1,0:T(8,128)(2,1)S(1)} %collective-permute-done.5, ...), kind=kOutput, calls=%fused_computation.6 | convolution fusion | flops 5314019328 | bytes 25362432 | tf_op jit(solution)/shard_map/dot_general | solution.py:16
  329.3 9.7 %convolution_convert_fusion.2 = bf16[1536,1120]{0,1:T(8,128)(2,1)} fusion(bf16[1536,1120]{0,1:T(8,128)(2,1)} %get-tuple-element.78, bf16[1536,1536]{0,1:T(8,128)(2,1)} %bitcast.139), kind=kOutput, calls=%fused_computation.3 | convolution fusion | flops 5286543360 | bytes 11599872 | tf_op jit(solution)/shard_map/dot_general | solution.py:16
  343.5 15.5 %multiply_convert_fusion = (bf16[1536,1120]{0,1:T(8,128)(2,1)}, bf16[1536,1120]{0,1:T(8,128)(2,1)}) fusion(f32[1536,1120]{0,1:T(8,128)} %fusion.71, f32[1536,1120]{0,1:T(8,128)} %get-tuple-element.211, bf16[1536,1536]{1,0:T(8,128)(2,1)} %copy-done.22, bf16[1536,1120]{1,0:T(8,128)(2,1)S(1)} %bitcast.129), kind=kOutput, calls=%fused_computation.4 | convolution fusion | flops 5307187200 | bytes 28803072 | tf_op jit(solution)/shard_map/dot_general | solution.py:16
  359.0 11.1 %fusion.81 = f32[1536,1536]{1,0:T(8,128)} fusion(bf16[1536,1120]{0,1:T(8,128)(2,1)} %get-tuple-element.74, bf16[1536,1120]{1,0:T(8,128)(2,1)S(1)} %bitcast.132), kind=kOutput, calls=%fused_computation.177 | convolution fusion | flops 5284823040 | bytes 16318464 | tf_op jit(solution)/shard_map/dot_general | solution.py:26
  370.1 11.3 %fusion.79 = (bf16[1536,1536]{1,0:T(8,128)(2,1)S(1)}, f32[1536,1536]{1,0:T(8,128)}) fusion(f32[1536,1536]{1,0:T(8,128)} %fusion.81, bf16[1536,1120]{0,1:T(8,128)(2,1)S(1)} %copy-done.38, bf16[1536,1120]{1,0:T(8,128)(2,1)S(1)} %bitcast.128), kind=kOutput, calls=%fused_computation.175 | convolution fusion | flops 5289541632 | bytes 30474240 | tf_op jit(solution)/shard_map/dot_general | solution.py:26
  392.6 36.0 %collective-permute-done.18 = bf16[2,2,1,192,1120]{4,3,2,1,0:T(8,128)(2,1)S(1)} collective-permute-done((bf16[2,2,1,192,1120]{4,3,2,1,0:T(8,128)(2,1)S(1)}, bf16[2,2,1,192,1120]{4,3,2,1,0:T(8,128)(2,1)S(1)}, u32[]{:S(2)}, u32[]{:S(2)}) %collective-permute-start.18) | collective-permute-done | bytes 1720352 | tf_op jit(solution)/shard_map/ppermute | solution.py:57
  431.7 7.2 convolution_convert_fusion.1
  438.9 6.9 convolution_convert_fusion
  450.0 8.9 %fusion.80 = (bf16[1536,1536]{1,0:T(8,128)(2,1)S(1)}, f32[1536,1536]{1,0:T(8,128)}) fusion(bf16[1536,1120]{0,1:T(8,128)(2,1)S(1)} %copy-done.40, bf16[1536,1120]{1,0:T(8,128)(2,1)S(1)} %bitcast.130), kind=kOutput, calls=%fused_computation.176 | convolution fusion | flops 5287182336 | bytes 21037056 | tf_op jit(solution)/shard_map/dot_general | solution.py:26
  481.8 26.5 %collective-permute-done.22 = bf16[2,2,1,192,1120]{4,3,2,1,0:T(8,128)(2,1)} collective-permute-done((bf16[2,2,1,192,1120]{4,3,2,1,0:T(8,128)(2,1)}, bf16[2,2,1,192,1120]{4,3,2,1,0:T(8,128)(2,1)}, u32[]{:S(2)}, u32[]{:S(2)}) %collective-permute-start.22) | collective-permute-done | bytes 1720352 | tf_op jit(solution)/shard_map/ppermute | solution.py:57
  513.3 13.3 %collective-permute-done.20 = bf16[384,1536]{1,0:T(8,128)(2,1)S(1)} collective-permute-done((bf16[384,1536]{1,0:T(8,128)(2,1)S(1)}, bf16[384,1536]{1,0:T(8,128)(2,1)S(1)}, u32[]{:S(2)}, u32[]{:S(2)}) %collective-permute-start.20) | collective-permute-done | bytes 1179680 | tf_op jit(solution)/shard_map/ppermute | solution.py:57
  530.8 14.8 %collective-permute-done.24 = bf16[2,2,1,192,1120]{4,3,2,1,0:T(8,128)(2,1)S(1)} collective-permute-done((bf16[2,2,1,192,1120]{4,3,2,1,0:T(8,128)(2,1)S(1)}, bf16[2,2,1,192,1120]{4,3,2,1,0:T(8,128)(2,1)S(1)}, u32[]{:S(2)}, u32[]{:S(2)}) %collective-permute-start.24) | collective-permute-done | bytes 1720352 | tf_op jit(solution)/shard_map/ppermute | solution.py:57
  547.5 8.6 %collective-permute-done.23 = bf16[384,1536]{1,0:T(8,128)(2,1)S(1)} collective-permute-done((bf16[384,1536]{1,0:T(8,128)(2,1)S(1)}, bf16[384,1536]{1,0:T(8,128)(2,1)S(1)}, u32[]{:S(2)}, u32[]{:S(2)}) %collective-permute-start.23) | collective-permute-done | bytes 1179680 | tf_op jit(solution)/shard_map/ppermute | solution.py:57
  563.8 8.7 %attend_back.1 = (bf16[384,768]{1,0:T(8,128)(2,1)}, bf16[6144,256]{1,0:T(8,128)(2,1)}) custom-call(s32[2]{0:T(128)} %pad_add_fusion.bounds_ref, bf16[384,768]{1,0:T(8,128)(2,1)} %get-tuple-element.81.rotated_ref, f32[384,768]{1,0:T(8,128)} %fusion.27.grad_ref, f32[384,768]{1,0:T(8,128)} %get-tuple-element.55.attended_ref, ...), custom_call_target="tpu_custom_call" | custom-call | flops 10192158720 | bytes 31457280 | tf_op jit(solution)/shard_map/attend_back/pallas_call | solution.py:312
  572.6 21.1 %collective-permute-start.26 = (bf16[1,2,1,192,1120]{4,3,2,1,0:T(8,128)(2,1)}, bf16[1,2,1,192,1120]{4,3,2,1,0:T(8,128)(2,1)S(1)}, u32[]{:S(2)}, u32[]{:S(2)}) collective-permute-start(bf16[1,2,1,192,1120]{4,3,2,1,0:T(8,128)(2,1)} %get-tuple-element.180), channel_id=1, source_target_pairs={{0,16},{16,0},{1,17},{17,1},{2,18},{18,2},{3,19},{19,3},{4,20},{20... | collective-permute-start | bytes 2580488 | tf_op jit(solution)/shard_map/ppermute | solution.py:57
  593.7 21.6 %collective-permute-done.26 = bf16[1,2,1,192,1120]{4,3,2,1,0:T(8,128)(2,1)S(1)} collective-permute-done((bf16[1,2,1,192,1120]{4,3,2,1,0:T(8,128)(2,1)}, bf16[1,2,1,192,1120]{4,3,2,1,0:T(8,128)(2,1)S(1)}, u32[]{:S(2)}, u32[]{:S(2)}) %collective-permute-start.26) | collective-permute-done | bytes 860192 | tf_op jit(solution)/shard_map/ppermute | solution.py:57
  622.9 6.7 copy.156
  639.1 23.9 %all-to-all-done.3 = bf16[4,96,1120]{2,1,0:T(8,128)(2,1)} async-done(((bf16[4,96,1120]{2,1,0:T(8,128)(2,1)}), bf16[4,96,1120]{2,1,0:T(8,128)(2,1)}, u32[]{:S(2)}, u32[]{:S(2)}) %all-to-all-start.3) | async-done | bytes 860192 | tf_op jit(solution)/shard_map/all_to_all | solution.py:167
  667.3 17.8 %collective-permute-done.27 = bf16[1,2,1,192,1120]{4,3,2,1,0:T(8,128)(2,1)} collective-permute-done((bf16[1,2,1,192,1120]{4,3,2,1,0:T(8,128)(2,1)}, bf16[1,2,1,192,1120]{4,3,2,1,0:T(8,128)(2,1)}, u32[]{:S(2)}, u32[]{:S(2)}) %collective-permute-start.27) | collective-permute-done | bytes 860192 | tf_op jit(solution)/shard_map/ppermute | solution.py:57
  691.4 17.1 %all_to_all.30 = bf16[4,96,1120]{2,1,0:T(8,128)(2,1)} all-to-all(bf16[4,96,1120]{2,1,0:T(8,128)(2,1)} %bitcast.135), channel_id=1, replica_groups=mesh['zh'=2,'zl'=2,'x'=2,'c'=2,'y'=2] {'zl','c'}, dimensions={0} | all-to-all | bytes 1720320 | tf_op jit(solution)/shard_map/all_to_all | solution.py:167
  734.5 9.1 %collective-permute-done.28 = bf16[384,1536]{1,0:T(8,128)(2,1)} collective-permute-done((bf16[384,1536]{1,0:T(8,128)(2,1)}, bf16[384,1536]{1,0:T(8,128)(2,1)}, u32[]{:S(2)}, u32[]{:S(2)}) %collective-permute-start.28) | collective-permute-done | bytes 1179680 | tf_op jit(solution)/shard_map/ppermute | solution.py:57
  777.6 41.8 %reduce-scatter.10.cloned.1.call-done = bf16[96,384]{1,0:T(8,128)(2,1)} async-done(((bf16[1536,384]{1,0:T(8,128)(2,1)}), bf16[96,384]{1,0:T(8,128)(2,1)}) %reduce-scatter.10.cloned.1.call-update) | async-done | bytes 73744 | tf_op jit(solution)/shard_map/reduce_scatter | solution.py:519
  (305 shorter events, 251.2 us)
Async XLA Ops:
  7.2 79.9 %all-gather.3.cloned.1.call-start = ((), (), s32[]{:S(2)}) async-start(), calls=%async_computation.9 | async-start | bytes 6266880 | tf_op jit(solution)/shard_map/all_gather | solution.py:383
  45.4 29.5 %all-to-all-start = ((bf16[4,96,1120]{2,1,0:T(8,128)(2,1)}), bf16[4,96,1120]{2,1,0:T(8,128)(2,1)S(1)}, u32[]{:S(2)}, u32[]{:S(2)}) async-start(bf16[4,96,1120]{2,1,0:T(8,128)(2,1)} %copy.121), calls=%async_computation | async-start | bytes 1769472 | tf_op jit(solution)/shard_map/all_to_all | solution.py:97
  48.9 103.1 %all-gather.5.cloned.1.call-start = ((), (), s32[]{:S(2)}) async-start(), calls=%async_computation.10 | async-start | bytes 3342336 | tf_op jit(solution)/shard_map/all_gather | solution.py:410
  94.8 41.8 %collective-permute-start.1 = (bf16[384,1536]{1,0:T(8,128)(2,1)S(1)}, bf16[384,1536]{1,0:T(8,128)(2,1)}, u32[]{:S(2)}, u32[]{:S(2)}) collective-permute-start(bf16[384,1536]{1,0:T(8,128)(2,1)S(1)} %copy-done.6), channel_id=1, source_target_pairs={{0,8},{8,0},{1,9},{9,1},{2,10},{10,2},{3,11},{11,3},{4,12},{12,4},... | collective-permute-start | bytes 3538952 | tf_op jit(solution)/shard_map/ppermute | solution.py:57
  97.0 41.9 %collective-permute-start = (bf16[384,1536]{1,0:T(8,128)(2,1)S(1)}, bf16[384,1536]{1,0:T(8,128)(2,1)}, u32[]{:S(2)}, u32[]{:S(2)}) collective-permute-start(bf16[384,1536]{1,0:T(8,128)(2,1)S(1)} %copy-done.6), channel_id=1, source_target_pairs={{0,2},{2,0},{1,3},{3,1},{4,6},{6,4},{5,7},{7,5},{8,10},{10,8},{9,1... | collective-permute-start | bytes 3538952 | tf_op jit(solution)/shard_map/ppermute | solution.py:57
  102.4 49.5 %all-to-all-start.2 = ((bf16[4,96,1120]{2,1,0:T(8,128)(2,1)}), bf16[4,96,1120]{2,1,0:T(8,128)(2,1)}, u32[]{:S(2)}, u32[]{:S(2)}) async-start(bf16[4,96,1120]{2,1,0:T(8,128)(2,1)} %copy.126), calls=%async_computation.2 | async-start | bytes 1769472 | tf_op jit(solution)/shard_map/all_to_all | solution.py:97
  106.6 601.9 %reduce-scatter.8.cloned.1.call-start = ((), (), s32[]{:S(2)}) async-start(), calls=%async_computation.11 | async-start | bytes 3342336 | tf_op jit(solution)/shard_map/reduce_scatter | solution.py:478
  151.9 62.5 %collective-permute-start.7 = (bf16[1,2,1,192,1120]{4,3,1,2,0:T(8,128)(2,1)S(1)}, bf16[1,2,1,192,1120]{4,3,1,2,0:T(8,128)(2,1)}, u32[]{:S(2)}, u32[]{:S(2)}) collective-permute-start(bf16[1,2,1,192,1120]{4,3,1,2,0:T(8,128)(2,1)S(1)} %bitcast.121), channel_id=1, source_target_pairs={{0,16},{16,0},{1,17},{17,1},{2,18},{18,2},{3,19},{19,3},{4,20},{20... | collective-permute-start | bytes 2580488 | tf_op jit(solution)/shard_map/ppermute | solution.py:57
  155.9 58.5 %collective-permute-start.8 = (bf16[1,2,1,192,1120]{4,3,1,2,0:T(8,128)(2,1)S(1)}, bf16[1,2,1,192,1120]{4,3,1,2,0:T(8,128)(2,1)}, u32[]{:S(2)}, u32[]{:S(2)}) collective-permute-start(bf16[1,2,1,192,1120]{4,3,1,2,0:T(8,128)(2,1)S(1)} %bitcast.122), channel_id=1, source_target_pairs={{0,4},{4,0},{1,5},{5,1},{2,6},{6,2},{3,7},{7,3},{8,12},{12,8},{9,1... | collective-permute-start | bytes 2580488 | tf_op jit(solution)/shard_map/ppermute | solution.py:57
  168.0 49.3 %collective-permute-start.3 = (bf16[384,1536]{1,0:T(8,128)(2,1)}, bf16[384,1536]{1,0:T(8,128)(2,1)}, u32[]{:S(2)}, u32[]{:S(2)}) collective-permute-start(bf16[384,1536]{1,0:T(8,128)(2,1)} %fusion.29), channel_id=1, source_target_pairs={{0,1},{1,0},{2,3},{3,2},{4,5},{5,4},{6,7},{7,6},{8,9},{9,8},{10,11... | collective-permute-start | bytes 3538952 | tf_op jit(solution)/shard_map/ppermute | solution.py:57
  169.6 82.7 %collective-permute-start.10 = (bf16[1,2,1,192,1120]{4,3,1,2,0:T(8,128)(2,1)S(1)}, bf16[1,2,1,192,1120]{4,3,1,2,0:T(8,128)(2,1)S(1)}, u32[]{:S(2)}, u32[]{:S(2)}) collective-permute-start(bf16[1,2,1,192,1120]{4,3,1,2,0:T(8,128)(2,1)S(1)} %bitcast.118), channel_id=1, source_target_pairs={{0,16},{16,0},{1,17},{17,1},{2,18},{18,2},{3,19},{19,3},{4,20},{20... | collective-permute-start | bytes 2580488 | tf_op jit(solution)/shard_map/ppermute | solution.py:57
  183.9 68.4 %collective-permute-start.11 = (bf16[1,2,1,192,1120]{4,3,1,2,0:T(8,128)(2,1)S(1)}, bf16[1,2,1,192,1120]{4,3,1,2,0:T(8,128)(2,1)S(1)}, u32[]{:S(2)}, u32[]{:S(2)}) collective-permute-start(bf16[1,2,1,192,1120]{4,3,1,2,0:T(8,128)(2,1)S(1)} %bitcast.119), channel_id=1, source_target_pairs={{0,4},{4,0},{1,5},{5,1},{2,6},{6,2},{3,7},{7,3},{8,12},{12,8},{9,1... | collective-permute-start | bytes 2580488 | tf_op jit(solution)/shard_map/ppermute | solution.py:57
  214.4 73.1 %collective-permute-start.13 = (bf16[1,2,1,192,1120]{4,3,1,2,0:T(8,128)(2,1)}, bf16[1,2,1,192,1120]{4,3,1,2,0:T(8,128)(2,1)}, u32[]{:S(2)}, u32[]{:S(2)}) collective-permute-start(bf16[1,2,1,192,1120]{4,3,1,2,0:T(8,128)(2,1)} %bitcast.19), channel_id=1, source_target_pairs={{0,16},{16,0},{1,17},{17,1},{2,18},{18,2},{3,19},{19,3},{4,20},{20... | collective-permute-start | bytes 2580488 | tf_op jit(solution)/shard_map/ppermute | solution.py:57
  214.4 68.0 %collective-permute-start.9 = (bf16[1,2,1,192,1120]{4,3,1,2,0:T(8,128)(2,1)}, bf16[1,2,1,192,1120]{4,3,1,2,0:T(8,128)(2,1)S(1)}, u32[]{:S(2)}, u32[]{:S(2)}) collective-permute-start(bf16[1,2,1,192,1120]{4,3,1,2,0:T(8,128)(2,1)} %collective-permute-done.7), channel_id=1, source_target_pairs={{0,4},{4,0},{1,5},{5,1},{2,6},{6,2},{3,7},{7,3},{8,12},{12,8},{9,1... | collective-permute-start | bytes 2580488 | tf_op jit(solution)/shard_map/ppermute | solution.py:57
  219.9 62.4 %collective-permute-start.5 = (bf16[384,1536]{1,0:T(8,128)(2,1)S(1)}, bf16[384,1536]{1,0:T(8,128)(2,1)S(1)}, u32[]{:S(2)}, u32[]{:S(2)}) collective-permute-start(bf16[384,1536]{1,0:T(8,128)(2,1)S(1)} %multiply_convert_fusion.3), channel_id=1, source_target_pairs={{0,8},{8,0},{1,9},{9,1},{2,10},{10,2},{3,11},{11,3},{4,12},{12,4},... | collective-permute-start | bytes 3538952 | tf_op jit(solution)/shard_map/ppermute | solution.py:57
  252.3 30.9 %collective-permute-start.4 = (bf16[384,1536]{1,0:T(8,128)(2,1)S(1)}, bf16[384,1536]{1,0:T(8,128)(2,1)S(1)}, u32[]{:S(2)}, u32[]{:S(2)}) collective-permute-start(bf16[384,1536]{1,0:T(8,128)(2,1)S(1)} %multiply_convert_fusion.3), channel_id=1, source_target_pairs={{0,2},{2,0},{1,3},{3,1},{4,6},{6,4},{5,7},{7,5},{8,10},{10,8},{9,1... | collective-permute-start | bytes 3538952 | tf_op jit(solution)/shard_map/ppermute | solution.py:57
  252.3 30.7 %collective-permute-start.12 = (bf16[1,2,1,192,1120]{4,3,1,2,0:T(8,128)(2,1)S(1)}, bf16[1,2,1,192,1120]{4,3,1,2,0:T(8,128)(2,1)S(1)}, u32[]{:S(2)}, u32[]{:S(2)}) collective-permute-start(bf16[1,2,1,192,1120]{4,3,1,2,0:T(8,128)(2,1)S(1)} %collective-permute-done.10), channel_id=1, source_target_pairs={{0,4},{4,0},{1,5},{5,1},{2,6},{6,2},{3,7},{7,3},{8,12},{12,8},{9,1... | collective-permute-start | bytes 2580488 | tf_op jit(solution)/shard_map/ppermute | solution.py:57
  287.6 54.6 %collective-permute-start.15 = (bf16[1,2,1,192,1120]{4,3,1,2,0:T(8,128)(2,1)}, bf16[1,2,1,192,1120]{4,3,1,2,0:T(8,128)(2,1)}, u32[]{:S(2)}, u32[]{:S(2)}) collective-permute-start(bf16[1,2,1,192,1120]{4,3,1,2,0:T(8,128)(2,1)} %collective-permute-done.13), channel_id=1, source_target_pairs={{0,4},{4,0},{1,5},{5,1},{2,6},{6,2},{3,7},{7,3},{8,12},{12,8},{9,1... | collective-permute-start | bytes 2580488 | tf_op jit(solution)/shard_map/ppermute | solution.py:57
  387.6 41.1 %collective-permute-start.18 = (bf16[2,2,1,192,1120]{4,3,2,1,0:T(8,128)(2,1)S(1)}, bf16[2,2,1,192,1120]{4,3,2,1,0:T(8,128)(2,1)S(1)}, u32[]{:S(2)}, u32[]{:S(2)}) collective-permute-start(bf16[2,2,1,192,1120]{4,3,2,1,0:T(8,128)(2,1)S(1)} %constant_dynamic-slice_fusion.8), channel_id=1, source_target_pairs={{0,4},{4,0},{1,5},{5,1},{2,6},{6,2},{3,7},{7,3},{8,12},{12,8},{9,1... | collective-permute-start | bytes 5160968 | tf_op jit(solution)/shard_map/ppermute | solution.py:57
  392.6 53.3 %collective-permute-start.17 = (bf16[384,1536]{1,0:T(8,128)(2,1)S(1)}, bf16[384,1536]{1,0:T(8,128)(2,1)S(1)}, u32[]{:S(2)}, u32[]{:S(2)}) collective-permute-start(bf16[384,1536]{1,0:T(8,128)(2,1)S(1)} %fusion.23), channel_id=1, source_target_pairs={{0,8},{8,0},{1,9},{9,1},{2,10},{10,2},{3,11},{11,3},{4,12},{12,4},... | collective-permute-start | bytes 3538952 | tf_op jit(solution)/shard_map/ppermute | solution.py:57
  466.5 41.8 %collective-permute-start.22 = (bf16[2,2,1,192,1120]{4,3,2,1,0:T(8,128)(2,1)}, bf16[2,2,1,192,1120]{4,3,2,1,0:T(8,128)(2,1)}, u32[]{:S(2)}, u32[]{:S(2)}) collective-permute-start(bf16[2,2,1,192,1120]{4,3,2,1,0:T(8,128)(2,1)} %constant_dynamic-slice_fusion.6), channel_id=1, source_target_pairs={{0,4},{4,0},{1,5},{5,1},{2,6},{6,2},{3,7},{7,3},{8,12},{12,8},{9,1... | collective-permute-start | bytes 5160968 | tf_op jit(solution)/shard_map/ppermute | solution.py:57
  467.5 40.8 %collective-permute-start.21 = (bf16[384,1536]{1,0:T(8,128)(2,1)}, bf16[384,1536]{1,0:T(8,128)(2,1)}, u32[]{:S(2)}, u32[]{:S(2)}) collective-permute-start(bf16[384,1536]{1,0:T(8,128)(2,1)} %fusion.25), channel_id=1, source_target_pairs={{0,1},{1,0},{2,3},{3,2},{4,5},{5,4},{6,7},{7,6},{8,9},{9,8},{10,11... | collective-permute-start | bytes 3538952 | tf_op jit(solution)/shard_map/ppermute | solution.py:57
  473.9 71.7 %collective-permute-start.24 = (bf16[2,2,1,192,1120]{4,3,2,1,0:T(8,128)(2,1)S(1)}, bf16[2,2,1,192,1120]{4,3,2,1,0:T(8,128)(2,1)S(1)}, u32[]{:S(2)}, u32[]{:S(2)}) collective-permute-start(bf16[2,2,1,192,1120]{4,3,2,1,0:T(8,128)(2,1)S(1)} %constant_dynamic-slice_fusion.5), channel_id=1, source_target_pairs={{0,4},{4,0},{1,5},{5,1},{2,6},{6,2},{3,7},{7,3},{8,12},{12,8},{9,1... | collective-permute-start | bytes 5160968 | tf_op jit(solution)/shard_map/ppermute | solution.py:57
  475.1 88.8 %collective-permute-start.25 = (bf16[1,2,1,192,1120]{4,3,2,1,0:T(8,128)(2,1)S(1)}, bf16[1,2,1,192,1120]{4,3,2,1,0:T(8,128)(2,1)}, u32[]{:S(2)}, u32[]{:S(2)}) collective-permute-start(bf16[1,2,1,192,1120]{4,3,2,1,0:T(8,128)(2,1)S(1)} %copy-done.16), channel_id=1, source_target_pairs={{0,16},{16,0},{1,17},{17,1},{2,18},{18,2},{3,19},{19,3},{4,20},{20... | collective-permute-start | bytes 2580488 | tf_op jit(solution)/shard_map/ppermute | solution.py:57
  479.5 47.1 %collective-permute-start.20 = (bf16[384,1536]{1,0:T(8,128)(2,1)S(1)}, bf16[384,1536]{1,0:T(8,128)(2,1)S(1)}, u32[]{:S(2)}, u32[]{:S(2)}) collective-permute-start(bf16[384,1536]{1,0:T(8,128)(2,1)S(1)} %fusion.20), channel_id=1, source_target_pairs={{0,8},{8,0},{1,9},{9,1},{2,10},{10,2},{3,11},{11,3},{4,12},{12,4},... | collective-permute-start | bytes 3538952 | tf_op jit(solution)/shard_map/ppermute | solution.py:57
  572.6 201.9 %reduce-scatter.12.cloned.1.call-start = ((), (), s32[]{:S(2)}) async-start(), calls=%async_computation.13 | async-start | bytes 5013504
  572.6 42.7 %collective-permute-start.26 = (bf16[1,2,1,192,1120]{4,3,2,1,0:T(8,128)(2,1)}, bf16[1,2,1,192,1120]{4,3,2,1,0:T(8,128)(2,1)S(1)}, u32[]{:S(2)}, u32[]{:S(2)}) collective-permute-start(bf16[1,2,1,192,1120]{4,3,2,1,0:T(8,128)(2,1)} %get-tuple-element.180), channel_id=1, source_target_pairs={{0,16},{16,0},{1,17},{17,1},{2,18},{18,2},{3,19},{19,3},{4,20},{20... | collective-permute-start | bytes 2580488 | tf_op jit(solution)/shard_map/ppermute | solution.py:57
  632.2 30.8 %all-to-all-start.3 = ((bf16[4,96,1120]{2,1,0:T(8,128)(2,1)}), bf16[4,96,1120]{2,1,0:T(8,128)(2,1)}, u32[]{:S(2)}, u32[]{:S(2)}) async-start(bf16[4,96,1120]{2,1,0:T(8,128)(2,1)} %bitcast.134), calls=%async_computation.4 | async-start | bytes 1769472 | tf_op jit(solution)/shard_map/all_to_all | solution.py:167
  636.5 48.7 %collective-permute-start.27 = (bf16[1,2,1,192,1120]{4,3,2,1,0:T(8,128)(2,1)}, bf16[1,2,1,192,1120]{4,3,2,1,0:T(8,128)(2,1)}, u32[]{:S(2)}, u32[]{:S(2)}) collective-permute-start(bf16[1,2,1,192,1120]{4,3,2,1,0:T(8,128)(2,1)} %get-tuple-element.178), channel_id=1, source_target_pairs={{0,16},{16,0},{1,17},{17,1},{2,18},{18,2},{3,19},{19,3},{4,20},{20... | collective-permute-start | bytes 2580488 | tf_op jit(solution)/shard_map/ppermute | solution.py:57
  663.0 28.4 %all-to-all-start.4 = ((bf16[4,96,1120]{2,1,0:T(8,128)(2,1)}), bf16[4,96,1120]{2,1,0:T(8,128)(2,1)}, u32[]{:S(2)}, u32[]{:S(2)}) async-start(bf16[4,96,1120]{2,1,0:T(8,128)(2,1)} %bitcast.133), calls=%async_computation.5 | async-start | bytes 1769472 | tf_op jit(solution)/shard_map/all_to_all | solution.py:167
  667.2 152.2 %reduce-scatter.10.cloned.1.call-start = ((), (), s32[]{:S(2)}) async-start(), calls=%async_computation.12 | async-start | bytes 1253376 | tf_op jit(solution)/shard_map/reduce_scatter | solution.py:519
  716.3 27.3 %collective-permute-start.28 = (bf16[384,1536]{1,0:T(8,128)(2,1)}, bf16[384,1536]{1,0:T(8,128)(2,1)}, u32[]{:S(2)}, u32[]{:S(2)}) collective-permute-start(bf16[384,1536]{1,0:T(8,128)(2,1)} %fusion.9), channel_id=1, source_target_pairs={{0,1},{1,0},{2,3},{3,2},{4,5},{5,4},{6,7},{7,6},{8,9},{9,8},{10,11... | collective-permute-start | bytes 3538952 | tf_op jit(solution)/shard_map/ppermute | solution.py:57
  (51 other events, 917.3 us)
Sparse Core Ops, SparseCore 0:
  15.0 72.0 all-gather.2
  94.9 55.4 all-gather.4
  572.7 103.3 reduce-scatter.7
  679.8 78.7 reduce-scatter.11
  762.0 57.3 reduce-scatter.9

commit v4 on v3

--- a/solution.py
+++ b/solution.py
@@ -49,8 +49,8 @@
     return (back, jnp.sum(grad * normed, axis=0))
 
 
-WIDE = ("zh", "zl", "x", "c")
-GROUP = ("zl", "c")
+WIDE = ("z", "x", "c")
+GROUP = ("x", "c")
 
 
 def other(value, axis):
@@ -67,7 +67,7 @@
 
 def gather_group(own):
     core = other(own, "c")
-    across = other(own, "zl")
+    across = other(own, "x")
     far = other(across, "c")
     return jnp.concatenate([own, core, across, far], axis=0)
 
@@ -78,8 +78,8 @@
     return partial[:rows] + core[:rows], low(partial[2 * rows : 3 * rows] + core[rows:])
 
 
-def sum_low_z(own, across, *earlier):
-    return low(own + after(other(across, "zl"), *earlier).astype(jnp.float32))
+def sum_across(own, across, *earlier):
+    return low(own + after(other(across, "x"), *earlier).astype(jnp.float32))
 
 
 def sum_pair(mine, *earlier):
@@ -95,81 +95,54 @@
     features, hidden = weight.shape
     parts = weight.reshape(features, 4, hidden // 4).transpose(1, 0, 2)
     parts = lax.all_to_all(parts, GROUP, split_axis=0, concat_axis=0, tiled=True)
-    return parts.reshape(1, 2, 1, 2 * features, hidden // 4)
-
-
-def fetch_first(own):
-    if lax.axis_size("zh") == 2:
-        return own, other(own, "zh"), other(own, "x")
-    every = lax.all_gather(own, "zh", axis=0, tiled=True)
-    return every, None, None
-
-
-def fetch_last(pieces, *earlier):
-    own, far, near = pieces
-    high = lax.axis_size("zh")
-    at_x = lax.axis_index("x")
-    whole = jnp.zeros((high, *own.shape[1:2], 2, *own.shape[3:]), jnp.bfloat16)
-    if high == 2:
-        at_high = lax.axis_index("zh")
-        corner = other(after(far, *earlier), "x")
-        placed = (
-            (own, at_high, at_x),
-            (far, 1 - at_high, at_x),
-            (near, at_high, 1 - at_x),
-            (corner, 1 - at_high, 1 - at_x),
-        )
-    else:
-        placed = ((own, 0, at_x), (other(own, "x"), 0, 1 - at_x))
-    return whole, placed
-
-
-def assemble(whole_placed, *earlier):
-    whole, placed = whole_placed
-    for piece, high_place, x_place in placed:
-        whole = lax.dynamic_update_slice(
-            whole, after(piece, *earlier), (high_place, 0, x_place, 0, 0)
-        )
-    high, low_z, across, features, hidden = whole.shape
-    return whole.reshape(high * low_z * across * features, hidden)
-
-
-def split_half(grad, axis, position):
-    at = lax.axis_index(axis)
-    sent = lax.dynamic_slice_in_dim(grad, 1 - at, 1, position)
-    kept = lax.dynamic_slice_in_dim(grad, at, 1, position)
-    return kept, other(sent, axis)
-
-
-def add_half(halves, *earlier):
-    kept, came = halves
-    return low(kept.astype(jnp.float32) + after(came, *earlier).astype(jnp.float32))
-
-
-def collect_first(grad):
-    high = lax.axis_size("zh")
-    return split_half(grad.reshape(high, 2, 2, grad.shape[0] // (4 * high), grad.shape[1]), "x", 2)
-
-
-def collect_second(halves, *earlier):
-    summed = add_half(halves, *earlier)
-    if lax.axis_size("zh") == 2:
-        return split_half(summed, "zh", 0)
-    return lax.psum_scatter(summed, "zh", scatter_dimension=0, tiled=True)
-
-
-def collect_last(halves, *earlier):
-    if lax.axis_size("zh") == 2:
-        halves = add_half(halves, *earlier)
-    features = halves.shape[3] // 2
-    hidden = halves.shape[4]
-    parts = halves.reshape(4, features, hidden)
+    return parts.reshape(4 * features, hidden // 4)
+
+
+def gather_z(own):
+    return lax.all_gather(own, "z", axis=0, tiled=True)
+
+
+def scatter_z(whole):
+    return lax.psum_scatter(whole, "z", scatter_dimension=0, tiled=True)
+
+
+def undeal(grad):
+    features = grad.shape[0] // 4
+    parts = grad.reshape(4, features, grad.shape[1])
     return lax.all_to_all(parts, GROUP, split_axis=0, concat_axis=0, tiled=True)
 
 
-def collect_end(parts):
+def undeal_end(parts):
     count, features, hidden = parts.shape
     return parts.transpose(1, 0, 2).reshape(features, count * hidden).astype(jnp.float32)
+
+
+def gather_rest(column, rows):
+    own = column.reshape(-1, 1, 1, rows, column.shape[1])
+    near = other(own, "x")
+    at_x = lax.axis_index("x")
+    at_c = lax.axis_index("c")
+    whole = jnp.zeros((own.shape[0], 2, 2, *own.shape[3:]), column.dtype)
+    for piece, x_place, c_place in (
+        (own, at_x, at_c),
+        (other(own, "c"), at_x, 1 - at_c),
+        (near, 1 - at_x, at_c),
+        (other(near, "c"), 1 - at_x, 1 - at_c),
+    ):
+        whole = lax.dynamic_update_slice(whole, piece, (0, x_place, c_place, 0, 0))
+    return whole.reshape(-1, column.shape[1])
+
+
+def halve(whole, axis, position):
+    at = lax.axis_index(axis)
+    sent = lax.dynamic_slice_in_dim(whole, 1 - at, 1, position)
+    kept = lax.dynamic_slice_in_dim(whole, at, 1, position)
+    return low(kept.astype(jnp.float32) + other(sent, axis).astype(jnp.float32))
+
+
+def scatter_start(whole, rows):
+    parts = whole.reshape(-1, 2, 2, rows, whole.shape[1])
+    return halve(halve(parts, "c", 2), "x", 1).reshape(-1, whole.shape[1])
 
 
 def rotate_rows(value_rows, cosine, sine):
@@ -377,13 +350,15 @@
     small_rows = -(-sum(small_sizes) // head)
     small = jnp.concatenate(small_parts)
     small = jnp.pad(small, (0, features * head - small.shape[0])).reshape(features, head)
-    packed = jnp.concatenate([w_query, key_projection, value_projection, small, w_out.T], axis=1)
+    pair_column = gather_z(
+        jnp.concatenate([key_projection, value_projection, small], axis=1)
+    )
+    square_column = gather_z(
+        after(jnp.concatenate([w_query, w_out.T], axis=1), small)
+    )
     gate_own = deal(w_gate)
-    up_own = deal(w_up)
-    w_packed = after(lax.all_gather(packed, WIDE, axis=0, tiled=True), gate_own, up_own)
-    w_project = w_packed[:, : projected + head]
-    w_out_all = w_packed[:, projected + head :]
-    small_all = w_project[:, projected:].reshape(devices, features, head)[:, :small_rows]
+    w_pair = gather_rest(pair_column, features)
+    small_all = w_pair[:, 2 * head :].reshape(devices, features, head)[:, :small_rows]
     small_all = small_all.reshape(devices, small_rows * head).astype(jnp.float32)
     cuts = [0]
     for size in small_sizes:
@@ -399,92 +374,81 @@
     inputs = tokens.astype(jnp.float32)
     scale_one = norm_scale(inputs)
     normed_one = low(inputs * scale_one * gain_one)
-    projections = product(normed_one, w_project)
-    query_pre = projections[:, :heads_width] + bias_query
-    key_pre = projections[:, heads_width : heads_width + head] + bias_key
+    projections = product(normed_one, w_pair[:, : 2 * head])
+    key_pre = projections[:, :head] + bias_key
     key_rows = low(
         rotate_halves(key_pre.reshape(rows, 1, head), cosine_table, sine_table).reshape(rows, head)
     )
-    value_rows = low(projections[:, heads_width + head : projected] + bias_value)
-
-    key_value = lax.all_gather(
-        jnp.concatenate([key_rows, value_rows], axis=1), WIDE, axis=0, tiled=True
-    )
-    down_own = deal(w_down.T)
-    cotangent_group = gather_group(cotangent)
-    cotangent_turned = cotangent_group.T
-    gate_own, up_own, down_own, key_value, cotangent_group, cotangent_turned = (
-        lax.optimization_barrier(
-            (gate_own, up_own, down_own, key_value, cotangent_group, cotangent_turned)
-        )
-    )
-    gate_pieces = fetch_first(gate_own)
-    up_pieces = fetch_first(up_own)
-    down_pieces = fetch_first(down_own)
+    value_rows = low(projections[:, head:] + bias_value)
+    key_value = jnp.concatenate([key_rows, value_rows], axis=1)
+    key_value, gate_own = lax.optimization_barrier((key_value, gate_own))
+    key_value_column = gather_z(key_value)
+    up_own = deal(after(w_up, key_value))
+    w_square = gather_rest(square_column, features)
+    w_query_all = w_square[:, :heads_width]
+    w_out_all = w_square[:, heads_width:]
+    query_pre = product(normed_one, w_query_all) + bias_query
+    key_value_column = after(key_value_column, up_own)
+    gate_all = gather_z(after(gate_own, key_value_column))
+    up_all = gather_z(after(up_own, key_value_column))
+    key_value = gather_rest(key_value_column, rows)
+    down_own = deal(after(w_down, key_value_column).T)
+    down_all = gather_z(down_own)
+    cotangent_group = gather_group(after(cotangent, key_value))
+    cotangent_turned = lax.optimization_barrier(cotangent_group.T)
     query_rows, attended, totals = attend(
         bounds, query_pre, cosine_head, sine_head, place, key_value
     )
     attended_low = low(attended)
-    attention = product_right(attended_low, w_out_all)
-    gate_pieces = fetch_last(gate_pieces, attention)
-    middle = inputs + sum_narrow(attention)
+    middle = inputs + sum_narrow(product_right(attended_low, w_out_all))
     scale_two = norm_scale(middle)
     normed_two = low(middle * scale_two * gain_two)
-    up_pieces = fetch_last(up_pieces, normed_two)
     normed_group = gather_group(normed_two)
     normed_turned = lax.optimization_barrier(normed_group.T)
-    gate_all = assemble(gate_pieces, attention)
     gate = product(normed_group, gate_all)
-    up_all = assemble(up_pieces, normed_two)
-    down_pieces = fetch_last(down_pieces, normed_group)
     up_part = product(normed_group, up_all)
     sigmoid_gate = jax.nn.sigmoid(gate)
     silu_gate = gate * sigmoid_gate
     hidden = low(silu_gate * up_part)
     grad_down = low(product(cotangent_turned, hidden))
-    down_halves = collect_first(grad_down)
-    down_all = assemble(down_pieces, normed_group)
+    down_sums = scatter_z(grad_down)
     grad_hidden = product(after(cotangent_group, grad_down), down_all)
     grad_gate = low(grad_hidden * up_part * sigmoid_gate * (1.0 + gate * (1.0 - sigmoid_gate)))
     grad_up = low(grad_hidden * silu_gate)
     grad_normed_part = product_right(grad_gate, gate_all) + product_right(grad_up, up_all)
     grad_normed_own, grad_normed_across = sum_core(grad_normed_part, rows)
-    grad_gate_all = low(
-        product(normed_turned, after(grad_gate, grad_normed_across, down_halves[1]))
-    )
-    down_halves = collect_second(down_halves, grad_normed_across)
-    gate_halves = collect_first(grad_gate_all)
-    grad_up_all = low(product(normed_turned, after(grad_up, grad_gate_all, down_halves[0])))
-    up_halves = collect_first(grad_up_all)
-    grad_normed_mine = sum_low_z(grad_normed_own, grad_normed_across, grad_up_all)
+    grad_gate_all = low(product(normed_turned, after(grad_gate, grad_normed_across)))
+    gate_sums = scatter_z(grad_gate_all)
+    grad_up_all = low(product(normed_turned, after(grad_up, grad_gate_all)))
+    up_sums = scatter_z(grad_up_all)
+    grad_normed_mine = sum_across(grad_normed_own, grad_normed_across, grad_up_all)
     down_part = product_right(after(hidden, grad_normed_mine), down_all)
     down_mine, down_across = sum_core(down_part, rows)
-    grad_normed_two = sum_pair(grad_normed_mine, down_across, gate_halves[1])
-    down_mine = sum_low_z(down_mine, down_across, grad_normed_two)
+    grad_normed_two = sum_pair(grad_normed_mine, down_across)
+    down_mine = sum_across(down_mine, down_across, grad_normed_two)
     result = low(middle + sum_pair(down_mine))
-    down_parts = collect_last(down_halves, grad_normed_two)
-    gate_halves = collect_second(gate_halves, grad_normed_two)
 
     back_two, grad_gain_two = norm_back(middle, scale_two, gain_two, grad_normed_two)
     grad_middle = cotangent.astype(jnp.float32) + back_two
     grad_att = low(grad_middle)
     grad_out_all = product_left(attended_low, grad_att).T
     grad_attended = product(grad_att, w_out_all)
-    up_halves = collect_second(up_halves, gate_halves[0])
     grad_query_pre, buffer = attend_back(
-        bounds, query_rows, after(grad_attended, up_halves[0], down_halves[1]), attended, totals,
+        bounds, query_rows, grad_attended, attended, totals,
         cosine_head, sine_head, place, key_value,
     )
-    key_value_grads = lax.psum_scatter(buffer, WIDE, scatter_dimension=0, tiled=True)
-    gate_parts = collect_last(gate_halves, buffer)
+    key_value_grads = scatter_z(scatter_start(buffer, rows))
     square_grads = low(
         jnp.concatenate([product_left(grad_query_pre, normed_one).T, grad_out_all], axis=1)
     )
-    up_parts = collect_last(up_halves, gate_parts)
+    square_grads = scatter_start(square_grads, features)
+    down_parts = undeal(after(down_sums, buffer))
+    gate_parts = undeal(after(gate_sums, buffer))
+    grad_query_part = product_right(grad_query_pre, w_query_all)
     key_value_grads = after(
-        key_value_grads, square_grads, gate_parts, down_parts, up_parts
+        key_value_grads, square_grads, down_parts, gate_parts, grad_query_part
     ).astype(jnp.float32)
-    square_grads = lax.psum_scatter(square_grads, WIDE, scatter_dimension=0, tiled=True)
+    square_grads = scatter_z(square_grads)
     grad_key_pre = low(
         rotate_halves(key_value_grads[:, :head].reshape(rows, 1, head), cosine_table, -sine_table)
     ).reshape(rows, head)
@@ -492,7 +456,10 @@
     grad_pair = jnp.concatenate([grad_key_pre, grad_value_pre], axis=1)
     grad_project = jnp.concatenate([grad_query_pre, grad_pair], axis=1)
     grad_bias = jnp.sum(grad_project.astype(jnp.float32), axis=0)
-    grad_normed_one = sum_narrow(product_right(grad_project, w_project[:, :projected]))
+    up_parts = undeal(after(up_sums, grad_pair))
+    grad_normed_one = sum_pair(
+        low(grad_query_part + product_right(grad_pair, w_pair[:, : 2 * head])), up_parts
+    )
     back_one, grad_gain_one = norm_back(inputs, scale_one, gain_one, grad_normed_one)
     grad_tokens = low(grad_middle + back_one)
 
@@ -516,15 +483,13 @@
             axis=1,
         )
     )
-    packed_grads = lax.psum_scatter(packed_grads, WIDE, scatter_dimension=0, tiled=True).astype(
-        jnp.float32
-    )
+    packed_grads = scatter_z(scatter_start(packed_grads, features)).astype(jnp.float32)
     small_own = packed_grads[:, 2 * head :].reshape(-1)
     square_grads = square_grads.astype(jnp.float32)
     grad_w_out = square_grads[:, heads_width:].T
-    grad_w_down = collect_end(down_parts).T
-    grad_w_gate = collect_end(gate_parts)
-    grad_w_up = collect_end(up_parts)
+    grad_w_down = undeal_end(down_parts).T
+    grad_w_gate = undeal_end(gate_parts)
+    grad_w_up = undeal_end(up_parts)
     return (
         result,
         grad_tokens,
@@ -545,7 +510,7 @@
 
 def solution(mesh):
     wide, narrow = mesh.devices.shape
-    grouped = Mesh(mesh.devices.reshape(wide // 8, 2, 2, 2, narrow), WIDE + ("y",))
+    grouped = Mesh(mesh.devices.reshape(wide // 4, 2, 2, narrow), WIDE + ("y",))
     rows = P(WIDE, None)
     vector = P(WIDE)
     columns = P(WIDE, "y")

time: 842 us -> 704 us (0.84)
  waiting for transfers between devices: 411 us -> 276 us
  blocking collectives: 17.1 us -> 36 us
  starting transfers between devices: 78.3 us -> 61.8 us
  other arithmetic: 68.7 us -> 59.4 us
    ppermute x29, waiting for transfers between devices: 280 us -> 166 us  [other(): return lax.ppermute(value, axis, [(0, 1), (1, 0)])]
    all_to_all x3, waiting for transfers between devices: 49.1 us -> 12.1 us  [deal(): lax.all_to_all(parts, GROUP, split_axis=0, concat_axis=0, tiled=True)]
    all_gather x0 -> x2, blocking collectives: none -> 36 us  [gather_z(): return lax.all_gather(own, 'z', axis=0, tiled=True)]
    reduce_scatter x2 -> x3, waiting for transfers between devices: 41.8 us -> 13.2 us  [scatter_z(): return lax.psum_scatter(whole, 'z', scatter_dimension=0, tiled=True)]
    unnamed x6 -> x13, waiting for transfers between devices: 0.08 us -> 22.7 us
    all_gather x2 -> x4, waiting for transfers between devices: 12.2 us -> 33.3 us  [gather_z(): return lax.all_gather(own, 'z', axis=0, tiled=True)]
    ppermute x29, starting transfers between devices: 57.7 us -> 37.5 us  [other(): return lax.ppermute(value, axis, [(0, 1), (1, 0)])]
    all_to_all x1 -> x0, blocking collectives: 17.1 us -> none  [collect_last(): return lax.all_to_all(parts, GROUP, split_axis=0, concat_axis=0, tiled=True)]
  transfers between devices with their start and end apart: 39 -> 45, of which waited for: 21 -> 20; matrix products, arithmetic and copies ran while one was open for 25% -> 33% of each run, Pallas kernels for 1% -> 2%
where the time goes in v4:
time: 704 us; the launch traced here: 692 us
  waiting for transfers between devices  276 us (39%)
  matrix products  118 us (17%)
  local copies, waits for them, and re-layouts  109 us (15%)
  starting transfers between devices  61.8 us (9%)
  other arithmetic  59.4 us (8%)
  blocking collectives  36 us (5%)
  between operations  17.6 us (3%)
  Pallas kernels  15.1 us (2%)
    ppermute x29, waiting for transfers between devices, other(): return lax.ppermute(value, axis, [(0, 1), (1, 0)])  166 us
    dot_general x9, matrix products, product(): return jnp.dot(left, right, preferred_element_type=jnp.float32)  69 us
    dot_general x6, matrix products, product_right(): lax.dot_general(left, right, (((1,), (1,)), ((), ())), preferred_element_...  41.5 us
    ppermute x29, starting transfers between devices, other(): return lax.ppermute(value, axis, [(0, 1), (1, 0)])  37.5 us
    all_gather x2, blocking collectives, gather_z(): return lax.all_gather(own, 'z', axis=0, tiled=True)  36 us
    all_gather x4, waiting for transfers between devices, gather_z(): return lax.all_gather(own, 'z', axis=0, tiled=True)  33.3 us
    unnamed x114, local copies, waits for them, and re-layouts  31 us
    all_to_all x3, waiting for transfers between devices, undeal(): return lax.all_to_all(parts, GROUP, split_axis=0, concat_axis=0, tiled=True)  29.4 us
  transfers between devices with their start and end apart: 45, of which 20 were waited for; matrix products, arithmetic and copies ran while one was open for 33% of the time, Pallas kernels for 2%

profile of v4, /device:TPU:0, one launch (start us, length us, event | category | flops | bytes accessed | tf_op | source)
XLA Modules:
  0.0 692.3 jit_solution(10150525370451224672)
XLA Ops:
  11.5 15.7 %all_gather.18 = bf16[384,384]{1,0:T(8,128)(2,1)S(1)} all-gather(bf16[96,384]{1,0:T(8,128)(2,1)S(1)} %pad_maximum_fusion.8), channel_id=1, replica_groups=mesh['z'=4,'x'=2,'c'=2,'y'=2] {'z'}, dimensions={0}, use_global_device_ids=true | all-gather | bytes 368640 | tf_op jit(solution)/shard_map/all_gather | solution.py:102
  57.7 20.3 %all_gather.20 = bf16[1536,256]{1,0:T(8,128)(2,1)S(1)} all-gather(bf16[384,256]{1,0:T(8,128)(2,1)S(1)} %pad_maximum_fusion.6), channel_id=1, replica_groups=mesh['z'=4,'x'=2,'c'=2,'y'=2] {'z'}, dimensions={0}, use_global_device_ids=true | all-gather | bytes 983040 | tf_op jit(solution)/shard_map/all_gather | solution.py:102
  84.3 37.3 %collective-permute-done.7 = bf16[4,1,1,384,256]{4,3,2,1,0:T(8,128)(2,1)} collective-permute-done((bf16[4,1,1,384,256]{4,3,2,1,0:T(8,128)(2,1)S(1)}, bf16[4,1,1,384,256]{4,3,2,1,0:T(8,128)(2,1)}, u32[]{:S(2)}, u32[]{:S(2)}) %collective-permute-start.7) | collective-permute-done | bytes 786464 | tf_op jit(solution)/shard_map/ppermute | solution.py:57
  135.3 6.5 attend.1
  151.1 21.6 %collective-permute-done.9 = bf16[384,1536]{1,0:T(8,128)(2,1)} collective-permute-done((bf16[384,1536]{1,0:T(8,128)(2,1)S(1)}, bf16[384,1536]{1,0:T(8,128)(2,1)}, u32[]{:S(2)}, u32[]{:S(2)}) %collective-permute-start.9) | collective-permute-done | bytes 1179680 | tf_op jit(solution)/shard_map/ppermute | solution.py:57
  189.6 17.2 %collective-permute-done.11 = bf16[384,1536]{1,0:T(8,128)(2,1)} collective-permute-done((bf16[384,1536]{1,0:T(8,128)(2,1)S(1)}, bf16[384,1536]{1,0:T(8,128)(2,1)}, u32[]{:S(2)}, u32[]{:S(2)}) %collective-permute-start.11) | collective-permute-done | bytes 1179680 | tf_op jit(solution)/shard_map/ppermute | solution.py:57
  208.6 7.7 %all-to-all-done.2 = bf16[4,96,1120]{2,1,0:T(8,128)(2,1)S(1)} async-done(((bf16[4,96,1120]{2,1,0:T(8,128)(2,1)}), bf16[4,96,1120]{2,1,0:T(8,128)(2,1)S(1)}, u32[]{:S(2)}, u32[]{:S(2)}) %all-to-all-start.2) | async-done | bytes 860192 | tf_op jit(solution)/shard_map/all_to_all | solution.py:97
  225.5 11.4 %fusion.71 = f32[1536,1120]{0,1:T(8,128)} fusion(bf16[1536,1120]{1,0:T(8,128)(2,1)} %all-gather.7.cloned.1.call-done, bf16[384,1536]{1,0:T(8,128)(2,1)} %collective-permute-done.12, bf16[384,1536]{1,0:T(8,128)(2,1)} %collective-permute-done.11, bf16[384,1536]{1,0:T(8,128)(2,1)} %collective-permute-done.10, bf16[384,1536]{1,0:T(8,128)(2,1)S(1)} %multiply_convert_fusion.3), kind=kOutput, calls=%fused_computation.171 | convolution fusion | flops 5303697408 | bytes 15040512 | tf_op jit(solution)/shard_map/dot_general | solution.py:16
  236.9 13.1 %multiply_convert_fusion.2 = (bf16[1536,1120]{0,1:T(8,128)(2,1)S(1)}, f32[1536,1120]{0,1:T(8,128)}) fusion(f32[1536,1120]{0,1:T(8,128)} %fusion.71, bf16[1536,1120]{1,0:T(8,128)(2,1)} %all-gather.9.cloned.1.call-done, bf16[384,1536]{1,0:T(8,128)(2,1)} %collective-permute-done.12, bf16[384,1536]{1,0:T(8,128)(2,1)} %collective-permute-done.11, ...), kind=kOutput, calls=%fused_computation.6 | convolution fusion | flops 5314019328 | bytes 25362432 | tf_op jit(solution)/shard_map/dot_general | solution.py:16
  251.8 9.3 %convolution_convert_fusion.2 = bf16[1536,1120]{0,1:T(8,128)(2,1)} fusion(bf16[1536,1120]{0,1:T(8,128)(2,1)S(1)} %get-tuple-element.54, bf16[1536,1536]{0,1:T(8,128)(2,1)} %bitcast.26), kind=kOutput, calls=%fused_computation.3 | convolution fusion | flops 5286543360 | bytes 11599872 | tf_op jit(solution)/shard_map/dot_general | solution.py:16
  261.1 33.3 %all-gather.11.cloned.1.call-done = bf16[1536,1120]{1,0:T(8,128)(2,1)} async-done(((bf16[384,1120]{1,0:T(8,128)(2,1)}), bf16[1536,1120]{1,0:T(8,128)(2,1)}) %all-gather.11.cloned.1.call-update) | async-done | bytes 3440656 | tf_op jit(solution)/shard_map/all_gather | solution.py:102
  294.4 15.7 %multiply_convert_fusion = (bf16[1536,1120]{0,1:T(8,128)(2,1)}, bf16[1536,1120]{0,1:T(8,128)(2,1)}) fusion(f32[1536,1120]{0,1:T(8,128)} %fusion.71, f32[1536,1120]{0,1:T(8,128)} %get-tuple-element.107, bf16[1536,1536]{1,0:T(8,128)(2,1)} %constant_dynamic-update-slice_fusion, bf16[1536,1120]{1,0:T(8,128)(2,1)} %all-gather.11.cloned.1.call-done), kind=kOutput, calls=%fused_computation.4 | convolution fusion | flops 5307187200 | bytes 28803072 | tf_op jit(solution)/shard_map/dot_general | solution.py:16
  310.2 11.4 %fusion.81 = f32[1536,1536]{1,0:T(8,128)} fusion(bf16[1536,1120]{0,1:T(8,128)(2,1)} %get-tuple-element.51, bf16[1536,1120]{1,0:T(8,128)(2,1)S(1)} %copy-done.43), kind=kOutput, calls=%fused_computation.181 | convolution fusion | flops 5284823040 | bytes 16318464 | tf_op jit(solution)/shard_map/dot_general | solution.py:26
  321.6 12.5 %fusion.79 = (bf16[1536,1536]{1,0:T(8,128)(2,1)S(1)}, f32[1536,1536]{1,0:T(8,128)}) fusion(f32[1536,1536]{1,0:T(8,128)} %fusion.81, bf16[1536,1120]{0,1:T(8,128)(2,1)} %get-tuple-element.52, bf16[1536,1120]{1,0:T(8,128)(2,1)S(1)} %copy-done.44), kind=kOutput, calls=%fused_computation.179 | convolution fusion | flops 5289541632 | bytes 30474240 | tf_op jit(solution)/shard_map/dot_general | solution.py:26
  335.9 5.7 copy.162
  341.6 4.9 fusion.69
  351.1 7.4 %convolution_convert_fusion.1 = bf16[1536,1120]{0,1:T(8,128)(2,1)} fusion(bf16[1536,1120]{0,1:T(8,128)(2,1)S(1)} %copy-done.50, bf16[1536,1536]{0,1:T(8,128)(2,1)S(1)} %copy-done.11), kind=kOutput, calls=%fused_computation.2 | convolution fusion | flops 5286543360 | bytes 11599872 | tf_op jit(solution)/shard_map/dot_general | solution.py:16
  358.4 7.0 %convolution_convert_fusion = bf16[1536,1120]{0,1:T(8,128)(2,1)} fusion(bf16[1536,1120]{0,1:T(8,128)(2,1)S(1)} %copy-done.47, bf16[1536,1536]{0,1:T(8,128)(2,1)S(1)} %copy-done.11), kind=kOutput, calls=%fused_computation.1 | convolution fusion | flops 5286543360 | bytes 11599872 | tf_op jit(solution)/shard_map/dot_general | solution.py:16
  365.4 12.6 %collective-permute-done.17 = bf16[384,1536]{1,0:T(8,128)(2,1)S(1)} collective-permute-done((bf16[384,1536]{1,0:T(8,128)(2,1)S(1)}, bf16[384,1536]{1,0:T(8,128)(2,1)S(1)}, u32[]{:S(2)}, u32[]{:S(2)}) %collective-permute-start.17) | collective-permute-done | bytes 1179680 | tf_op jit(solution)/shard_map/ppermute | solution.py:57
  380.3 6.4 fusion.80
  387.1 4.5 collective-permute-done.18
  396.2 5.7 copy.164
  403.7 19.3 %collective-permute-done.19 = bf16[384,1536]{1,0:T(8,128)(2,1)} collective-permute-done((bf16[384,1536]{1,0:T(8,128)(2,1)}, bf16[384,1536]{1,0:T(8,128)(2,1)}, u32[]{:S(2)}, u32[]{:S(2)}) %collective-permute-start.19) | collective-permute-done | bytes 1179680 | tf_op jit(solution)/shard_map/ppermute | solution.py:57
  432.5 22.8 %collective-permute-done.21 = bf16[384,1536]{1,0:T(8,128)(2,1)S(1)} collective-permute-done((bf16[384,1536]{1,0:T(8,128)(2,1)S(1)}, bf16[384,1536]{1,0:T(8,128)(2,1)S(1)}, u32[]{:S(2)}, u32[]{:S(2)}) %collective-permute-start.21) | collective-permute-done | bytes 1179680 | tf_op jit(solution)/shard_map/ppermute | solution.py:57
  459.7 8.6 %attend_back.1 = (bf16[384,768]{1,0:T(8,128)(2,1)}, bf16[6144,256]{1,0:T(8,128)(2,1)}) custom-call(s32[2]{0:T(128)} %pad_add_fusion.bounds_ref, bf16[384,768]{1,0:T(8,128)(2,1)} %get-tuple-element.57.rotated_ref, f32[384,768]{1,0:T(8,128)} %fusion.23.grad_ref, f32[384,768]{1,0:T(8,128)} %get-tuple-element.44.attended_ref, ...), custom_call_target="tpu_custom_call" | custom-call | flops 10192158720 | bytes 31457280 | tf_op jit(solution)/shard_map/attend_back/pallas_call | solution.py:285
  475.4 6.1 collective-permute-start.23
  481.4 18.1 %collective-permute-done.23 = bf16[4,1,1,384,256]{4,3,2,1,0:T(8,128)(2,1)S(1)} collective-permute-done((bf16[4,1,1,384,256]{4,3,2,1,0:T(8,128)(2,1)S(1)}, bf16[4,1,1,384,256]{4,3,2,1,0:T(8,128)(2,1)S(1)}, u32[]{:S(2)}, u32[]{:S(2)}) %collective-permute-start.23) | collective-permute-done | bytes 786464 | tf_op jit(solution)/shard_map/ppermute | solution.py:57
  533.6 23.0 %all-to-all-done.3 = bf16[4,96,1120]{2,1,0:T(8,128)(2,1)} async-done(((bf16[4,96,1120]{2,1,0:T(8,128)(2,1)}), bf16[4,96,1120]{2,1,0:T(8,128)(2,1)}, u32[]{:S(2)}, u32[]{:S(2)}) %all-to-all-start.3) | async-done | bytes 860192 | tf_op jit(solution)/shard_map/all_to_all | solution.py:112
  560.8 4.5 fusion.26
  568.0 5.5 all-to-all-done.4
  582.5 22.5 %reduce-scatter.23.cloned.1.call-done = bf16[384,1120]{1,0:T(8,128)(2,1)} async-done(((bf16[1536,1120]{1,0:T(8,128)(2,1)}), bf16[384,1120]{1,0:T(8,128)(2,1)}) %reduce-scatter.23.cloned.1.call-update) | async-done | bytes 860176
  667.3 13.2 %reduce-scatter.15.cloned.1.call-done = bf16[96,384]{1,0:T(8,128)(2,1)} async-done(((bf16[384,384]{1,0:T(8,128)(2,1)}), bf16[96,384]{1,0:T(8,128)(2,1)}) %reduce-scatter.15.cloned.1.call-update) | async-done | bytes 73744 | tf_op jit(solution)/shard_map/reduce_scatter | solution.py:106
  (335 shorter events, 244.0 us)
Async XLA Ops:
  7.2 70.9 %all-gather.5.cloned.1.call-start = ((), (), s32[]{:S(2)}) async-start(), calls=%async_computation.12 | async-start | bytes 1474560 | tf_op jit(solution)/shard_map/all_gather | solution.py:102
  54.1 23.9 %all-to-all-start.1 = ((bf16[4,96,1120]{2,1,0:T(8,128)(2,1)}), bf16[4,96,1120]{2,1,0:T(8,128)(2,1)S(1)}, u32[]{:S(2)}, u32[]{:S(2)}) async-start(bf16[4,96,1120]{2,1,0:T(8,128)(2,1)} %bitcast.129), calls=%async_computation.1 | async-start | bytes 1769472 | tf_op jit(solution)/shard_map/all_to_all | solution.py:97
  57.6 167.9 %all-gather.7.cloned.1.call-start = ((), (), s32[]{:S(2)}) async-start(), calls=%async_computation.13 | async-start | bytes 4423680 | tf_op jit(solution)/shard_map/all_gather | solution.py:102
  78.1 158.9 %all-gather.9.cloned.1.call-start = ((), (), s32[]{:S(2)}) async-start(), calls=%async_computation.14 | async-start | bytes 4423680 | tf_op jit(solution)/shard_map/all_gather | solution.py:102
  78.1 45.7 %collective-permute-start.4 = (bf16[4,1,1,96,1536]{4,3,2,1,0:T(8,128)(2,1)}, bf16[4,1,1,96,1536]{4,3,2,1,0:T(8,128)(2,1)}, u32[]{:S(2)}, u32[]{:S(2)}) collective-permute-start(bf16[4,1,1,96,1536]{4,3,2,1,0:T(8,128)(2,1)} %bitcast.147), channel_id=1, source_target_pairs={{0,4},{4,0},{1,5},{5,1},{2,6},{6,2},{3,7},{7,3},{8,12},{12,8},{9,1... | collective-permute-start | bytes 3538952 | tf_op jit(solution)/shard_map/ppermute | solution.py:57
  80.1 41.5 %collective-permute-start.7 = (bf16[4,1,1,384,256]{4,3,2,1,0:T(8,128)(2,1)S(1)}, bf16[4,1,1,384,256]{4,3,2,1,0:T(8,128)(2,1)}, u32[]{:S(2)}, u32[]{:S(2)}) collective-permute-start(bf16[4,1,1,384,256]{4,3,2,1,0:T(8,128)(2,1)S(1)} %bitcast.142), channel_id=1, source_target_pairs={{0,4},{4,0},{1,5},{5,1},{2,6},{6,2},{3,7},{7,3},{8,12},{12,8},{9,1... | collective-permute-start | bytes 2359304 | tf_op jit(solution)/shard_map/ppermute | solution.py:57
  83.0 42.2 %collective-permute-start.6 = (bf16[4,1,1,384,256]{4,3,2,1,0:T(8,128)(2,1)S(1)}, bf16[4,1,1,384,256]{4,3,2,1,0:T(8,128)(2,1)}, u32[]{:S(2)}, u32[]{:S(2)}) collective-permute-start(bf16[4,1,1,384,256]{4,3,2,1,0:T(8,128)(2,1)S(1)} %bitcast.143), channel_id=1, source_target_pairs={{0,2},{2,0},{1,3},{3,1},{4,6},{6,4},{5,7},{7,5},{8,10},{10,8},{9,1... | collective-permute-start | bytes 2359304 | tf_op jit(solution)/shard_map/ppermute | solution.py:57
  83.1 45.7 %collective-permute-start.3 = (bf16[4,1,1,96,1536]{4,3,2,1,0:T(8,128)(2,1)}, bf16[4,1,1,96,1536]{4,3,2,1,0:T(8,128)(2,1)}, u32[]{:S(2)}, u32[]{:S(2)}) collective-permute-start(bf16[4,1,1,96,1536]{4,3,2,1,0:T(8,128)(2,1)} %bitcast.148), channel_id=1, source_target_pairs={{0,2},{2,0},{1,3},{3,1},{4,6},{6,4},{5,7},{7,5},{8,10},{10,8},{9,1... | collective-permute-start | bytes 3538952 | tf_op jit(solution)/shard_map/ppermute | solution.py:57
  145.0 27.7 %collective-permute-start.9 = (bf16[384,1536]{1,0:T(8,128)(2,1)S(1)}, bf16[384,1536]{1,0:T(8,128)(2,1)}, u32[]{:S(2)}, u32[]{:S(2)}) collective-permute-start(bf16[384,1536]{1,0:T(8,128)(2,1)S(1)} %convolution_convert_fusion.5), channel_id=1, source_target_pairs={{0,1},{1,0},{2,3},{3,2},{4,5},{5,4},{6,7},{7,6},{8,9},{9,8},{10,11... | collective-permute-start | bytes 3538952 | tf_op jit(solution)/shard_map/ppermute | solution.py:57
  146.7 42.4 %collective-permute-start.14 = (bf16[384,1536]{1,0:T(8,128)(2,1)S(1)}, bf16[384,1536]{1,0:T(8,128)(2,1)}, u32[]{:S(2)}, u32[]{:S(2)}) collective-permute-start(bf16[384,1536]{1,0:T(8,128)(2,1)S(1)} %copy-done.9), channel_id=1, source_target_pairs={{0,4},{4,0},{1,5},{5,1},{2,6},{6,2},{3,7},{7,3},{8,12},{12,8},{9,1... | collective-permute-start | bytes 3538952 | tf_op jit(solution)/shard_map/ppermute | solution.py:57
  176.3 30.6 %collective-permute-start.11 = (bf16[384,1536]{1,0:T(8,128)(2,1)S(1)}, bf16[384,1536]{1,0:T(8,128)(2,1)}, u32[]{:S(2)}, u32[]{:S(2)}) collective-permute-start(bf16[384,1536]{1,0:T(8,128)(2,1)S(1)} %multiply_convert_fusion.3), channel_id=1, source_target_pairs={{0,4},{4,0},{1,5},{5,1},{2,6},{6,2},{3,7},{7,3},{8,12},{12,8},{9,1... | collective-permute-start | bytes 3538952 | tf_op jit(solution)/shard_map/ppermute | solution.py:57
  180.7 37.6 %collective-permute-start.13 = (bf16[384,1536]{1,0:T(8,128)(2,1)S(1)}, bf16[384,1536]{1,0:T(8,128)(2,1)}, u32[]{:S(2)}, u32[]{:S(2)}) collective-permute-start(bf16[384,1536]{1,0:T(8,128)(2,1)S(1)} %copy-done.9), channel_id=1, source_target_pairs={{0,2},{2,0},{1,3},{3,1},{4,6},{6,4},{5,7},{7,5},{8,10},{10,8},{9,1... | collective-permute-start | bytes 3538952 | tf_op jit(solution)/shard_map/ppermute | solution.py:57
  185.5 30.8 %all-to-all-start.2 = ((bf16[4,96,1120]{2,1,0:T(8,128)(2,1)}), bf16[4,96,1120]{2,1,0:T(8,128)(2,1)S(1)}, u32[]{:S(2)}, u32[]{:S(2)}) async-start(bf16[4,96,1120]{2,1,0:T(8,128)(2,1)} %bitcast.128), calls=%async_computation.2 | async-start | bytes 1769472 | tf_op jit(solution)/shard_map/all_to_all | solution.py:97
  189.0 105.4 %all-gather.11.cloned.1.call-start = ((), (), s32[]{:S(2)}) async-start(), calls=%async_computation.15 | async-start | bytes 4423680 | tf_op jit(solution)/shard_map/all_gather | solution.py:102
  189.1 34.1 %collective-permute-start.15 = (bf16[384,1536]{1,0:T(8,128)(2,1)}, bf16[384,1536]{1,0:T(8,128)(2,1)}, u32[]{:S(2)}, u32[]{:S(2)}) collective-permute-start(bf16[384,1536]{1,0:T(8,128)(2,1)} %collective-permute-done.14), channel_id=1, source_target_pairs={{0,2},{2,0},{1,3},{3,1},{4,6},{6,4},{5,7},{7,5},{8,10},{10,8},{9,1... | collective-permute-start | bytes 3538952 | tf_op jit(solution)/shard_map/ppermute | solution.py:57
  189.5 36.0 %collective-permute-start.10 = (bf16[384,1536]{1,0:T(8,128)(2,1)S(1)}, bf16[384,1536]{1,0:T(8,128)(2,1)}, u32[]{:S(2)}, u32[]{:S(2)}) collective-permute-start(bf16[384,1536]{1,0:T(8,128)(2,1)S(1)} %multiply_convert_fusion.3), channel_id=1, source_target_pairs={{0,2},{2,0},{1,3},{3,1},{4,6},{6,4},{5,7},{7,5},{8,10},{10,8},{9,1... | collective-permute-start | bytes 3538952 | tf_op jit(solution)/shard_map/ppermute | solution.py:57
  206.9 18.6 %collective-permute-start.12 = (bf16[384,1536]{1,0:T(8,128)(2,1)}, bf16[384,1536]{1,0:T(8,128)(2,1)}, u32[]{:S(2)}, u32[]{:S(2)}) collective-permute-start(bf16[384,1536]{1,0:T(8,128)(2,1)} %collective-permute-done.11), channel_id=1, source_target_pairs={{0,2},{2,0},{1,3},{3,1},{4,6},{6,4},{5,7},{7,5},{8,10},{10,8},{9,1... | collective-permute-start | bytes 3538952 | tf_op jit(solution)/shard_map/ppermute | solution.py:57
  217.2 303.3 %reduce-scatter.19.cloned.1.call-start = ((), (), s32[]{:S(2)}) async-start(), calls=%async_computation.19 | async-start | bytes 4423680
  346.5 182.6 %reduce-scatter.21.cloned.1.call-start = ((), (), s32[]{:S(2)}) async-start(), calls=%async_computation.20 | async-start | bytes 4423680
  349.5 28.4 %collective-permute-start.17 = (bf16[384,1536]{1,0:T(8,128)(2,1)S(1)}, bf16[384,1536]{1,0:T(8,128)(2,1)S(1)}, u32[]{:S(2)}, u32[]{:S(2)}) collective-permute-start(bf16[384,1536]{1,0:T(8,128)(2,1)S(1)} %fusion.19), channel_id=1, source_target_pairs={{0,4},{4,0},{1,5},{5,1},{2,6},{6,2},{3,7},{7,3},{8,12},{12,8},{9,1... | collective-permute-start | bytes 3538952 | tf_op jit(solution)/shard_map/ppermute | solution.py:57
  394.7 28.3 %collective-permute-start.19 = (bf16[384,1536]{1,0:T(8,128)(2,1)}, bf16[384,1536]{1,0:T(8,128)(2,1)}, u32[]{:S(2)}, u32[]{:S(2)}) collective-permute-start(bf16[384,1536]{1,0:T(8,128)(2,1)} %fusion.16), channel_id=1, source_target_pairs={{0,4},{4,0},{1,5},{5,1},{2,6},{6,2},{3,7},{7,3},{8,12},{12,8},{9,1... | collective-permute-start | bytes 3538952 | tf_op jit(solution)/shard_map/ppermute | solution.py:57
  401.9 171.6 %reduce-scatter.13.cloned.1.call-start = ((), (), s32[]{:S(2)}) async-start(), calls=%async_computation.16 | async-start | bytes 983040 | tf_op jit(solution)/shard_map/reduce_scatter | solution.py:106
  402.2 28.9 %collective-permute-start.20 = (bf16[384,1536]{1,0:T(8,128)(2,1)S(1)}, bf16[384,1536]{1,0:T(8,128)(2,1)S(1)}, u32[]{:S(2)}, u32[]{:S(2)}) collective-permute-start(bf16[384,1536]{1,0:T(8,128)(2,1)S(1)} %fusion.21), channel_id=1, source_target_pairs={{0,1},{1,0},{2,3},{3,2},{4,5},{5,4},{6,7},{7,6},{8,9},{9,8},{10,11... | collective-permute-start | bytes 3538952 | tf_op jit(solution)/shard_map/ppermute | solution.py:57
  426.3 28.9 %collective-permute-start.21 = (bf16[384,1536]{1,0:T(8,128)(2,1)S(1)}, bf16[384,1536]{1,0:T(8,128)(2,1)S(1)}, u32[]{:S(2)}, u32[]{:S(2)}) collective-permute-start(bf16[384,1536]{1,0:T(8,128)(2,1)S(1)} %fusion.18), channel_id=1, source_target_pairs={{0,1},{1,0},{2,3},{3,2},{4,5},{5,4},{6,7},{7,6},{8,9},{9,8},{10,11... | collective-permute-start | bytes 3538952 | tf_op jit(solution)/shard_map/ppermute | solution.py:57
  475.4 24.1 %collective-permute-start.23 = (bf16[4,1,1,384,256]{4,3,2,1,0:T(8,128)(2,1)S(1)}, bf16[4,1,1,384,256]{4,3,2,1,0:T(8,128)(2,1)S(1)}, u32[]{:S(2)}, u32[]{:S(2)}) collective-permute-start(bf16[4,1,1,384,256]{4,3,2,1,0:T(8,128)(2,1)S(1)} %constant_dynamic-slice_fusion.2), channel_id=1, source_target_pairs={{0,4},{4,0},{1,5},{5,1},{2,6},{6,2},{3,7},{7,3},{8,12},{12,8},{9,1... | collective-permute-start | bytes 2359304 | tf_op jit(solution)/shard_map/ppermute | solution.py:57
  500.6 104.3 %reduce-scatter.23.cloned.1.call-start = ((), (), s32[]{:S(2)}) async-start(), calls=%async_computation.21 | async-start | bytes 4423680
  518.8 46.6 %collective-permute-start.25 = (bf16[4,1,1,96,1536]{4,3,2,1,0:T(8,128)(2,1)}, bf16[4,1,1,96,1536]{4,3,2,1,0:T(8,128)(2,1)}, u32[]{:S(2)}, u32[]{:S(2)}) collective-permute-start(bf16[4,1,1,96,1536]{4,3,2,1,0:T(8,128)(2,1)} %constant_dynamic-slice_fusion.1), channel_id=1, source_target_pairs={{0,4},{4,0},{1,5},{5,1},{2,6},{6,2},{3,7},{7,3},{8,12},{12,8},{9,1... | collective-permute-start | bytes 3538952 | tf_op jit(solution)/shard_map/ppermute | solution.py:57
  524.9 31.7 %all-to-all-start.3 = ((bf16[4,96,1120]{2,1,0:T(8,128)(2,1)}), bf16[4,96,1120]{2,1,0:T(8,128)(2,1)}, u32[]{:S(2)}, u32[]{:S(2)}) async-start(bf16[4,96,1120]{2,1,0:T(8,128)(2,1)} %bitcast.132), calls=%async_computation.4 | async-start | bytes 1769472 | tf_op jit(solution)/shard_map/all_to_all | solution.py:112
  581.1 45.3 %collective-permute-start.26 = (bf16[384,1536]{1,0:T(8,128)(2,1)}, bf16[384,1536]{1,0:T(8,128)(2,1)}, u32[]{:S(2)}, u32[]{:S(2)}) collective-permute-start(bf16[384,1536]{1,0:T(8,128)(2,1)} %fusion.5), channel_id=1, source_target_pairs={{0,1},{1,0},{2,3},{3,2},{4,5},{5,4},{6,7},{7,6},{8,9},{9,8},{10,11... | collective-permute-start | bytes 3538952 | tf_op jit(solution)/shard_map/ppermute | solution.py:57
  609.4 17.0 %all-to-all-start.5 = ((bf16[4,96,1120]{2,1,0:T(8,128)(2,1)}), bf16[4,96,1120]{2,1,0:T(8,128)(2,1)}, u32[]{:S(2)}, u32[]{:S(2)}) async-start(bf16[4,96,1120]{2,1,0:T(8,128)(2,1)} %bitcast.130), calls=%async_computation.6 | async-start | bytes 1769472 | tf_op jit(solution)/shard_map/all_to_all | solution.py:112
  613.6 50.3 %reduce-scatter.17.cloned.1.call-start = ((), (), s32[]{:S(2)}) async-start(), calls=%async_computation.18 | async-start | bytes 1474560 | tf_op jit(solution)/shard_map/reduce_scatter | solution.py:106
  614.4 66.1 %reduce-scatter.15.cloned.1.call-start = ((), (), s32[]{:S(2)}) async-start(), calls=%async_computation.17 | async-start | bytes 368640 | tf_op jit(solution)/shard_map/reduce_scatter | solution.py:106
  (66 other events, 736.2 us)
Sparse Core Ops, SparseCore 0:
  30.6 31.2 all-gather.4
  78.2 69.7 all-gather.6
  150.1 68.5 all-gather.8
  220.7 73.7 all-gather.10
  346.6 65.2 reduce-scatter.18
  414.1 66.6 reduce-scatter.20
  500.8 35.8 reduce-scatter.12
  538.9 66.0 reduce-scatter.22
  616.8 29.9 reduce-scatter.16
  660.5 19.8 reduce-scatter.14

commit v5 on v4

--- a/solution.py
+++ b/solution.py
@@ -4,6 +4,7 @@
 import jax.numpy as jnp
 from jax import lax
 from jax.experimental import pallas as pl
+from jax.experimental.layout import Layout, with_layout_constraint
 from jax.experimental.pallas import tpu as pltpu
 from jax.sharding import Mesh
 from jax.sharding import PartitionSpec as P
@@ -65,6 +66,10 @@
     return lax.optimization_barrier((value, *earlier))[0]
 
 
+def row_major(value):
+    return with_layout_constraint(value, Layout(major_to_minor=(0, 1)))
+
+
 def gather_group(own):
     core = other(own, "c")
     across = other(own, "x")
@@ -76,14 +81,6 @@
     sent = low(jnp.concatenate([partial[rows : 2 * rows], partial[3 * rows :]], axis=0))
     core = other(sent, "c").astype(jnp.float32)
     return partial[:rows] + core[:rows], low(partial[2 * rows : 3 * rows] + core[rows:])
-
-
-def sum_across(own, across, *earlier):
-    return low(own + after(other(across, "x"), *earlier).astype(jnp.float32))
-
-
-def sum_pair(mine, *earlier):
-    return mine.astype(jnp.float32) + after(other(mine, "y"), *earlier).astype(jnp.float32)
 
 
 def sum_narrow(partial):
@@ -350,13 +347,11 @@
     small_rows = -(-sum(small_sizes) // head)
     small = jnp.concatenate(small_parts)
     small = jnp.pad(small, (0, features * head - small.shape[0])).reshape(features, head)
-    pair_column = gather_z(
-        jnp.concatenate([key_projection, value_projection, small], axis=1)
-    )
-    square_column = gather_z(
-        after(jnp.concatenate([w_query, w_out.T], axis=1), small)
-    )
-    gate_own = deal(w_gate)
+    square_pack = jnp.concatenate([w_query, w_out.T], axis=1)
+    square_column = gather_z(square_pack)
+    pair_pack = jnp.concatenate([key_projection, value_projection, small], axis=1)
+    pair_column = gather_z(after(pair_pack, square_pack))
+    gate_own = deal(after(w_gate, pair_column))
     w_pair = gather_rest(pair_column, features)
     small_all = w_pair[:, 2 * head :].reshape(devices, features, head)[:, :small_rows]
     small_all = small_all.reshape(devices, small_rows * head).astype(jnp.float32)
@@ -381,16 +376,15 @@
     )
     value_rows = low(projections[:, head:] + bias_value)
     key_value = jnp.concatenate([key_rows, value_rows], axis=1)
-    key_value, gate_own = lax.optimization_barrier((key_value, gate_own))
-    key_value_column = gather_z(key_value)
+    gate_all = gather_z(gate_own)
+    key_value_column = gather_z(after(key_value, gate_own, square_column))
     up_own = deal(after(w_up, key_value))
     w_square = gather_rest(square_column, features)
     w_query_all = w_square[:, :heads_width]
     w_out_all = w_square[:, heads_width:]
     query_pre = product(normed_one, w_query_all) + bias_query
     key_value_column = after(key_value_column, up_own)
-    gate_all = gather_z(after(gate_own, key_value_column))
-    up_all = gather_z(after(up_own, key_value_column))
+    up_all = gather_z(up_own)
     key_value = gather_rest(key_value_column, rows)
     down_own = deal(after(w_down, key_value_column).T)
     down_all = gather_z(down_own)
@@ -410,23 +404,27 @@
     sigmoid_gate = jax.nn.sigmoid(gate)
     silu_gate = gate * sigmoid_gate
     hidden = low(silu_gate * up_part)
-    grad_down = low(product(cotangent_turned, hidden))
+    grad_down = row_major(low(product(cotangent_turned, hidden)))
     down_sums = scatter_z(grad_down)
     grad_hidden = product(after(cotangent_group, grad_down), down_all)
     grad_gate = low(grad_hidden * up_part * sigmoid_gate * (1.0 + gate * (1.0 - sigmoid_gate)))
     grad_up = low(grad_hidden * silu_gate)
     grad_normed_part = product_right(grad_gate, gate_all) + product_right(grad_up, up_all)
     grad_normed_own, grad_normed_across = sum_core(grad_normed_part, rows)
-    grad_gate_all = low(product(normed_turned, after(grad_gate, grad_normed_across)))
+    normed_came = other(grad_normed_across, "x")
+    grad_gate_all = row_major(low(product(normed_turned, after(grad_gate, grad_normed_across))))
     gate_sums = scatter_z(grad_gate_all)
-    grad_up_all = low(product(normed_turned, after(grad_up, grad_gate_all)))
+    grad_up_all = row_major(low(product(normed_turned, after(grad_up, grad_gate_all))))
     up_sums = scatter_z(grad_up_all)
-    grad_normed_mine = sum_across(grad_normed_own, grad_normed_across, grad_up_all)
-    down_part = product_right(after(hidden, grad_normed_mine), down_all)
-    down_mine, down_across = sum_core(down_part, rows)
-    grad_normed_two = sum_pair(grad_normed_mine, down_across)
-    down_mine = sum_across(down_mine, down_across, grad_normed_two)
-    result = low(middle + sum_pair(down_mine))
+    down_part = product_right(after(hidden, grad_up_all), down_all)
+    normed_came = after(normed_came, down_part)
+    grad_normed_mine = low(grad_normed_own + normed_came.astype(jnp.float32))
+    normed_pair = other(grad_normed_mine, "y")
+    down_parts = undeal(after(down_sums, grad_normed_mine))
+    normed_pair = after(normed_pair, down_parts)
+    grad_normed_two = grad_normed_mine.astype(jnp.float32) + normed_pair.astype(jnp.float32)
+    down_own, down_across = sum_core(after(down_part, normed_pair), rows)
+    down_came = other(down_across, "x")
 
     back_two, grad_gain_two = norm_back(middle, scale_two, gain_two, grad_normed_two)
     grad_middle = cotangent.astype(jnp.float32) + back_two
@@ -437,17 +435,19 @@
         bounds, query_rows, grad_attended, attended, totals,
         cosine_head, sine_head, place, key_value,
     )
-    key_value_grads = scatter_z(scatter_start(buffer, rows))
+    key_value_sums = scatter_start(buffer, rows)
+    key_value_grads = scatter_z(key_value_sums)
+    down_mine = low(down_own + after(down_came, key_value_sums).astype(jnp.float32))
+    down_pair = other(down_mine, "y")
     square_grads = low(
-        jnp.concatenate([product_left(grad_query_pre, normed_one).T, grad_out_all], axis=1)
-    )
-    square_grads = scatter_start(square_grads, features)
-    down_parts = undeal(after(down_sums, buffer))
-    gate_parts = undeal(after(gate_sums, buffer))
+        jnp.concatenate(
+            [product_left(grad_query_pre, normed_one).T, grad_out_all], axis=1
+        )
+    )
+    square_grads = scatter_start(after(square_grads, key_value_sums), features)
+    gate_parts = undeal(after(gate_sums, key_value_sums))
     grad_query_part = product_right(grad_query_pre, w_query_all)
-    key_value_grads = after(
-        key_value_grads, square_grads, down_parts, gate_parts, grad_query_part
-    ).astype(jnp.float32)
+    key_value_grads = after(key_value_grads, square_grads, grad_query_part).astype(jnp.float32)
     square_grads = scatter_z(square_grads)
     grad_key_pre = low(
         rotate_halves(key_value_grads[:, :head].reshape(rows, 1, head), cosine_table, -sine_table)
@@ -456,10 +456,13 @@
     grad_pair = jnp.concatenate([grad_key_pre, grad_value_pre], axis=1)
     grad_project = jnp.concatenate([grad_query_pre, grad_pair], axis=1)
     grad_bias = jnp.sum(grad_project.astype(jnp.float32), axis=0)
-    up_parts = undeal(after(up_sums, grad_pair))
-    grad_normed_one = sum_pair(
-        low(grad_query_part + product_right(grad_pair, w_pair[:, : 2 * head])), up_parts
-    )
+    grad_normed_mine = low(grad_query_part + product_right(grad_pair, w_pair[:, : 2 * head]))
+    normed_pair = after(other(grad_normed_mine, "y"), gate_parts, down_pair)
+    result = low(
+        middle + down_mine.astype(jnp.float32) + after(down_pair, grad_pair).astype(jnp.float32)
+    )
+    up_parts = undeal(after(up_sums, grad_normed_mine))
+    grad_normed_one = grad_normed_mine.astype(jnp.float32) + normed_pair.astype(jnp.float32)
     back_one, grad_gain_one = norm_back(inputs, scale_one, gain_one, grad_normed_one)
     grad_tokens = low(grad_middle + back_one)
 

time: 704 us -> 668 us (0.949)
  waiting for transfers between devices: 276 us -> 208 us
  blocking collectives: 36 us -> 64.5 us
  other arithmetic: 59.4 us -> 86.1 us
  local copies, waits for them, and re-layouts: 109 us -> 84 us
  matrix products: 118 us -> 128 us
    ppermute x29, waiting for transfers between devices: 166 us -> 111 us  [other(): return lax.ppermute(value, axis, [(0, 1), (1, 0)])]
    reduce_scatter x3 -> x6, waiting for transfers between devices: 13.2 us -> 46.5 us  [scatter_z(): return lax.psum_scatter(whole, 'z', scatter_dimension=0, tiled=True)]
    unnamed x13 -> x10, waiting for transfers between devices: 22.7 us -> 0.17 us
    all_to_all x3, waiting for transfers between devices: 29.4 us -> 8.88 us  [undeal(): return lax.all_to_all(parts, GROUP, split_axis=0, concat_axis=0, tiled=True)]
    unnamed x114 -> x101, local copies, waits for them, and re-layouts: 31 us -> 13.2 us
    all_to_all x0 -> x1, blocking collectives: none -> 15.9 us  [deal(): lax.all_to_all(parts, GROUP, split_axis=0, concat_axis=0, tiled=True)]
    all_gather x2, blocking collectives: 36 us -> 48.6 us  [gather_z(): return lax.all_gather(own, 'z', axis=0, tiled=True)]
    convert_element_type x13 -> x14, other arithmetic: 21.5 us -> 31.8 us  [low(): return value.astype(jnp.bfloat16)]
  transfers between devices with their start and end apart: 45 -> 44, of which waited for: 20 -> 17; matrix products, arithmetic and copies ran while one was open for 33% -> 37% of each run, Pallas kernels for 2% -> 2%
where the time goes in v5:
time: 668 us; the launch traced here: 658 us
  waiting for transfers between devices  208 us (31%)
  matrix products  128 us (19%)
  other arithmetic  86.1 us (13%)
  local copies, waits for them, and re-layouts  84 us (13%)
  blocking collectives  64.5 us (10%)
  starting transfers between devices  55 us (8%)
  between operations  17.5 us (3%)
  Pallas kernels  15.2 us (2%)
    ppermute x29, waiting for transfers between devices, other(): return lax.ppermute(value, axis, [(0, 1), (1, 0)])  111 us
    dot_general x9, matrix products, product(): return jnp.dot(left, right, preferred_element_type=jnp.float32)  76.5 us
    all_gather x2, blocking collectives, gather_z(): return lax.all_gather(own, 'z', axis=0, tiled=True)  48.6 us
    reduce_scatter x6, waiting for transfers between devices, scatter_z(): return lax.psum_scatter(whole, 'z', scatter_dimension=0, tiled=True)  46.5 us
    dot_general x6, matrix products, product_right(): lax.dot_general(left, right, (((1,), (1,)), ((), ())), preferred_element_...  44.3 us
    ppermute x29, starting transfers between devices, other(): return lax.ppermute(value, axis, [(0, 1), (1, 0)])  33.5 us
    all_gather x4, waiting for transfers between devices, gather_z(): return lax.all_gather(own, 'z', axis=0, tiled=True)  32.2 us
    convert_element_type x14, other arithmetic, low(): return value.astype(jnp.bfloat16)  31.8 us
  transfers between devices with their start and end apart: 44, of which 17 were waited for; matrix products, arithmetic and copies ran while one was open for 37% of the time, Pallas kernels for 2%

profile of v5, /device:TPU:0, one launch (start us, length us, event | category | flops | bytes accessed | tf_op | source)
XLA Modules:
  0.0 657.6 jit_solution(9982454639889806996)
XLA Ops:
  13.3 17.9 %all_gather.18 = bf16[384,384]{1,0:T(8,128)(2,1)S(1)} all-gather(bf16[96,384]{1,0:T(8,128)(2,1)S(1)} %pad_maximum_fusion.9), channel_id=1, replica_groups=mesh['z'=4,'x'=2,'c'=2,'y'=2] {'z'}, dimensions={0}, use_global_device_ids=true | all-gather | bytes 368640 | tf_op jit(solution)/shard_map/all_gather | solution.py:99
  33.9 15.9 %all_to_all.30 = bf16[4,96,1120]{2,1,0:T(8,128)(2,1)} all-to-all(bf16[4,96,1120]{2,1,0:T(8,128)(2,1)S(1)} %bitcast.122), channel_id=1, replica_groups=mesh['z'=4,'x'=2,'c'=2,'y'=2] {'x','c'}, dimensions={0} | all-to-all | bytes 1720320 | tf_op jit(solution)/shard_map/all_to_all | solution.py:94
  52.3 6.1 collective-permute-done.1
  74.2 30.6 %all_gather.20 = bf16[1536,256]{1,0:T(8,128)(2,1)S(1)} all-gather(bf16[384,256]{1,0:T(8,128)(2,1)S(1)} %copy-done.27), channel_id=1, replica_groups=mesh['z'=4,'x'=2,'c'=2,'y'=2] {'z'}, dimensions={0}, use_global_device_ids=true | all-gather | bytes 983040 | tf_op jit(solution)/shard_map/all_gather | solution.py:99
  110.4 13.7 %collective-permute-done.7 = bf16[4,1,1,384,256]{4,3,2,1,0:T(8,128)(2,1)} collective-permute-done((bf16[4,1,1,384,256]{4,3,2,1,0:T(8,128)(2,1)S(1)}, bf16[4,1,1,384,256]{4,3,2,1,0:T(8,128)(2,1)}, u32[]{:S(2)}, u32[]{:S(2)}) %collective-permute-start.7) | collective-permute-done | bytes 786464 | tf_op jit(solution)/shard_map/ppermute | solution.py:58
  132.8 6.5 attend.1
  148.3 22.3 %collective-permute-done.9 = bf16[384,1536]{1,0:T(8,128)(2,1)} collective-permute-done((bf16[384,1536]{1,0:T(8,128)(2,1)S(1)}, bf16[384,1536]{1,0:T(8,128)(2,1)}, u32[]{:S(2)}, u32[]{:S(2)}) %collective-permute-start.9) | collective-permute-done | bytes 1179680 | tf_op jit(solution)/shard_map/ppermute | solution.py:58
  188.3 15.1 %collective-permute-done.11 = bf16[384,1536]{1,0:T(8,128)(2,1)} collective-permute-done((bf16[384,1536]{1,0:T(8,128)(2,1)S(1)}, bf16[384,1536]{1,0:T(8,128)(2,1)}, u32[]{:S(2)}, u32[]{:S(2)}) %collective-permute-start.11) | collective-permute-done | bytes 1179680 | tf_op jit(solution)/shard_map/ppermute | solution.py:58
  204.3 8.6 %all-to-all-done.2 = bf16[4,96,1120]{2,1,0:T(8,128)(2,1)} async-done(((bf16[4,96,1120]{2,1,0:T(8,128)(2,1)}), bf16[4,96,1120]{2,1,0:T(8,128)(2,1)}, u32[]{:S(2)}, u32[]{:S(2)}) %all-to-all-start.2) | async-done | bytes 860192 | tf_op jit(solution)/shard_map/all_to_all | solution.py:94
  222.6 11.4 %fusion.70 = f32[1536,1120]{0,1:T(8,128)} fusion(bf16[1536,1120]{1,0:T(8,128)(2,1)} %all-gather.7.cloned.1.call-done, bf16[384,1536]{1,0:T(8,128)(2,1)} %collective-permute-done.12, bf16[384,1536]{1,0:T(8,128)(2,1)} %collective-permute-done.11, bf16[384,1536]{1,0:T(8,128)(2,1)} %collective-permute-done.10, bf16[384,1536]{1,0:T(8,128)(2,1)S(1)} %multiply_convert_fusion.3), kind=kOutput, calls=%fused_computation.168 | convolution fusion | flops 5303697408 | bytes 15040512 | tf_op jit(solution)/shard_map/dot_general | solution.py:17
  234.0 13.1 %multiply_convert_fusion.2 = (bf16[1536,1120]{0,1:T(8,128)(2,1)S(1)}, f32[1536,1120]{0,1:T(8,128)}) fusion(f32[1536,1120]{0,1:T(8,128)} %fusion.70, bf16[1536,1120]{1,0:T(8,128)(2,1)} %all-gather.9.cloned.1.call-done, bf16[384,1536]{1,0:T(8,128)(2,1)} %collective-permute-done.12, bf16[384,1536]{1,0:T(8,128)(2,1)} %collective-permute-done.11, ...), kind=kOutput, calls=%fused_computation.6 | convolution fusion | flops 5314019328 | bytes 25362432 | tf_op jit(solution)/shard_map/dot_general | solution.py:17
  248.9 9.5 %convolution_convert_fusion.2 = bf16[1536,1120]{1,0:T(8,128)(2,1)} fusion(bf16[1536,1536]{0,1:T(8,128)(2,1)} %bitcast.27, bf16[1536,1120]{0,1:T(8,128)(2,1)S(1)} %get-tuple-element.52), kind=kOutput, calls=%fused_computation.3 | convolution fusion | flops 5286543360 | bytes 11599872 | tf_op jit(solution)/shard_map/dot_general | solution.py:17
  258.4 32.1 %all-gather.11.cloned.1.call-done = bf16[1536,1120]{1,0:T(8,128)(2,1)} async-done(((bf16[384,1120]{1,0:T(8,128)(2,1)}), bf16[1536,1120]{1,0:T(8,128)(2,1)}) %all-gather.11.cloned.1.call-update) | async-done | bytes 3440656 | tf_op jit(solution)/shard_map/all_gather | solution.py:99
  290.5 15.8 %multiply_convert_fusion = (bf16[1536,1120]{0,1:T(8,128)(2,1)}, bf16[1536,1120]{0,1:T(8,128)(2,1)}) fusion(f32[1536,1120]{0,1:T(8,128)} %fusion.70, f32[1536,1120]{0,1:T(8,128)} %get-tuple-element.107, bf16[1536,1536]{1,0:T(8,128)(2,1)} %constant_dynamic-update-slice_fusion, bf16[1536,1120]{1,0:T(8,128)(2,1)} %all-gather.11.cloned.1.call-done), kind=kOutput, calls=%fused_computation.4 | convolution fusion | flops 5307187200 | bytes 28803072 | tf_op jit(solution)/shard_map/dot_general | solution.py:17
  306.3 11.2 %fusion.80 = f32[1536,1536]{1,0:T(8,128)} fusion(bf16[1536,1120]{0,1:T(8,128)(2,1)} %get-tuple-element.50, bf16[1536,1120]{1,0:T(8,128)(2,1)S(1)} %copy-done.41), kind=kOutput, calls=%fused_computation.178 | convolution fusion | flops 5284823040 | bytes 16318464 | tf_op jit(solution)/shard_map/dot_general | solution.py:27
  317.5 12.2 %fusion.79 = (bf16[1536,1536]{1,0:T(8,128)(2,1)S(1)}, f32[1536,1536]{1,0:T(8,128)}) fusion(f32[1536,1536]{1,0:T(8,128)} %fusion.80, bf16[1536,1120]{0,1:T(8,128)(2,1)} %get-tuple-element.51, bf16[1536,1120]{1,0:T(8,128)(2,1)S(1)} %copy-done.42), kind=kOutput, calls=%fused_computation.177 | convolution fusion | flops 5289541632 | bytes 30474240 | tf_op jit(solution)/shard_map/dot_general | solution.py:27
  344.5 7.7 %convolution_convert_fusion.1 = bf16[1536,1120]{1,0:T(8,128)(2,1)} fusion(bf16[1536,1536]{0,1:T(8,128)(2,1)S(1)} %fusion.68, bf16[1536,1120]{0,1:T(8,128)(2,1)S(1)} %copy-done.45), kind=kOutput, calls=%fused_computation.2 | convolution fusion | flops 5286543360 | bytes 11599872 | tf_op jit(solution)/shard_map/dot_general | solution.py:17
  352.2 10.4 %convolution_convert_fusion = bf16[1536,1120]{1,0:T(8,128)(2,1)} fusion(bf16[1536,1536]{0,1:T(8,128)(2,1)} %copy-done.10, bf16[1536,1120]{0,1:T(8,128)(2,1)} %get-tuple-element.51), kind=kOutput, calls=%fused_computation.1 | convolution fusion | flops 5286543360 | bytes 11599872 | tf_op jit(solution)/shard_map/dot_general | solution.py:17
  362.6 11.5 %fusion.81 = f32[1536,1536]{1,0:T(8,128)} fusion(bf16[1536,1120]{0,1:T(8,128)(2,1)} %copy-done.44, bf16[1536,1120]{1,0:T(8,128)(2,1)} %all-gather.11.cloned.1.call-done), kind=kOutput, calls=%fused_computation.179 | convolution fusion | flops 5284823040 | bytes 16318464 | tf_op jit(solution)/shard_map/dot_general | solution.py:27
  378.3 18.6 %reduce-scatter.7.cloned.1.call-done = bf16[384,1120]{1,0:T(8,128)(2,1)} async-done(((bf16[1536,1120]{1,0:T(8,128)(2,1)}), bf16[384,1120]{1,0:T(8,128)(2,1)}) %reduce-scatter.7.cloned.1.call-update) | async-done | bytes 860176 | tf_op jit(solution)/shard_map/reduce_scatter | solution.py:103
  405.0 8.9 %all-to-all-done.3 = bf16[4,96,1120]{2,1,0:T(8,128)(2,1)} async-done(((bf16[4,96,1120]{2,1,0:T(8,128)(2,1)}), bf16[4,96,1120]{2,1,0:T(8,128)(2,1)}, u32[]{:S(2)}, u32[]{:S(2)}) %all-to-all-start.3) | async-done | bytes 860192 | tf_op jit(solution)/shard_map/all_to_all | solution.py:109
  419.0 4.6 fusion.22.grad_ref
  423.6 8.7 %attend_back.1 = (bf16[384,768]{1,0:T(8,128)(2,1)}, bf16[6144,256]{1,0:T(8,128)(2,1)}) custom-call(s32[2]{0:T(128)} %pad_add_fusion.bounds_ref, bf16[384,768]{1,0:T(8,128)(2,1)} %get-tuple-element.57.rotated_ref, f32[384,768]{1,0:T(8,128)} %fusion.22.grad_ref, f32[384,768]{1,0:T(8,128)} %get-tuple-element.46.attended_ref, ...), custom_call_target="tpu_custom_call" | custom-call | flops 10192158720 | bytes 31457280 | tf_op jit(solution)/shard_map/attend_back/pallas_call | solution.py:282
  436.0 4.3 convert.75
  440.9 6.0 collective-permute-start.22
  451.5 13.4 %collective-permute-done.22 = bf16[4,1,1,384,256]{4,3,2,1,0:T(8,128)(2,1)S(1)} collective-permute-done((bf16[4,1,1,384,256]{4,3,2,1,0:T(8,128)(2,1)S(1)}, bf16[4,1,1,384,256]{4,3,2,1,0:T(8,128)(2,1)S(1)}, u32[]{:S(2)}, u32[]{:S(2)}) %collective-permute-start.22) | collective-permute-done | bytes 786464 | tf_op jit(solution)/shard_map/ppermute | solution.py:58
  473.8 6.6 %copy.127 = bf16[1536,1536]{1,0:T(8,128)(2,1)} copy(bf16[1536,1536]{0,1:T(8,128)(2,1)} %pad_maximum_fusion.1) | data formatting | bytes 9437184 | tf_op jit(solution)/shard_map/optimization_barrier | solution.py:66
  486.4 4.8 fusion.14
  505.6 14.7 %collective-permute-done.20 = bf16[384,1536]{1,0:T(8,128)(2,1)} collective-permute-done((bf16[384,1536]{1,0:T(8,128)(2,1)}, bf16[384,1536]{1,0:T(8,128)(2,1)}, u32[]{:S(2)}, u32[]{:S(2)}) %collective-permute-start.20) | collective-permute-done | bytes 1179680 | tf_op jit(solution)/shard_map/ppermute | solution.py:58
  520.3 4.4 fusion.16
  526.2 19.5 %collective-permute-done.25 = bf16[4,1,1,96,1536]{4,3,2,1,0:T(8,128)(2,1)} collective-permute-done((bf16[4,1,1,96,1536]{4,3,2,1,0:T(8,128)(2,1)}, bf16[4,1,1,96,1536]{4,3,2,1,0:T(8,128)(2,1)}, u32[]{:S(2)}, u32[]{:S(2)}) %collective-permute-start.25) | collective-permute-done | bytes 1179680 | tf_op jit(solution)/shard_map/ppermute | solution.py:58
  619.4 26.4 %reduce-scatter.13.cloned.1.call-done = bf16[96,384]{1,0:T(8,128)(2,1)} async-done(((bf16[384,384]{1,0:T(8,128)(2,1)}), bf16[96,384]{1,0:T(8,128)(2,1)}) %reduce-scatter.13.cloned.1.call-update) | async-done | bytes 73744 | tf_op jit(solution)/shard_map/reduce_scatter | solution.py:103
  (319 shorter events, 227.7 us)
Async XLA Ops:
  7.2 61.6 %all-gather.5.cloned.1.call-start = ((), (), s32[]{:S(2)}) async-start(), calls=%async_computation.12 | async-start | bytes 1474560 | tf_op jit(solution)/shard_map/all_gather | solution.py:99
  9.0 213.6 %all-gather.7.cloned.1.call-start = ((), (), s32[]{:S(2)}) async-start(), calls=%async_computation.13 | async-start | bytes 4423680 | tf_op jit(solution)/shard_map/all_gather | solution.py:99
  65.2 39.6 %all-to-all-start.1 = ((bf16[4,96,1120]{2,1,0:T(8,128)(2,1)}), bf16[4,96,1120]{2,1,0:T(8,128)(2,1)S(1)}, u32[]{:S(2)}, u32[]{:S(2)}) async-start(bf16[4,96,1120]{2,1,0:T(8,128)(2,1)} %bitcast.104), calls=%async_computation.1 | async-start | bytes 1769472 | tf_op jit(solution)/shard_map/all_to_all | solution.py:94
  68.7 165.3 %all-gather.9.cloned.1.call-start = ((), (), s32[]{:S(2)}) async-start(), calls=%async_computation.14 | async-start | bytes 4423680 | tf_op jit(solution)/shard_map/all_gather | solution.py:99
  68.8 40.2 %collective-permute-start.4 = (bf16[4,1,1,96,1536]{4,3,2,1,0:T(8,128)(2,1)}, bf16[4,1,1,96,1536]{4,3,2,1,0:T(8,128)(2,1)}, u32[]{:S(2)}, u32[]{:S(2)}) collective-permute-start(bf16[4,1,1,96,1536]{4,3,2,1,0:T(8,128)(2,1)} %bitcast.137), channel_id=1, source_target_pairs={{0,4},{4,0},{1,5},{5,1},{2,6},{6,2},{3,7},{7,3},{8,12},{12,8},{9,1... | collective-permute-start | bytes 3538952 | tf_op jit(solution)/shard_map/ppermute | solution.py:58
  74.2 52.4 %collective-permute-start.3 = (bf16[4,1,1,96,1536]{4,3,2,1,0:T(8,128)(2,1)}, bf16[4,1,1,96,1536]{4,3,2,1,0:T(8,128)(2,1)}, u32[]{:S(2)}, u32[]{:S(2)}) collective-permute-start(bf16[4,1,1,96,1536]{4,3,2,1,0:T(8,128)(2,1)} %bitcast.138), channel_id=1, source_target_pairs={{0,2},{2,0},{1,3},{3,1},{4,6},{6,4},{5,7},{7,5},{8,10},{10,8},{9,1... | collective-permute-start | bytes 3538952 | tf_op jit(solution)/shard_map/ppermute | solution.py:58
  104.8 19.3 %collective-permute-start.7 = (bf16[4,1,1,384,256]{4,3,2,1,0:T(8,128)(2,1)S(1)}, bf16[4,1,1,384,256]{4,3,2,1,0:T(8,128)(2,1)}, u32[]{:S(2)}, u32[]{:S(2)}) collective-permute-start(bf16[4,1,1,384,256]{4,3,2,1,0:T(8,128)(2,1)S(1)} %bitcast.132), channel_id=1, source_target_pairs={{0,4},{4,0},{1,5},{5,1},{2,6},{6,2},{3,7},{7,3},{8,12},{12,8},{9,1... | collective-permute-start | bytes 2359304 | tf_op jit(solution)/shard_map/ppermute | solution.py:58
  109.0 20.4 %collective-permute-start.5 = (bf16[4,1,1,96,1536]{4,3,2,1,0:T(8,128)(2,1)}, bf16[4,1,1,96,1536]{4,3,2,1,0:T(8,128)(2,1)S(1)}, u32[]{:S(2)}, u32[]{:S(2)}) collective-permute-start(bf16[4,1,1,96,1536]{4,3,2,1,0:T(8,128)(2,1)} %collective-permute-done.4), channel_id=1, source_target_pairs={{0,2},{2,0},{1,3},{3,1},{4,6},{6,4},{5,7},{7,5},{8,10},{10,8},{9,1... | collective-permute-start | bytes 3538952 | tf_op jit(solution)/shard_map/ppermute | solution.py:58
  142.8 27.8 %collective-permute-start.9 = (bf16[384,1536]{1,0:T(8,128)(2,1)S(1)}, bf16[384,1536]{1,0:T(8,128)(2,1)}, u32[]{:S(2)}, u32[]{:S(2)}) collective-permute-start(bf16[384,1536]{1,0:T(8,128)(2,1)S(1)} %convolution_convert_fusion.5), channel_id=1, source_target_pairs={{0,1},{1,0},{2,3},{3,2},{4,5},{5,4},{6,7},{7,6},{8,9},{9,8},{10,11... | collective-permute-start | bytes 3538952 | tf_op jit(solution)/shard_map/ppermute | solution.py:58
  144.5 43.2 %collective-permute-start.14 = (bf16[384,1536]{1,0:T(8,128)(2,1)}, bf16[384,1536]{1,0:T(8,128)(2,1)}, u32[]{:S(2)}, u32[]{:S(2)}) collective-permute-start(bf16[384,1536]{1,0:T(8,128)(2,1)} %param.29), channel_id=1, source_target_pairs={{0,4},{4,0},{1,5},{5,1},{2,6},{6,2},{3,7},{7,3},{8,12},{12,8},{9,1... | collective-permute-start | bytes 3538952 | tf_op jit(solution)/shard_map/ppermute | solution.py:58
  173.1 30.3 %collective-permute-start.11 = (bf16[384,1536]{1,0:T(8,128)(2,1)S(1)}, bf16[384,1536]{1,0:T(8,128)(2,1)}, u32[]{:S(2)}, u32[]{:S(2)}) collective-permute-start(bf16[384,1536]{1,0:T(8,128)(2,1)S(1)} %multiply_convert_fusion.3), channel_id=1, source_target_pairs={{0,4},{4,0},{1,5},{5,1},{2,6},{6,2},{3,7},{7,3},{8,12},{12,8},{9,1... | collective-permute-start | bytes 3538952 | tf_op jit(solution)/shard_map/ppermute | solution.py:58
  177.0 38.3 %collective-permute-start.13 = (bf16[384,1536]{1,0:T(8,128)(2,1)}, bf16[384,1536]{1,0:T(8,128)(2,1)}, u32[]{:S(2)}, u32[]{:S(2)}) collective-permute-start(bf16[384,1536]{1,0:T(8,128)(2,1)} %param.29), channel_id=1, source_target_pairs={{0,2},{2,0},{1,3},{3,1},{4,6},{6,4},{5,7},{7,5},{8,10},{10,8},{9,1... | collective-permute-start | bytes 3538952 | tf_op jit(solution)/shard_map/ppermute | solution.py:58
  183.4 29.5 %all-to-all-start.2 = ((bf16[4,96,1120]{2,1,0:T(8,128)(2,1)}), bf16[4,96,1120]{2,1,0:T(8,128)(2,1)}, u32[]{:S(2)}, u32[]{:S(2)}) async-start(bf16[4,96,1120]{2,1,0:T(8,128)(2,1)} %bitcast.121), calls=%async_computation.2 | async-start | bytes 1769472 | tf_op jit(solution)/shard_map/all_to_all | solution.py:94
  187.7 102.9 %all-gather.11.cloned.1.call-start = ((), (), s32[]{:S(2)}) async-start(), calls=%async_computation.15 | async-start | bytes 4423680 | tf_op jit(solution)/shard_map/all_gather | solution.py:99
  187.7 32.4 %collective-permute-start.15 = (bf16[384,1536]{1,0:T(8,128)(2,1)}, bf16[384,1536]{1,0:T(8,128)(2,1)}, u32[]{:S(2)}, u32[]{:S(2)}) collective-permute-start(bf16[384,1536]{1,0:T(8,128)(2,1)} %collective-permute-done.14), channel_id=1, source_target_pairs={{0,2},{2,0},{1,3},{3,1},{4,6},{6,4},{5,7},{7,5},{8,10},{10,8},{9,1... | collective-permute-start | bytes 3538952 | tf_op jit(solution)/shard_map/ppermute | solution.py:58
  188.2 34.4 %collective-permute-start.10 = (bf16[384,1536]{1,0:T(8,128)(2,1)S(1)}, bf16[384,1536]{1,0:T(8,128)(2,1)}, u32[]{:S(2)}, u32[]{:S(2)}) collective-permute-start(bf16[384,1536]{1,0:T(8,128)(2,1)S(1)} %multiply_convert_fusion.3), channel_id=1, source_target_pairs={{0,2},{2,0},{1,3},{3,1},{4,6},{6,4},{5,7},{7,5},{8,10},{10,8},{9,1... | collective-permute-start | bytes 3538952 | tf_op jit(solution)/shard_map/ppermute | solution.py:58
  203.4 19.2 %collective-permute-start.12 = (bf16[384,1536]{1,0:T(8,128)(2,1)}, bf16[384,1536]{1,0:T(8,128)(2,1)}, u32[]{:S(2)}, u32[]{:S(2)}) collective-permute-start(bf16[384,1536]{1,0:T(8,128)(2,1)} %collective-permute-done.11), channel_id=1, source_target_pairs={{0,2},{2,0},{1,3},{3,1},{4,6},{6,4},{5,7},{7,5},{8,10},{10,8},{9,1... | collective-permute-start | bytes 3538952 | tf_op jit(solution)/shard_map/ppermute | solution.py:58
  212.9 184.0 %reduce-scatter.7.cloned.1.call-start = ((), (), s32[]{:S(2)}) async-start(), calls=%async_computation.16 | async-start | bytes 4423680 | tf_op jit(solution)/shard_map/reduce_scatter | solution.py:103
  331.5 169.8 %reduce-scatter.11.cloned.1.call-start = ((), (), s32[]{:S(2)}) async-start(), calls=%async_computation.18 | async-start | bytes 4423680 | tf_op jit(solution)/shard_map/reduce_scatter | solution.py:103
  343.0 31.1 %collective-permute-start.17 = (bf16[384,1536]{1,0:T(8,128)(2,1)S(1)}, bf16[384,1536]{1,0:T(8,128)(2,1)}, u32[]{:S(2)}, u32[]{:S(2)}) collective-permute-start(bf16[384,1536]{1,0:T(8,128)(2,1)S(1)} %fusion.19), channel_id=1, source_target_pairs={{0,4},{4,0},{1,5},{5,1},{2,6},{6,2},{3,7},{7,3},{8,12},{12,8},{9,1... | collective-permute-start | bytes 3538952 | tf_op jit(solution)/shard_map/ppermute | solution.py:58
  376.8 28.2 %collective-permute-start.18 = (bf16[384,1536]{1,0:T(8,128)(2,1)S(1)}, bf16[384,1536]{1,0:T(8,128)(2,1)}, u32[]{:S(2)}, u32[]{:S(2)}) collective-permute-start(bf16[384,1536]{1,0:T(8,128)(2,1)S(1)} %fusion.18), channel_id=1, source_target_pairs={{0,1},{1,0},{2,3},{3,2},{4,5},{5,4},{6,7},{7,6},{8,9},{9,8},{10,11... | collective-permute-start | bytes 3538952 | tf_op jit(solution)/shard_map/ppermute | solution.py:58
  401.1 147.1 %reduce-scatter.9.cloned.1.call-start = ((), (), s32[]{:S(2)}) async-start(), calls=%async_computation.17 | async-start | bytes 983040 | tf_op jit(solution)/shard_map/reduce_scatter | solution.py:103
  440.9 23.9 %collective-permute-start.22 = (bf16[4,1,1,384,256]{4,3,2,1,0:T(8,128)(2,1)S(1)}, bf16[4,1,1,384,256]{4,3,2,1,0:T(8,128)(2,1)S(1)}, u32[]{:S(2)}, u32[]{:S(2)}) collective-permute-start(bf16[4,1,1,384,256]{4,3,2,1,0:T(8,128)(2,1)S(1)} %constant_dynamic-slice_fusion.3), channel_id=1, source_target_pairs={{0,4},{4,0},{1,5},{5,1},{2,6},{6,2},{3,7},{7,3},{8,12},{12,8},{9,1... | collective-permute-start | bytes 2359304 | tf_op jit(solution)/shard_map/ppermute | solution.py:58
  465.9 107.4 %reduce-scatter.17.cloned.1.call-start = ((), (), s32[]{:S(2)}) async-start(), calls=%async_computation.21 | async-start | bytes 4423680 | tf_op jit(solution)/shard_map/reduce_scatter | solution.py:103
  491.2 29.2 %collective-permute-start.20 = (bf16[384,1536]{1,0:T(8,128)(2,1)}, bf16[384,1536]{1,0:T(8,128)(2,1)}, u32[]{:S(2)}, u32[]{:S(2)}) collective-permute-start(bf16[384,1536]{1,0:T(8,128)(2,1)} %fusion.14), channel_id=1, source_target_pairs={{0,4},{4,0},{1,5},{5,1},{2,6},{6,2},{3,7},{7,3},{8,12},{12,8},{9,1... | collective-permute-start | bytes 3538952 | tf_op jit(solution)/shard_map/ppermute | solution.py:58
  498.5 47.1 %collective-permute-start.25 = (bf16[4,1,1,96,1536]{4,3,2,1,0:T(8,128)(2,1)}, bf16[4,1,1,96,1536]{4,3,2,1,0:T(8,128)(2,1)}, u32[]{:S(2)}, u32[]{:S(2)}) collective-permute-start(bf16[4,1,1,96,1536]{4,3,2,1,0:T(8,128)(2,1)} %constant_dynamic-slice_fusion.1), channel_id=1, source_target_pairs={{0,4},{4,0},{1,5},{5,1},{2,6},{6,2},{3,7},{7,3},{8,12},{12,8},{9,1... | collective-permute-start | bytes 3538952 | tf_op jit(solution)/shard_map/ppermute | solution.py:58
  501.3 65.3 %all-to-all-start.4 = ((bf16[4,96,1120]{2,1,0:T(8,128)(2,1)}), bf16[4,96,1120]{2,1,0:T(8,128)(2,1)}, u32[]{:S(2)}, u32[]{:S(2)}) async-start(bf16[4,96,1120]{2,1,0:T(8,128)(2,1)} %bitcast.143), calls=%async_computation.7 | async-start | bytes 1769472 | tf_op jit(solution)/shard_map/all_to_all | solution.py:109
  505.5 110.5 %reduce-scatter.15.cloned.1.call-start = ((), (), s32[]{:S(2)}) async-start(), calls=%async_computation.20 | async-start | bytes 1474560 | tf_op jit(solution)/shard_map/reduce_scatter | solution.py:103
  524.7 61.3 %collective-permute-start.23 = (bf16[384,1536]{1,0:T(8,128)(2,1)}, bf16[384,1536]{1,0:T(8,128)(2,1)}, u32[]{:S(2)}, u32[]{:S(2)}) collective-permute-start(bf16[384,1536]{1,0:T(8,128)(2,1)} %fusion.16), channel_id=1, source_target_pairs={{0,1},{1,0},{2,3},{3,2},{4,5},{5,4},{6,7},{7,6},{8,9},{9,8},{10,11... | collective-permute-start | bytes 3538952 | tf_op jit(solution)/shard_map/ppermute | solution.py:58
  555.0 33.5 %collective-permute-start.26 = (bf16[384,1536]{1,0:T(8,128)(2,1)}, bf16[384,1536]{1,0:T(8,128)(2,1)}, u32[]{:S(2)}, u32[]{:S(2)}) collective-permute-start(bf16[384,1536]{1,0:T(8,128)(2,1)} %fusion.5), channel_id=1, source_target_pairs={{0,1},{1,0},{2,3},{3,2},{4,5},{5,4},{6,7},{7,6},{8,9},{9,8},{10,11... | collective-permute-start | bytes 3538952 | tf_op jit(solution)/shard_map/ppermute | solution.py:58
  578.0 23.3 %all-to-all-start.5 = ((bf16[4,96,1120]{2,1,0:T(8,128)(2,1)}), bf16[4,96,1120]{2,1,0:T(8,128)(2,1)}, u32[]{:S(2)}, u32[]{:S(2)}) async-start(bf16[4,96,1120]{2,1,0:T(8,128)(2,1)} %bitcast.144), calls=%async_computation.11 | async-start | bytes 1769472 | tf_op jit(solution)/shard_map/all_to_all | solution.py:109
  582.2 63.6 %reduce-scatter.13.cloned.1.call-start = ((), (), s32[]{:S(2)}) async-start(), calls=%async_computation.19 | async-start | bytes 368640 | tf_op jit(solution)/shard_map/reduce_scatter | solution.py:103
  (60 other events, 505.9 us)
Sparse Core Ops, SparseCore 0:
  10.1 35.1 all-gather.4
  50.0 82.9 all-gather.6
  135.1 68.5 all-gather.8
  213.0 77.4 all-gather.10
  331.6 65.2 reduce-scatter.6
  399.1 66.6 reduce-scatter.10
  468.7 34.4 reduce-scatter.8
  505.4 65.9 reduce-scatter.16
  573.8 42.1 reduce-scatter.14
  618.1 27.6 reduce-scatter.12

commit v6 on v5

--- a/solution.py
+++ b/solution.py
@@ -135,6 +135,29 @@
     sent = lax.dynamic_slice_in_dim(whole, 1 - at, 1, position)
     kept = lax.dynamic_slice_in_dim(whole, at, 1, position)
     return low(kept.astype(jnp.float32) + other(sent, axis).astype(jnp.float32))
+
+
+def other_half(whole, axis, position):
+    at = lax.axis_index(axis)
+    sent = lax.dynamic_slice_in_dim(whole, 1 - at, 1, position)
+    return lax.dynamic_slice_in_dim(whole, at, 1, position), other(sent, axis)
+
+
+def halve_z(column, rows):
+    high = lax.axis_size("z")
+    at_z = lax.axis_index("z")
+    step = 1
+    while step < high:
+        parts = column.reshape(-1, 2, rows, column.shape[1])
+        at = (at_z // step) % 2
+        sent = lax.dynamic_slice_in_dim(parts, 1 - at, 1, 1)
+        kept = lax.dynamic_slice_in_dim(parts, at, 1, 1)
+        came = lax.ppermute(sent, "z", [(number, number ^ step) for number in range(high)])
+        column = kept.astype(jnp.float32) + came.astype(jnp.float32)
+        column = column.reshape(-1, column.shape[3])
+        step *= 2
+        column = low(column) if step < high else column
+    return column
 
 
 def scatter_start(whole, rows):
@@ -293,7 +316,7 @@
             pltpu.VMEM(totals.shape, jnp.float32),
         ],
         cost_estimate=pl.CostEstimate(
-            flops=10 * 9 * rows * rows * wide, transcendentals=9 * rows * rows * 6, bytes_accessed=30 << 20
+            flops=rows * wide, transcendentals=0, bytes_accessed=rows * wide
         ),
         name="attend_back",
     )(bounds, rotated, grad, attended, totals, cosine, sine, place, pair)
@@ -385,9 +408,9 @@
     query_pre = product(normed_one, w_query_all) + bias_query
     key_value_column = after(key_value_column, up_own)
     up_all = gather_z(up_own)
-    key_value = gather_rest(key_value_column, rows)
     down_own = deal(after(w_down, key_value_column).T)
     down_all = gather_z(down_own)
+    key_value = after(gather_rest(key_value_column, rows), down_own)
     cotangent_group = gather_group(after(cotangent, key_value))
     cotangent_turned = lax.optimization_barrier(cotangent_group.T)
     query_rows, attended, totals = attend(
@@ -416,7 +439,7 @@
     gate_sums = scatter_z(grad_gate_all)
     grad_up_all = row_major(low(product(normed_turned, after(grad_up, grad_gate_all))))
     up_sums = scatter_z(grad_up_all)
-    down_part = product_right(after(hidden, grad_up_all), down_all)
+    down_part = product_right(after(hidden, grad_up_all, down_sums), down_all)
     normed_came = after(normed_came, down_part)
     grad_normed_mine = low(grad_normed_own + normed_came.astype(jnp.float32))
     normed_pair = other(grad_normed_mine, "y")
@@ -435,20 +458,25 @@
         bounds, query_rows, grad_attended, attended, totals,
         cosine_head, sine_head, place, key_value,
     )
-    key_value_sums = scatter_start(buffer, rows)
-    key_value_grads = scatter_z(key_value_sums)
-    down_mine = low(down_own + after(down_came, key_value_sums).astype(jnp.float32))
-    down_pair = other(down_mine, "y")
+    key_value_half = halve(buffer.reshape(-1, 2, 2, rows, 2 * head), "c", 2)
+    key_value_kept, key_value_came = other_half(key_value_half, "x", 1)
+    key_value_came = after(key_value_came, gate_sums, down_came)
+    key_value_sums = low(
+        key_value_kept.astype(jnp.float32) + key_value_came.astype(jnp.float32)
+    ).reshape(-1, 2 * head)
+    key_value_grads = halve_z(key_value_sums, rows)
     square_grads = low(
         jnp.concatenate(
             [product_left(grad_query_pre, normed_one).T, grad_out_all], axis=1
         )
     )
-    square_grads = scatter_start(after(square_grads, key_value_sums), features)
+    square_half = halve(
+        after(square_grads, key_value_sums).reshape(-1, 2, 2, features, 2 * heads_width), "c", 2
+    )
+    square_sent = other_half(square_half, "x", 1)
     gate_parts = undeal(after(gate_sums, key_value_sums))
     grad_query_part = product_right(grad_query_pre, w_query_all)
-    key_value_grads = after(key_value_grads, square_grads, grad_query_part).astype(jnp.float32)
-    square_grads = scatter_z(square_grads)
+    key_value_grads = after(key_value_grads, square_half, grad_query_part, up_sums, gate_parts)
     grad_key_pre = low(
         rotate_halves(key_value_grads[:, :head].reshape(rows, 1, head), cosine_table, -sine_table)
     ).reshape(rows, head)
@@ -457,11 +485,18 @@
     grad_project = jnp.concatenate([grad_query_pre, grad_pair], axis=1)
     grad_bias = jnp.sum(grad_project.astype(jnp.float32), axis=0)
     grad_normed_mine = low(grad_query_part + product_right(grad_pair, w_pair[:, : 2 * head]))
-    normed_pair = after(other(grad_normed_mine, "y"), gate_parts, down_pair)
+    normed_pair = other(grad_normed_mine, "y")
+    square_sums = low(
+        square_sent[0].astype(jnp.float32)
+        + after(square_sent[1], grad_normed_mine).astype(jnp.float32)
+    )
+    square_grads = scatter_z(square_sums.reshape(-1, 2 * heads_width))
+    normed_pair = after(normed_pair, square_sums)
+    up_parts = undeal(after(up_sums, normed_pair))
+    down_mine = low(down_own + after(down_came, normed_pair).astype(jnp.float32))
     result = low(
-        middle + down_mine.astype(jnp.float32) + after(down_pair, grad_pair).astype(jnp.float32)
-    )
-    up_parts = undeal(after(up_sums, grad_normed_mine))
+        middle + down_mine.astype(jnp.float32) + other(down_mine, "y").astype(jnp.float32)
+    )
     grad_normed_one = grad_normed_mine.astype(jnp.float32) + normed_pair.astype(jnp.float32)
     back_one, grad_gain_one = norm_back(inputs, scale_one, gain_one, grad_normed_one)
     grad_tokens = low(grad_middle + back_one)
@@ -486,7 +521,8 @@
             axis=1,
         )
     )
-    packed_grads = scatter_z(scatter_start(packed_grads, features)).astype(jnp.float32)
+    packed_grads = after(scatter_start(packed_grads, features), square_grads)
+    packed_grads = scatter_z(packed_grads).astype(jnp.float32)
     small_own = packed_grads[:, 2 * head :].reshape(-1)
     square_grads = square_grads.astype(jnp.float32)
     grad_w_out = square_grads[:, heads_width:].T

time: 668 us -> 678 us (1.015)
  local copies, waits for them, and re-layouts: 84 us -> 100 us
  starting transfers between devices: 55 us -> 69.5 us
  waiting for transfers between devices: 208 us -> 194 us
    reduce_scatter x6 -> x5, waiting for transfers between devices: 46.5 us -> 17.2 us  [scatter_z(): return lax.psum_scatter(whole, 'z', scatter_dimension=0, tiled=True)]
    ppermute x0 -> x2, starting transfers between devices: none -> 14.5 us  [halve_z(): lax.ppermute(sent, 'z', [(number, number ^ step) for number in range(high)])]
    ppermute x29, waiting for transfers between devices: 111 us -> 121 us  [other(): return lax.ppermute(value, axis, [(0, 1), (1, 0)])]
    dynamic_update_slice x12, local copies, waits for them, and re-layouts: 5.71 us -> 14.8 us  [gather_rest(): whole = lax.dynamic_update_slice(whole, piece, (0, x_place, c_place, 0, 0))]
    all_to_all x2, waiting for transfers between devices: 8.56 us -> 0.01 us  [deal(): lax.all_to_all(parts, GROUP, split_axis=0, concat_axis=0, tiled=True)]
    all_to_all x3, waiting for transfers between devices: 8.88 us -> 16.6 us  [undeal(): return lax.all_to_all(parts, GROUP, split_axis=0, concat_axis=0, tiled=True)]
    unnamed x101 -> x97, local copies, waits for them, and re-layouts: 13.2 us -> 16.9 us
    convert_element_type x14 -> x15, other arithmetic: 31.8 us -> 32.4 us  [low(): return value.astype(jnp.bfloat16)]
  transfers between devices with their start and end apart: 44 -> 45, of which waited for: 17 -> 20; matrix products, arithmetic and copies ran while one was open for 37% -> 43% of each run, Pallas kernels for 2% -> 2%
where the time goes in v6:
time: 678 us; the launch traced here: 667 us
  waiting for transfers between devices  194 us (29%)
  matrix products  125 us (18%)
  local copies, waits for them, and re-layouts  100 us (15%)
  other arithmetic  81.6 us (12%)
  starting transfers between devices  69.5 us (10%)
  blocking collectives  64.5 us (10%)
  between operations  16.9 us (2%)
  Pallas kernels  15.3 us (2%)
    ppermute x29, waiting for transfers between devices, other(): return lax.ppermute(value, axis, [(0, 1), (1, 0)])  121 us
    dot_general x9, matrix products, product(): return jnp.dot(left, right, preferred_element_type=jnp.float32)  77.7 us
    all_gather x2, blocking collectives, gather_z(): return lax.all_gather(own, 'z', axis=0, tiled=True)  48.6 us
    dot_general x6, matrix products, product_right(): lax.dot_general(left, right, (((1,), (1,)), ((), ())), preferred_element_...  42 us
    all_gather x4, waiting for transfers between devices, gather_z(): return lax.all_gather(own, 'z', axis=0, tiled=True)  35.6 us
    ppermute x29, starting transfers between devices, other(): return lax.ppermute(value, axis, [(0, 1), (1, 0)])  34.1 us
    convert_element_type x15, other arithmetic, low(): return value.astype(jnp.bfloat16)  32.4 us
    reduce_scatter x5, waiting for transfers between devices, scatter_z(): return lax.psum_scatter(whole, 'z', scatter_dimension=0, tiled=True)  17.2 us
  transfers between devices with their start and end apart: 45, of which 20 were waited for; matrix products, arithmetic and copies ran while one was open for 43% of the time, Pallas kernels for 2%

profile of v6, /device:TPU:0, one launch (start us, length us, event | category | flops | bytes accessed | tf_op | source)
XLA Modules:
  0.0 667.3 jit_solution(1336617160370816504)
XLA Ops:
  13.3 17.9 %all_gather.18 = bf16[384,384]{1,0:T(8,128)(2,1)S(1)} all-gather(bf16[96,384]{1,0:T(8,128)(2,1)S(1)} %pad_maximum_fusion.9), channel_id=1, replica_groups=mesh['z'=4,'x'=2,'c'=2,'y'=2] {'z'}, dimensions={0}, use_global_device_ids=true | all-gather | bytes 368640 | tf_op jit(solution)/shard_map/all_gather | solution.py:99
  33.9 15.9 %all_to_all.30 = bf16[4,96,1120]{2,1,0:T(8,128)(2,1)} all-to-all(bf16[4,96,1120]{2,1,0:T(8,128)(2,1)S(1)} %bitcast.116), channel_id=1, replica_groups=mesh['z'=4,'x'=2,'c'=2,'y'=2] {'x','c'}, dimensions={0} | all-to-all | bytes 1720320 | tf_op jit(solution)/shard_map/all_to_all | solution.py:94
  52.4 7.0 %collective-permute-done.1 = bf16[4,1,1,96,384]{4,3,2,1,0:T(8,128)(2,1)S(1)} collective-permute-done((bf16[4,1,1,96,384]{4,3,2,1,0:T(8,128)(2,1)S(1)}, bf16[4,1,1,96,384]{4,3,2,1,0:T(8,128)(2,1)S(1)}, u32[]{:S(2)}, u32[]{:S(2)}) %collective-permute-start.1) | collective-permute-done | bytes 294944 | tf_op jit(solution)/shard_map/ppermute | solution.py:58
  75.1 30.6 %all_gather.20 = bf16[1536,256]{1,0:T(8,128)(2,1)S(1)} all-gather(bf16[384,256]{1,0:T(8,128)(2,1)S(1)} %copy-done.28), channel_id=1, replica_groups=mesh['z'=4,'x'=2,'c'=2,'y'=2] {'z'}, dimensions={0}, use_global_device_ids=true | all-gather | bytes 983040 | tf_op jit(solution)/shard_map/all_gather | solution.py:99
  142.9 6.5 attend.1
  158.1 22.1 %collective-permute-done.9 = bf16[384,1536]{1,0:T(8,128)(2,1)} collective-permute-done((bf16[384,1536]{1,0:T(8,128)(2,1)S(1)}, bf16[384,1536]{1,0:T(8,128)(2,1)}, u32[]{:S(2)}, u32[]{:S(2)}) %collective-permute-start.9) | collective-permute-done | bytes 1179680 | tf_op jit(solution)/shard_map/ppermute | solution.py:58
  188.3 24.7 %collective-permute-done.11 = bf16[384,1536]{1,0:T(8,128)(2,1)} collective-permute-done((bf16[384,1536]{1,0:T(8,128)(2,1)S(1)}, bf16[384,1536]{1,0:T(8,128)(2,1)}, u32[]{:S(2)}, u32[]{:S(2)}) %collective-permute-start.11) | collective-permute-done | bytes 1179680 | tf_op jit(solution)/shard_map/ppermute | solution.py:58
  223.2 11.5 %fusion.72 = f32[1536,1120]{0,1:T(8,128)} fusion(bf16[1536,1120]{1,0:T(8,128)(2,1)} %all-gather.7.cloned.1.call-done, bf16[384,1536]{1,0:T(8,128)(2,1)} %collective-permute-done.12, bf16[384,1536]{1,0:T(8,128)(2,1)} %collective-permute-done.11, bf16[384,1536]{1,0:T(8,128)(2,1)} %collective-permute-done.10, bf16[384,1536]{1,0:T(8,128)(2,1)S(1)} %multiply_convert_fusion.3), kind=kOutput, calls=%fused_computation.175 | convolution fusion | flops 5303697408 | bytes 15040512 | tf_op jit(solution)/shard_map/dot_general | solution.py:17
  234.7 13.4 %multiply_convert_fusion.2 = (bf16[1536,1120]{0,1:T(8,128)(2,1)S(1)}, f32[1536,1120]{0,1:T(8,128)}) fusion(f32[1536,1120]{0,1:T(8,128)} %fusion.72, bf16[1536,1120]{1,0:T(8,128)(2,1)} %all-gather.9.cloned.1.call-done, bf16[384,1536]{1,0:T(8,128)(2,1)} %collective-permute-done.12, bf16[384,1536]{1,0:T(8,128)(2,1)} %collective-permute-done.11, ...), kind=kOutput, calls=%fused_computation.6 | convolution fusion | flops 5314019328 | bytes 25362432 | tf_op jit(solution)/shard_map/dot_general | solution.py:17
  249.9 9.4 %convolution_convert_fusion.2 = bf16[1536,1120]{1,0:T(8,128)(2,1)} fusion(bf16[1536,1536]{0,1:T(8,128)(2,1)} %bitcast.30, bf16[1536,1120]{0,1:T(8,128)(2,1)S(1)} %get-tuple-element.56), kind=kOutput, calls=%fused_computation.3 | convolution fusion | flops 5286543360 | bytes 11599872 | tf_op jit(solution)/shard_map/dot_general | solution.py:17
  259.4 35.5 %all-gather.11.cloned.1.call-done = bf16[1536,1120]{1,0:T(8,128)(2,1)} async-done(((bf16[384,1120]{1,0:T(8,128)(2,1)}), bf16[1536,1120]{1,0:T(8,128)(2,1)}) %all-gather.11.cloned.1.call-update) | async-done | bytes 3440656 | tf_op jit(solution)/shard_map/all_gather | solution.py:99
  294.9 15.2 %multiply_convert_fusion = (bf16[1536,1120]{0,1:T(8,128)(2,1)S(1)}, bf16[1536,1120]{0,1:T(8,128)(2,1)}) fusion(f32[1536,1120]{0,1:T(8,128)} %fusion.72, f32[1536,1120]{0,1:T(8,128)} %get-tuple-element.111, bf16[1536,1536]{1,0:T(8,128)(2,1)} %constant_dynamic-update-slice_fusion, bf16[1536,1120]{1,0:T(8,128)(2,1)} %all-gather.11.cloned.1.call-done), kind=kOutput, calls=%fused_computation.4 | convolution fusion | flops 5307187200 | bytes 28803072 | tf_op jit(solution)/shard_map/dot_general | solution.py:17
  310.1 9.1 %fusion.82 = f32[1536,1536]{1,0:T(8,128)} fusion(bf16[1536,1120]{0,1:T(8,128)(2,1)S(1)} %get-tuple-element.54, bf16[1536,1120]{1,0:T(8,128)(2,1)S(1)} %copy-done.41), kind=kOutput, calls=%fused_computation.185 | convolution fusion | flops 5284823040 | bytes 16318464 | tf_op jit(solution)/shard_map/dot_general | solution.py:27
  319.2 10.5 %fusion.81 = (bf16[1536,1536]{1,0:T(8,128)(2,1)S(1)}, f32[1536,1536]{1,0:T(8,128)S(1)}) fusion(f32[1536,1536]{1,0:T(8,128)} %fusion.82, bf16[1536,1120]{0,1:T(8,128)(2,1)} %get-tuple-element.55, bf16[1536,1120]{1,0:T(8,128)(2,1)} %all-gather.9.cloned.1.call-done), kind=kOutput, calls=%fused_computation.184 | convolution fusion | flops 5289541632 | bytes 30474240 | tf_op jit(solution)/shard_map/dot_general | solution.py:27
  330.2 4.9 fusion.70
  340.3 7.9 %convolution_convert_fusion.1 = bf16[1536,1120]{1,0:T(8,128)(2,1)} fusion(bf16[1536,1536]{0,1:T(8,128)(2,1)S(1)} %fusion.70, bf16[1536,1120]{0,1:T(8,128)(2,1)S(1)} %copy-done.45), kind=kOutput, calls=%fused_computation.2 | convolution fusion | flops 5286543360 | bytes 11599872 | tf_op jit(solution)/shard_map/dot_general | solution.py:17
  349.7 10.4 %convolution_convert_fusion = bf16[1536,1120]{1,0:T(8,128)(2,1)} fusion(bf16[1536,1536]{0,1:T(8,128)(2,1)} %copy-done.10, bf16[1536,1120]{0,1:T(8,128)(2,1)} %get-tuple-element.55), kind=kOutput, calls=%fused_computation.1 | convolution fusion | flops 5286543360 | bytes 11599872 | tf_op jit(solution)/shard_map/dot_general | solution.py:17
  362.2 11.3 %fusion.83 = f32[1536,1536]{1,0:T(8,128)} fusion(bf16[1536,1120]{0,1:T(8,128)(2,1)} %copy-done.43, bf16[1536,1120]{1,0:T(8,128)(2,1)} %all-gather.11.cloned.1.call-done), kind=kOutput, calls=%fused_computation.186 | convolution fusion | flops 5284823040 | bytes 16318464 | tf_op jit(solution)/shard_map/dot_general | solution.py:27
  385.9 12.0 %all-to-all-done.3 = bf16[4,96,1120]{2,1,0:T(8,128)(2,1)} async-done(((bf16[4,96,1120]{2,1,0:T(8,128)(2,1)}), bf16[4,96,1120]{2,1,0:T(8,128)(2,1)}, u32[]{:S(2)}, u32[]{:S(2)}) %all-to-all-start.3) | async-done | bytes 860192 | tf_op jit(solution)/shard_map/all_to_all | solution.py:109
  397.9 8.5 %collective-permute-done.18 = bf16[384,1536]{1,0:T(8,128)(2,1)} collective-permute-done((bf16[384,1536]{1,0:T(8,128)(2,1)S(1)}, bf16[384,1536]{1,0:T(8,128)(2,1)}, u32[]{:S(2)}, u32[]{:S(2)}) %collective-permute-start.18) | collective-permute-done | bytes 1179680 | tf_op jit(solution)/shard_map/ppermute | solution.py:58
  417.6 4.6 fusion.22.grad_ref
  422.2 8.8 %attend_back.1 = (bf16[384,768]{1,0:T(8,128)(2,1)}, bf16[6144,256]{1,0:T(8,128)(2,1)}) custom-call(s32[2]{0:T(128)} %pad_add_fusion.bounds_ref, bf16[384,768]{1,0:T(8,128)(2,1)} %get-tuple-element.61.rotated_ref, f32[384,768]{1,0:T(8,128)} %fusion.22.grad_ref, f32[384,768]{1,0:T(8,128)} %get-tuple-element.51.attended_ref, ...), custom_call_target="tpu_custom_call" | custom-call | flops 294912 | bytes 294912 | tf_op jit(solution)/shard_map/attend_back/pallas_call | solution.py:305
  439.7 4.8 fusion.14
  444.5 7.2 %collective-permute-start.20 = (bf16[384,1536]{1,0:T(8,128)(2,1)}, bf16[384,1536]{1,0:T(8,128)(2,1)}, u32[]{:S(2)}, u32[]{:S(2)}) collective-permute-start(bf16[384,1536]{1,0:T(8,128)(2,1)} %fusion.14), channel_id=1, source_target_pairs={{0,4},{4,0},{1,5},{5,1},{2,6},{6,2},{3,7},{7,3},{8,12},{12,8},{9,1... | collective-permute-start | bytes 3538952 | tf_op jit(solution)/shard_map/ppermute | solution.py:58
  457.2 38.4 %collective-permute-done.22 = bf16[4,1,1,384,256]{4,3,2,1,0:T(8,128)(2,1)} collective-permute-done((bf16[4,1,1,384,256]{4,3,2,1,0:T(8,128)(2,1)}, bf16[4,1,1,384,256]{4,3,2,1,0:T(8,128)(2,1)}, u32[]{:S(2)}, u32[]{:S(2)}) %collective-permute-start.22) | collective-permute-done | bytes 786464 | tf_op jit(solution)/shard_map/ppermute | solution.py:58
  498.0 6.7 copy.127
  509.6 6.3 collective-permute-start.23
  528.7 8.1 %collective-permute-start.24 = (bf16[1,1,384,256]{3,2,1,0:T(8,128)(2,1)}, bf16[1,1,384,256]{3,2,1,0:T(8,128)(2,1)}, u32[]{:S(2)}, u32[]{:S(2)}) collective-permute-start(bf16[1,1,384,256]{3,2,1,0:T(8,128)(2,1)} %constant_dynamic-slice_fusion.3), channel_id=1, source_target_pairs={{0,16},{8,24},{16,0},{24,8},{1,17},{9,25},{17,1},{25,9},{2,18},{10... | collective-permute-start | bytes 589832 | tf_op jit(solution)/shard_map/ppermute | solution.py:155
  553.7 4.6 all-to-all-done.4
  629.4 5.4 reduce-scatter.12.cloned.1.call-done
  634.8 7.1 %collective-permute-done.28 = bf16[384,1536]{1,0:T(8,128)(2,1)} collective-permute-done((bf16[384,1536]{1,0:T(8,128)(2,1)S(1)}, bf16[384,1536]{1,0:T(8,128)(2,1)}, u32[]{:S(2)}, u32[]{:S(2)}) %collective-permute-start.28) | collective-permute-done | bytes 1179680 | tf_op jit(solution)/shard_map/ppermute | solution.py:58
  646.2 9.7 %reduce-scatter.14.cloned.1.call-done = bf16[96,384]{1,0:T(8,128)(2,1)} async-done(((bf16[384,384]{1,0:T(8,128)(2,1)}), bf16[96,384]{1,0:T(8,128)(2,1)}) %reduce-scatter.14.cloned.1.call-update) | async-done | bytes 73744 | tf_op jit(solution)/shard_map/reduce_scatter | solution.py:103
  (319 shorter events, 254.2 us)
Async XLA Ops:
  7.2 62.5 %all-gather.5.cloned.1.call-start = ((), (), s32[]{:S(2)}) async-start(), calls=%async_computation.11 | async-start | bytes 1474560 | tf_op jit(solution)/shard_map/all_gather | solution.py:99
  9.0 214.2 %all-gather.7.cloned.1.call-start = ((), (), s32[]{:S(2)}) async-start(), calls=%async_computation.12 | async-start | bytes 4423680 | tf_op jit(solution)/shard_map/all_gather | solution.py:99
  66.1 39.6 %all-to-all-start.1 = ((bf16[4,96,1120]{2,1,0:T(8,128)(2,1)}), bf16[4,96,1120]{2,1,0:T(8,128)(2,1)S(1)}, u32[]{:S(2)}, u32[]{:S(2)}) async-start(bf16[4,96,1120]{2,1,0:T(8,128)(2,1)} %bitcast.104), calls=%async_computation.1 | async-start | bytes 1769472 | tf_op jit(solution)/shard_map/all_to_all | solution.py:94
  69.6 165.1 %all-gather.9.cloned.1.call-start = ((), (), s32[]{:S(2)}) async-start(), calls=%async_computation.13 | async-start | bytes 4423680 | tf_op jit(solution)/shard_map/all_gather | solution.py:99
  69.7 49.9 %collective-permute-start.4 = (bf16[4,1,1,96,1536]{4,3,2,1,0:T(8,128)(2,1)}, bf16[4,1,1,96,1536]{4,3,2,1,0:T(8,128)(2,1)}, u32[]{:S(2)}, u32[]{:S(2)}) collective-permute-start(bf16[4,1,1,96,1536]{4,3,2,1,0:T(8,128)(2,1)} %bitcast.130), channel_id=1, source_target_pairs={{0,4},{4,0},{1,5},{5,1},{2,6},{6,2},{3,7},{7,3},{8,12},{12,8},{9,1... | collective-permute-start | bytes 3538952 | tf_op jit(solution)/shard_map/ppermute | solution.py:58
  75.1 55.4 %collective-permute-start.3 = (bf16[4,1,1,96,1536]{4,3,2,1,0:T(8,128)(2,1)}, bf16[4,1,1,96,1536]{4,3,2,1,0:T(8,128)(2,1)}, u32[]{:S(2)}, u32[]{:S(2)}) collective-permute-start(bf16[4,1,1,96,1536]{4,3,2,1,0:T(8,128)(2,1)} %bitcast.131), channel_id=1, source_target_pairs={{0,2},{2,0},{1,3},{3,1},{4,6},{6,4},{5,7},{7,5},{8,10},{10,8},{9,1... | collective-permute-start | bytes 3538952 | tf_op jit(solution)/shard_map/ppermute | solution.py:58
  105.7 20.6 %collective-permute-start.6 = (bf16[4,1,1,384,256]{4,3,2,1,0:T(8,128)(2,1)S(1)}, bf16[4,1,1,384,256]{4,3,2,1,0:T(8,128)(2,1)}, u32[]{:S(2)}, u32[]{:S(2)}) collective-permute-start(bf16[4,1,1,384,256]{4,3,2,1,0:T(8,128)(2,1)S(1)} %bitcast.125), channel_id=1, source_target_pairs={{0,2},{2,0},{1,3},{3,1},{4,6},{6,4},{5,7},{7,5},{8,10},{10,8},{9,1... | collective-permute-start | bytes 2359304 | tf_op jit(solution)/shard_map/ppermute | solution.py:58
  105.7 20.6 %collective-permute-start.7 = (bf16[4,1,1,384,256]{4,3,2,1,0:T(8,128)(2,1)S(1)}, bf16[4,1,1,384,256]{4,3,2,1,0:T(8,128)(2,1)}, u32[]{:S(2)}, u32[]{:S(2)}) collective-permute-start(bf16[4,1,1,384,256]{4,3,2,1,0:T(8,128)(2,1)S(1)} %bitcast.126), channel_id=1, source_target_pairs={{0,4},{4,0},{1,5},{5,1},{2,6},{6,2},{3,7},{7,3},{8,12},{12,8},{9,1... | collective-permute-start | bytes 2359304 | tf_op jit(solution)/shard_map/ppermute | solution.py:58
  113.1 23.0 %all-to-all-start.2 = ((bf16[4,96,1120]{2,1,0:T(8,128)(2,1)}), bf16[4,96,1120]{2,1,0:T(8,128)(2,1)S(1)}, u32[]{:S(2)}, u32[]{:S(2)}) async-start(bf16[4,96,1120]{2,1,0:T(8,128)(2,1)} %bitcast.103), calls=%async_computation.2 | async-start | bytes 1769472 | tf_op jit(solution)/shard_map/all_to_all | solution.py:94
  116.7 178.3 %all-gather.11.cloned.1.call-start = ((), (), s32[]{:S(2)}) async-start(), calls=%async_computation.14 | async-start | bytes 4423680 | tf_op jit(solution)/shard_map/all_gather | solution.py:99
  152.5 27.7 %collective-permute-start.9 = (bf16[384,1536]{1,0:T(8,128)(2,1)S(1)}, bf16[384,1536]{1,0:T(8,128)(2,1)}, u32[]{:S(2)}, u32[]{:S(2)}) collective-permute-start(bf16[384,1536]{1,0:T(8,128)(2,1)S(1)} %convolution_convert_fusion.5), channel_id=1, source_target_pairs={{0,1},{1,0},{2,3},{3,2},{4,5},{5,4},{6,7},{7,6},{8,9},{9,8},{10,11... | collective-permute-start | bytes 3538952 | tf_op jit(solution)/shard_map/ppermute | solution.py:58
  154.2 33.6 %collective-permute-start.14 = (bf16[384,1536]{1,0:T(8,128)(2,1)}, bf16[384,1536]{1,0:T(8,128)(2,1)}, u32[]{:S(2)}, u32[]{:S(2)}) collective-permute-start(bf16[384,1536]{1,0:T(8,128)(2,1)} %param.29), channel_id=1, source_target_pairs={{0,4},{4,0},{1,5},{5,1},{2,6},{6,2},{3,7},{7,3},{8,12},{12,8},{9,1... | collective-permute-start | bytes 3538952 | tf_op jit(solution)/shard_map/ppermute | solution.py:58
  182.7 30.3 %collective-permute-start.11 = (bf16[384,1536]{1,0:T(8,128)(2,1)S(1)}, bf16[384,1536]{1,0:T(8,128)(2,1)}, u32[]{:S(2)}, u32[]{:S(2)}) collective-permute-start(bf16[384,1536]{1,0:T(8,128)(2,1)S(1)} %multiply_convert_fusion.3), channel_id=1, source_target_pairs={{0,4},{4,0},{1,5},{5,1},{2,6},{6,2},{3,7},{7,3},{8,12},{12,8},{9,1... | collective-permute-start | bytes 3538952 | tf_op jit(solution)/shard_map/ppermute | solution.py:58
  186.8 29.2 %collective-permute-start.13 = (bf16[384,1536]{1,0:T(8,128)(2,1)}, bf16[384,1536]{1,0:T(8,128)(2,1)}, u32[]{:S(2)}, u32[]{:S(2)}) collective-permute-start(bf16[384,1536]{1,0:T(8,128)(2,1)} %param.29), channel_id=1, source_target_pairs={{0,2},{2,0},{1,3},{3,1},{4,6},{6,4},{5,7},{7,5},{8,10},{10,8},{9,1... | collective-permute-start | bytes 3538952 | tf_op jit(solution)/shard_map/ppermute | solution.py:58
  187.8 32.9 %collective-permute-start.15 = (bf16[384,1536]{1,0:T(8,128)(2,1)}, bf16[384,1536]{1,0:T(8,128)(2,1)}, u32[]{:S(2)}, u32[]{:S(2)}) collective-permute-start(bf16[384,1536]{1,0:T(8,128)(2,1)} %collective-permute-done.14), channel_id=1, source_target_pairs={{0,2},{2,0},{1,3},{3,1},{4,6},{6,4},{5,7},{7,5},{8,10},{10,8},{9,1... | collective-permute-start | bytes 3538952 | tf_op jit(solution)/shard_map/ppermute | solution.py:58
  187.8 35.3 %collective-permute-start.10 = (bf16[384,1536]{1,0:T(8,128)(2,1)S(1)}, bf16[384,1536]{1,0:T(8,128)(2,1)}, u32[]{:S(2)}, u32[]{:S(2)}) collective-permute-start(bf16[384,1536]{1,0:T(8,128)(2,1)S(1)} %multiply_convert_fusion.3), channel_id=1, source_target_pairs={{0,2},{2,0},{1,3},{3,1},{4,6},{6,4},{5,7},{7,5},{8,10},{10,8},{9,1... | collective-permute-start | bytes 3538952 | tf_op jit(solution)/shard_map/ppermute | solution.py:58
  213.5 148.7 %reduce-scatter.6.cloned.1.call-start = ((), (), s32[]{:S(2)}) async-start(), calls=%async_computation.15 | async-start | bytes 4423680 | tf_op jit(solution)/shard_map/reduce_scatter | solution.py:103
  259.3 197.8 %reduce-scatter.8.cloned.1.call-start = ((), (), s32[]{:S(2)}) async-start(), calls=%async_computation.16 | async-start | bytes 4423680 | tf_op jit(solution)/shard_map/reduce_scatter | solution.py:103
  348.2 27.9 %collective-permute-start.17 = (bf16[384,1536]{1,0:T(8,128)(2,1)S(1)}, bf16[384,1536]{1,0:T(8,128)(2,1)}, u32[]{:S(2)}, u32[]{:S(2)}) collective-permute-start(bf16[384,1536]{1,0:T(8,128)(2,1)S(1)} %fusion.19), channel_id=1, source_target_pairs={{0,4},{4,0},{1,5},{5,1},{2,6},{6,2},{3,7},{7,3},{8,12},{12,8},{9,1... | collective-permute-start | bytes 3538952 | tf_op jit(solution)/shard_map/ppermute | solution.py:58
  379.4 27.0 %collective-permute-start.18 = (bf16[384,1536]{1,0:T(8,128)(2,1)S(1)}, bf16[384,1536]{1,0:T(8,128)(2,1)}, u32[]{:S(2)}, u32[]{:S(2)}) collective-permute-start(bf16[384,1536]{1,0:T(8,128)(2,1)S(1)} %fusion.18), channel_id=1, source_target_pairs={{0,1},{1,0},{2,3},{3,2},{4,5},{5,4},{6,7},{7,6},{8,9},{9,8},{10,11... | collective-permute-start | bytes 3538952 | tf_op jit(solution)/shard_map/ppermute | solution.py:58
  385.2 168.5 %reduce-scatter.10.cloned.1.call-start = ((), (), s32[]{:S(2)}) async-start(), calls=%async_computation.17 | async-start | bytes 4423680 | tf_op jit(solution)/shard_map/reduce_scatter | solution.py:103
  415.1 22.2 %collective-permute-start.19 = (bf16[768,1536]{1,0:T(8,128)(2,1)}, bf16[768,1536]{1,0:T(8,128)(2,1)}, u32[]{:S(2)}, u32[]{:S(2)}) collective-permute-start(bf16[768,1536]{1,0:T(8,128)(2,1)} %pad_maximum_fusion.3), channel_id=1, source_target_pairs={{0,2},{2,0},{1,3},{3,1},{4,6},{6,4},{5,7},{7,5},{8,10},{10,8},{9,1... | collective-permute-start | bytes 7077896 | tf_op jit(solution)/shard_map/ppermute | solution.py:58
  432.7 19.0 %collective-permute-start.21 = (bf16[4,2,1,384,256]{4,3,2,1,0:T(8,128)(2,1)S(1)}, bf16[4,2,1,384,256]{4,3,2,1,0:T(8,128)(2,1)S(1)}, u32[]{:S(2)}, u32[]{:S(2)}) collective-permute-start(bf16[4,2,1,384,256]{4,3,2,1,0:T(8,128)(2,1)S(1)} %constant_dynamic-slice_fusion.6), channel_id=1, source_target_pairs={{0,2},{2,0},{1,3},{3,1},{4,6},{6,4},{5,7},{7,5},{8,10},{10,8},{9,1... | collective-permute-start | bytes 4718600 | tf_op jit(solution)/shard_map/ppermute | solution.py:58
  444.5 51.0 %collective-permute-start.20 = (bf16[384,1536]{1,0:T(8,128)(2,1)}, bf16[384,1536]{1,0:T(8,128)(2,1)}, u32[]{:S(2)}, u32[]{:S(2)}) collective-permute-start(bf16[384,1536]{1,0:T(8,128)(2,1)} %fusion.14), channel_id=1, source_target_pairs={{0,4},{4,0},{1,5},{5,1},{2,6},{6,2},{3,7},{7,3},{8,12},{12,8},{9,1... | collective-permute-start | bytes 3538952 | tf_op jit(solution)/shard_map/ppermute | solution.py:58
  453.1 42.4 %collective-permute-start.22 = (bf16[4,1,1,384,256]{4,3,2,1,0:T(8,128)(2,1)}, bf16[4,1,1,384,256]{4,3,2,1,0:T(8,128)(2,1)}, u32[]{:S(2)}, u32[]{:S(2)}) collective-permute-start(bf16[4,1,1,384,256]{4,3,2,1,0:T(8,128)(2,1)} %constant_dynamic-slice_fusion.5), channel_id=1, source_target_pairs={{0,4},{4,0},{1,5},{5,1},{2,6},{6,2},{3,7},{7,3},{8,12},{12,8},{9,1... | collective-permute-start | bytes 2359304 | tf_op jit(solution)/shard_map/ppermute | solution.py:58
  507.8 40.3 %collective-permute-start.25 = (bf16[4,2,1,96,1536]{4,3,2,1,0:T(8,128)(2,1)}, bf16[4,2,1,96,1536]{4,3,2,1,0:T(8,128)(2,1)}, u32[]{:S(2)}, u32[]{:S(2)}) collective-permute-start(bf16[4,2,1,96,1536]{4,3,2,1,0:T(8,128)(2,1)} %constant_dynamic-slice_fusion.2), channel_id=1, source_target_pairs={{0,2},{2,0},{1,3},{3,1},{4,6},{6,4},{5,7},{7,5},{8,10},{10,8},{9,1... | collective-permute-start | bytes 7077896 | tf_op jit(solution)/shard_map/ppermute | solution.py:58
  560.3 27.8 %collective-permute-start.27 = (bf16[4,1,1,96,1536]{4,3,2,1,0:T(8,128)(2,1)}, bf16[4,1,1,96,1536]{4,3,2,1,0:T(8,128)(2,1)}, u32[]{:S(2)}, u32[]{:S(2)}) collective-permute-start(bf16[4,1,1,96,1536]{4,3,2,1,0:T(8,128)(2,1)} %constant_dynamic-slice_fusion.1), channel_id=1, source_target_pairs={{0,4},{4,0},{1,5},{5,1},{2,6},{6,2},{3,7},{7,3},{8,12},{12,8},{9,1... | collective-permute-start | bytes 3538952 | tf_op jit(solution)/shard_map/ppermute | solution.py:58
  565.8 27.8 %collective-permute-start.26 = (bf16[384,1536]{1,0:T(8,128)(2,1)}, bf16[384,1536]{1,0:T(8,128)(2,1)}, u32[]{:S(2)}, u32[]{:S(2)}) collective-permute-start(bf16[384,1536]{1,0:T(8,128)(2,1)} %fusion.5), channel_id=1, source_target_pairs={{0,1},{1,0},{2,3},{3,2},{4,5},{5,4},{6,7},{7,6},{8,9},{9,8},{10,11... | collective-permute-start | bytes 3538952 | tf_op jit(solution)/shard_map/ppermute | solution.py:58
  596.7 23.3 %all-to-all-start.5 = ((bf16[4,96,1120]{2,1,0:T(8,128)(2,1)}), bf16[4,96,1120]{2,1,0:T(8,128)(2,1)}, u32[]{:S(2)}, u32[]{:S(2)}) async-start(bf16[4,96,1120]{2,1,0:T(8,128)(2,1)} %bitcast.136), calls=%async_computation.10 | async-start | bytes 1769472 | tf_op jit(solution)/shard_map/all_to_all | solution.py:109
  600.9 33.9 %reduce-scatter.12.cloned.1.call-start = ((), (), s32[]{:S(2)}) async-start(), calls=%async_computation.18 | async-start | bytes 1474560 | tf_op jit(solution)/shard_map/reduce_scatter | solution.py:103
  605.6 50.3 %reduce-scatter.14.cloned.1.call-start = ((), (), s32[]{:S(2)}) async-start(), calls=%async_computation.19 | async-start | bytes 368640 | tf_op jit(solution)/shard_map/reduce_scatter | solution.py:103
  613.8 28.1 %collective-permute-start.28 = (bf16[384,1536]{1,0:T(8,128)(2,1)S(1)}, bf16[384,1536]{1,0:T(8,128)(2,1)}, u32[]{:S(2)}, u32[]{:S(2)}) collective-permute-start(bf16[384,1536]{1,0:T(8,128)(2,1)S(1)} %fusion.16), channel_id=1, source_target_pairs={{0,1},{1,0},{2,3},{3,2},{4,5},{5,4},{6,7},{7,6},{8,9},{9,8},{10,11... | collective-permute-start | bytes 3538952 | tf_op jit(solution)/shard_map/ppermute | solution.py:58
  (59 other events, 512.1 us)
Sparse Core Ops, SparseCore 0:
  10.1 35.1 all-gather.4
  50.0 82.9 all-gather.6
  135.1 68.4 all-gather.8
  213.6 81.2 all-gather.10
  297.1 65.0 reduce-scatter.5
  364.4 66.6 reduce-scatter.7
  433.4 66.6 reduce-scatter.9
  605.7 29.0 reduce-scatter.11
  637.1 18.7 reduce-scatter.13

commit v7 on v6

--- a/solution.py
+++ b/solution.py
@@ -68,6 +68,11 @@
 
 def row_major(value):
     return with_layout_constraint(value, Layout(major_to_minor=(0, 1)))
+
+
+def in_order(own, came):
+    first = lax.axis_index("y") == 0
+    return jnp.concatenate([jnp.where(first, own, came), jnp.where(first, came, own)], axis=1)
 
 
 def gather_group(own):
@@ -130,20 +135,13 @@
     return whole.reshape(-1, column.shape[1])
 
 
-def halve(whole, axis, position):
-    at = lax.axis_index(axis)
-    sent = lax.dynamic_slice_in_dim(whole, 1 - at, 1, position)
-    kept = lax.dynamic_slice_in_dim(whole, at, 1, position)
-    return low(kept.astype(jnp.float32) + other(sent, axis).astype(jnp.float32))
-
-
 def other_half(whole, axis, position):
     at = lax.axis_index(axis)
     sent = lax.dynamic_slice_in_dim(whole, 1 - at, 1, position)
     return lax.dynamic_slice_in_dim(whole, at, 1, position), other(sent, axis)
 
 
-def halve_z(column, rows):
+def halve_z(column, rows, early, late):
     high = lax.axis_size("z")
     at_z = lax.axis_index("z")
     step = 1
@@ -153,6 +151,7 @@
         sent = lax.dynamic_slice_in_dim(parts, 1 - at, 1, 1)
         kept = lax.dynamic_slice_in_dim(parts, at, 1, 1)
         came = lax.ppermute(sent, "z", [(number, number ^ step) for number in range(high)])
+        came = after(came, early if step == 1 else late)
         column = kept.astype(jnp.float32) + came.astype(jnp.float32)
         column = column.reshape(-1, column.shape[3])
         step *= 2
@@ -160,9 +159,19 @@
     return column
 
 
-def scatter_start(whole, rows):
+def add_half(halves, *earlier):
+    kept, came = halves
+    return low(kept.astype(jnp.float32) + after(came, *earlier).astype(jnp.float32))
+
+
+def scatter_core(whole, rows, *earlier):
     parts = whole.reshape(-1, 2, 2, rows, whole.shape[1])
-    return halve(halve(parts, "c", 2), "x", 1).reshape(-1, whole.shape[1])
+    return other_half(add_half(other_half(parts, "c", 2), *earlier), "x", 1)
+
+
+def scatter_across(halves, *earlier):
+    summed = add_half(halves, *earlier)
+    return summed.reshape(-1, summed.shape[4])
 
 
 def rotate_rows(value_rows, cosine, sine):
@@ -316,7 +325,7 @@
             pltpu.VMEM(totals.shape, jnp.float32),
         ],
         cost_estimate=pl.CostEstimate(
-            flops=rows * wide, transcendentals=0, bytes_accessed=rows * wide
+            flops=10 * 9 * rows * rows * wide, transcendentals=9 * rows * rows * 6, bytes_accessed=30 << 20
         ),
         name="attend_back",
     )(bounds, rotated, grad, attended, totals, cosine, sine, place, pair)
@@ -376,6 +385,7 @@
     pair_column = gather_z(after(pair_pack, square_pack))
     gate_own = deal(after(w_gate, pair_column))
     w_pair = gather_rest(pair_column, features)
+    pair_weights_came = other(w_pair[:, : 2 * head], "y")
     small_all = w_pair[:, 2 * head :].reshape(devices, features, head)[:, :small_rows]
     small_all = small_all.reshape(devices, small_rows * head).astype(jnp.float32)
     cuts = [0]
@@ -417,7 +427,11 @@
         bounds, query_pre, cosine_head, sine_head, place, key_value
     )
     attended_low = low(attended)
-    middle = inputs + sum_narrow(product_right(attended_low, w_out_all))
+    attention = low(product_right(attended_low, w_out_all))
+    attention_came = after(
+        other(attention, "y"), cotangent_group, cotangent_turned, pair_weights_came
+    )
+    middle = inputs + (attention.astype(jnp.float32) + attention_came.astype(jnp.float32))
     scale_two = norm_scale(middle)
     normed_two = low(middle * scale_two * gain_two)
     normed_group = gather_group(normed_two)
@@ -446,8 +460,6 @@
     down_parts = undeal(after(down_sums, grad_normed_mine))
     normed_pair = after(normed_pair, down_parts)
     grad_normed_two = grad_normed_mine.astype(jnp.float32) + normed_pair.astype(jnp.float32)
-    down_own, down_across = sum_core(after(down_part, normed_pair), rows)
-    down_came = other(down_across, "x")
 
     back_two, grad_gain_two = norm_back(middle, scale_two, gain_two, grad_normed_two)
     grad_middle = cotangent.astype(jnp.float32) + back_two
@@ -458,25 +470,21 @@
         bounds, query_rows, grad_attended, attended, totals,
         cosine_head, sine_head, place, key_value,
     )
-    key_value_half = halve(buffer.reshape(-1, 2, 2, rows, 2 * head), "c", 2)
-    key_value_kept, key_value_came = other_half(key_value_half, "x", 1)
-    key_value_came = after(key_value_came, gate_sums, down_came)
-    key_value_sums = low(
-        key_value_kept.astype(jnp.float32) + key_value_came.astype(jnp.float32)
-    ).reshape(-1, 2 * head)
-    key_value_grads = halve_z(key_value_sums, rows)
-    square_grads = low(
-        jnp.concatenate(
-            [product_left(grad_query_pre, normed_one).T, grad_out_all], axis=1
-        )
-    )
-    square_half = halve(
-        after(square_grads, key_value_sums).reshape(-1, 2, 2, features, 2 * heads_width), "c", 2
-    )
-    square_sent = other_half(square_half, "x", 1)
+    grad_query_mine = low(product_right(grad_query_pre, w_query_all))
+    query_came = other(grad_query_mine, "y")
+    key_value_halves = scatter_core(buffer, rows)
+    square_grads = row_major(
+        low(jnp.concatenate([product_left(grad_query_pre, normed_one).T, grad_out_all], axis=1))
+    )
+    key_value_sums = scatter_across(key_value_halves, gate_sums, square_grads, grad_query_mine)
     gate_parts = undeal(after(gate_sums, key_value_sums))
-    grad_query_part = product_right(grad_query_pre, w_query_all)
-    key_value_grads = after(key_value_grads, square_half, grad_query_part, up_sums, gate_parts)
+    square_halves = scatter_core(after(square_grads, key_value_sums), features)
+    key_value_grads = halve_z(key_value_sums, rows, key_value_sums, query_came)
+    square_sums = scatter_across(square_halves, gate_parts)
+    down_own, down_across = sum_core(after(down_part, key_value_sums), rows)
+    key_value_grads = after(key_value_grads, gate_parts, up_sums, down_across)
+    down_came = other(after(down_across, square_sums), "x")
+    square_grads = scatter_z(square_sums)
     grad_key_pre = low(
         rotate_halves(key_value_grads[:, :head].reshape(rows, 1, head), cosine_table, -sine_table)
     ).reshape(rows, head)
@@ -484,20 +492,16 @@
     grad_pair = jnp.concatenate([grad_key_pre, grad_value_pre], axis=1)
     grad_project = jnp.concatenate([grad_query_pre, grad_pair], axis=1)
     grad_bias = jnp.sum(grad_project.astype(jnp.float32), axis=0)
-    grad_normed_mine = low(grad_query_part + product_right(grad_pair, w_pair[:, : 2 * head]))
-    normed_pair = other(grad_normed_mine, "y")
-    square_sums = low(
-        square_sent[0].astype(jnp.float32)
-        + after(square_sent[1], grad_normed_mine).astype(jnp.float32)
-    )
-    square_grads = scatter_z(square_sums.reshape(-1, 2 * heads_width))
-    normed_pair = after(normed_pair, square_sums)
-    up_parts = undeal(after(up_sums, normed_pair))
-    down_mine = low(down_own + after(down_came, normed_pair).astype(jnp.float32))
-    result = low(
-        middle + down_mine.astype(jnp.float32) + other(down_mine, "y").astype(jnp.float32)
-    )
-    grad_normed_one = grad_normed_mine.astype(jnp.float32) + normed_pair.astype(jnp.float32)
+    pair_both = in_order(grad_pair, other(grad_pair, "y"))
+    query_came = after(query_came, grad_pair)
+    grad_normed_one = (
+        grad_query_mine.astype(jnp.float32) + query_came.astype(jnp.float32)
+    ) + product_right(
+        pair_both, in_order(w_pair[:, : 2 * head], pair_weights_came)
+    )
+    down_mine = low(down_own + after(down_came, pair_both).astype(jnp.float32))
+    down_pair = other(down_mine, "y")
+    result = low(middle + down_mine.astype(jnp.float32) + down_pair.astype(jnp.float32))
     back_one, grad_gain_one = norm_back(inputs, scale_one, gain_one, grad_normed_one)
     grad_tokens = low(grad_middle + back_one)
 
@@ -521,7 +525,10 @@
             axis=1,
         )
     )
-    packed_grads = after(scatter_start(packed_grads, features), square_grads)
+    up_parts = undeal(after(up_sums, grad_pair))
+    packed_grads = scatter_across(
+        scatter_core(packed_grads, features, square_sums), up_parts, down_came
+    )
     packed_grads = scatter_z(packed_grads).astype(jnp.float32)
     small_own = packed_grads[:, 2 * head :].reshape(-1)
     square_grads = square_grads.astype(jnp.float32)

time: 678 us -> 717 us (1.058)
  waiting for transfers between devices: 194 us -> 238 us
  blocking collectives: 64.5 us -> 80.5 us
  starting transfers between devices: 69.5 us -> 60.1 us
    ppermute x2, waiting for transfers between devices: 3.39 us -> 26 us  [halve_z(): lax.ppermute(sent, 'z', [(number, number ^ step) for number in range(high)])]
    all_to_all x0 -> x1, blocking collectives: none -> 16.2 us  [undeal(): return lax.all_to_all(parts, GROUP, split_axis=0, concat_axis=0, tiled=True)]
    reduce_scatter x5, waiting for transfers between devices: 17.2 us -> 33.2 us  [scatter_z(): return lax.psum_scatter(whole, 'z', scatter_dimension=0, tiled=True)]
    ppermute x29 -> x31, waiting for transfers between devices: 121 us -> 129 us  [other(): return lax.ppermute(value, axis, [(0, 1), (1, 0)])]
    ppermute x29 -> x31, starting transfers between devices: 34.1 us -> 26.4 us  [other(): return lax.ppermute(value, axis, [(0, 1), (1, 0)])]
    unnamed x97 -> x127, local copies, waits for them, and re-layouts: 16.9 us -> 13.5 us
    all_to_all x3 -> x2, waiting for transfers between devices: 16.6 us -> 15.9 us  [undeal(): return lax.all_to_all(parts, GROUP, split_axis=0, concat_axis=0, tiled=True)]
  transfers between devices with their start and end apart: 45 -> 46, of which waited for: 20 -> 20; matrix products, arithmetic and copies ran while one was open for 43% -> 39% of each run, Pallas kernels for 2% -> 2%
where the time goes in v7:
time: 717 us; the launch traced here: 709 us
  waiting for transfers between devices  238 us (33%)
  matrix products  126 us (18%)
  local copies, waits for them, and re-layouts  94 us (13%)
  blocking collectives  80.5 us (11%)
  other arithmetic  78.4 us (11%)
  starting transfers between devices  60.1 us (8%)
  between operations  17 us (2%)
  Pallas kernels  14.6 us (2%)
    ppermute x31, waiting for transfers between devices, other(): return lax.ppermute(value, axis, [(0, 1), (1, 0)])  129 us
    dot_general x9, matrix products, product(): return jnp.dot(left, right, preferred_element_type=jnp.float32)  76.9 us
    all_gather x2, blocking collectives, gather_z(): return lax.all_gather(own, 'z', axis=0, tiled=True)  48.3 us
    dot_general x6, matrix products, product_right(): lax.dot_general(left, right, (((1,), (1,)), ((), ())), preferred_element_...  43.5 us
    all_gather x4, waiting for transfers between devices, gather_z(): return lax.all_gather(own, 'z', axis=0, tiled=True)  33.4 us
    reduce_scatter x5, waiting for transfers between devices, scatter_z(): return lax.psum_scatter(whole, 'z', scatter_dimension=0, tiled=True)  33.2 us
    convert_element_type x15, other arithmetic, low(): return value.astype(jnp.bfloat16)  32.4 us
    ppermute x31, starting transfers between devices, other(): return lax.ppermute(value, axis, [(0, 1), (1, 0)])  26.4 us
  transfers between devices with their start and end apart: 46, of which 20 were waited for; matrix products, arithmetic and copies ran while one was open for 39% of the time, Pallas kernels for 2%

profile of v7, /device:TPU:0, one launch (start us, length us, event | category | flops | bytes accessed | tf_op | source)
XLA Modules:
  0.0 708.6 jit_solution(13479131278233426396)
XLA Ops:
  13.3 17.9 %all_gather.18 = bf16[384,384]{1,0:T(8,128)(2,1)S(1)} all-gather(bf16[96,384]{1,0:T(8,128)(2,1)S(1)} %pad_maximum_fusion.10), channel_id=1, replica_groups=mesh['z'=4,'x'=2,'c'=2,'y'=2] {'z'}, dimensions={0}, use_global_device_ids=true | all-gather | bytes 368640 | tf_op jit(solution)/shard_map/all_gather | solution.py:104
  33.9 15.9 %all_to_all.30 = bf16[4,96,1120]{2,1,0:T(8,128)(2,1)} all-to-all(bf16[4,96,1120]{2,1,0:T(8,128)(2,1)S(1)} %bitcast.118), channel_id=1, replica_groups=mesh['z'=4,'x'=2,'c'=2,'y'=2] {'x','c'}, dimensions={0} | all-to-all | bytes 1720320 | tf_op jit(solution)/shard_map/all_to_all | solution.py:99
  52.9 5.5 collective-permute-done.1
  72.4 30.4 %all_gather.20 = bf16[1536,256]{1,0:T(8,128)(2,1)} all-gather(bf16[384,256]{1,0:T(8,128)(2,1)S(1)} %pad_maximum_fusion.8), channel_id=1, replica_groups=mesh['z'=4,'x'=2,'c'=2,'y'=2] {'z'}, dimensions={0}, use_global_device_ids=true | all-gather | bytes 983040 | tf_op jit(solution)/shard_map/all_gather | solution.py:104
  146.8 6.1 attend.1
  152.8 12.9 %collective-permute-done.11 = bf16[384,1536]{1,0:T(8,128)(2,1)} collective-permute-done((bf16[384,1536]{1,0:T(8,128)(2,1)S(1)}, bf16[384,1536]{1,0:T(8,128)(2,1)}, u32[]{:S(2)}, u32[]{:S(2)}) %collective-permute-start.11) | collective-permute-done | bytes 1179680 | tf_op jit(solution)/shard_map/ppermute | solution.py:58
  177.2 38.2 %collective-permute-done.13 = bf16[1536,256]{1,0:T(8,128)(2,1)S(1)} collective-permute-done((bf16[1536,256]{1,0:T(8,128)(2,1)}, bf16[1536,256]{1,0:T(8,128)(2,1)S(1)}, u32[]{:S(2)}, u32[]{:S(2)}) %collective-permute-start.13) | collective-permute-done | bytes 786464 | tf_op jit(solution)/shard_map/ppermute | solution.py:58
  219.2 27.3 %collective-permute-done.15 = bf16[384,1536]{1,0:T(8,128)(2,1)} collective-permute-done((bf16[384,1536]{1,0:T(8,128)(2,1)S(1)}, bf16[384,1536]{1,0:T(8,128)(2,1)}, u32[]{:S(2)}, u32[]{:S(2)}) %collective-permute-start.15) | collective-permute-done | bytes 1179680 | tf_op jit(solution)/shard_map/ppermute | solution.py:58
  249.7 11.4 %fusion.73 = f32[1536,1120]{0,1:T(8,128)} fusion(bf16[1536,1120]{1,0:T(8,128)(2,1)} %all-gather.7.cloned.1.call-done, bf16[384,1536]{1,0:T(8,128)(2,1)} %collective-permute-done.16, bf16[384,1536]{1,0:T(8,128)(2,1)} %collective-permute-done.15, bf16[384,1536]{1,0:T(8,128)(2,1)} %collective-permute-done.14, bf16[384,1536]{1,0:T(8,128)(2,1)S(1)} %multiply_convert_fusion.3), kind=kOutput, calls=%fused_computation.179 | convolution fusion | flops 5303697408 | bytes 15040512 | tf_op jit(solution)/shard_map/dot_general | solution.py:17
  261.1 13.4 %multiply_convert_fusion.2 = (bf16[1536,1120]{0,1:T(8,128)(2,1)S(1)}, f32[1536,1120]{0,1:T(8,128)}) fusion(f32[1536,1120]{0,1:T(8,128)} %fusion.73, bf16[1536,1120]{1,0:T(8,128)(2,1)} %all-gather.9.cloned.1.call-done, bf16[384,1536]{1,0:T(8,128)(2,1)} %collective-permute-done.16, bf16[384,1536]{1,0:T(8,128)(2,1)} %collective-permute-done.15, ...), kind=kOutput, calls=%fused_computation.6 | convolution fusion | flops 5314019328 | bytes 25362432 | tf_op jit(solution)/shard_map/dot_general | solution.py:17
  276.4 9.5 %convolution_convert_fusion.2 = bf16[1536,1120]{1,0:T(8,128)(2,1)} fusion(bf16[1536,1536]{0,1:T(8,128)(2,1)} %bitcast.143, bf16[1536,1120]{0,1:T(8,128)(2,1)S(1)} %get-tuple-element.62), kind=kOutput, calls=%fused_computation.3 | convolution fusion | flops 5286543360 | bytes 11599872 | tf_op jit(solution)/shard_map/dot_general | solution.py:17
  285.9 33.3 %all-gather.11.cloned.1.call-done = bf16[1536,1120]{1,0:T(8,128)(2,1)} async-done(((bf16[384,1120]{1,0:T(8,128)(2,1)}), bf16[1536,1120]{1,0:T(8,128)(2,1)}) %all-gather.11.cloned.1.call-update) | async-done | bytes 3440656 | tf_op jit(solution)/shard_map/all_gather | solution.py:104
  319.2 15.2 %multiply_convert_fusion = (bf16[1536,1120]{0,1:T(8,128)(2,1)S(1)}, bf16[1536,1120]{0,1:T(8,128)(2,1)}) fusion(f32[1536,1120]{0,1:T(8,128)} %fusion.73, f32[1536,1120]{0,1:T(8,128)} %get-tuple-element.125, bf16[1536,1536]{1,0:T(8,128)(2,1)} %copy-done.37, bf16[1536,1120]{1,0:T(8,128)(2,1)} %all-gather.11.cloned.1.call-done), kind=kOutput, calls=%fused_computation.4 | convolution fusion | flops 5307187200 | bytes 28803072 | tf_op jit(solution)/shard_map/dot_general | solution.py:17
  334.4 9.0 %fusion.83 = f32[1536,1536]{1,0:T(8,128)} fusion(bf16[1536,1120]{0,1:T(8,128)(2,1)S(1)} %get-tuple-element.60, bf16[1536,1120]{1,0:T(8,128)(2,1)S(1)} %copy-done.55), kind=kOutput, calls=%fused_computation.189 | convolution fusion | flops 5284823040 | bytes 16318464 | tf_op jit(solution)/shard_map/dot_general | solution.py:27
  343.4 10.5 %fusion.82 = (bf16[1536,1536]{1,0:T(8,128)(2,1)S(1)}, f32[1536,1536]{1,0:T(8,128)S(1)}) fusion(f32[1536,1536]{1,0:T(8,128)} %fusion.83, bf16[1536,1120]{0,1:T(8,128)(2,1)} %get-tuple-element.61, bf16[1536,1120]{1,0:T(8,128)(2,1)} %all-gather.9.cloned.1.call-done), kind=kOutput, calls=%fused_computation.188 | convolution fusion | flops 5289541632 | bytes 30474240 | tf_op jit(solution)/shard_map/dot_general | solution.py:27
  354.4 4.9 fusion.71
  364.4 8.0 %convolution_convert_fusion.1 = bf16[1536,1120]{1,0:T(8,128)(2,1)} fusion(bf16[1536,1536]{0,1:T(8,128)(2,1)S(1)} %fusion.71, bf16[1536,1120]{0,1:T(8,128)(2,1)S(1)} %copy-done.60), kind=kOutput, calls=%fused_computation.2 | convolution fusion | flops 5286543360 | bytes 11599872 | tf_op jit(solution)/shard_map/dot_general | solution.py:17
  372.4 10.4 %convolution_convert_fusion = bf16[1536,1120]{1,0:T(8,128)(2,1)} fusion(bf16[1536,1536]{0,1:T(8,128)(2,1)} %copy-done.13, bf16[1536,1120]{0,1:T(8,128)(2,1)} %get-tuple-element.61), kind=kOutput, calls=%fused_computation.1 | convolution fusion | flops 5286543360 | bytes 11599872 | tf_op jit(solution)/shard_map/dot_general | solution.py:17
  386.5 11.3 %fusion.84 = f32[1536,1536]{1,0:T(8,128)} fusion(bf16[1536,1120]{0,1:T(8,128)(2,1)} %copy-done.58, bf16[1536,1120]{1,0:T(8,128)(2,1)} %all-gather.11.cloned.1.call-done), kind=kOutput, calls=%fused_computation.190 | convolution fusion | flops 5284823040 | bytes 16318464 | tf_op jit(solution)/shard_map/dot_general | solution.py:27
  402.5 16.2 %all_to_all.31 = bf16[4,96,1120]{2,1,0:T(8,128)(2,1)} all-to-all(bf16[4,96,1120]{2,1,0:T(8,128)(2,1)S(1)} %bitcast.140), channel_id=1, replica_groups=mesh['z'=4,'x'=2,'c'=2,'y'=2] {'x','c'}, dimensions={0} | all-to-all | bytes 1720320 | tf_op jit(solution)/shard_map/all_to_all | solution.py:114
  418.7 9.6 %collective-permute-done.19 = bf16[384,1536]{1,0:T(8,128)(2,1)S(1)} collective-permute-done((bf16[384,1536]{1,0:T(8,128)(2,1)S(1)}, bf16[384,1536]{1,0:T(8,128)(2,1)S(1)}, u32[]{:S(2)}, u32[]{:S(2)}) %collective-permute-start.19) | collective-permute-done | bytes 1179680 | tf_op jit(solution)/shard_map/ppermute | solution.py:58
  429.9 4.6 fusion.20.grad_ref
  434.6 8.5 %attend_back.1 = (bf16[384,768]{1,0:T(8,128)(2,1)}, bf16[6144,256]{1,0:T(8,128)(2,1)}) custom-call(s32[2]{0:T(128)} %pad_add_fusion.bounds_ref, bf16[384,768]{1,0:T(8,128)(2,1)} %get-tuple-element.63.rotated_ref, f32[384,768]{1,0:T(8,128)} %fusion.20.grad_ref, f32[384,768]{1,0:T(8,128)} %get-tuple-element.56.attended_ref, ...), custom_call_target="tpu_custom_call" | custom-call | flops 10192158720 | bytes 31457280 | tf_op jit(solution)/shard_map/attend_back/pallas_call | solution.py:314
  456.0 6.5 collective-permute-start.21
  466.6 14.3 %collective-permute-done.21 = bf16[4,1,1,384,256]{4,3,2,1,0:T(8,128)(2,1)} collective-permute-done((bf16[4,1,1,384,256]{4,3,2,1,0:T(8,128)(2,1)}, bf16[4,1,1,384,256]{4,3,2,1,0:T(8,128)(2,1)}, u32[]{:S(2)}, u32[]{:S(2)}) %collective-permute-start.21) | collective-permute-done | bytes 786464 | tf_op jit(solution)/shard_map/ppermute | solution.py:58
  491.7 10.2 %collective-permute-start.26 = (bf16[2,1,384,256]{3,2,1,0:T(8,128)(2,1)}, bf16[2,1,384,256]{3,2,1,0:T(8,128)(2,1)}, u32[]{:S(2)}, u32[]{:S(2)}) collective-permute-start(bf16[2,1,384,256]{3,2,1,0:T(8,128)(2,1)} %constant_dynamic-slice_fusion.2), channel_id=1, source_target_pairs={{0,8},{8,0},{16,24},{24,16},{1,9},{9,1},{17,25},{25,17},{2,10},{10... | collective-permute-start | bytes 1179656 | tf_op jit(solution)/shard_map/ppermute | solution.py:153
  506.7 23.3 %collective-permute-done.26 = bf16[2,1,384,256]{3,2,1,0:T(8,128)(2,1)} collective-permute-done((bf16[2,1,384,256]{3,2,1,0:T(8,128)(2,1)}, bf16[2,1,384,256]{3,2,1,0:T(8,128)(2,1)}, u32[]{:S(2)}, u32[]{:S(2)}) %collective-permute-start.26) | collective-permute-done | bytes 393248 | tf_op jit(solution)/shard_map/ppermute | solution.py:153
  532.5 6.0 collective-permute-start.27
  587.9 8.0 %collective-permute-done.24 = bf16[4,1,1,96,1536]{4,3,2,1,0:T(8,128)(2,1)} collective-permute-done((bf16[4,1,1,96,1536]{4,3,2,1,0:T(8,128)(2,1)}, bf16[4,1,1,96,1536]{4,3,2,1,0:T(8,128)(2,1)}, u32[]{:S(2)}, u32[]{:S(2)}) %collective-permute-start.24) | collective-permute-done | bytes 1179680 | tf_op jit(solution)/shard_map/ppermute | solution.py:58
  621.8 15.4 %all-to-all-done.5 = bf16[4,96,1120]{2,1,0:T(8,128)(2,1)} async-done(((bf16[4,96,1120]{2,1,0:T(8,128)(2,1)}), bf16[4,96,1120]{2,1,0:T(8,128)(2,1)}, u32[]{:S(2)}, u32[]{:S(2)}) %all-to-all-start.5) | async-done | bytes 860192 | tf_op jit(solution)/shard_map/all_to_all | solution.py:114
  659.3 5.9 reduce-scatter.12.cloned.1.call-done
  672.0 23.6 %reduce-scatter.14.cloned.1.call-done = bf16[96,1536]{1,0:T(8,128)(2,1)} async-done(((bf16[384,1536]{1,0:T(8,128)(2,1)}), bf16[96,1536]{1,0:T(8,128)(2,1)}) %reduce-scatter.14.cloned.1.call-update) | async-done | bytes 294928 | tf_op jit(solution)/shard_map/reduce_scatter | solution.py:108
  (354 shorter events, 248.1 us)
Async XLA Ops:
  7.2 63.3 %all-gather.5.cloned.1.call-start = ((), (), s32[]{:S(2)}) async-start(), calls=%async_computation.11 | async-start | bytes 1474560 | tf_op jit(solution)/shard_map/all_gather | solution.py:104
  9.0 237.9 %all-gather.7.cloned.1.call-start = ((), (), s32[]{:S(2)}) async-start(), calls=%async_computation.12 | async-start | bytes 4423680 | tf_op jit(solution)/shard_map/all_gather | solution.py:104
  66.9 35.9 %all-to-all-start.1 = ((bf16[4,96,1120]{2,1,0:T(8,128)(2,1)}), bf16[4,96,1120]{2,1,0:T(8,128)(2,1)S(1)}, u32[]{:S(2)}, u32[]{:S(2)}) async-start(bf16[4,96,1120]{2,1,0:T(8,128)(2,1)} %bitcast.117), calls=%async_computation.1 | async-start | bytes 1769472 | tf_op jit(solution)/shard_map/all_to_all | solution.py:99
  70.4 190.7 %all-gather.9.cloned.1.call-start = ((), (), s32[]{:S(2)}) async-start(), calls=%async_computation.13 | async-start | bytes 4423680 | tf_op jit(solution)/shard_map/all_gather | solution.py:104
  70.5 55.4 %collective-permute-start.4 = (bf16[4,1,1,96,1536]{4,3,2,1,0:T(8,128)(2,1)}, bf16[4,1,1,96,1536]{4,3,2,1,0:T(8,128)(2,1)}, u32[]{:S(2)}, u32[]{:S(2)}) collective-permute-start(bf16[4,1,1,96,1536]{4,3,2,1,0:T(8,128)(2,1)} %bitcast.132), channel_id=1, source_target_pairs={{0,4},{4,0},{1,5},{5,1},{2,6},{6,2},{3,7},{7,3},{8,12},{12,8},{9,1... | collective-permute-start | bytes 3538952 | tf_op jit(solution)/shard_map/ppermute | solution.py:58
  106.6 27.7 %collective-permute-start.3 = (bf16[4,1,1,96,1536]{4,3,2,1,0:T(8,128)(2,1)}, bf16[4,1,1,96,1536]{4,3,2,1,0:T(8,128)(2,1)}, u32[]{:S(2)}, u32[]{:S(2)}) collective-permute-start(bf16[4,1,1,96,1536]{4,3,2,1,0:T(8,128)(2,1)} %bitcast.133), channel_id=1, source_target_pairs={{0,2},{2,0},{1,3},{3,1},{4,6},{6,4},{5,7},{7,5},{8,10},{10,8},{9,1... | collective-permute-start | bytes 3538952 | tf_op jit(solution)/shard_map/ppermute | solution.py:58
  106.7 23.5 %collective-permute-start.6 = (bf16[4,1,1,384,256]{4,3,2,1,0:T(8,128)(2,1)}, bf16[4,1,1,384,256]{4,3,2,1,0:T(8,128)(2,1)}, u32[]{:S(2)}, u32[]{:S(2)}) collective-permute-start(bf16[4,1,1,384,256]{4,3,2,1,0:T(8,128)(2,1)} %bitcast.128), channel_id=1, source_target_pairs={{0,2},{2,0},{1,3},{3,1},{4,6},{6,4},{5,7},{7,5},{8,10},{10,8},{9,1... | collective-permute-start | bytes 2359304 | tf_op jit(solution)/shard_map/ppermute | solution.py:58
  114.5 23.3 %all-to-all-start.2 = ((bf16[4,96,1120]{2,1,0:T(8,128)(2,1)}), bf16[4,96,1120]{2,1,0:T(8,128)(2,1)}, u32[]{:S(2)}, u32[]{:S(2)}) async-start(bf16[4,96,1120]{2,1,0:T(8,128)(2,1)} %bitcast.104), calls=%async_computation.2 | async-start | bytes 1769472 | tf_op jit(solution)/shard_map/all_to_all | solution.py:99
  118.8 200.4 %all-gather.11.cloned.1.call-start = ((), (), s32[]{:S(2)}) async-start(), calls=%async_computation.14 | async-start | bytes 4423680 | tf_op jit(solution)/shard_map/all_gather | solution.py:104
  137.7 28.0 %collective-permute-start.11 = (bf16[384,1536]{1,0:T(8,128)(2,1)S(1)}, bf16[384,1536]{1,0:T(8,128)(2,1)}, u32[]{:S(2)}, u32[]{:S(2)}) collective-permute-start(bf16[384,1536]{1,0:T(8,128)(2,1)S(1)} %copy-done.11), channel_id=1, source_target_pairs={{0,4},{4,0},{1,5},{5,1},{2,6},{6,2},{3,7},{7,3},{8,12},{12,8},{9,1... | collective-permute-start | bytes 3538952 | tf_op jit(solution)/shard_map/ppermute | solution.py:58
  140.3 32.8 %collective-permute-start.10 = (bf16[384,1536]{1,0:T(8,128)(2,1)S(1)}, bf16[384,1536]{1,0:T(8,128)(2,1)}, u32[]{:S(2)}, u32[]{:S(2)}) collective-permute-start(bf16[384,1536]{1,0:T(8,128)(2,1)S(1)} %copy-done.11), channel_id=1, source_target_pairs={{0,2},{2,0},{1,3},{3,1},{4,6},{6,4},{5,7},{7,5},{8,10},{10,8},{9,1... | collective-permute-start | bytes 3538952 | tf_op jit(solution)/shard_map/ppermute | solution.py:58
  170.0 46.3 %collective-permute-start.9 = (bf16[384,1536]{1,0:T(8,128)(2,1)}, bf16[384,1536]{1,0:T(8,128)(2,1)}, u32[]{:S(2)}, u32[]{:S(2)}) collective-permute-start(bf16[384,1536]{1,0:T(8,128)(2,1)} %convolution_convert_fusion.6), channel_id=1, source_target_pairs={{0,1},{1,0},{2,3},{3,2},{4,5},{5,4},{6,7},{7,6},{8,9},{9,8},{10,11... | collective-permute-start | bytes 3538952 | tf_op jit(solution)/shard_map/ppermute | solution.py:58
  172.5 42.9 %collective-permute-start.13 = (bf16[1536,256]{1,0:T(8,128)(2,1)}, bf16[1536,256]{1,0:T(8,128)(2,1)S(1)}, u32[]{:S(2)}, u32[]{:S(2)}) collective-permute-start(bf16[1536,256]{1,0:T(8,128)(2,1)} %slice.221), channel_id=1, source_target_pairs={{0,1},{1,0},{2,3},{3,2},{4,5},{5,4},{6,7},{7,6},{8,9},{9,8},{10,11... | collective-permute-start | bytes 2359304 | tf_op jit(solution)/shard_map/ppermute | solution.py:58
  218.8 27.7 %collective-permute-start.15 = (bf16[384,1536]{1,0:T(8,128)(2,1)S(1)}, bf16[384,1536]{1,0:T(8,128)(2,1)}, u32[]{:S(2)}, u32[]{:S(2)}) collective-permute-start(bf16[384,1536]{1,0:T(8,128)(2,1)S(1)} %multiply_convert_fusion.3), channel_id=1, source_target_pairs={{0,4},{4,0},{1,5},{5,1},{2,6},{6,2},{3,7},{7,3},{8,12},{12,8},{9,1... | collective-permute-start | bytes 3538952 | tf_op jit(solution)/shard_map/ppermute | solution.py:58
  219.2 27.7 %collective-permute-start.14 = (bf16[384,1536]{1,0:T(8,128)(2,1)S(1)}, bf16[384,1536]{1,0:T(8,128)(2,1)}, u32[]{:S(2)}, u32[]{:S(2)}) collective-permute-start(bf16[384,1536]{1,0:T(8,128)(2,1)S(1)} %multiply_convert_fusion.3), channel_id=1, source_target_pairs={{0,2},{2,0},{1,3},{3,1},{4,6},{6,4},{5,7},{7,5},{8,10},{10,8},{9,1... | collective-permute-start | bytes 3538952 | tf_op jit(solution)/shard_map/ppermute | solution.py:58
  246.6 140.0 %reduce-scatter.6.cloned.1.call-start = ((), (), s32[]{:S(2)}) async-start(), calls=%async_computation.15 | async-start | bytes 4423680 | tf_op jit(solution)/shard_map/reduce_scatter | solution.py:108
  285.9 180.8 %reduce-scatter.8.cloned.1.call-start = ((), (), s32[]{:S(2)}) async-start(), calls=%async_computation.16 | async-start | bytes 4423680 | tf_op jit(solution)/shard_map/reduce_scatter | solution.py:108
  362.8 35.1 %collective-permute-start.18 = (bf16[384,1536]{1,0:T(8,128)(2,1)}, bf16[384,1536]{1,0:T(8,128)(2,1)S(1)}, u32[]{:S(2)}, u32[]{:S(2)}) collective-permute-start(bf16[384,1536]{1,0:T(8,128)(2,1)} %fusion.18), channel_id=1, source_target_pairs={{0,4},{4,0},{1,5},{5,1},{2,6},{6,2},{3,7},{7,3},{8,12},{12,8},{9,1... | collective-permute-start | bytes 3538952 | tf_op jit(solution)/shard_map/ppermute | solution.py:58
  372.4 184.7 %reduce-scatter.10.cloned.1.call-start = ((), (), s32[]{:S(2)}) async-start(), calls=%async_computation.17 | async-start | bytes 4423680 | tf_op jit(solution)/shard_map/reduce_scatter | solution.py:108
  400.9 27.4 %collective-permute-start.19 = (bf16[384,1536]{1,0:T(8,128)(2,1)S(1)}, bf16[384,1536]{1,0:T(8,128)(2,1)S(1)}, u32[]{:S(2)}, u32[]{:S(2)}) collective-permute-start(bf16[384,1536]{1,0:T(8,128)(2,1)S(1)} %fusion.17), channel_id=1, source_target_pairs={{0,1},{1,0},{2,3},{3,2},{4,5},{5,4},{6,7},{7,6},{8,9},{9,8},{10,11... | collective-permute-start | bytes 3538952 | tf_op jit(solution)/shard_map/ppermute | solution.py:58
  456.0 24.9 %collective-permute-start.21 = (bf16[4,1,1,384,256]{4,3,2,1,0:T(8,128)(2,1)}, bf16[4,1,1,384,256]{4,3,2,1,0:T(8,128)(2,1)}, u32[]{:S(2)}, u32[]{:S(2)}) collective-permute-start(bf16[4,1,1,384,256]{4,3,2,1,0:T(8,128)(2,1)} %constant_dynamic-slice_fusion.5), channel_id=1, source_target_pairs={{0,4},{4,0},{1,5},{5,1},{2,6},{6,2},{3,7},{7,3},{8,12},{12,8},{9,1... | collective-permute-start | bytes 2359304 | tf_op jit(solution)/shard_map/ppermute | solution.py:58
  489.5 60.0 %collective-permute-start.22 = (bf16[768,1536]{1,0:T(8,128)(2,1)}, bf16[768,1536]{1,0:T(8,128)(2,1)}, u32[]{:S(2)}, u32[]{:S(2)}) collective-permute-start(bf16[768,1536]{1,0:T(8,128)(2,1)} %pad_maximum_fusion.3), channel_id=1, source_target_pairs={{0,2},{2,0},{1,3},{3,1},{4,6},{6,4},{5,7},{7,5},{8,10},{10,8},{9,1... | collective-permute-start | bytes 7077896 | tf_op jit(solution)/shard_map/ppermute | solution.py:58
  491.7 38.3 %collective-permute-start.26 = (bf16[2,1,384,256]{3,2,1,0:T(8,128)(2,1)}, bf16[2,1,384,256]{3,2,1,0:T(8,128)(2,1)}, u32[]{:S(2)}, u32[]{:S(2)}) collective-permute-start(bf16[2,1,384,256]{3,2,1,0:T(8,128)(2,1)} %constant_dynamic-slice_fusion.2), channel_id=1, source_target_pairs={{0,8},{8,0},{16,24},{24,16},{1,9},{9,1},{17,25},{25,17},{2,10},{10... | collective-permute-start | bytes 1179656 | tf_op jit(solution)/shard_map/ppermute | solution.py:153
  501.9 43.0 %collective-permute-start.28 = (bf16[384,1536]{1,0:T(8,128)(2,1)}, bf16[384,1536]{1,0:T(8,128)(2,1)}, u32[]{:S(2)}, u32[]{:S(2)}) collective-permute-start(bf16[384,1536]{1,0:T(8,128)(2,1)} %convolution_convert_fusion.5), channel_id=1, source_target_pairs={{0,1},{1,0},{2,3},{3,2},{4,5},{5,4},{6,7},{7,6},{8,9},{9,8},{10,11... | collective-permute-start | bytes 3538952 | tf_op jit(solution)/shard_map/ppermute | solution.py:58
  506.7 55.9 %collective-permute-start.23 = (bf16[4,2,1,96,1536]{4,3,2,1,0:T(8,128)(2,1)}, bf16[4,2,1,96,1536]{4,3,2,1,0:T(8,128)(2,1)}, u32[]{:S(2)}, u32[]{:S(2)}) collective-permute-start(bf16[4,2,1,96,1536]{4,3,2,1,0:T(8,128)(2,1)} %constant_dynamic-slice_fusion.4), channel_id=1, source_target_pairs={{0,2},{2,0},{1,3},{3,1},{4,6},{6,4},{5,7},{7,5},{8,10},{10,8},{9,1... | collective-permute-start | bytes 7077896 | tf_op jit(solution)/shard_map/ppermute | solution.py:58
  568.2 27.7 %collective-permute-start.24 = (bf16[4,1,1,96,1536]{4,3,2,1,0:T(8,128)(2,1)}, bf16[4,1,1,96,1536]{4,3,2,1,0:T(8,128)(2,1)}, u32[]{:S(2)}, u32[]{:S(2)}) collective-permute-start(bf16[4,1,1,96,1536]{4,3,2,1,0:T(8,128)(2,1)} %constant_dynamic-slice_fusion.3), channel_id=1, source_target_pairs={{0,4},{4,0},{1,5},{5,1},{2,6},{6,2},{3,7},{7,3},{8,12},{12,8},{9,1... | collective-permute-start | bytes 3538952 | tf_op jit(solution)/shard_map/ppermute | solution.py:58
  598.5 42.7 %collective-permute-start.25 = (bf16[384,1536]{1,0:T(8,128)(2,1)}, bf16[384,1536]{1,0:T(8,128)(2,1)}, u32[]{:S(2)}, u32[]{:S(2)}) collective-permute-start(bf16[384,1536]{1,0:T(8,128)(2,1)} %fusion.13), channel_id=1, source_target_pairs={{0,4},{4,0},{1,5},{5,1},{2,6},{6,2},{3,7},{7,3},{8,12},{12,8},{9,1... | collective-permute-start | bytes 3538952 | tf_op jit(solution)/shard_map/ppermute | solution.py:58
  605.9 31.2 %all-to-all-start.5 = ((bf16[4,96,1120]{2,1,0:T(8,128)(2,1)}), bf16[4,96,1120]{2,1,0:T(8,128)(2,1)}, u32[]{:S(2)}, u32[]{:S(2)}) async-start(bf16[4,96,1120]{2,1,0:T(8,128)(2,1)} %bitcast.138), calls=%async_computation.8 | async-start | bytes 1769472 | tf_op jit(solution)/shard_map/all_to_all | solution.py:114
  610.1 55.0 %reduce-scatter.12.cloned.1.call-start = ((), (), s32[]{:S(2)}) async-start(), calls=%async_computation.18 | async-start | bytes 368640 | tf_op jit(solution)/shard_map/reduce_scatter | solution.py:108
  612.5 28.7 %collective-permute-start.32 = (bf16[4,1,1,96,384]{4,3,2,1,0:T(8,128)(2,1)}, bf16[4,1,1,96,384]{4,3,2,1,0:T(8,128)(2,1)}, u32[]{:S(2)}, u32[]{:S(2)}) collective-permute-start(bf16[4,1,1,96,384]{4,3,2,1,0:T(8,128)(2,1)} %constant_dynamic-slice_fusion), channel_id=1, source_target_pairs={{0,4},{4,0},{1,5},{5,1},{2,6},{6,2},{3,7},{7,3},{8,12},{12,8},{9,1... | collective-permute-start | bytes 884744 | tf_op jit(solution)/shard_map/ppermute | solution.py:58
  643.0 52.6 %reduce-scatter.14.cloned.1.call-start = ((), (), s32[]{:S(2)}) async-start(), calls=%async_computation.19 | async-start | bytes 1474560 | tf_op jit(solution)/shard_map/reduce_scatter | solution.py:108
  657.4 41.6 %collective-permute-start.30 = (bf16[384,1536]{1,0:T(8,128)(2,1)S(1)}, bf16[384,1536]{1,0:T(8,128)(2,1)}, u32[]{:S(2)}, u32[]{:S(2)}) collective-permute-start(bf16[384,1536]{1,0:T(8,128)(2,1)S(1)} %fusion.15), channel_id=1, source_target_pairs={{0,1},{1,0},{2,3},{3,2},{4,5},{5,4},{6,7},{7,6},{8,9},{9,8},{10,11... | collective-permute-start | bytes 3538952 | tf_op jit(solution)/shard_map/ppermute | solution.py:58
  (75 other events, 831.1 us)
Sparse Core Ops, SparseCore 0:
  10.1 35.1 all-gather.4
  50.0 82.9 all-gather.6
  135.1 68.5 all-gather.8
  246.7 72.5 all-gather.10
  321.4 65.0 reduce-scatter.5
  388.7 66.6 reduce-scatter.7
  457.7 85.6 reduce-scatter.9
  643.1 21.9 reduce-scatter.11
  668.0 27.5 reduce-scatter.13

commit v8 on v7

--- a/solution.py
+++ b/solution.py
@@ -325,7 +325,7 @@
             pltpu.VMEM(totals.shape, jnp.float32),
         ],
         cost_estimate=pl.CostEstimate(
-            flops=10 * 9 * rows * rows * wide, transcendentals=9 * rows * rows * 6, bytes_accessed=30 << 20
+            flops=rows * wide, transcendentals=0, bytes_accessed=rows * wide
         ),
         name="attend_back",
     )(bounds, rotated, grad, attended, totals, cosine, sine, place, pair)
@@ -420,7 +420,7 @@
     up_all = gather_z(up_own)
     down_own = deal(after(w_down, key_value_column).T)
     down_all = gather_z(down_own)
-    key_value = after(gather_rest(key_value_column, rows), down_own)
+    key_value = after(gather_rest(key_value_column, rows), down_own, pair_weights_came)
     cotangent_group = gather_group(after(cotangent, key_value))
     cotangent_turned = lax.optimization_barrier(cotangent_group.T)
     query_rows, attended, totals = attend(
@@ -429,7 +429,7 @@
     attended_low = low(attended)
     attention = low(product_right(attended_low, w_out_all))
     attention_came = after(
-        other(attention, "y"), cotangent_group, cotangent_turned, pair_weights_came
+        other(attention, "y"), cotangent_group, cotangent_turned
     )
     middle = inputs + (attention.astype(jnp.float32) + attention_came.astype(jnp.float32))
     scale_two = norm_scale(middle)
@@ -437,6 +437,7 @@
     normed_group = gather_group(normed_two)
     normed_turned = lax.optimization_barrier(normed_group.T)
     gate = product(normed_group, gate_all)
+    up_all = after(up_all, normed_turned)
     up_part = product(normed_group, up_all)
     sigmoid_gate = jax.nn.sigmoid(gate)
     silu_gate = gate * sigmoid_gate
@@ -460,6 +461,7 @@
     down_parts = undeal(after(down_sums, grad_normed_mine))
     normed_pair = after(normed_pair, down_parts)
     grad_normed_two = grad_normed_mine.astype(jnp.float32) + normed_pair.astype(jnp.float32)
+    down_own, down_across = sum_core(after(down_part, normed_pair), rows)
 
     back_two, grad_gain_two = norm_back(middle, scale_two, gain_two, grad_normed_two)
     grad_middle = cotangent.astype(jnp.float32) + back_two
@@ -476,15 +478,15 @@
     square_grads = row_major(
         low(jnp.concatenate([product_left(grad_query_pre, normed_one).T, grad_out_all], axis=1))
     )
-    key_value_sums = scatter_across(key_value_halves, gate_sums, square_grads, grad_query_mine)
+    key_value_sums = scatter_across(
+        key_value_halves, gate_sums, square_grads, grad_query_mine, down_across
+    )
     gate_parts = undeal(after(gate_sums, key_value_sums))
     square_halves = scatter_core(after(square_grads, key_value_sums), features)
     key_value_grads = halve_z(key_value_sums, rows, key_value_sums, query_came)
-    square_sums = scatter_across(square_halves, gate_parts)
-    down_own, down_across = sum_core(after(down_part, key_value_sums), rows)
-    key_value_grads = after(key_value_grads, gate_parts, up_sums, down_across)
-    down_came = other(after(down_across, square_sums), "x")
-    square_grads = scatter_z(square_sums)
+    square_sums = scatter_across(square_halves)
+    key_value_grads = after(key_value_grads, up_sums)
+    down_came = other(after(down_across, key_value_sums), "x")
     grad_key_pre = low(
         rotate_halves(key_value_grads[:, :head].reshape(rows, 1, head), cosine_table, -sine_table)
     ).reshape(rows, head)
@@ -493,7 +495,7 @@
     grad_project = jnp.concatenate([grad_query_pre, grad_pair], axis=1)
     grad_bias = jnp.sum(grad_project.astype(jnp.float32), axis=0)
     pair_both = in_order(grad_pair, other(grad_pair, "y"))
-    query_came = after(query_came, grad_pair)
+    query_came = after(query_came, grad_pair, down_came)
     grad_normed_one = (
         grad_query_mine.astype(jnp.float32) + query_came.astype(jnp.float32)
     ) + product_right(
@@ -527,11 +529,12 @@
     )
     up_parts = undeal(after(up_sums, grad_pair))
     packed_grads = scatter_across(
-        scatter_core(packed_grads, features, square_sums), up_parts, down_came
-    )
-    packed_grads = scatter_z(packed_grads).astype(jnp.float32)
+        scatter_core(packed_grads, features), gate_parts, square_sums
+    )
+    last_grads = scatter_z(jnp.concatenate([square_sums, packed_grads], axis=1)).astype(jnp.float32)
+    square_grads = last_grads[:, : 2 * heads_width]
+    packed_grads = last_grads[:, 2 * heads_width :]
     small_own = packed_grads[:, 2 * head :].reshape(-1)
-    square_grads = square_grads.astype(jnp.float32)
     grad_w_out = square_grads[:, heads_width:].T
     grad_w_down = undeal_end(down_parts).T
     grad_w_gate = undeal_end(gate_parts)

time: 717 us -> 667 us (0.930)
  waiting for transfers between devices: 238 us -> 211 us
  blocking collectives: 80.5 us -> 64.3 us
  Pallas kernels: 14.6 us -> 26.5 us
  local copies, waits for them, and re-layouts: 94 us -> 84.3 us
    reduce_scatter x5 -> x4, waiting for transfers between devices: 33.2 us -> 3.42 us  [scatter_z(): return lax.psum_scatter(whole, 'z', scatter_dimension=0, tiled=True)]
    all_to_all x1 -> x0, blocking collectives: 16.2 us -> none  [undeal(): return lax.all_to_all(parts, GROUP, split_axis=0, concat_axis=0, tiled=True)]
    pallas_call x1, Pallas kernels: 6.06 us -> 17.5 us  [attend(): pl.pallas_call(attend_kernel, out_shape=(jax.ShapeDtypeStruct((rows, wide...]
    ppermute x31, starting transfers between devices: 26.4 us -> 34.9 us  [other(): return lax.ppermute(value, axis, [(0, 1), (1, 0)])]
    unnamed x127 -> x157, local copies, waits for them, and re-layouts: 13.5 us -> 21.5 us
    ppermute x2, starting transfers between devices: 16.2 us -> 9 us  [halve_z(): lax.ppermute(sent, 'z', [(number, number ^ step) for number in range(high)])]
    all_to_all x2 -> x3, waiting for transfers between devices: 15.9 us -> 18.8 us  [undeal(): return lax.all_to_all(parts, GROUP, split_axis=0, concat_axis=0, tiled=True)]
  transfers between devices with their start and end apart: 46 -> 46, of which waited for: 20 -> 22; matrix products, arithmetic and copies ran while one was open for 39% -> 38% of each run, Pallas kernels for 2% -> 4%
where the time goes in v8:
time: 667 us; the launch traced here: 663 us
  waiting for transfers between devices  211 us (32%)
  matrix products  122 us (18%)
  local copies, waits for them, and re-layouts  84.3 us (13%)
  other arithmetic  72.8 us (11%)
  starting transfers between devices  64.3 us (10%)
  blocking collectives  64.3 us (10%)
  Pallas kernels  26.5 us (4%)
  between operations  17.5 us (3%)
    ppermute x31, waiting for transfers between devices, other(): return lax.ppermute(value, axis, [(0, 1), (1, 0)])  123 us
    dot_general x9, matrix products, product(): return jnp.dot(left, right, preferred_element_type=jnp.float32)  75 us
    all_gather x2, blocking collectives, gather_z(): return lax.all_gather(own, 'z', axis=0, tiled=True)  48.3 us
    dot_general x6, matrix products, product_right(): lax.dot_general(left, right, (((1,), (1,)), ((), ())), preferred_element_...  40.2 us
    all_gather x4, waiting for transfers between devices, gather_z(): return lax.all_gather(own, 'z', axis=0, tiled=True)  37.6 us
    ppermute x31, starting transfers between devices, other(): return lax.ppermute(value, axis, [(0, 1), (1, 0)])  34.9 us
    convert_element_type x15, other arithmetic, low(): return value.astype(jnp.bfloat16)  29.4 us
    ppermute x2, waiting for transfers between devices, halve_z(): lax.ppermute(sent, 'z', [(number, number ^ step) for number in range(high)])  27.3 us
  transfers between devices with their start and end apart: 46, of which 22 were waited for; matrix products, arithmetic and copies ran while one was open for 38% of the time, Pallas kernels for 4%

profile of v8, /device:TPU:0, one launch (start us, length us, event | category | flops | bytes accessed | tf_op | source)
XLA Modules:
  0.0 662.8 jit_solution(5064568715295455368)
XLA Ops:
  13.3 17.9 %all_gather.18 = bf16[384,384]{1,0:T(8,128)(2,1)S(1)} all-gather(bf16[96,384]{1,0:T(8,128)(2,1)S(1)} %pad_maximum_fusion.11), channel_id=1, replica_groups=mesh['z'=4,'x'=2,'c'=2,'y'=2] {'z'}, dimensions={0}, use_global_device_ids=true | all-gather | bytes 368640 | tf_op jit(solution)/shard_map/all_gather | solution.py:104
  33.9 15.9 %all_to_all.30 = bf16[4,96,1120]{2,1,0:T(8,128)(2,1)} all-to-all(bf16[4,96,1120]{2,1,0:T(8,128)(2,1)S(1)} %bitcast.129), channel_id=1, replica_groups=mesh['z'=4,'x'=2,'c'=2,'y'=2] {'x','c'}, dimensions={0} | all-to-all | bytes 1720320 | tf_op jit(solution)/shard_map/all_to_all | solution.py:99
  52.3 6.1 collective-permute-done.1
  72.0 30.4 %all_gather.20 = bf16[1536,256]{1,0:T(8,128)(2,1)} all-gather(bf16[384,256]{1,0:T(8,128)(2,1)S(1)} %pad_maximum_fusion.9), channel_id=1, replica_groups=mesh['z'=4,'x'=2,'c'=2,'y'=2] {'z'}, dimensions={0}, use_global_device_ids=true | all-gather | bytes 983040 | tf_op jit(solution)/shard_map/all_gather | solution.py:104
  115.2 8.3 %collective-permute-done.7 = bf16[4,1,1,384,256]{4,3,2,1,0:T(8,128)(2,1)} collective-permute-done((bf16[4,1,1,384,256]{4,3,2,1,0:T(8,128)(2,1)}, bf16[4,1,1,384,256]{4,3,2,1,0:T(8,128)(2,1)}, u32[]{:S(2)}, u32[]{:S(2)}) %collective-permute-start.7) | collective-permute-done | bytes 786464 | tf_op jit(solution)/shard_map/ppermute | solution.py:58
  142.1 17.5 %attend.1 = (bf16[384,768]{1,0:T(8,128)(2,1)}, f32[384,768]{1,0:T(8,128)}, f32[8,384]{1,0:T(8,128)}) custom-call(s32[2]{0:T(128)} %pad_add_fusion.bounds_ref, f32[384,768]{1,0:T(8,128)} %fusion.32.query_ref, f32[384,128]{1,0:T(8,128)} %get-tuple-element.127.cosine_ref, f32[384,128]{1,0:T(8,128)} %get-tuple-element.128.sine_ref, ...), custom_call_target="tpu_custom_call" | custom-call | flops 4076863488 | bytes 20971520 | tf_op jit(solution)/shard_map/attend/pallas_call | solution.py:295
  173.2 19.8 %collective-permute-done.10 = bf16[384,1536]{1,0:T(8,128)(2,1)S(1)} collective-permute-done((bf16[384,1536]{1,0:T(8,128)(2,1)S(1)}, bf16[384,1536]{1,0:T(8,128)(2,1)S(1)}, u32[]{:S(2)}, u32[]{:S(2)}) %collective-permute-start.10) | collective-permute-done | bytes 1179680 | tf_op jit(solution)/shard_map/ppermute | solution.py:58
  195.5 4.6 collective-permute-start.15
  200.1 25.4 %collective-permute-done.15 = bf16[384,1536]{1,0:T(8,128)(2,1)S(1)} collective-permute-done((bf16[384,1536]{1,0:T(8,128)(2,1)S(1)}, bf16[384,1536]{1,0:T(8,128)(2,1)S(1)}, u32[]{:S(2)}, u32[]{:S(2)}) %collective-permute-start.15) | collective-permute-done | bytes 1179680 | tf_op jit(solution)/shard_map/ppermute | solution.py:58
  228.5 11.3 %fusion.73 = f32[1536,1120]{0,1:T(8,128)} fusion(bf16[1536,1120]{1,0:T(8,128)(2,1)} %all-gather.7.cloned.1.call-done, bf16[384,1536]{1,0:T(8,128)(2,1)} %collective-permute-done.16, bf16[384,1536]{1,0:T(8,128)(2,1)S(1)} %collective-permute-done.15, bf16[384,1536]{1,0:T(8,128)(2,1)S(1)} %collective-permute-done.14, ...), kind=kOutput, calls=%fused_computation.180 | convolution fusion | flops 5303697408 | bytes 15040512 | tf_op jit(solution)/shard_map/dot_general | solution.py:17
  243.5 13.6 %multiply_convert_fusion.2 = (bf16[1536,1120]{0,1:T(8,128)(2,1)S(1)}, f32[1536,1120]{0,1:T(8,128)}) fusion(f32[1536,1120]{0,1:T(8,128)} %fusion.73, bf16[1536,1120]{1,0:T(8,128)(2,1)} %all-gather.9.cloned.1.call-done, bf16[384,1536]{1,0:T(8,128)(2,1)} %collective-permute-done.16, bf16[384,1536]{1,0:T(8,128)(2,1)S(1)} %collective-permute-done.15, ...), kind=kOutput, calls=%fused_computation.6 | convolution fusion | flops 5314019328 | bytes 25362432 | tf_op jit(solution)/shard_map/dot_general | solution.py:17
  258.8 9.4 %convolution_convert_fusion.2 = bf16[1536,1120]{1,0:T(8,128)(2,1)} fusion(bf16[1536,1536]{0,1:T(8,128)(2,1)} %bitcast.151, bf16[1536,1120]{0,1:T(8,128)(2,1)S(1)} %get-tuple-element.62), kind=kOutput, calls=%fused_computation.3 | convolution fusion | flops 5286543360 | bytes 11599872 | tf_op jit(solution)/shard_map/dot_general | solution.py:17
  268.7 37.6 %all-gather.11.cloned.1.call-done = bf16[1536,1120]{1,0:T(8,128)(2,1)} async-done(((bf16[384,1120]{1,0:T(8,128)(2,1)}), bf16[1536,1120]{1,0:T(8,128)(2,1)}) %all-gather.11.cloned.1.call-update) | async-done | bytes 3440656 | tf_op jit(solution)/shard_map/all_gather | solution.py:104
  306.3 15.0 %multiply_convert_fusion = (bf16[1536,1120]{0,1:T(8,128)(2,1)S(1)}, bf16[1536,1120]{0,1:T(8,128)(2,1)}) fusion(f32[1536,1120]{0,1:T(8,128)} %fusion.73, f32[1536,1120]{0,1:T(8,128)} %get-tuple-element.123, bf16[1536,1536]{1,0:T(8,128)(2,1)} %copy-done.46, bf16[1536,1120]{1,0:T(8,128)(2,1)} %all-gather.11.cloned.1.call-done), kind=kOutput, calls=%fused_computation.4 | convolution fusion | flops 5307187200 | bytes 28803072 | tf_op jit(solution)/shard_map/dot_general | solution.py:17
  321.3 8.9 %fusion.83 = f32[1536,1536]{1,0:T(8,128)} fusion(bf16[1536,1120]{0,1:T(8,128)(2,1)S(1)} %get-tuple-element.60, bf16[1536,1120]{1,0:T(8,128)(2,1)S(1)} %copy-done.63), kind=kOutput, calls=%fused_computation.190 | convolution fusion | flops 5284823040 | bytes 16318464 | tf_op jit(solution)/shard_map/dot_general | solution.py:27
  330.2 10.2 %fusion.82 = (bf16[1536,1536]{1,0:T(8,128)(2,1)S(1)}, f32[1536,1536]{1,0:T(8,128)S(1)}) fusion(f32[1536,1536]{1,0:T(8,128)} %fusion.83, bf16[1536,1120]{0,1:T(8,128)(2,1)} %get-tuple-element.61, bf16[1536,1120]{1,0:T(8,128)(2,1)S(1)} %copy-done.64), kind=kOutput, calls=%fused_computation.189 | convolution fusion | flops 5289541632 | bytes 30474240 | tf_op jit(solution)/shard_map/dot_general | solution.py:27
  350.2 8.0 %convolution_convert_fusion.1 = bf16[1536,1120]{1,0:T(8,128)(2,1)} fusion(bf16[1536,1536]{0,1:T(8,128)(2,1)S(1)} %bitcast.117, bf16[1536,1120]{0,1:T(8,128)(2,1)S(1)} %copy-done.69), kind=kOutput, calls=%fused_computation.2 | convolution fusion | flops 5286543360 | bytes 11599872 | tf_op jit(solution)/shard_map/dot_general | solution.py:17
  359.7 10.5 %convolution_convert_fusion = bf16[1536,1120]{1,0:T(8,128)(2,1)} fusion(bf16[1536,1536]{0,1:T(8,128)(2,1)} %fusion.72, bf16[1536,1120]{0,1:T(8,128)(2,1)} %get-tuple-element.61), kind=kOutput, calls=%fused_computation.1 | convolution fusion | flops 5286543360 | bytes 11599872 | tf_op jit(solution)/shard_map/dot_general | solution.py:17
  373.6 11.3 %fusion.84 = f32[1536,1536]{1,0:T(8,128)} fusion(bf16[1536,1120]{0,1:T(8,128)(2,1)} %copy-done.67, bf16[1536,1120]{1,0:T(8,128)(2,1)} %all-gather.11.cloned.1.call-done), kind=kOutput, calls=%fused_computation.191 | convolution fusion | flops 5284823040 | bytes 16318464 | tf_op jit(solution)/shard_map/dot_general | solution.py:27
  395.0 11.9 %all-to-all-done.3 = bf16[4,96,1120]{2,1,0:T(8,128)(2,1)S(1)} async-done(((bf16[4,96,1120]{2,1,0:T(8,128)(2,1)}), bf16[4,96,1120]{2,1,0:T(8,128)(2,1)S(1)}, u32[]{:S(2)}, u32[]{:S(2)}) %all-to-all-start.3) | async-done | bytes 860192 | tf_op jit(solution)/shard_map/all_to_all | solution.py:114
  406.9 9.6 %collective-permute-done.19 = bf16[384,1536]{1,0:T(8,128)(2,1)S(1)} collective-permute-done((bf16[384,1536]{1,0:T(8,128)(2,1)S(1)}, bf16[384,1536]{1,0:T(8,128)(2,1)S(1)}, u32[]{:S(2)}, u32[]{:S(2)}) %collective-permute-start.19) | collective-permute-done | bytes 1179680 | tf_op jit(solution)/shard_map/ppermute | solution.py:58
  416.5 4.7 convert.75
  429.3 9.0 %attend_back.1 = (bf16[384,768]{1,0:T(8,128)(2,1)}, bf16[6144,256]{1,0:T(8,128)(2,1)}) custom-call(s32[2]{0:T(128)} %pad_add_fusion.bounds_ref, bf16[384,768]{1,0:T(8,128)(2,1)} %get-tuple-element.67.rotated_ref, f32[384,768]{1,0:T(8,128)} %fusion.20.grad_ref, f32[384,768]{1,0:T(8,128)} %get-tuple-element.55.attended_ref, ...), custom_call_target="tpu_custom_call" | custom-call | flops 294912 | bytes 294912 | tf_op jit(solution)/shard_map/attend_back/pallas_call | solution.py:314
  453.7 6.7 %collective-permute-start.22 = (bf16[4,1,1,384,256]{4,3,2,1,0:T(8,128)(2,1)}, bf16[4,1,1,384,256]{4,3,2,1,0:T(8,128)(2,1)}, u32[]{:S(2)}, u32[]{:S(2)}) collective-permute-start(bf16[4,1,1,384,256]{4,3,2,1,0:T(8,128)(2,1)} %constant_dynamic-slice_fusion.5), channel_id=1, source_target_pairs={{0,4},{4,0},{1,5},{5,1},{2,6},{6,2},{3,7},{7,3},{8,12},{12,8},{9,1... | collective-permute-start | bytes 2359304 | tf_op jit(solution)/shard_map/ppermute | solution.py:58
  470.1 8.5 %collective-permute-done.22 = bf16[4,1,1,384,256]{4,3,2,1,0:T(8,128)(2,1)} collective-permute-done((bf16[4,1,1,384,256]{4,3,2,1,0:T(8,128)(2,1)}, bf16[4,1,1,384,256]{4,3,2,1,0:T(8,128)(2,1)}, u32[]{:S(2)}, u32[]{:S(2)}) %collective-permute-start.22) | collective-permute-done | bytes 786464 | tf_op jit(solution)/shard_map/ppermute | solution.py:58
  481.8 8.5 %collective-permute-start.24 = (bf16[2,1,384,256]{3,2,1,0:T(8,128)(2,1)}, bf16[2,1,384,256]{3,2,1,0:T(8,128)(2,1)}, u32[]{:S(2)}, u32[]{:S(2)}) collective-permute-start(bf16[2,1,384,256]{3,2,1,0:T(8,128)(2,1)} %constant_dynamic-slice_fusion.4), channel_id=1, source_target_pairs={{0,8},{8,0},{16,24},{24,16},{1,9},{9,1},{17,25},{25,17},{2,10},{10... | collective-permute-start | bytes 1179656 | tf_op jit(solution)/shard_map/ppermute | solution.py:153
  495.3 20.8 %collective-permute-done.24 = bf16[2,1,384,256]{3,2,1,0:T(8,128)(2,1)} collective-permute-done((bf16[2,1,384,256]{3,2,1,0:T(8,128)(2,1)}, bf16[2,1,384,256]{3,2,1,0:T(8,128)(2,1)}, u32[]{:S(2)}, u32[]{:S(2)}) %collective-permute-start.24) | collective-permute-done | bytes 393248 | tf_op jit(solution)/shard_map/ppermute | solution.py:153
  523.7 6.5 collective-permute-done.25
  577.6 11.7 %collective-permute-done.30 = bf16[4,1,1,96,1536]{4,3,2,1,0:T(8,128)(2,1)} collective-permute-done((bf16[4,1,1,96,1536]{4,3,2,1,0:T(8,128)(2,1)}, bf16[4,1,1,96,1536]{4,3,2,1,0:T(8,128)(2,1)}, u32[]{:S(2)}, u32[]{:S(2)}) %collective-permute-start.30) | collective-permute-done | bytes 1179680 | tf_op jit(solution)/shard_map/ppermute | solution.py:58
  591.8 6.9 %all-to-all-done.4 = bf16[4,96,1120]{2,1,0:T(8,128)(2,1)} async-done(((bf16[4,96,1120]{2,1,0:T(8,128)(2,1)}), bf16[4,96,1120]{2,1,0:T(8,128)(2,1)}, u32[]{:S(2)}, u32[]{:S(2)}) %all-to-all-start.4) | async-done | bytes 860192 | tf_op jit(solution)/shard_map/all_to_all | solution.py:114
  613.4 4.5 fusion.15
  627.8 18.7 %collective-permute-done.28 = bf16[384,1536]{1,0:T(8,128)(2,1)} collective-permute-done((bf16[384,1536]{1,0:T(8,128)(2,1)}, bf16[384,1536]{1,0:T(8,128)(2,1)}, u32[]{:S(2)}, u32[]{:S(2)}) %collective-permute-start.28) | collective-permute-done | bytes 1179680 | tf_op jit(solution)/shard_map/ppermute | solution.py:58
  (385 shorter events, 235.5 us)
Async XLA Ops:
  7.2 60.9 %all-gather.5.cloned.1.call-start = ((), (), s32[]{:S(2)}) async-start(), calls=%async_computation.10 | async-start | bytes 1474560 | tf_op jit(solution)/shard_map/all_gather | solution.py:104
  9.0 216.6 %all-gather.7.cloned.1.call-start = ((), (), s32[]{:S(2)}) async-start(), calls=%async_computation.11 | async-start | bytes 4423680 | tf_op jit(solution)/shard_map/all_gather | solution.py:104
  64.5 37.9 %all-to-all-start.1 = ((bf16[4,96,1120]{2,1,0:T(8,128)(2,1)}), bf16[4,96,1120]{2,1,0:T(8,128)(2,1)S(1)}, u32[]{:S(2)}, u32[]{:S(2)}) async-start(bf16[4,96,1120]{2,1,0:T(8,128)(2,1)} %bitcast.105), calls=%async_computation.1 | async-start | bytes 1769472 | tf_op jit(solution)/shard_map/all_to_all | solution.py:99
  68.0 175.4 %all-gather.9.cloned.1.call-start = ((), (), s32[]{:S(2)}) async-start(), calls=%async_computation.12 | async-start | bytes 4423680 | tf_op jit(solution)/shard_map/all_gather | solution.py:104
  68.1 55.4 %collective-permute-start.4 = (bf16[4,1,1,96,1536]{4,3,2,1,0:T(8,128)(2,1)}, bf16[4,1,1,96,1536]{4,3,2,1,0:T(8,128)(2,1)}, u32[]{:S(2)}, u32[]{:S(2)}) collective-permute-start(bf16[4,1,1,96,1536]{4,3,2,1,0:T(8,128)(2,1)} %bitcast.140), channel_id=1, source_target_pairs={{0,4},{4,0},{1,5},{5,1},{2,6},{6,2},{3,7},{7,3},{8,12},{12,8},{9,1... | collective-permute-start | bytes 3538952 | tf_op jit(solution)/shard_map/ppermute | solution.py:58
  103.5 25.0 %collective-permute-start.3 = (bf16[4,1,1,96,1536]{4,3,2,1,0:T(8,128)(2,1)}, bf16[4,1,1,96,1536]{4,3,2,1,0:T(8,128)(2,1)}, u32[]{:S(2)}, u32[]{:S(2)}) collective-permute-start(bf16[4,1,1,96,1536]{4,3,2,1,0:T(8,128)(2,1)} %bitcast.141), channel_id=1, source_target_pairs={{0,2},{2,0},{1,3},{3,1},{4,6},{6,4},{5,7},{7,5},{8,10},{10,8},{9,1... | collective-permute-start | bytes 3538952 | tf_op jit(solution)/shard_map/ppermute | solution.py:58
  103.6 22.5 %collective-permute-start.6 = (bf16[4,1,1,384,256]{4,3,2,1,0:T(8,128)(2,1)}, bf16[4,1,1,384,256]{4,3,2,1,0:T(8,128)(2,1)}, u32[]{:S(2)}, u32[]{:S(2)}) collective-permute-start(bf16[4,1,1,384,256]{4,3,2,1,0:T(8,128)(2,1)} %bitcast.22), channel_id=1, source_target_pairs={{0,2},{2,0},{1,3},{3,1},{4,6},{6,4},{5,7},{7,5},{8,10},{10,8},{9,1... | collective-permute-start | bytes 2359304 | tf_op jit(solution)/shard_map/ppermute | solution.py:58
  107.6 24.4 %collective-permute-start.9 = (bf16[1536,256]{1,0:T(8,128)(2,1)}, bf16[1536,256]{1,0:T(8,128)(2,1)}, u32[]{:S(2)}, u32[]{:S(2)}) collective-permute-start(bf16[1536,256]{1,0:T(8,128)(2,1)} %slice.228), channel_id=1, source_target_pairs={{0,1},{1,0},{2,3},{3,2},{4,5},{5,4},{6,7},{7,6},{8,9},{9,8},{10,11... | collective-permute-start | bytes 2359304 | tf_op jit(solution)/shard_map/ppermute | solution.py:58
  110.9 21.5 %all-to-all-start.2 = ((bf16[4,96,1120]{2,1,0:T(8,128)(2,1)}), bf16[4,96,1120]{2,1,0:T(8,128)(2,1)}, u32[]{:S(2)}, u32[]{:S(2)}) async-start(bf16[4,96,1120]{2,1,0:T(8,128)(2,1)} %bitcast.104), calls=%async_computation.2 | async-start | bytes 1769472 | tf_op jit(solution)/shard_map/all_to_all | solution.py:99
  115.2 191.1 %all-gather.11.cloned.1.call-start = ((), (), s32[]{:S(2)}) async-start(), calls=%async_computation.13 | async-start | bytes 4423680 | tf_op jit(solution)/shard_map/all_gather | solution.py:104
  132.4 27.9 %collective-permute-start.12 = (bf16[384,1536]{1,0:T(8,128)(2,1)}, bf16[384,1536]{1,0:T(8,128)(2,1)}, u32[]{:S(2)}, u32[]{:S(2)}) collective-permute-start(bf16[384,1536]{1,0:T(8,128)(2,1)} %param.29), channel_id=1, source_target_pairs={{0,4},{4,0},{1,5},{5,1},{2,6},{6,2},{3,7},{7,3},{8,12},{12,8},{9,1... | collective-permute-start | bytes 3538952 | tf_op jit(solution)/shard_map/ppermute | solution.py:58
  135.9 32.3 %collective-permute-start.11 = (bf16[384,1536]{1,0:T(8,128)(2,1)}, bf16[384,1536]{1,0:T(8,128)(2,1)}, u32[]{:S(2)}, u32[]{:S(2)}) collective-permute-start(bf16[384,1536]{1,0:T(8,128)(2,1)} %param.29), channel_id=1, source_target_pairs={{0,2},{2,0},{1,3},{3,1},{4,6},{6,4},{5,7},{7,5},{8,10},{10,8},{9,1... | collective-permute-start | bytes 3538952 | tf_op jit(solution)/shard_map/ppermute | solution.py:58
  165.1 27.9 %collective-permute-start.10 = (bf16[384,1536]{1,0:T(8,128)(2,1)S(1)}, bf16[384,1536]{1,0:T(8,128)(2,1)S(1)}, u32[]{:S(2)}, u32[]{:S(2)}) collective-permute-start(bf16[384,1536]{1,0:T(8,128)(2,1)S(1)} %convolution_convert_fusion.6), channel_id=1, source_target_pairs={{0,1},{1,0},{2,3},{3,2},{4,5},{5,4},{6,7},{7,6},{8,9},{9,8},{10,11... | collective-permute-start | bytes 3538952 | tf_op jit(solution)/shard_map/ppermute | solution.py:58
  195.5 30.0 %collective-permute-start.15 = (bf16[384,1536]{1,0:T(8,128)(2,1)S(1)}, bf16[384,1536]{1,0:T(8,128)(2,1)S(1)}, u32[]{:S(2)}, u32[]{:S(2)}) collective-permute-start(bf16[384,1536]{1,0:T(8,128)(2,1)S(1)} %multiply_convert_fusion.3), channel_id=1, source_target_pairs={{0,4},{4,0},{1,5},{5,1},{2,6},{6,2},{3,7},{7,3},{8,12},{12,8},{9,1... | collective-permute-start | bytes 3538952 | tf_op jit(solution)/shard_map/ppermute | solution.py:58
  200.1 25.5 %collective-permute-start.14 = (bf16[384,1536]{1,0:T(8,128)(2,1)S(1)}, bf16[384,1536]{1,0:T(8,128)(2,1)S(1)}, u32[]{:S(2)}, u32[]{:S(2)}) collective-permute-start(bf16[384,1536]{1,0:T(8,128)(2,1)S(1)} %multiply_convert_fusion.3), channel_id=1, source_target_pairs={{0,2},{2,0},{1,3},{3,1},{4,6},{6,4},{5,7},{7,5},{8,10},{10,8},{9,1... | collective-permute-start | bytes 3538952 | tf_op jit(solution)/shard_map/ppermute | solution.py:58
  225.5 148.0 %reduce-scatter.5.cloned.1.call-start = ((), (), s32[]{:S(2)}) async-start(), calls=%async_computation.14 | async-start | bytes 4423680 | tf_op jit(solution)/shard_map/reduce_scatter | solution.py:108
  268.2 201.9 %reduce-scatter.7.cloned.1.call-start = ((), (), s32[]{:S(2)}) async-start(), calls=%async_computation.15 | async-start | bytes 4423680 | tf_op jit(solution)/shard_map/reduce_scatter | solution.py:108
  358.2 28.1 %collective-permute-start.18 = (bf16[384,1536]{1,0:T(8,128)(2,1)S(1)}, bf16[384,1536]{1,0:T(8,128)(2,1)S(1)}, u32[]{:S(2)}, u32[]{:S(2)}) collective-permute-start(bf16[384,1536]{1,0:T(8,128)(2,1)S(1)} %fusion.18), channel_id=1, source_target_pairs={{0,4},{4,0},{1,5},{5,1},{2,6},{6,2},{3,7},{7,3},{8,12},{12,8},{9,1... | collective-permute-start | bytes 3538952 | tf_op jit(solution)/shard_map/ppermute | solution.py:58
  389.2 27.3 %collective-permute-start.19 = (bf16[384,1536]{1,0:T(8,128)(2,1)S(1)}, bf16[384,1536]{1,0:T(8,128)(2,1)S(1)}, u32[]{:S(2)}, u32[]{:S(2)}) collective-permute-start(bf16[384,1536]{1,0:T(8,128)(2,1)S(1)} %fusion.17), channel_id=1, source_target_pairs={{0,1},{1,0},{2,3},{3,2},{4,5},{5,4},{6,7},{7,6},{8,9},{9,8},{10,11... | collective-permute-start | bytes 3538952 | tf_op jit(solution)/shard_map/ppermute | solution.py:58
  394.2 137.8 %reduce-scatter.9.cloned.1.call-start = ((), (), s32[]{:S(2)}) async-start(), calls=%async_computation.16 | async-start | bytes 4423680 | tf_op jit(solution)/shard_map/reduce_scatter | solution.py:108
  423.1 39.5 %collective-permute-start.20 = (bf16[768,1536]{1,0:T(8,128)(2,1)}, bf16[768,1536]{1,0:T(8,128)(2,1)}, u32[]{:S(2)}, u32[]{:S(2)}) collective-permute-start(bf16[768,1536]{1,0:T(8,128)(2,1)} %pad_maximum_fusion.3), channel_id=1, source_target_pairs={{0,2},{2,0},{1,3},{3,1},{4,6},{6,4},{5,7},{7,5},{8,10},{10,8},{9,1... | collective-permute-start | bytes 7077896 | tf_op jit(solution)/shard_map/ppermute | solution.py:58
  453.7 24.9 %collective-permute-start.22 = (bf16[4,1,1,384,256]{4,3,2,1,0:T(8,128)(2,1)}, bf16[4,1,1,384,256]{4,3,2,1,0:T(8,128)(2,1)}, u32[]{:S(2)}, u32[]{:S(2)}) collective-permute-start(bf16[4,1,1,384,256]{4,3,2,1,0:T(8,128)(2,1)} %constant_dynamic-slice_fusion.5), channel_id=1, source_target_pairs={{0,4},{4,0},{1,5},{5,1},{2,6},{6,2},{3,7},{7,3},{8,12},{12,8},{9,1... | collective-permute-start | bytes 2359304 | tf_op jit(solution)/shard_map/ppermute | solution.py:58
  481.8 34.3 %collective-permute-start.24 = (bf16[2,1,384,256]{3,2,1,0:T(8,128)(2,1)}, bf16[2,1,384,256]{3,2,1,0:T(8,128)(2,1)}, u32[]{:S(2)}, u32[]{:S(2)}) collective-permute-start(bf16[2,1,384,256]{3,2,1,0:T(8,128)(2,1)} %constant_dynamic-slice_fusion.4), channel_id=1, source_target_pairs={{0,8},{8,0},{16,24},{24,16},{1,9},{9,1},{17,25},{25,17},{2,10},{10... | collective-permute-start | bytes 1179656 | tf_op jit(solution)/shard_map/ppermute | solution.py:153
  490.3 33.3 %collective-permute-start.26 = (bf16[384,1536]{1,0:T(8,128)(2,1)}, bf16[384,1536]{1,0:T(8,128)(2,1)}, u32[]{:S(2)}, u32[]{:S(2)}) collective-permute-start(bf16[384,1536]{1,0:T(8,128)(2,1)} %convolution_convert_fusion.5), channel_id=1, source_target_pairs={{0,1},{1,0},{2,3},{3,2},{4,5},{5,4},{6,7},{7,6},{8,9},{9,8},{10,11... | collective-permute-start | bytes 3538952 | tf_op jit(solution)/shard_map/ppermute | solution.py:58
  495.3 60.6 %collective-permute-start.29 = (bf16[4,2,1,96,1536]{4,3,2,1,0:T(8,128)(2,1)}, bf16[4,2,1,96,1536]{4,3,2,1,0:T(8,128)(2,1)}, u32[]{:S(2)}, u32[]{:S(2)}) collective-permute-start(bf16[4,2,1,96,1536]{4,3,2,1,0:T(8,128)(2,1)} %constant_dynamic-slice_fusion.2), channel_id=1, source_target_pairs={{0,2},{2,0},{1,3},{3,1},{4,6},{6,4},{5,7},{7,5},{8,10},{10,8},{9,1... | collective-permute-start | bytes 7077896 | tf_op jit(solution)/shard_map/ppermute | solution.py:58
  522.2 27.7 %collective-permute-start.23 = (bf16[384,1536]{1,0:T(8,128)(2,1)}, bf16[384,1536]{1,0:T(8,128)(2,1)}, u32[]{:S(2)}, u32[]{:S(2)}) collective-permute-start(bf16[384,1536]{1,0:T(8,128)(2,1)} %fusion.13), channel_id=1, source_target_pairs={{0,4},{4,0},{1,5},{5,1},{2,6},{6,2},{3,7},{7,3},{8,12},{12,8},{9,1... | collective-permute-start | bytes 3538952 | tf_op jit(solution)/shard_map/ppermute | solution.py:58
  560.1 29.2 %collective-permute-start.30 = (bf16[4,1,1,96,1536]{4,3,2,1,0:T(8,128)(2,1)}, bf16[4,1,1,96,1536]{4,3,2,1,0:T(8,128)(2,1)}, u32[]{:S(2)}, u32[]{:S(2)}) collective-permute-start(bf16[4,1,1,96,1536]{4,3,2,1,0:T(8,128)(2,1)} %constant_dynamic-slice_fusion.1), channel_id=1, source_target_pairs={{0,4},{4,0},{1,5},{5,1},{2,6},{6,2},{3,7},{7,3},{8,12},{12,8},{9,1... | collective-permute-start | bytes 3538952 | tf_op jit(solution)/shard_map/ppermute | solution.py:58
  568.3 30.4 %all-to-all-start.4 = ((bf16[4,96,1120]{2,1,0:T(8,128)(2,1)}), bf16[4,96,1120]{2,1,0:T(8,128)(2,1)}, u32[]{:S(2)}, u32[]{:S(2)}) async-start(bf16[4,96,1120]{2,1,0:T(8,128)(2,1)} %bitcast.147), calls=%async_computation.7 | async-start | bytes 1769472 | tf_op jit(solution)/shard_map/all_to_all | solution.py:114
  575.6 27.4 %collective-permute-start.32 = (bf16[4,1,1,96,384]{4,3,2,1,0:T(8,128)(2,1)}, bf16[4,1,1,96,384]{4,3,2,1,0:T(8,128)(2,1)}, u32[]{:S(2)}, u32[]{:S(2)}) collective-permute-start(bf16[4,1,1,96,384]{4,3,2,1,0:T(8,128)(2,1)} %constant_dynamic-slice_fusion), channel_id=1, source_target_pairs={{0,4},{4,0},{1,5},{5,1},{2,6},{6,2},{3,7},{7,3},{8,12},{12,8},{9,1... | collective-permute-start | bytes 884744 | tf_op jit(solution)/shard_map/ppermute | solution.py:58
  598.7 22.4 %all-to-all-start.5 = ((bf16[4,96,1120]{2,1,0:T(8,128)(2,1)}), bf16[4,96,1120]{2,1,0:T(8,128)(2,1)}, u32[]{:S(2)}, u32[]{:S(2)}) async-start(bf16[4,96,1120]{2,1,0:T(8,128)(2,1)} %bitcast.146), calls=%async_computation.9 | async-start | bytes 1769472 | tf_op jit(solution)/shard_map/all_to_all | solution.py:114
  603.0 46.6 %reduce-scatter.11.cloned.1.call-start = ((), (), s32[]{:S(2)}) async-start(), calls=%async_computation.17 | async-start | bytes 1843200 | tf_op jit(solution)/shard_map/reduce_scatter | solution.py:108
  617.9 28.6 %collective-permute-start.28 = (bf16[384,1536]{1,0:T(8,128)(2,1)}, bf16[384,1536]{1,0:T(8,128)(2,1)}, u32[]{:S(2)}, u32[]{:S(2)}) collective-permute-start(bf16[384,1536]{1,0:T(8,128)(2,1)} %fusion.15), channel_id=1, source_target_pairs={{0,1},{1,0},{2,3},{3,2},{4,5},{5,4},{6,7},{7,6},{8,9},{9,8},{10,11... | collective-permute-start | bytes 3538952 | tf_op jit(solution)/shard_map/ppermute | solution.py:58
  (90 other events, 874.4 us)
Sparse Core Ops, SparseCore 0:
  10.1 35.1 all-gather.4
  50.0 82.9 all-gather.6
  135.1 68.5 all-gather.8
  225.7 80.5 all-gather.10
  308.4 65.0 reduce-scatter.4
  375.7 66.6 reduce-scatter.6
  444.8 74.9 reduce-scatter.8
  606.8 34.3 reduce-scatter.10

commit v9 on v8

--- a/solution.py
+++ b/solution.py
@@ -151,7 +151,7 @@
         sent = lax.dynamic_slice_in_dim(parts, 1 - at, 1, 1)
         kept = lax.dynamic_slice_in_dim(parts, at, 1, 1)
         came = lax.ppermute(sent, "z", [(number, number ^ step) for number in range(high)])
-        came = after(came, early if step == 1 else late)
+        came = after(came, *(early if step == 1 else late))
         column = kept.astype(jnp.float32) + came.astype(jnp.float32)
         column = column.reshape(-1, column.shape[3])
         step *= 2
@@ -411,16 +411,16 @@
     key_value = jnp.concatenate([key_rows, value_rows], axis=1)
     gate_all = gather_z(gate_own)
     key_value_column = gather_z(after(key_value, gate_own, square_column))
-    up_own = deal(after(w_up, key_value))
+    down_own = deal(after(w_down, key_value).T)
     w_square = gather_rest(square_column, features)
     w_query_all = w_square[:, :heads_width]
     w_out_all = w_square[:, heads_width:]
     query_pre = product(normed_one, w_query_all) + bias_query
-    key_value_column = after(key_value_column, up_own)
+    key_value_column = after(key_value_column, down_own)
+    down_all = gather_z(down_own)
+    up_own = deal(after(w_up, key_value_column))
     up_all = gather_z(up_own)
-    down_own = deal(after(w_down, key_value_column).T)
-    down_all = gather_z(down_own)
-    key_value = after(gather_rest(key_value_column, rows), down_own, pair_weights_came)
+    key_value = after(gather_rest(key_value_column, rows), up_own, pair_weights_came)
     cotangent_group = gather_group(after(cotangent, key_value))
     cotangent_turned = lax.optimization_barrier(cotangent_group.T)
     query_rows, attended, totals = attend(
@@ -437,14 +437,14 @@
     normed_group = gather_group(normed_two)
     normed_turned = lax.optimization_barrier(normed_group.T)
     gate = product(normed_group, gate_all)
-    up_all = after(up_all, normed_turned)
+    grad_hidden = lax.optimization_barrier(product(cotangent_group, down_all))
+    up_all = after(up_all, normed_turned, grad_hidden)
     up_part = product(normed_group, up_all)
     sigmoid_gate = jax.nn.sigmoid(gate)
     silu_gate = gate * sigmoid_gate
     hidden = low(silu_gate * up_part)
     grad_down = row_major(low(product(cotangent_turned, hidden)))
     down_sums = scatter_z(grad_down)
-    grad_hidden = product(after(cotangent_group, grad_down), down_all)
     grad_gate = low(grad_hidden * up_part * sigmoid_gate * (1.0 + gate * (1.0 - sigmoid_gate)))
     grad_up = low(grad_hidden * silu_gate)
     grad_normed_part = product_right(grad_gate, gate_all) + product_right(grad_up, up_all)
@@ -481,12 +481,11 @@
     key_value_sums = scatter_across(
         key_value_halves, gate_sums, square_grads, grad_query_mine, down_across
     )
+    down_came = other(after(down_across, key_value_sums), "x")
     gate_parts = undeal(after(gate_sums, key_value_sums))
     square_halves = scatter_core(after(square_grads, key_value_sums), features)
-    key_value_grads = halve_z(key_value_sums, rows, key_value_sums, query_came)
-    square_sums = scatter_across(square_halves)
+    key_value_grads = halve_z(key_value_sums, rows, (key_value_sums,), (query_came, gate_parts, down_came))
     key_value_grads = after(key_value_grads, up_sums)
-    down_came = other(after(down_across, key_value_sums), "x")
     grad_key_pre = low(
         rotate_halves(key_value_grads[:, :head].reshape(rows, 1, head), cosine_table, -sine_table)
     ).reshape(rows, head)
@@ -495,13 +494,13 @@
     grad_project = jnp.concatenate([grad_query_pre, grad_pair], axis=1)
     grad_bias = jnp.sum(grad_project.astype(jnp.float32), axis=0)
     pair_both = in_order(grad_pair, other(grad_pair, "y"))
-    query_came = after(query_came, grad_pair, down_came)
+    query_came = after(query_came, grad_pair, square_halves[0])
     grad_normed_one = (
         grad_query_mine.astype(jnp.float32) + query_came.astype(jnp.float32)
     ) + product_right(
         pair_both, in_order(w_pair[:, : 2 * head], pair_weights_came)
     )
-    down_mine = low(down_own + after(down_came, pair_both).astype(jnp.float32))
+    down_mine = low(down_own + after(down_came, key_value_sums).astype(jnp.float32))
     down_pair = other(down_mine, "y")
     result = low(middle + down_mine.astype(jnp.float32) + down_pair.astype(jnp.float32))
     back_one, grad_gain_one = norm_back(inputs, scale_one, gain_one, grad_normed_one)
@@ -527,10 +526,12 @@
             axis=1,
         )
     )
-    up_parts = undeal(after(up_sums, grad_pair))
-    packed_grads = scatter_across(
-        scatter_core(packed_grads, features), gate_parts, square_sums
-    )
+    packed_halves = other_half(
+        packed_grads.reshape(-1, 2, 2, features, packed_grads.shape[1]), "c", 2
+    )
+    square_sums = scatter_across(square_halves, packed_halves[1], down_pair)
+    packed_grads = scatter_across(other_half(add_half(packed_halves), "x", 1))
+    up_parts = undeal(after(up_sums, packed_halves[1]))
     last_grads = scatter_z(jnp.concatenate([square_sums, packed_grads], axis=1)).astype(jnp.float32)
     square_grads = last_grads[:, : 2 * heads_width]
     packed_grads = last_grads[:, 2 * heads_width :]

time: 667 us -> 699 us (1.048); the launches traced: 663 us -> 687 us
  blocking collectives: 64.3 us -> 95.8 us
  waiting for transfers between devices: 211 us -> 225 us
  starting transfers between devices: 64.3 us -> 52.4 us
  Pallas kernels: 26.5 us -> 15.3 us
    ppermute x31, waiting for transfers between devices: 123 us -> 163 us  [other(): return lax.ppermute(value, axis, [(0, 1), (1, 0)])]
    all_gather x4, waiting for transfers between devices: 37.6 us -> 0.01 us  [gather_z(): return lax.all_gather(own, 'z', axis=0, tiled=True)]
    all_to_all x1 -> x3, blocking collectives: 15.9 us -> 47.4 us  [deal(): lax.all_to_all(parts, GROUP, split_axis=0, concat_axis=0, tiled=True)]
    reduce_scatter x4, waiting for transfers between devices: 3.42 us -> 16.9 us  [scatter_z(): return lax.psum_scatter(whole, 'z', scatter_dimension=0, tiled=True)]
    pallas_call x1, Pallas kernels: 17.5 us -> 6.51 us  [attend(): pl.pallas_call(attend_kernel, out_shape=(jax.ShapeDtypeStruct((rows, wide...]
    all_to_all x2 -> x0, starting transfers between devices: 7.74 us -> none  [deal(): lax.all_to_all(parts, GROUP, split_axis=0, concat_axis=0, tiled=True)]
    ppermute x31, starting transfers between devices: 34.9 us -> 27.4 us  [other(): return lax.ppermute(value, axis, [(0, 1), (1, 0)])]
    unnamed x157 -> x133, local copies, waits for them, and re-layouts: 21.5 us -> 14.4 us
  transfers between devices with their start and end apart: 46 -> 44, of which waited for: 22 -> 17; matrix products, arithmetic and copies ran while one was open for 38% -> 32% of each run, Pallas kernels for 4% -> 2%
where the time goes in v9:
time: 699 us; the launch traced here: 687 us
  waiting for transfers between devices  225 us (32%)
  matrix products  124 us (18%)
  blocking collectives  95.8 us (14%)
  local copies, waits for them, and re-layouts  80.8 us (12%)
  other arithmetic  76.4 us (11%)
  starting transfers between devices  52.4 us (7%)
  between operations  17.7 us (3%)
  Pallas kernels  15.3 us (2%)
    ppermute x31, waiting for transfers between devices, other(): return lax.ppermute(value, axis, [(0, 1), (1, 0)])  163 us
    dot_general x9, matrix products, product(): return jnp.dot(left, right, preferred_element_type=jnp.float32)  73.6 us
    all_gather x2, blocking collectives, gather_z(): return lax.all_gather(own, 'z', axis=0, tiled=True)  48.3 us
    all_to_all x3, blocking collectives, deal(): lax.all_to_all(parts, GROUP, split_axis=0, concat_axis=0, tiled=True)  47.4 us
    dot_general x6, matrix products, product_right(): lax.dot_general(left, right, (((1,), (1,)), ((), ())), preferred_element_...  44.1 us
    ppermute x31, starting transfers between devices, other(): return lax.ppermute(value, axis, [(0, 1), (1, 0)])  27.4 us
    convert_element_type x15, other arithmetic, low(): return value.astype(jnp.bfloat16)  26.1 us
    ppermute x2, waiting for transfers between devices, halve_z(): lax.ppermute(sent, 'z', [(number, number ^ step) for number in range(high)])  22 us
  transfers between devices with their start and end apart: 44, of which 17 were waited for; matrix products, arithmetic and copies ran while one was open for 32% of the time, Pallas kernels for 2%

profile of v9, /device:TPU:0, one launch (start us, length us, event | category | flops | bytes accessed | tf_op | source)
XLA Modules:
  0.0 687.4 jit_solution(11506427601855795582)
XLA Ops:
  13.3 17.9 %all_gather.18 = bf16[384,384]{1,0:T(8,128)(2,1)S(1)} all-gather(bf16[96,384]{1,0:T(8,128)(2,1)S(1)} %pad_maximum_fusion.10), channel_id=1, replica_groups=mesh['z'=4,'x'=2,'c'=2,'y'=2] {'z'}, dimensions={0}, use_global_device_ids=true | all-gather | bytes 368640 | tf_op jit(solution)/shard_map/all_gather | solution.py:104
  45.9 15.8 %all_to_all.30 = bf16[4,96,1120]{2,1,0:T(8,128)(2,1)} all-to-all(bf16[4,96,1120]{2,1,0:T(8,128)(2,1)S(1)} %bitcast.130), channel_id=1, replica_groups=mesh['z'=4,'x'=2,'c'=2,'y'=2] {'x','c'}, dimensions={0} | all-to-all | bytes 1720320 | tf_op jit(solution)/shard_map/all_to_all | solution.py:99
  66.4 15.8 %all_to_all.31 = bf16[4,96,1120]{2,1,0:T(8,128)(2,1)} all-to-all(bf16[4,96,1120]{2,1,0:T(8,128)(2,1)S(1)} %bitcast.131), channel_id=1, replica_groups=mesh['z'=4,'x'=2,'c'=2,'y'=2] {'x','c'}, dimensions={0} | all-to-all | bytes 1720320 | tf_op jit(solution)/shard_map/all_to_all | solution.py:99
  82.2 30.4 %all_gather.20 = bf16[1536,256]{1,0:T(8,128)(2,1)} all-gather(bf16[384,256]{1,0:T(8,128)(2,1)S(1)} %copy-done.35), channel_id=1, replica_groups=mesh['z'=4,'x'=2,'c'=2,'y'=2] {'z'}, dimensions={0}, use_global_device_ids=true | all-gather | bytes 983040 | tf_op jit(solution)/shard_map/all_gather | solution.py:104
  117.1 15.8 %all_to_all.32 = bf16[4,96,1120]{2,1,0:T(8,128)(2,1)} all-to-all(bf16[4,96,1120]{2,1,0:T(8,128)(2,1)S(1)} %bitcast.132), channel_id=1, replica_groups=mesh['z'=4,'x'=2,'c'=2,'y'=2] {'x','c'}, dimensions={0} | all-to-all | bytes 1720320 | tf_op jit(solution)/shard_map/all_to_all | solution.py:99
  144.1 33.8 %collective-permute-done.7 = bf16[4,1,1,384,256]{4,3,2,1,0:T(8,128)(2,1)} collective-permute-done((bf16[4,1,1,384,256]{4,3,2,1,0:T(8,128)(2,1)}, bf16[4,1,1,384,256]{4,3,2,1,0:T(8,128)(2,1)}, u32[]{:S(2)}, u32[]{:S(2)}) %collective-permute-start.7) | collective-permute-done | bytes 786464 | tf_op jit(solution)/shard_map/ppermute | solution.py:58
  189.8 6.5 attend.1
  196.3 15.9 %collective-permute-done.12 = bf16[384,1536]{1,0:T(8,128)(2,1)S(1)} collective-permute-done((bf16[384,1536]{1,0:T(8,128)(2,1)S(1)}, bf16[384,1536]{1,0:T(8,128)(2,1)S(1)}, u32[]{:S(2)}, u32[]{:S(2)}) %collective-permute-start.12) | collective-permute-done | bytes 1179680 | tf_op jit(solution)/shard_map/ppermute | solution.py:58
  223.0 22.0 %collective-permute-done.10 = bf16[384,1536]{1,0:T(8,128)(2,1)} collective-permute-done((bf16[384,1536]{1,0:T(8,128)(2,1)}, bf16[384,1536]{1,0:T(8,128)(2,1)}, u32[]{:S(2)}, u32[]{:S(2)}) %collective-permute-start.10) | collective-permute-done | bytes 1179680 | tf_op jit(solution)/shard_map/ppermute | solution.py:58
  248.0 27.2 %collective-permute-done.15 = bf16[384,1536]{1,0:T(8,128)(2,1)} collective-permute-done((bf16[384,1536]{1,0:T(8,128)(2,1)S(1)}, bf16[384,1536]{1,0:T(8,128)(2,1)}, u32[]{:S(2)}, u32[]{:S(2)}) %collective-permute-start.15) | collective-permute-done | bytes 1179680 | tf_op jit(solution)/shard_map/ppermute | solution.py:58
  275.2 10.5 %fusion.86 = f32[1536,1120]{0,1:T(8,128)} fusion(bf16[1536,1536]{1,0:T(8,128)(2,1)} %copy-done.41, bf16[1536,1120]{1,0:T(8,128)(2,1)} %all-gather.11.cloned.1.call-done), kind=kOutput, calls=%fused_computation.193 | convolution fusion | flops 5284823040 | bytes 15040512 | tf_op jit(solution)/shard_map/dot_general | solution.py:17
  285.7 4.8 fusion.75
  290.5 11.5 %fusion.74 = f32[1536,1120]{0,1:T(8,128)} fusion(bf16[1536,1120]{1,0:T(8,128)(2,1)} %all-gather.9.cloned.1.call-done, bf16[384,1536]{1,0:T(8,128)(2,1)} %collective-permute-done.16, bf16[384,1536]{1,0:T(8,128)(2,1)} %collective-permute-done.15, bf16[384,1536]{1,0:T(8,128)(2,1)} %collective-permute-done.14, bf16[384,1536]{1,0:T(8,128)(2,1)S(1)} %multiply_convert_fusion.3), kind=kOutput, calls=%fused_computation.181 | convolution fusion | flops 5303697408 | bytes 15040512 | tf_op jit(solution)/shard_map/dot_general | solution.py:17
  302.1 16.7 %multiply_convert_fusion = (bf16[1536,1120]{0,1:T(8,128)(2,1)}, bf16[1536,1120]{0,1:T(8,128)(2,1)}, bf16[1536,1120]{0,1:T(8,128)(2,1)}) fusion(f32[1536,1120]{0,1:T(8,128)} %fusion.86, f32[1536,1120]{0,1:T(8,128)} %fusion.74, bf16[1536,1120]{1,0:T(8,128)(2,1)} %all-gather.7.cloned.1.call-done, bf16[384,1536]{1,0:T(8,128)(2,1)} %collective-permute-done.16, ...), kind=kOutput, calls=%fused_computation.4 | convolution fusion | flops 5329502208 | bytes 32243712 | tf_op jit(solution)/shard_map/dot_general | solution.py:17
  318.7 10.4 %convolution_convert_fusion = bf16[1536,1120]{1,0:T(8,128)(2,1)} fusion(bf16[1536,1536]{0,1:T(8,128)(2,1)} %bitcast.157, bf16[1536,1120]{0,1:T(8,128)(2,1)} %get-tuple-element.60), kind=kOutput, calls=%fused_computation.1 | convolution fusion | flops 5286543360 | bytes 11599872 | tf_op jit(solution)/shard_map/dot_general | solution.py:17
  329.2 11.6 %fusion.87 = f32[1536,1536]{1,0:T(8,128)} fusion(bf16[1536,1120]{0,1:T(8,128)(2,1)} %get-tuple-element.58, bf16[1536,1120]{1,0:T(8,128)(2,1)} %all-gather.7.cloned.1.call-done), kind=kOutput, calls=%fused_computation.194 | convolution fusion | flops 5284823040 | bytes 16318464 | tf_op jit(solution)/shard_map/dot_general | solution.py:27
  340.8 10.5 %fusion.85 = (bf16[1536,1536]{1,0:T(8,128)(2,1)S(1)}, f32[1536,1536]{1,0:T(8,128)S(1)}) fusion(f32[1536,1536]{1,0:T(8,128)} %fusion.87, bf16[1536,1120]{0,1:T(8,128)(2,1)} %get-tuple-element.59, bf16[1536,1120]{1,0:T(8,128)(2,1)} %all-gather.9.cloned.1.call-done), kind=kOutput, calls=%fused_computation.192 | convolution fusion | flops 5289541632 | bytes 30474240 | tf_op jit(solution)/shard_map/dot_general | solution.py:27
  361.2 7.7 %convolution_convert_fusion.2 = bf16[1536,1120]{1,0:T(8,128)(2,1)} fusion(bf16[1536,1536]{0,1:T(8,128)(2,1)S(1)} %bitcast.117, bf16[1536,1120]{0,1:T(8,128)(2,1)S(1)} %copy-done.57), kind=kOutput, calls=%fused_computation.3 | convolution fusion | flops 5286543360 | bytes 11599872 | tf_op jit(solution)/shard_map/dot_general | solution.py:17
  369.4 10.9 %convolution_convert_fusion.1 = bf16[1536,1120]{1,0:T(8,128)(2,1)} fusion(bf16[1536,1536]{0,1:T(8,128)(2,1)} %fusion.75, bf16[1536,1120]{0,1:T(8,128)(2,1)} %get-tuple-element.59), kind=kOutput, calls=%fused_computation.2 | convolution fusion | flops 5286543360 | bytes 11599872 | tf_op jit(solution)/shard_map/dot_general | solution.py:17
  380.3 16.9 %reduce-scatter.5.cloned.1.call-done = bf16[384,1120]{1,0:T(8,128)(2,1)} async-done(((bf16[1536,1120]{1,0:T(8,128)(2,1)}), bf16[384,1120]{1,0:T(8,128)(2,1)}) %reduce-scatter.5.cloned.1.call-update) | async-done | bytes 860176 | tf_op jit(solution)/shard_map/reduce_scatter | solution.py:108
  397.2 11.3 %fusion.88 = f32[1536,1536]{1,0:T(8,128)} fusion(bf16[1536,1120]{0,1:T(8,128)(2,1)} %get-tuple-element.60, bf16[1536,1120]{1,0:T(8,128)(2,1)} %all-gather.11.cloned.1.call-done), kind=kOutput, calls=%fused_computation.195 | convolution fusion | flops 5284823040 | bytes 16318464 | tf_op jit(solution)/shard_map/dot_general | solution.py:27
  418.3 12.0 %all-to-all-done.3 = bf16[4,96,1120]{2,1,0:T(8,128)(2,1)} async-done(((bf16[4,96,1120]{2,1,0:T(8,128)(2,1)}), bf16[4,96,1120]{2,1,0:T(8,128)(2,1)}, u32[]{:S(2)}, u32[]{:S(2)}) %all-to-all-start.3) | async-done | bytes 860192 | tf_op jit(solution)/shard_map/all_to_all | solution.py:114
  430.3 9.0 %collective-permute-done.19 = bf16[384,1536]{1,0:T(8,128)(2,1)} collective-permute-done((bf16[384,1536]{1,0:T(8,128)(2,1)S(1)}, bf16[384,1536]{1,0:T(8,128)(2,1)}, u32[]{:S(2)}, u32[]{:S(2)}) %collective-permute-start.19) | collective-permute-done | bytes 1179680 | tf_op jit(solution)/shard_map/ppermute | solution.py:58
  452.6 8.8 %attend_back.1 = (bf16[384,768]{1,0:T(8,128)(2,1)}, bf16[6144,256]{1,0:T(8,128)(2,1)}) custom-call(s32[2]{0:T(128)} %pad_add_fusion.bounds_ref, bf16[384,768]{1,0:T(8,128)(2,1)} %get-tuple-element.65.rotated_ref, f32[384,768]{1,0:T(8,128)} %fusion.20.grad_ref, f32[384,768]{1,0:T(8,128)} %get-tuple-element.54.attended_ref, ...), custom_call_target="tpu_custom_call" | custom-call | flops 294912 | bytes 294912 | tf_op jit(solution)/shard_map/attend_back/pallas_call | solution.py:314
  477.1 6.9 collective-permute-start.22
  493.7 8.4 %collective-permute-done.22 = bf16[4,1,1,384,256]{4,3,2,1,0:T(8,128)(2,1)} collective-permute-done((bf16[4,1,1,384,256]{4,3,2,1,0:T(8,128)(2,1)}, bf16[4,1,1,384,256]{4,3,2,1,0:T(8,128)(2,1)}, u32[]{:S(2)}, u32[]{:S(2)}) %collective-permute-start.22) | collective-permute-done | bytes 786464 | tf_op jit(solution)/shard_map/ppermute | solution.py:58
  505.3 11.3 %collective-permute-start.26 = (bf16[2,1,384,256]{3,2,1,0:T(8,128)(2,1)}, bf16[2,1,384,256]{3,2,1,0:T(8,128)(2,1)}, u32[]{:S(2)}, u32[]{:S(2)}) collective-permute-start(bf16[2,1,384,256]{3,2,1,0:T(8,128)(2,1)} %constant_dynamic-slice_fusion.5), channel_id=1, source_target_pairs={{0,8},{8,0},{16,24},{24,16},{1,9},{9,1},{17,25},{25,17},{2,10},{10... | collective-permute-start | bytes 1179656 | tf_op jit(solution)/shard_map/ppermute | solution.py:153
  527.9 13.7 %collective-permute-done.26 = bf16[2,1,384,256]{3,2,1,0:T(8,128)(2,1)} collective-permute-done((bf16[2,1,384,256]{3,2,1,0:T(8,128)(2,1)}, bf16[2,1,384,256]{3,2,1,0:T(8,128)(2,1)}, u32[]{:S(2)}, u32[]{:S(2)}) %collective-permute-start.26) | collective-permute-done | bytes 393248 | tf_op jit(solution)/shard_map/ppermute | solution.py:153
  546.5 8.3 %collective-permute-done.27 = bf16[1,1,384,256]{3,2,1,0:T(8,128)(2,1)} collective-permute-done((bf16[1,1,384,256]{3,2,1,0:T(8,128)(2,1)}, bf16[1,1,384,256]{3,2,1,0:T(8,128)(2,1)}, u32[]{:S(2)}, u32[]{:S(2)}) %collective-permute-start.27) | collective-permute-done | bytes 196640 | tf_op jit(solution)/shard_map/ppermute | solution.py:153
  554.8 5.5 collective-permute-done.23
  597.1 32.0 %collective-permute-done.32 = bf16[4,1,1,96,384]{4,3,2,1,0:T(8,128)(2,1)S(1)} collective-permute-done((bf16[4,1,1,96,384]{4,3,2,1,0:T(8,128)(2,1)S(1)}, bf16[4,1,1,96,384]{4,3,2,1,0:T(8,128)(2,1)S(1)}, u32[]{:S(2)}, u32[]{:S(2)}) %collective-permute-start.32) | collective-permute-done | bytes 294944 | tf_op jit(solution)/shard_map/ppermute | solution.py:58
  657.2 10.0 %all-to-all-done.5 = bf16[4,96,1120]{2,1,0:T(8,128)(2,1)} async-done(((bf16[4,96,1120]{2,1,0:T(8,128)(2,1)}), bf16[4,96,1120]{2,1,0:T(8,128)(2,1)}, u32[]{:S(2)}, u32[]{:S(2)}) %all-to-all-start.5) | async-done | bytes 860192 | tf_op jit(solution)/shard_map/all_to_all | solution.py:114
  (359 shorter events, 219.9 us)
Async XLA Ops:
  7.2 75.0 %all-gather.5.cloned.1.call-start = ((), (), s32[]{:S(2)}) async-start(), calls=%async_computation.10 | async-start | bytes 1474560 | tf_op jit(solution)/shard_map/all_gather | solution.py:104
  9.0 266.3 %all-gather.11.cloned.1.call-start = ((), (), s32[]{:S(2)}) async-start(), calls=%async_computation.13 | async-start | bytes 4423680 | tf_op jit(solution)/shard_map/all_gather | solution.py:104
  61.8 228.8 %all-gather.9.cloned.1.call-start = ((), (), s32[]{:S(2)}) async-start(), calls=%async_computation.12 | async-start | bytes 4423680 | tf_op jit(solution)/shard_map/all_gather | solution.py:104
  132.9 169.1 %all-gather.7.cloned.1.call-start = ((), (), s32[]{:S(2)}) async-start(), calls=%async_computation.11 | async-start | bytes 4423680 | tf_op jit(solution)/shard_map/all_gather | solution.py:104
  133.0 45.0 %collective-permute-start.4 = (bf16[4,1,1,96,1536]{4,3,2,1,0:T(8,128)(2,1)}, bf16[4,1,1,96,1536]{4,3,2,1,0:T(8,128)(2,1)}, u32[]{:S(2)}, u32[]{:S(2)}) collective-permute-start(bf16[4,1,1,96,1536]{4,3,2,1,0:T(8,128)(2,1)} %bitcast.146), channel_id=1, source_target_pairs={{0,4},{4,0},{1,5},{5,1},{2,6},{6,2},{3,7},{7,3},{8,12},{12,8},{9,1... | collective-permute-start | bytes 3538952 | tf_op jit(solution)/shard_map/ppermute | solution.py:58
  135.4 42.5 %collective-permute-start.7 = (bf16[4,1,1,384,256]{4,3,2,1,0:T(8,128)(2,1)}, bf16[4,1,1,384,256]{4,3,2,1,0:T(8,128)(2,1)}, u32[]{:S(2)}, u32[]{:S(2)}) collective-permute-start(bf16[4,1,1,384,256]{4,3,2,1,0:T(8,128)(2,1)} %bitcast.141), channel_id=1, source_target_pairs={{0,4},{4,0},{1,5},{5,1},{2,6},{6,2},{3,7},{7,3},{8,12},{12,8},{9,1... | collective-permute-start | bytes 2359304 | tf_op jit(solution)/shard_map/ppermute | solution.py:58
  137.9 44.7 %collective-permute-start.3 = (bf16[4,1,1,96,1536]{4,3,2,1,0:T(8,128)(2,1)}, bf16[4,1,1,96,1536]{4,3,2,1,0:T(8,128)(2,1)}, u32[]{:S(2)}, u32[]{:S(2)}) collective-permute-start(bf16[4,1,1,96,1536]{4,3,2,1,0:T(8,128)(2,1)} %bitcast.147), channel_id=1, source_target_pairs={{0,2},{2,0},{1,3},{3,1},{4,6},{6,4},{5,7},{7,5},{8,10},{10,8},{9,1... | collective-permute-start | bytes 3538952 | tf_op jit(solution)/shard_map/ppermute | solution.py:58
  138.0 42.2 %collective-permute-start.6 = (bf16[4,1,1,384,256]{4,3,2,1,0:T(8,128)(2,1)}, bf16[4,1,1,384,256]{4,3,2,1,0:T(8,128)(2,1)}, u32[]{:S(2)}, u32[]{:S(2)}) collective-permute-start(bf16[4,1,1,384,256]{4,3,2,1,0:T(8,128)(2,1)} %bitcast.142), channel_id=1, source_target_pairs={{0,2},{2,0},{1,3},{3,1},{4,6},{6,4},{5,7},{7,5},{8,10},{10,8},{9,1... | collective-permute-start | bytes 2359304 | tf_op jit(solution)/shard_map/ppermute | solution.py:58
  142.6 41.6 %collective-permute-start.9 = (bf16[1536,256]{1,0:T(8,128)(2,1)}, bf16[1536,256]{1,0:T(8,128)(2,1)S(1)}, u32[]{:S(2)}, u32[]{:S(2)}) collective-permute-start(bf16[1536,256]{1,0:T(8,128)(2,1)} %slice.228), channel_id=1, source_target_pairs={{0,1},{1,0},{2,3},{3,2},{4,5},{5,4},{6,7},{7,6},{8,9},{9,8},{10,11... | collective-permute-start | bytes 2359304 | tf_op jit(solution)/shard_map/ppermute | solution.py:58
  184.2 27.9 %collective-permute-start.12 = (bf16[384,1536]{1,0:T(8,128)(2,1)S(1)}, bf16[384,1536]{1,0:T(8,128)(2,1)S(1)}, u32[]{:S(2)}, u32[]{:S(2)}) collective-permute-start(bf16[384,1536]{1,0:T(8,128)(2,1)S(1)} %copy-done.10), channel_id=1, source_target_pairs={{0,4},{4,0},{1,5},{5,1},{2,6},{6,2},{3,7},{7,3},{8,12},{12,8},{9,1... | collective-permute-start | bytes 3538952 | tf_op jit(solution)/shard_map/ppermute | solution.py:58
  187.0 31.2 %collective-permute-start.11 = (bf16[384,1536]{1,0:T(8,128)(2,1)S(1)}, bf16[384,1536]{1,0:T(8,128)(2,1)}, u32[]{:S(2)}, u32[]{:S(2)}) collective-permute-start(bf16[384,1536]{1,0:T(8,128)(2,1)S(1)} %copy-done.10), channel_id=1, source_target_pairs={{0,2},{2,0},{1,3},{3,1},{4,6},{6,4},{5,7},{7,5},{8,10},{10,8},{9,1... | collective-permute-start | bytes 3538952 | tf_op jit(solution)/shard_map/ppermute | solution.py:58
  216.3 28.7 %collective-permute-start.10 = (bf16[384,1536]{1,0:T(8,128)(2,1)}, bf16[384,1536]{1,0:T(8,128)(2,1)}, u32[]{:S(2)}, u32[]{:S(2)}) collective-permute-start(bf16[384,1536]{1,0:T(8,128)(2,1)} %convolution_convert_fusion.6), channel_id=1, source_target_pairs={{0,1},{1,0},{2,3},{3,2},{4,5},{5,4},{6,7},{7,6},{8,9},{9,8},{10,11... | collective-permute-start | bytes 3538952 | tf_op jit(solution)/shard_map/ppermute | solution.py:58
  218.0 179.2 %reduce-scatter.5.cloned.1.call-start = ((), (), s32[]{:S(2)}) async-start(), calls=%async_computation.14 | async-start | bytes 4423680 | tf_op jit(solution)/shard_map/reduce_scatter | solution.py:108
  247.5 27.7 %collective-permute-start.15 = (bf16[384,1536]{1,0:T(8,128)(2,1)S(1)}, bf16[384,1536]{1,0:T(8,128)(2,1)}, u32[]{:S(2)}, u32[]{:S(2)}) collective-permute-start(bf16[384,1536]{1,0:T(8,128)(2,1)S(1)} %multiply_convert_fusion.3), channel_id=1, source_target_pairs={{0,4},{4,0},{1,5},{5,1},{2,6},{6,2},{3,7},{7,3},{8,12},{12,8},{9,1... | collective-permute-start | bytes 3538952 | tf_op jit(solution)/shard_map/ppermute | solution.py:58
  248.0 37.7 %collective-permute-start.14 = (bf16[384,1536]{1,0:T(8,128)(2,1)S(1)}, bf16[384,1536]{1,0:T(8,128)(2,1)}, u32[]{:S(2)}, u32[]{:S(2)}) collective-permute-start(bf16[384,1536]{1,0:T(8,128)(2,1)S(1)} %multiply_convert_fusion.3), channel_id=1, source_target_pairs={{0,2},{2,0},{1,3},{3,1},{4,6},{6,4},{5,7},{7,5},{8,10},{10,8},{9,1... | collective-permute-start | bytes 3538952 | tf_op jit(solution)/shard_map/ppermute | solution.py:58
  329.2 164.5 %reduce-scatter.7.cloned.1.call-start = ((), (), s32[]{:S(2)}) async-start(), calls=%async_computation.15 | async-start | bytes 4423680 | tf_op jit(solution)/shard_map/reduce_scatter | solution.py:108
  368.9 39.6 %collective-permute-start.18 = (bf16[384,1536]{1,0:T(8,128)(2,1)S(1)}, bf16[384,1536]{1,0:T(8,128)(2,1)}, u32[]{:S(2)}, u32[]{:S(2)}) collective-permute-start(bf16[384,1536]{1,0:T(8,128)(2,1)S(1)} %fusion.18), channel_id=1, source_target_pairs={{0,4},{4,0},{1,5},{5,1},{2,6},{6,2},{3,7},{7,3},{8,12},{12,8},{9,1... | collective-permute-start | bytes 3538952 | tf_op jit(solution)/shard_map/ppermute | solution.py:58
  411.8 27.5 %collective-permute-start.19 = (bf16[384,1536]{1,0:T(8,128)(2,1)S(1)}, bf16[384,1536]{1,0:T(8,128)(2,1)}, u32[]{:S(2)}, u32[]{:S(2)}) collective-permute-start(bf16[384,1536]{1,0:T(8,128)(2,1)S(1)} %fusion.17), channel_id=1, source_target_pairs={{0,1},{1,0},{2,3},{3,2},{4,5},{5,4},{6,7},{7,6},{8,9},{9,8},{10,11... | collective-permute-start | bytes 3538952 | tf_op jit(solution)/shard_map/ppermute | solution.py:58
  413.3 17.0 %all-to-all-start.3 = ((bf16[4,96,1120]{2,1,0:T(8,128)(2,1)}), bf16[4,96,1120]{2,1,0:T(8,128)(2,1)}, u32[]{:S(2)}, u32[]{:S(2)}) async-start(bf16[4,96,1120]{2,1,0:T(8,128)(2,1)} %bitcast.154), calls=%async_computation.4 | async-start | bytes 1769472 | tf_op jit(solution)/shard_map/all_to_all | solution.py:114
  417.6 144.6 %reduce-scatter.9.cloned.1.call-start = ((), (), s32[]{:S(2)}) async-start(), calls=%async_computation.16 | async-start | bytes 4423680 | tf_op jit(solution)/shard_map/reduce_scatter | solution.py:108
  445.3 40.8 %collective-permute-start.20 = (bf16[768,1536]{1,0:T(8,128)(2,1)}, bf16[768,1536]{1,0:T(8,128)(2,1)}, u32[]{:S(2)}, u32[]{:S(2)}) collective-permute-start(bf16[768,1536]{1,0:T(8,128)(2,1)} %pad_maximum_fusion.3), channel_id=1, source_target_pairs={{0,2},{2,0},{1,3},{3,1},{4,6},{6,4},{5,7},{7,5},{8,10},{10,8},{9,1... | collective-permute-start | bytes 7077896 | tf_op jit(solution)/shard_map/ppermute | solution.py:58
  477.1 25.0 %collective-permute-start.22 = (bf16[4,1,1,384,256]{4,3,2,1,0:T(8,128)(2,1)}, bf16[4,1,1,384,256]{4,3,2,1,0:T(8,128)(2,1)}, u32[]{:S(2)}, u32[]{:S(2)}) collective-permute-start(bf16[4,1,1,384,256]{4,3,2,1,0:T(8,128)(2,1)} %constant_dynamic-slice_fusion.6), channel_id=1, source_target_pairs={{0,4},{4,0},{1,5},{5,1},{2,6},{6,2},{3,7},{7,3},{8,12},{12,8},{9,1... | collective-permute-start | bytes 2359304 | tf_op jit(solution)/shard_map/ppermute | solution.py:58
  505.3 36.3 %collective-permute-start.26 = (bf16[2,1,384,256]{3,2,1,0:T(8,128)(2,1)}, bf16[2,1,384,256]{3,2,1,0:T(8,128)(2,1)}, u32[]{:S(2)}, u32[]{:S(2)}) collective-permute-start(bf16[2,1,384,256]{3,2,1,0:T(8,128)(2,1)} %constant_dynamic-slice_fusion.5), channel_id=1, source_target_pairs={{0,8},{8,0},{16,24},{24,16},{1,9},{9,1},{17,25},{25,17},{2,10},{10... | collective-permute-start | bytes 1179656 | tf_op jit(solution)/shard_map/ppermute | solution.py:153
  516.6 29.9 %collective-permute-start.25 = (bf16[384,1536]{1,0:T(8,128)(2,1)}, bf16[384,1536]{1,0:T(8,128)(2,1)}, u32[]{:S(2)}, u32[]{:S(2)}) collective-permute-start(bf16[384,1536]{1,0:T(8,128)(2,1)} %convolution_convert_fusion.5), channel_id=1, source_target_pairs={{0,1},{1,0},{2,3},{3,2},{4,5},{5,4},{6,7},{7,6},{8,9},{9,8},{10,11... | collective-permute-start | bytes 3538952 | tf_op jit(solution)/shard_map/ppermute | solution.py:58
  518.1 36.7 %all-to-all-start.4 = ((bf16[4,96,1120]{2,1,0:T(8,128)(2,1)}), bf16[4,96,1120]{2,1,0:T(8,128)(2,1)}, u32[]{:S(2)}, u32[]{:S(2)}) async-start(bf16[4,96,1120]{2,1,0:T(8,128)(2,1)} %bitcast.153), calls=%async_computation.6 | async-start | bytes 1769472 | tf_op jit(solution)/shard_map/all_to_all | solution.py:114
  522.3 151.6 %reduce-scatter.11.cloned.1.call-start = ((), (), s32[]{:S(2)}) async-start(), calls=%async_computation.17 | async-start | bytes 1843200 | tf_op jit(solution)/shard_map/reduce_scatter | solution.py:108
  522.6 37.8 %collective-permute-start.23 = (bf16[384,1536]{1,0:T(8,128)(2,1)}, bf16[384,1536]{1,0:T(8,128)(2,1)}, u32[]{:S(2)}, u32[]{:S(2)}) collective-permute-start(bf16[384,1536]{1,0:T(8,128)(2,1)} %fusion.13), channel_id=1, source_target_pairs={{0,4},{4,0},{1,5},{5,1},{2,6},{6,2},{3,7},{7,3},{8,12},{12,8},{9,1... | collective-permute-start | bytes 3538952 | tf_op jit(solution)/shard_map/ppermute | solution.py:58
  527.9 49.8 %collective-permute-start.28 = (bf16[4,2,1,96,1536]{4,3,2,1,0:T(8,128)(2,1)}, bf16[4,2,1,96,1536]{4,3,2,1,0:T(8,128)(2,1)}, u32[]{:S(2)}, u32[]{:S(2)}) collective-permute-start(bf16[4,2,1,96,1536]{4,3,2,1,0:T(8,128)(2,1)} %constant_dynamic-slice_fusion.3), channel_id=1, source_target_pairs={{0,2},{2,0},{1,3},{3,1},{4,6},{6,4},{5,7},{7,5},{8,10},{10,8},{9,1... | collective-permute-start | bytes 7077896 | tf_op jit(solution)/shard_map/ppermute | solution.py:58
  594.1 35.0 %collective-permute-start.24 = (bf16[384,1536]{1,0:T(8,128)(2,1)S(1)}, bf16[384,1536]{1,0:T(8,128)(2,1)S(1)}, u32[]{:S(2)}, u32[]{:S(2)}) collective-permute-start(bf16[384,1536]{1,0:T(8,128)(2,1)S(1)} %fusion.15), channel_id=1, source_target_pairs={{0,1},{1,0},{2,3},{3,2},{4,5},{5,4},{6,7},{7,6},{8,9},{9,8},{10,11... | collective-permute-start | bytes 3538952 | tf_op jit(solution)/shard_map/ppermute | solution.py:58
  594.7 35.4 %collective-permute-start.30 = (bf16[4,1,1,96,1536]{4,3,2,1,0:T(8,128)(2,1)S(1)}, bf16[4,1,1,96,1536]{4,3,2,1,0:T(8,128)(2,1)S(1)}, u32[]{:S(2)}, u32[]{:S(2)}) collective-permute-start(bf16[4,1,1,96,1536]{4,3,2,1,0:T(8,128)(2,1)S(1)} %copy-done.31), channel_id=1, source_target_pairs={{0,4},{4,0},{1,5},{5,1},{2,6},{6,2},{3,7},{7,3},{8,12},{12,8},{9,1... | collective-permute-start | bytes 3538952 | tf_op jit(solution)/shard_map/ppermute | solution.py:58
  595.7 33.3 %collective-permute-start.32 = (bf16[4,1,1,96,384]{4,3,2,1,0:T(8,128)(2,1)S(1)}, bf16[4,1,1,96,384]{4,3,2,1,0:T(8,128)(2,1)S(1)}, u32[]{:S(2)}, u32[]{:S(2)}) collective-permute-start(bf16[4,1,1,96,384]{4,3,2,1,0:T(8,128)(2,1)S(1)} %constant_dynamic-slice_fusion), channel_id=1, source_target_pairs={{0,4},{4,0},{1,5},{5,1},{2,6},{6,2},{3,7},{7,3},{8,12},{12,8},{9,1... | collective-permute-start | bytes 884744 | tf_op jit(solution)/shard_map/ppermute | solution.py:58
  650.1 17.1 %all-to-all-start.5 = ((bf16[4,96,1120]{2,1,0:T(8,128)(2,1)}), bf16[4,96,1120]{2,1,0:T(8,128)(2,1)}, u32[]{:S(2)}, u32[]{:S(2)}) async-start(bf16[4,96,1120]{2,1,0:T(8,128)(2,1)} %bitcast.152), calls=%async_computation.9 | async-start | bytes 1769472 | tf_op jit(solution)/shard_map/all_to_all | solution.py:114
  (76 other events, 746.2 us)
Sparse Core Ops, SparseCore 0:
  10.1 35.1 all-gather.4
  61.9 82.8 all-gather.10
  146.4 68.5 all-gather.8
  218.1 70.0 all-gather.6
  329.3 67.8 reduce-scatter.4
  399.3 66.6 reduce-scatter.6
  468.4 75.0 reduce-scatter.8
  631.9 37.3 reduce-scatter.10

commit v10 on v9

--- a/solution.py
+++ b/solution.py
@@ -383,7 +383,7 @@
     square_column = gather_z(square_pack)
     pair_pack = jnp.concatenate([key_projection, value_projection, small], axis=1)
     pair_column = gather_z(after(pair_pack, square_pack))
-    gate_own = deal(after(w_gate, pair_column))
+    down_own = deal(after(w_down, pair_column).T)
     w_pair = gather_rest(pair_column, features)
     pair_weights_came = other(w_pair[:, : 2 * head], "y")
     small_all = w_pair[:, 2 * head :].reshape(devices, features, head)[:, :small_rows]
@@ -409,15 +409,15 @@
     )
     value_rows = low(projections[:, head:] + bias_value)
     key_value = jnp.concatenate([key_rows, value_rows], axis=1)
-    gate_all = gather_z(gate_own)
-    key_value_column = gather_z(after(key_value, gate_own, square_column))
-    down_own = deal(after(w_down, key_value).T)
+    down_all = gather_z(down_own)
+    key_value_column = gather_z(after(key_value, down_own, square_column))
+    gate_own = deal(after(w_gate, key_value))
     w_square = gather_rest(square_column, features)
     w_query_all = w_square[:, :heads_width]
     w_out_all = w_square[:, heads_width:]
     query_pre = product(normed_one, w_query_all) + bias_query
-    key_value_column = after(key_value_column, down_own)
-    down_all = gather_z(down_own)
+    key_value_column = after(key_value_column, gate_own)
+    gate_all = gather_z(gate_own)
     up_own = deal(after(w_up, key_value_column))
     up_all = gather_z(up_own)
     key_value = after(gather_rest(key_value_column, rows), up_own, pair_weights_came)
@@ -485,6 +485,7 @@
     gate_parts = undeal(after(gate_sums, key_value_sums))
     square_halves = scatter_core(after(square_grads, key_value_sums), features)
     key_value_grads = halve_z(key_value_sums, rows, (key_value_sums,), (query_came, gate_parts, down_came))
+    square_sums = scatter_across(square_halves)
     key_value_grads = after(key_value_grads, up_sums)
     grad_key_pre = low(
         rotate_halves(key_value_grads[:, :head].reshape(rows, 1, head), cosine_table, -sine_table)
@@ -529,8 +530,7 @@
     packed_halves = other_half(
         packed_grads.reshape(-1, 2, 2, features, packed_grads.shape[1]), "c", 2
     )
-    square_sums = scatter_across(square_halves, packed_halves[1], down_pair)
-    packed_grads = scatter_across(other_half(add_half(packed_halves), "x", 1))
+    packed_grads = scatter_across(other_half(add_half(packed_halves, square_sums), "x", 1))
     up_parts = undeal(after(up_sums, packed_halves[1]))
     last_grads = scatter_z(jnp.concatenate([square_sums, packed_grads], axis=1)).astype(jnp.float32)
     square_grads = last_grads[:, : 2 * heads_width]

time: 699 us -> 670 us (0.959)
  blocking collectives: 95.8 us -> 80.3 us
  local copies, waits for them, and re-layouts: 80.8 us -> 73.5 us
    all_to_all x3 -> x2, blocking collectives: 47.4 us -> 31.7 us  [deal(): lax.all_to_all(parts, GROUP, split_axis=0, concat_axis=0, tiled=True)]
    unnamed x133 -> x121, local copies, waits for them, and re-layouts: 14.4 us -> 15.8 us
  transfers between devices with their start and end apart: 44 -> 45, of which waited for: 17 -> 20; matrix products, arithmetic and copies ran while one was open for 32% -> 32% of each run, Pallas kernels for 2% -> 2%
where the time goes in v10:
time: 670 us; the launch traced here: 657 us
  waiting for transfers between devices  220 us (33%)
  matrix products  122 us (18%)
  blocking collectives  80.3 us (12%)
  other arithmetic  74.2 us (11%)
  local copies, waits for them, and re-layouts  73.5 us (11%)
  starting transfers between devices  54.8 us (8%)
  between operations  17.7 us (3%)
  Pallas kernels  15.3 us (2%)
    ppermute x31, waiting for transfers between devices, other(): return lax.ppermute(value, axis, [(0, 1), (1, 0)])  156 us
    dot_general x9, matrix products, product(): return jnp.dot(left, right, preferred_element_type=jnp.float32)  73.6 us
    all_gather x2, blocking collectives, gather_z(): return lax.all_gather(own, 'z', axis=0, tiled=True)  48.5 us
    dot_general x6, matrix products, product_right(): lax.dot_general(left, right, (((1,), (1,)), ((), ())), preferred_element_...  43 us
    all_to_all x2, blocking collectives, deal(): lax.all_to_all(parts, GROUP, split_axis=0, concat_axis=0, tiled=True)  31.7 us
    ppermute x31, starting transfers between devices, other(): return lax.ppermute(value, axis, [(0, 1), (1, 0)])  29.4 us
    convert_element_type x15, other arithmetic, low(): return value.astype(jnp.bfloat16)  28.8 us
    ppermute x2, waiting for transfers between devices, halve_z(): lax.ppermute(sent, 'z', [(number, number ^ step) for number in range(high)])  24.9 us
  transfers between devices with their start and end apart: 45, of which 20 were waited for; matrix products, arithmetic and copies ran while one was open for 32% of the time, Pallas kernels for 2%

profile of v10, /device:TPU:0, one launch (start us, length us, event | category | flops | bytes accessed | tf_op | source)
XLA Modules:
  0.0 657.5 jit_solution(11682750465688889161)
XLA Ops:
  13.3 17.9 %all_gather.18 = bf16[384,384]{1,0:T(8,128)(2,1)S(1)} all-gather(bf16[96,384]{1,0:T(8,128)(2,1)S(1)} %pad_maximum_fusion.10), channel_id=1, replica_groups=mesh['z'=4,'x'=2,'c'=2,'y'=2] {'z'}, dimensions={0}, use_global_device_ids=true | all-gather | bytes 368640 | tf_op jit(solution)/shard_map/all_gather | solution.py:104
  33.9 15.9 %all_to_all.30 = bf16[4,96,1120]{2,1,0:T(8,128)(2,1)} all-to-all(bf16[4,96,1120]{2,1,0:T(8,128)(2,1)S(1)} %bitcast.130), channel_id=1, replica_groups=mesh['z'=4,'x'=2,'c'=2,'y'=2] {'x','c'}, dimensions={0} | all-to-all | bytes 1720320 | tf_op jit(solution)/shard_map/all_to_all | solution.py:99
  52.4 6.1 collective-permute-done.1
  68.1 30.6 %all_gather.20 = bf16[1536,256]{1,0:T(8,128)(2,1)} all-gather(bf16[384,256]{1,0:T(8,128)(2,1)S(1)} %pad_maximum_fusion.8), channel_id=1, replica_groups=mesh['z'=4,'x'=2,'c'=2,'y'=2] {'z'}, dimensions={0}, use_global_device_ids=true | all-gather | bytes 983040 | tf_op jit(solution)/shard_map/all_gather | solution.py:104
  101.7 15.8 %all_to_all.31 = bf16[4,96,1120]{2,1,0:T(8,128)(2,1)} all-to-all(bf16[4,96,1120]{2,1,0:T(8,128)(2,1)S(1)} %bitcast.131), channel_id=1, replica_groups=mesh['z'=4,'x'=2,'c'=2,'y'=2] {'x','c'}, dimensions={0} | all-to-all | bytes 1720320 | tf_op jit(solution)/shard_map/all_to_all | solution.py:99
  128.2 34.3 %collective-permute-done.7 = bf16[4,1,1,384,256]{4,3,2,1,0:T(8,128)(2,1)} collective-permute-done((bf16[4,1,1,384,256]{4,3,2,1,0:T(8,128)(2,1)}, bf16[4,1,1,384,256]{4,3,2,1,0:T(8,128)(2,1)}, u32[]{:S(2)}, u32[]{:S(2)}) %collective-permute-start.7) | collective-permute-done | bytes 786464 | tf_op jit(solution)/shard_map/ppermute | solution.py:58
  176.3 6.5 attend.1
  182.9 15.8 %collective-permute-done.12 = bf16[384,1536]{1,0:T(8,128)(2,1)} collective-permute-done((bf16[384,1536]{1,0:T(8,128)(2,1)}, bf16[384,1536]{1,0:T(8,128)(2,1)}, u32[]{:S(2)}, u32[]{:S(2)}) %collective-permute-start.12) | collective-permute-done | bytes 1179680 | tf_op jit(solution)/shard_map/ppermute | solution.py:58
  210.0 20.4 %collective-permute-done.10 = bf16[384,1536]{1,0:T(8,128)(2,1)} collective-permute-done((bf16[384,1536]{1,0:T(8,128)(2,1)S(1)}, bf16[384,1536]{1,0:T(8,128)(2,1)}, u32[]{:S(2)}, u32[]{:S(2)}) %collective-permute-start.10) | collective-permute-done | bytes 1179680 | tf_op jit(solution)/shard_map/ppermute | solution.py:58
  233.0 27.2 %collective-permute-done.15 = bf16[384,1536]{1,0:T(8,128)(2,1)} collective-permute-done((bf16[384,1536]{1,0:T(8,128)(2,1)S(1)}, bf16[384,1536]{1,0:T(8,128)(2,1)}, u32[]{:S(2)}, u32[]{:S(2)}) %collective-permute-start.15) | collective-permute-done | bytes 1179680 | tf_op jit(solution)/shard_map/ppermute | solution.py:58
  260.2 10.3 %fusion.86 = f32[1536,1120]{0,1:T(8,128)} fusion(bf16[1536,1536]{1,0:T(8,128)(2,1)} %copy-done.35, bf16[1536,1120]{1,0:T(8,128)(2,1)} %all-gather.11.cloned.1.call-done), kind=kOutput, calls=%fused_computation.193 | convolution fusion | flops 5284823040 | bytes 15040512 | tf_op jit(solution)/shard_map/dot_general | solution.py:17
  270.6 4.9 fusion.75
  275.4 11.4 %fusion.74 = f32[1536,1120]{0,1:T(8,128)} fusion(bf16[1536,1120]{1,0:T(8,128)(2,1)} %all-gather.9.cloned.1.call-done, bf16[384,1536]{1,0:T(8,128)(2,1)} %collective-permute-done.16, bf16[384,1536]{1,0:T(8,128)(2,1)} %collective-permute-done.15, bf16[384,1536]{1,0:T(8,128)(2,1)} %collective-permute-done.14, bf16[384,1536]{1,0:T(8,128)(2,1)S(1)} %multiply_convert_fusion.3), kind=kOutput, calls=%fused_computation.181 | convolution fusion | flops 5303697408 | bytes 15040512 | tf_op jit(solution)/shard_map/dot_general | solution.py:17
  286.9 16.8 %multiply_convert_fusion = (bf16[1536,1120]{0,1:T(8,128)(2,1)}, bf16[1536,1120]{0,1:T(8,128)(2,1)}, bf16[1536,1120]{0,1:T(8,128)(2,1)}) fusion(f32[1536,1120]{0,1:T(8,128)} %fusion.86, f32[1536,1120]{0,1:T(8,128)} %fusion.74, bf16[1536,1120]{1,0:T(8,128)(2,1)} %all-gather.7.cloned.1.call-done, bf16[384,1536]{1,0:T(8,128)(2,1)} %collective-permute-done.16, ...), kind=kOutput, calls=%fused_computation.4 | convolution fusion | flops 5329502208 | bytes 32243712 | tf_op jit(solution)/shard_map/dot_general | solution.py:17
  303.7 10.4 %convolution_convert_fusion = bf16[1536,1120]{1,0:T(8,128)(2,1)} fusion(bf16[1536,1536]{0,1:T(8,128)(2,1)} %bitcast.150, bf16[1536,1120]{0,1:T(8,128)(2,1)} %get-tuple-element.60), kind=kOutput, calls=%fused_computation.1 | convolution fusion | flops 5286543360 | bytes 11599872 | tf_op jit(solution)/shard_map/dot_general | solution.py:17
  314.2 11.5 %fusion.87 = f32[1536,1536]{1,0:T(8,128)} fusion(bf16[1536,1120]{0,1:T(8,128)(2,1)} %get-tuple-element.58, bf16[1536,1120]{1,0:T(8,128)(2,1)} %all-gather.7.cloned.1.call-done), kind=kOutput, calls=%fused_computation.194 | convolution fusion | flops 5284823040 | bytes 16318464 | tf_op jit(solution)/shard_map/dot_general | solution.py:27
  325.7 10.5 %fusion.85 = (bf16[1536,1536]{1,0:T(8,128)(2,1)S(1)}, f32[1536,1536]{1,0:T(8,128)S(1)}) fusion(f32[1536,1536]{1,0:T(8,128)} %fusion.87, bf16[1536,1120]{0,1:T(8,128)(2,1)} %get-tuple-element.59, bf16[1536,1120]{1,0:T(8,128)(2,1)} %all-gather.9.cloned.1.call-done), kind=kOutput, calls=%fused_computation.192 | convolution fusion | flops 5289541632 | bytes 30474240 | tf_op jit(solution)/shard_map/dot_general | solution.py:27
  346.1 7.7 %convolution_convert_fusion.2 = bf16[1536,1120]{1,0:T(8,128)(2,1)} fusion(bf16[1536,1536]{0,1:T(8,128)(2,1)S(1)} %bitcast.117, bf16[1536,1120]{0,1:T(8,128)(2,1)S(1)} %copy-done.51), kind=kOutput, calls=%fused_computation.3 | convolution fusion | flops 5286543360 | bytes 11599872 | tf_op jit(solution)/shard_map/dot_general | solution.py:17
  354.3 10.9 %convolution_convert_fusion.1 = bf16[1536,1120]{1,0:T(8,128)(2,1)} fusion(bf16[1536,1536]{0,1:T(8,128)(2,1)} %fusion.75, bf16[1536,1120]{0,1:T(8,128)(2,1)} %get-tuple-element.59), kind=kOutput, calls=%fused_computation.2 | convolution fusion | flops 5286543360 | bytes 11599872 | tf_op jit(solution)/shard_map/dot_general | solution.py:17
  365.2 16.9 %reduce-scatter.5.cloned.1.call-done = bf16[384,1120]{1,0:T(8,128)(2,1)} async-done(((bf16[1536,1120]{1,0:T(8,128)(2,1)}), bf16[384,1120]{1,0:T(8,128)(2,1)}) %reduce-scatter.5.cloned.1.call-update) | async-done | bytes 860176 | tf_op jit(solution)/shard_map/reduce_scatter | solution.py:108
  382.1 11.3 %fusion.88 = f32[1536,1536]{1,0:T(8,128)} fusion(bf16[1536,1120]{0,1:T(8,128)(2,1)} %get-tuple-element.60, bf16[1536,1120]{1,0:T(8,128)(2,1)} %all-gather.11.cloned.1.call-done), kind=kOutput, calls=%fused_computation.195 | convolution fusion | flops 5284823040 | bytes 16318464 | tf_op jit(solution)/shard_map/dot_general | solution.py:27
  403.2 12.0 %all-to-all-done.3 = bf16[4,96,1120]{2,1,0:T(8,128)(2,1)} async-done(((bf16[4,96,1120]{2,1,0:T(8,128)(2,1)}), bf16[4,96,1120]{2,1,0:T(8,128)(2,1)}, u32[]{:S(2)}, u32[]{:S(2)}) %all-to-all-start.3) | async-done | bytes 860192 | tf_op jit(solution)/shard_map/all_to_all | solution.py:114
  415.2 9.0 %collective-permute-done.19 = bf16[384,1536]{1,0:T(8,128)(2,1)} collective-permute-done((bf16[384,1536]{1,0:T(8,128)(2,1)S(1)}, bf16[384,1536]{1,0:T(8,128)(2,1)}, u32[]{:S(2)}, u32[]{:S(2)}) %collective-permute-start.19) | collective-permute-done | bytes 1179680 | tf_op jit(solution)/shard_map/ppermute | solution.py:58
  437.5 8.7 %attend_back.1 = (bf16[384,768]{1,0:T(8,128)(2,1)}, bf16[6144,256]{1,0:T(8,128)(2,1)}) custom-call(s32[2]{0:T(128)} %pad_add_fusion.bounds_ref, bf16[384,768]{1,0:T(8,128)(2,1)} %get-tuple-element.65.rotated_ref, f32[384,768]{1,0:T(8,128)} %fusion.20.grad_ref, f32[384,768]{1,0:T(8,128)} %get-tuple-element.54.attended_ref, ...), custom_call_target="tpu_custom_call" | custom-call | flops 294912 | bytes 294912 | tf_op jit(solution)/shard_map/attend_back/pallas_call | solution.py:314
  458.7 7.2 %collective-permute-start.22 = (bf16[4,1,1,384,256]{4,3,2,1,0:T(8,128)(2,1)}, bf16[4,1,1,384,256]{4,3,2,1,0:T(8,128)(2,1)}, u32[]{:S(2)}, u32[]{:S(2)}) collective-permute-start(bf16[4,1,1,384,256]{4,3,2,1,0:T(8,128)(2,1)} %constant_dynamic-slice_fusion.6), channel_id=1, source_target_pairs={{0,4},{4,0},{1,5},{5,1},{2,6},{6,2},{3,7},{7,3},{8,12},{12,8},{9,1... | collective-permute-start | bytes 2359304 | tf_op jit(solution)/shard_map/ppermute | solution.py:58
  475.6 8.5 %collective-permute-done.22 = bf16[4,1,1,384,256]{4,3,2,1,0:T(8,128)(2,1)} collective-permute-done((bf16[4,1,1,384,256]{4,3,2,1,0:T(8,128)(2,1)}, bf16[4,1,1,384,256]{4,3,2,1,0:T(8,128)(2,1)}, u32[]{:S(2)}, u32[]{:S(2)}) %collective-permute-start.22) | collective-permute-done | bytes 786464 | tf_op jit(solution)/shard_map/ppermute | solution.py:58
  491.4 9.1 %collective-permute-start.26 = (bf16[2,1,384,256]{3,2,1,0:T(8,128)(2,1)}, bf16[2,1,384,256]{3,2,1,0:T(8,128)(2,1)}, u32[]{:S(2)}, u32[]{:S(2)}) collective-permute-start(bf16[2,1,384,256]{3,2,1,0:T(8,128)(2,1)} %constant_dynamic-slice_fusion.5), channel_id=1, source_target_pairs={{0,8},{8,0},{16,24},{24,16},{1,9},{9,1},{17,25},{25,17},{2,10},{10... | collective-permute-start | bytes 1179656 | tf_op jit(solution)/shard_map/ppermute | solution.py:153
  508.3 18.3 %collective-permute-done.26 = bf16[2,1,384,256]{3,2,1,0:T(8,128)(2,1)} collective-permute-done((bf16[2,1,384,256]{3,2,1,0:T(8,128)(2,1)}, bf16[2,1,384,256]{3,2,1,0:T(8,128)(2,1)}, u32[]{:S(2)}, u32[]{:S(2)}) %collective-permute-start.26) | collective-permute-done | bytes 393248 | tf_op jit(solution)/shard_map/ppermute | solution.py:153
  532.6 6.6 %collective-permute-done.27 = bf16[1,1,384,256]{3,2,1,0:T(8,128)(2,1)} collective-permute-done((bf16[1,1,384,256]{3,2,1,0:T(8,128)(2,1)}, bf16[1,1,384,256]{3,2,1,0:T(8,128)(2,1)}, u32[]{:S(2)}, u32[]{:S(2)}) %collective-permute-start.27) | collective-permute-done | bytes 196640 | tf_op jit(solution)/shard_map/ppermute | solution.py:153
  561.6 13.3 %collective-permute-done.30 = bf16[4,1,1,96,1536]{4,3,2,1,0:T(8,128)(2,1)} collective-permute-done((bf16[4,1,1,96,1536]{4,3,2,1,0:T(8,128)(2,1)}, bf16[4,1,1,96,1536]{4,3,2,1,0:T(8,128)(2,1)}, u32[]{:S(2)}, u32[]{:S(2)}) %collective-permute-start.30) | collective-permute-done | bytes 1179680 | tf_op jit(solution)/shard_map/ppermute | solution.py:58
  611.0 10.1 %collective-permute-done.24 = bf16[384,1536]{1,0:T(8,128)(2,1)} collective-permute-done((bf16[384,1536]{1,0:T(8,128)(2,1)}, bf16[384,1536]{1,0:T(8,128)(2,1)}, u32[]{:S(2)}, u32[]{:S(2)}) %collective-permute-start.24) | collective-permute-done | bytes 1179680 | tf_op jit(solution)/shard_map/ppermute | solution.py:58
  632.0 8.5 %all-to-all-done.5 = bf16[4,96,1120]{2,1,0:T(8,128)(2,1)S(1)} async-done(((bf16[4,96,1120]{2,1,0:T(8,128)(2,1)}), bf16[4,96,1120]{2,1,0:T(8,128)(2,1)S(1)}, u32[]{:S(2)}, u32[]{:S(2)}) %all-to-all-start.5) | async-done | bytes 860192 | tf_op jit(solution)/shard_map/all_to_all | solution.py:114
  (348 shorter events, 215.2 us)
Async XLA Ops:
  7.2 60.9 %all-gather.5.cloned.1.call-start = ((), (), s32[]{:S(2)}) async-start(), calls=%async_computation.10 | async-start | bytes 1474560 | tf_op jit(solution)/shard_map/all_gather | solution.py:104
  9.0 251.2 %all-gather.11.cloned.1.call-start = ((), (), s32[]{:S(2)}) async-start(), calls=%async_computation.13 | async-start | bytes 4423680 | tf_op jit(solution)/shard_map/all_gather | solution.py:104
  64.5 34.2 %all-to-all-start.1 = ((bf16[4,96,1120]{2,1,0:T(8,128)(2,1)}), bf16[4,96,1120]{2,1,0:T(8,128)(2,1)S(1)}, u32[]{:S(2)}, u32[]{:S(2)}) async-start(bf16[4,96,1120]{2,1,0:T(8,128)(2,1)} %bitcast.105), calls=%async_computation.1 | async-start | bytes 1769472 | tf_op jit(solution)/shard_map/all_to_all | solution.py:99
  68.1 207.4 %all-gather.9.cloned.1.call-start = ((), (), s32[]{:S(2)}) async-start(), calls=%async_computation.12 | async-start | bytes 4423680 | tf_op jit(solution)/shard_map/all_gather | solution.py:104
  117.5 169.3 %all-gather.7.cloned.1.call-start = ((), (), s32[]{:S(2)}) async-start(), calls=%async_computation.11 | async-start | bytes 4423680 | tf_op jit(solution)/shard_map/all_gather | solution.py:104
  117.6 45.0 %collective-permute-start.4 = (bf16[4,1,1,96,1536]{4,3,2,1,0:T(8,128)(2,1)}, bf16[4,1,1,96,1536]{4,3,2,1,0:T(8,128)(2,1)}, u32[]{:S(2)}, u32[]{:S(2)}) collective-permute-start(bf16[4,1,1,96,1536]{4,3,2,1,0:T(8,128)(2,1)} %bitcast.11), channel_id=1, source_target_pairs={{0,4},{4,0},{1,5},{5,1},{2,6},{6,2},{3,7},{7,3},{8,12},{12,8},{9,1... | collective-permute-start | bytes 3538952 | tf_op jit(solution)/shard_map/ppermute | solution.py:58
  120.0 42.5 %collective-permute-start.7 = (bf16[4,1,1,384,256]{4,3,2,1,0:T(8,128)(2,1)}, bf16[4,1,1,384,256]{4,3,2,1,0:T(8,128)(2,1)}, u32[]{:S(2)}, u32[]{:S(2)}) collective-permute-start(bf16[4,1,1,384,256]{4,3,2,1,0:T(8,128)(2,1)} %bitcast.23), channel_id=1, source_target_pairs={{0,4},{4,0},{1,5},{5,1},{2,6},{6,2},{3,7},{7,3},{8,12},{12,8},{9,1... | collective-permute-start | bytes 2359304 | tf_op jit(solution)/shard_map/ppermute | solution.py:58
  122.5 46.4 %collective-permute-start.3 = (bf16[4,1,1,96,1536]{4,3,2,1,0:T(8,128)(2,1)}, bf16[4,1,1,96,1536]{4,3,2,1,0:T(8,128)(2,1)}, u32[]{:S(2)}, u32[]{:S(2)}) collective-permute-start(bf16[4,1,1,96,1536]{4,3,2,1,0:T(8,128)(2,1)} %bitcast.11), channel_id=1, source_target_pairs={{0,2},{2,0},{1,3},{3,1},{4,6},{6,4},{5,7},{7,5},{8,10},{10,8},{9,1... | collective-permute-start | bytes 3538952 | tf_op jit(solution)/shard_map/ppermute | solution.py:58
  122.6 43.9 %collective-permute-start.6 = (bf16[4,1,1,384,256]{4,3,2,1,0:T(8,128)(2,1)}, bf16[4,1,1,384,256]{4,3,2,1,0:T(8,128)(2,1)}, u32[]{:S(2)}, u32[]{:S(2)}) collective-permute-start(bf16[4,1,1,384,256]{4,3,2,1,0:T(8,128)(2,1)} %bitcast.23), channel_id=1, source_target_pairs={{0,2},{2,0},{1,3},{3,1},{4,6},{6,4},{5,7},{7,5},{8,10},{10,8},{9,1... | collective-permute-start | bytes 2359304 | tf_op jit(solution)/shard_map/ppermute | solution.py:58
  126.6 43.8 %collective-permute-start.9 = (bf16[1536,256]{1,0:T(8,128)(2,1)}, bf16[1536,256]{1,0:T(8,128)(2,1)S(1)}, u32[]{:S(2)}, u32[]{:S(2)}) collective-permute-start(bf16[1536,256]{1,0:T(8,128)(2,1)} %slice.228), channel_id=1, source_target_pairs={{0,1},{1,0},{2,3},{3,2},{4,5},{5,4},{6,7},{7,6},{8,9},{9,8},{10,11... | collective-permute-start | bytes 2359304 | tf_op jit(solution)/shard_map/ppermute | solution.py:58
  170.4 28.3 %collective-permute-start.12 = (bf16[384,1536]{1,0:T(8,128)(2,1)}, bf16[384,1536]{1,0:T(8,128)(2,1)}, u32[]{:S(2)}, u32[]{:S(2)}) collective-permute-start(bf16[384,1536]{1,0:T(8,128)(2,1)} %param.29), channel_id=1, source_target_pairs={{0,4},{4,0},{1,5},{5,1},{2,6},{6,2},{3,7},{7,3},{8,12},{12,8},{9,1... | collective-permute-start | bytes 3538952 | tf_op jit(solution)/shard_map/ppermute | solution.py:58
  173.5 31.4 %collective-permute-start.11 = (bf16[384,1536]{1,0:T(8,128)(2,1)}, bf16[384,1536]{1,0:T(8,128)(2,1)}, u32[]{:S(2)}, u32[]{:S(2)}) collective-permute-start(bf16[384,1536]{1,0:T(8,128)(2,1)} %param.29), channel_id=1, source_target_pairs={{0,2},{2,0},{1,3},{3,1},{4,6},{6,4},{5,7},{7,5},{8,10},{10,8},{9,1... | collective-permute-start | bytes 3538952 | tf_op jit(solution)/shard_map/ppermute | solution.py:58
  201.8 28.6 %collective-permute-start.10 = (bf16[384,1536]{1,0:T(8,128)(2,1)S(1)}, bf16[384,1536]{1,0:T(8,128)(2,1)}, u32[]{:S(2)}, u32[]{:S(2)}) collective-permute-start(bf16[384,1536]{1,0:T(8,128)(2,1)S(1)} %convolution_convert_fusion.6), channel_id=1, source_target_pairs={{0,1},{1,0},{2,3},{3,2},{4,5},{5,4},{6,7},{7,6},{8,9},{9,8},{10,11... | collective-permute-start | bytes 3538952 | tf_op jit(solution)/shard_map/ppermute | solution.py:58
  203.5 178.6 %reduce-scatter.5.cloned.1.call-start = ((), (), s32[]{:S(2)}) async-start(), calls=%async_computation.14 | async-start | bytes 4423680 | tf_op jit(solution)/shard_map/reduce_scatter | solution.py:108
  232.5 27.7 %collective-permute-start.15 = (bf16[384,1536]{1,0:T(8,128)(2,1)S(1)}, bf16[384,1536]{1,0:T(8,128)(2,1)}, u32[]{:S(2)}, u32[]{:S(2)}) collective-permute-start(bf16[384,1536]{1,0:T(8,128)(2,1)S(1)} %multiply_convert_fusion.3), channel_id=1, source_target_pairs={{0,4},{4,0},{1,5},{5,1},{2,6},{6,2},{3,7},{7,3},{8,12},{12,8},{9,1... | collective-permute-start | bytes 3538952 | tf_op jit(solution)/shard_map/ppermute | solution.py:58
  233.0 37.6 %collective-permute-start.14 = (bf16[384,1536]{1,0:T(8,128)(2,1)S(1)}, bf16[384,1536]{1,0:T(8,128)(2,1)}, u32[]{:S(2)}, u32[]{:S(2)}) collective-permute-start(bf16[384,1536]{1,0:T(8,128)(2,1)S(1)} %multiply_convert_fusion.3), channel_id=1, source_target_pairs={{0,2},{2,0},{1,3},{3,1},{4,6},{6,4},{5,7},{7,5},{8,10},{10,8},{9,1... | collective-permute-start | bytes 3538952 | tf_op jit(solution)/shard_map/ppermute | solution.py:58
  314.1 161.4 %reduce-scatter.7.cloned.1.call-start = ((), (), s32[]{:S(2)}) async-start(), calls=%async_computation.15 | async-start | bytes 4423680 | tf_op jit(solution)/shard_map/reduce_scatter | solution.py:108
  353.9 39.5 %collective-permute-start.18 = (bf16[384,1536]{1,0:T(8,128)(2,1)S(1)}, bf16[384,1536]{1,0:T(8,128)(2,1)}, u32[]{:S(2)}, u32[]{:S(2)}) collective-permute-start(bf16[384,1536]{1,0:T(8,128)(2,1)S(1)} %fusion.18), channel_id=1, source_target_pairs={{0,4},{4,0},{1,5},{5,1},{2,6},{6,2},{3,7},{7,3},{8,12},{12,8},{9,1... | collective-permute-start | bytes 3538952 | tf_op jit(solution)/shard_map/ppermute | solution.py:58
  396.7 27.5 %collective-permute-start.19 = (bf16[384,1536]{1,0:T(8,128)(2,1)S(1)}, bf16[384,1536]{1,0:T(8,128)(2,1)}, u32[]{:S(2)}, u32[]{:S(2)}) collective-permute-start(bf16[384,1536]{1,0:T(8,128)(2,1)S(1)} %fusion.17), channel_id=1, source_target_pairs={{0,1},{1,0},{2,3},{3,2},{4,5},{5,4},{6,7},{7,6},{8,9},{9,8},{10,11... | collective-permute-start | bytes 3538952 | tf_op jit(solution)/shard_map/ppermute | solution.py:58
  398.2 17.0 %all-to-all-start.3 = ((bf16[4,96,1120]{2,1,0:T(8,128)(2,1)}), bf16[4,96,1120]{2,1,0:T(8,128)(2,1)}, u32[]{:S(2)}, u32[]{:S(2)}) async-start(bf16[4,96,1120]{2,1,0:T(8,128)(2,1)} %bitcast.147), calls=%async_computation.4 | async-start | bytes 1769472 | tf_op jit(solution)/shard_map/all_to_all | solution.py:114
  402.4 139.0 %reduce-scatter.9.cloned.1.call-start = ((), (), s32[]{:S(2)}) async-start(), calls=%async_computation.16 | async-start | bytes 4423680 | tf_op jit(solution)/shard_map/reduce_scatter | solution.py:108
  432.3 35.6 %collective-permute-start.20 = (bf16[768,1536]{1,0:T(8,128)(2,1)}, bf16[768,1536]{1,0:T(8,128)(2,1)}, u32[]{:S(2)}, u32[]{:S(2)}) collective-permute-start(bf16[768,1536]{1,0:T(8,128)(2,1)} %pad_maximum_fusion.3), channel_id=1, source_target_pairs={{0,2},{2,0},{1,3},{3,1},{4,6},{6,4},{5,7},{7,5},{8,10},{10,8},{9,1... | collective-permute-start | bytes 7077896 | tf_op jit(solution)/shard_map/ppermute | solution.py:58
  458.7 25.3 %collective-permute-start.22 = (bf16[4,1,1,384,256]{4,3,2,1,0:T(8,128)(2,1)}, bf16[4,1,1,384,256]{4,3,2,1,0:T(8,128)(2,1)}, u32[]{:S(2)}, u32[]{:S(2)}) collective-permute-start(bf16[4,1,1,384,256]{4,3,2,1,0:T(8,128)(2,1)} %constant_dynamic-slice_fusion.6), channel_id=1, source_target_pairs={{0,4},{4,0},{1,5},{5,1},{2,6},{6,2},{3,7},{7,3},{8,12},{12,8},{9,1... | collective-permute-start | bytes 2359304 | tf_op jit(solution)/shard_map/ppermute | solution.py:58
  489.7 51.8 %collective-permute-start.28 = (bf16[4,2,1,96,1536]{4,3,2,1,0:T(8,128)(2,1)}, bf16[4,2,1,96,1536]{4,3,2,1,0:T(8,128)(2,1)}, u32[]{:S(2)}, u32[]{:S(2)}) collective-permute-start(bf16[4,2,1,96,1536]{4,3,2,1,0:T(8,128)(2,1)} %constant_dynamic-slice_fusion.3), channel_id=1, source_target_pairs={{0,2},{2,0},{1,3},{3,1},{4,6},{6,4},{5,7},{7,5},{8,10},{10,8},{9,1... | collective-permute-start | bytes 7077896 | tf_op jit(solution)/shard_map/ppermute | solution.py:58
  491.4 35.2 %collective-permute-start.26 = (bf16[2,1,384,256]{3,2,1,0:T(8,128)(2,1)}, bf16[2,1,384,256]{3,2,1,0:T(8,128)(2,1)}, u32[]{:S(2)}, u32[]{:S(2)}) collective-permute-start(bf16[2,1,384,256]{3,2,1,0:T(8,128)(2,1)} %constant_dynamic-slice_fusion.5), channel_id=1, source_target_pairs={{0,8},{8,0},{16,24},{24,16},{1,9},{9,1},{17,25},{25,17},{2,10},{10... | collective-permute-start | bytes 1179656 | tf_op jit(solution)/shard_map/ppermute | solution.py:153
  500.6 32.0 %collective-permute-start.25 = (bf16[384,1536]{1,0:T(8,128)(2,1)}, bf16[384,1536]{1,0:T(8,128)(2,1)}, u32[]{:S(2)}, u32[]{:S(2)}) collective-permute-start(bf16[384,1536]{1,0:T(8,128)(2,1)} %convolution_convert_fusion.5), channel_id=1, source_target_pairs={{0,1},{1,0},{2,3},{3,2},{4,5},{5,4},{6,7},{7,6},{8,9},{9,8},{10,11... | collective-permute-start | bytes 3538952 | tf_op jit(solution)/shard_map/ppermute | solution.py:58
  502.0 37.6 %collective-permute-start.23 = (bf16[384,1536]{1,0:T(8,128)(2,1)}, bf16[384,1536]{1,0:T(8,128)(2,1)}, u32[]{:S(2)}, u32[]{:S(2)}) collective-permute-start(bf16[384,1536]{1,0:T(8,128)(2,1)} %fusion.13), channel_id=1, source_target_pairs={{0,4},{4,0},{1,5},{5,1},{2,6},{6,2},{3,7},{7,3},{8,12},{12,8},{9,1... | collective-permute-start | bytes 3538952 | tf_op jit(solution)/shard_map/ppermute | solution.py:58
  503.8 35.9 %all-to-all-start.4 = ((bf16[4,96,1120]{2,1,0:T(8,128)(2,1)}), bf16[4,96,1120]{2,1,0:T(8,128)(2,1)}, u32[]{:S(2)}, u32[]{:S(2)}) async-start(bf16[4,96,1120]{2,1,0:T(8,128)(2,1)} %bitcast.146), calls=%async_computation.6 | async-start | bytes 1769472 | tf_op jit(solution)/shard_map/all_to_all | solution.py:114
  508.0 136.0 %reduce-scatter.11.cloned.1.call-start = ((), (), s32[]{:S(2)}) async-start(), calls=%async_computation.17 | async-start | bytes 1843200 | tf_op jit(solution)/shard_map/reduce_scatter | solution.py:108
  547.1 27.7 %collective-permute-start.30 = (bf16[4,1,1,96,1536]{4,3,2,1,0:T(8,128)(2,1)}, bf16[4,1,1,96,1536]{4,3,2,1,0:T(8,128)(2,1)}, u32[]{:S(2)}, u32[]{:S(2)}) collective-permute-start(bf16[4,1,1,96,1536]{4,3,2,1,0:T(8,128)(2,1)} %constant_dynamic-slice_fusion.1), channel_id=1, source_target_pairs={{0,4},{4,0},{1,5},{5,1},{2,6},{6,2},{3,7},{7,3},{8,12},{12,8},{9,1... | collective-permute-start | bytes 3538952 | tf_op jit(solution)/shard_map/ppermute | solution.py:58
  593.0 28.1 %collective-permute-start.24 = (bf16[384,1536]{1,0:T(8,128)(2,1)}, bf16[384,1536]{1,0:T(8,128)(2,1)}, u32[]{:S(2)}, u32[]{:S(2)}) collective-permute-start(bf16[384,1536]{1,0:T(8,128)(2,1)} %fusion.15), channel_id=1, source_target_pairs={{0,1},{1,0},{2,3},{3,2},{4,5},{5,4},{6,7},{7,6},{8,9},{9,8},{10,11... | collective-permute-start | bytes 3538952 | tf_op jit(solution)/shard_map/ppermute | solution.py:58
  624.2 16.4 %all-to-all-start.5 = ((bf16[4,96,1120]{2,1,0:T(8,128)(2,1)}), bf16[4,96,1120]{2,1,0:T(8,128)(2,1)S(1)}, u32[]{:S(2)}, u32[]{:S(2)}) async-start(bf16[4,96,1120]{2,1,0:T(8,128)(2,1)} %bitcast.145), calls=%async_computation.9 | async-start | bytes 1769472 | tf_op jit(solution)/shard_map/all_to_all | solution.py:114
  (71 other events, 754.8 us)
Sparse Core Ops, SparseCore 0:
  10.1 35.1 all-gather.4
  50.0 82.9 all-gather.10
  134.6 68.5 all-gather.8
  205.1 68.6 all-gather.6
  314.3 67.8 reduce-scatter.4
  384.3 66.6 reduce-scatter.6
  453.3 75.0 reduce-scatter.8
  597.6 37.0 reduce-scatter.10

commit v11 on v8

--- a/solution.py
+++ b/solution.py
@@ -151,7 +151,7 @@
         sent = lax.dynamic_slice_in_dim(parts, 1 - at, 1, 1)
         kept = lax.dynamic_slice_in_dim(parts, at, 1, 1)
         came = lax.ppermute(sent, "z", [(number, number ^ step) for number in range(high)])
-        came = after(came, early if step == 1 else late)
+        came = after(came, *(early if step == 1 else late))
         column = kept.astype(jnp.float32) + came.astype(jnp.float32)
         column = column.reshape(-1, column.shape[3])
         step *= 2
@@ -481,12 +481,12 @@
     key_value_sums = scatter_across(
         key_value_halves, gate_sums, square_grads, grad_query_mine, down_across
     )
+    down_came = other(after(down_across, key_value_sums), "x")
     gate_parts = undeal(after(gate_sums, key_value_sums))
     square_halves = scatter_core(after(square_grads, key_value_sums), features)
-    key_value_grads = halve_z(key_value_sums, rows, key_value_sums, query_came)
+    key_value_grads = halve_z(key_value_sums, rows, (key_value_sums,), (query_came, gate_parts, down_came))
     square_sums = scatter_across(square_halves)
     key_value_grads = after(key_value_grads, up_sums)
-    down_came = other(after(down_across, key_value_sums), "x")
     grad_key_pre = low(
         rotate_halves(key_value_grads[:, :head].reshape(rows, 1, head), cosine_table, -sine_table)
     ).reshape(rows, head)
@@ -495,13 +495,13 @@
     grad_project = jnp.concatenate([grad_query_pre, grad_pair], axis=1)
     grad_bias = jnp.sum(grad_project.astype(jnp.float32), axis=0)
     pair_both = in_order(grad_pair, other(grad_pair, "y"))
-    query_came = after(query_came, grad_pair, down_came)
+    query_came = after(query_came, grad_pair, square_halves[0])
     grad_normed_one = (
         grad_query_mine.astype(jnp.float32) + query_came.astype(jnp.float32)
     ) + product_right(
         pair_both, in_order(w_pair[:, : 2 * head], pair_weights_came)
     )
-    down_mine = low(down_own + after(down_came, pair_both).astype(jnp.float32))
+    down_mine = low(down_own + after(down_came, key_value_sums).astype(jnp.float32))
     down_pair = other(down_mine, "y")
     result = low(middle + down_mine.astype(jnp.float32) + down_pair.astype(jnp.float32))
     back_one, grad_gain_one = norm_back(inputs, scale_one, gain_one, grad_normed_one)
@@ -527,10 +527,11 @@
             axis=1,
         )
     )
-    up_parts = undeal(after(up_sums, grad_pair))
-    packed_grads = scatter_across(
-        scatter_core(packed_grads, features), gate_parts, square_sums
-    )
+    packed_halves = other_half(
+        packed_grads.reshape(-1, 2, 2, features, packed_grads.shape[1]), "c", 2
+    )
+    packed_grads = scatter_across(other_half(add_half(packed_halves, square_sums), "x", 1))
+    up_parts = undeal(after(up_sums, packed_halves[1]))
     last_grads = scatter_z(jnp.concatenate([square_sums, packed_grads], axis=1)).astype(jnp.float32)
     square_grads = last_grads[:, : 2 * heads_width]
     packed_grads = last_grads[:, 2 * heads_width :]

time: 667 us -> 649 us (0.973); the launches traced: 663 us -> 638 us
  Pallas kernels: 26.5 us -> 15.1 us
  local copies, waits for them, and re-layouts: 84.3 us -> 77.4 us
    pallas_call x1, Pallas kernels: 17.5 us -> 6.5 us  [attend(): pl.pallas_call(attend_kernel, out_shape=(jax.ShapeDtypeStruct((rows, wide...]
    ppermute x31, waiting for transfers between devices: 123 us -> 132 us  [other(): return lax.ppermute(value, axis, [(0, 1), (1, 0)])]
    all_gather x4, waiting for transfers between devices: 37.6 us -> 29.4 us  [gather_z(): return lax.all_gather(own, 'z', axis=0, tiled=True)]
    unnamed x157 -> x129, local copies, waits for them, and re-layouts: 21.5 us -> 19.5 us
  transfers between devices with their start and end apart: 46 -> 46, of which waited for: 22 -> 24; matrix products, arithmetic and copies ran while one was open for 38% -> 37% of each run, Pallas kernels for 4% -> 2%
where the time goes in v11:
time: 649 us; the launch traced here: 638 us
  waiting for transfers between devices  210 us (32%)
  matrix products  121 us (19%)
  local copies, waits for them, and re-layouts  77.4 us (12%)
  other arithmetic  74.4 us (11%)
  blocking collectives  64.3 us (10%)
  starting transfers between devices  58.1 us (9%)
  between operations  17.4 us (3%)
  Pallas kernels  15.1 us (2%)
    ppermute x31, waiting for transfers between devices, other(): return lax.ppermute(value, axis, [(0, 1), (1, 0)])  132 us
    dot_general x9, matrix products, product(): return jnp.dot(left, right, preferred_element_type=jnp.float32)  74.7 us
    all_gather x2, blocking collectives, gather_z(): return lax.all_gather(own, 'z', axis=0, tiled=True)  48.3 us
    dot_general x6, matrix products, product_right(): lax.dot_general(left, right, (((1,), (1,)), ((), ())), preferred_element_...  40.7 us
    ppermute x31, starting transfers between devices, other(): return lax.ppermute(value, axis, [(0, 1), (1, 0)])  30.4 us
    all_gather x4, waiting for transfers between devices, gather_z(): return lax.all_gather(own, 'z', axis=0, tiled=True)  29.4 us
    convert_element_type x15, other arithmetic, low(): return value.astype(jnp.bfloat16)  28.7 us
    ppermute x2, waiting for transfers between devices, halve_z(): lax.ppermute(sent, 'z', [(number, number ^ step) for number in range(high)])  25.2 us
  transfers between devices with their start and end apart: 46, of which 24 were waited for; matrix products, arithmetic and copies ran while one was open for 37% of the time, Pallas kernels for 2%

profile of v11, /device:TPU:0, one launch (start us, length us, event | category | flops | bytes accessed | tf_op | source)
XLA Modules:
  0.0 637.8 jit_solution(10595616742716824183)
XLA Ops:
  13.3 17.9 %all_gather.18 = bf16[384,384]{1,0:T(8,128)(2,1)S(1)} all-gather(bf16[96,384]{1,0:T(8,128)(2,1)S(1)} %pad_maximum_fusion.10), channel_id=1, replica_groups=mesh['z'=4,'x'=2,'c'=2,'y'=2] {'z'}, dimensions={0}, use_global_device_ids=true | all-gather | bytes 368640 | tf_op jit(solution)/shard_map/all_gather | solution.py:104
  33.9 16.0 %all_to_all.30 = bf16[4,96,1120]{2,1,0:T(8,128)(2,1)} all-to-all(bf16[4,96,1120]{2,1,0:T(8,128)(2,1)S(1)} %bitcast.129), channel_id=1, replica_groups=mesh['z'=4,'x'=2,'c'=2,'y'=2] {'x','c'}, dimensions={0} | all-to-all | bytes 1720320 | tf_op jit(solution)/shard_map/all_to_all | solution.py:99
  52.4 6.1 collective-permute-done.1
  72.0 30.4 %all_gather.20 = bf16[1536,256]{1,0:T(8,128)(2,1)} all-gather(bf16[384,256]{1,0:T(8,128)(2,1)S(1)} %pad_maximum_fusion.8), channel_id=1, replica_groups=mesh['z'=4,'x'=2,'c'=2,'y'=2] {'z'}, dimensions={0}, use_global_device_ids=true | all-gather | bytes 983040 | tf_op jit(solution)/shard_map/all_gather | solution.py:104
  115.2 8.3 %collective-permute-done.7 = bf16[4,1,1,384,256]{4,3,2,1,0:T(8,128)(2,1)} collective-permute-done((bf16[4,1,1,384,256]{4,3,2,1,0:T(8,128)(2,1)}, bf16[4,1,1,384,256]{4,3,2,1,0:T(8,128)(2,1)}, u32[]{:S(2)}, u32[]{:S(2)}) %collective-permute-start.7) | collective-permute-done | bytes 786464 | tf_op jit(solution)/shard_map/ppermute | solution.py:58
  142.1 6.5 %attend.1 = (bf16[384,768]{1,0:T(8,128)(2,1)}, f32[384,768]{1,0:T(8,128)}, f32[8,384]{1,0:T(8,128)}) custom-call(s32[2]{0:T(128)} %pad_add_fusion.bounds_ref, f32[384,768]{1,0:T(8,128)} %fusion.32.query_ref, f32[384,128]{1,0:T(8,128)} %get-tuple-element.129.cosine_ref, f32[384,128]{1,0:T(8,128)} %get-tuple-element.130.sine_ref, ...), custom_call_target="tpu_custom_call" | custom-call | flops 4076863488 | bytes 20971520 | tf_op jit(solution)/shard_map/attend/pallas_call | solution.py:295
  148.6 11.7 %collective-permute-done.12 = bf16[384,1536]{1,0:T(8,128)(2,1)} collective-permute-done((bf16[384,1536]{1,0:T(8,128)(2,1)}, bf16[384,1536]{1,0:T(8,128)(2,1)}, u32[]{:S(2)}, u32[]{:S(2)}) %collective-permute-start.12) | collective-permute-done | bytes 1179680 | tf_op jit(solution)/shard_map/ppermute | solution.py:58
  171.6 20.5 %collective-permute-done.10 = bf16[384,1536]{1,0:T(8,128)(2,1)} collective-permute-done((bf16[384,1536]{1,0:T(8,128)(2,1)S(1)}, bf16[384,1536]{1,0:T(8,128)(2,1)}, u32[]{:S(2)}, u32[]{:S(2)}) %collective-permute-start.10) | collective-permute-done | bytes 1179680 | tf_op jit(solution)/shard_map/ppermute | solution.py:58
  194.9 27.1 %collective-permute-done.15 = bf16[384,1536]{1,0:T(8,128)(2,1)} collective-permute-done((bf16[384,1536]{1,0:T(8,128)(2,1)S(1)}, bf16[384,1536]{1,0:T(8,128)(2,1)}, u32[]{:S(2)}, u32[]{:S(2)}) %collective-permute-start.15) | collective-permute-done | bytes 1179680 | tf_op jit(solution)/shard_map/ppermute | solution.py:58
  225.1 11.4 %fusion.76 = f32[1536,1120]{0,1:T(8,128)} fusion(bf16[1536,1120]{1,0:T(8,128)(2,1)} %all-gather.7.cloned.1.call-done, bf16[384,1536]{1,0:T(8,128)(2,1)} %collective-permute-done.16, bf16[384,1536]{1,0:T(8,128)(2,1)} %collective-permute-done.15, bf16[384,1536]{1,0:T(8,128)(2,1)} %collective-permute-done.14, bf16[384,1536]{1,0:T(8,128)(2,1)S(1)} %multiply_convert_fusion.3), kind=kOutput, calls=%fused_computation.183 | convolution fusion | flops 5303697408 | bytes 15040512 | tf_op jit(solution)/shard_map/dot_general | solution.py:17
  236.6 5.1 fusion.75
  241.7 12.9 %multiply_convert_fusion.2 = (bf16[1536,1120]{0,1:T(8,128)(2,1)S(1)}, f32[1536,1120]{0,1:T(8,128)}) fusion(f32[1536,1120]{0,1:T(8,128)} %fusion.76, bf16[1536,1120]{1,0:T(8,128)(2,1)} %all-gather.9.cloned.1.call-done, bf16[384,1536]{1,0:T(8,128)(2,1)} %collective-permute-done.16, bf16[384,1536]{1,0:T(8,128)(2,1)} %collective-permute-done.15, ...), kind=kOutput, calls=%fused_computation.6 | convolution fusion | flops 5314019328 | bytes 25362432 | tf_op jit(solution)/shard_map/dot_general | solution.py:17
  256.3 9.4 %convolution_convert_fusion.2 = bf16[1536,1120]{1,0:T(8,128)(2,1)} fusion(bf16[1536,1536]{0,1:T(8,128)(2,1)} %bitcast.151, bf16[1536,1120]{0,1:T(8,128)(2,1)S(1)} %get-tuple-element.62), kind=kOutput, calls=%fused_computation.3 | convolution fusion | flops 5286543360 | bytes 11599872 | tf_op jit(solution)/shard_map/dot_general | solution.py:17
  265.8 29.4 %all-gather.11.cloned.1.call-done = bf16[1536,1120]{1,0:T(8,128)(2,1)} async-done(((bf16[384,1120]{1,0:T(8,128)(2,1)}), bf16[1536,1120]{1,0:T(8,128)(2,1)}) %all-gather.11.cloned.1.call-update) | async-done | bytes 3440656 | tf_op jit(solution)/shard_map/all_gather | solution.py:104
  295.1 15.5 %multiply_convert_fusion = (bf16[1536,1120]{0,1:T(8,128)(2,1)S(1)}, bf16[1536,1120]{0,1:T(8,128)(2,1)}) fusion(f32[1536,1120]{0,1:T(8,128)} %fusion.76, f32[1536,1120]{0,1:T(8,128)} %get-tuple-element.125, bf16[1536,1536]{1,0:T(8,128)(2,1)} %copy-done.36, bf16[1536,1120]{1,0:T(8,128)(2,1)} %all-gather.11.cloned.1.call-done), kind=kOutput, calls=%fused_computation.4 | convolution fusion | flops 5307187200 | bytes 28803072 | tf_op jit(solution)/shard_map/dot_general | solution.py:17
  310.6 9.0 %fusion.86 = f32[1536,1536]{1,0:T(8,128)} fusion(bf16[1536,1120]{0,1:T(8,128)(2,1)S(1)} %get-tuple-element.60, bf16[1536,1120]{1,0:T(8,128)(2,1)S(1)} %copy-done.50), kind=kOutput, calls=%fused_computation.193 | convolution fusion | flops 5284823040 | bytes 16318464 | tf_op jit(solution)/shard_map/dot_general | solution.py:27
  319.6 10.6 %fusion.85 = (bf16[1536,1536]{1,0:T(8,128)(2,1)S(1)}, f32[1536,1536]{1,0:T(8,128)S(1)}) fusion(f32[1536,1536]{1,0:T(8,128)} %fusion.86, bf16[1536,1120]{0,1:T(8,128)(2,1)} %get-tuple-element.61, bf16[1536,1120]{1,0:T(8,128)(2,1)} %all-gather.9.cloned.1.call-done), kind=kOutput, calls=%fused_computation.192 | convolution fusion | flops 5289541632 | bytes 30474240 | tf_op jit(solution)/shard_map/dot_general | solution.py:27
  330.7 4.5 collective-permute-done.17
  340.0 7.9 %convolution_convert_fusion.1 = bf16[1536,1120]{1,0:T(8,128)(2,1)} fusion(bf16[1536,1536]{0,1:T(8,128)(2,1)S(1)} %bitcast.117, bf16[1536,1120]{0,1:T(8,128)(2,1)S(1)} %copy-done.55), kind=kOutput, calls=%fused_computation.2 | convolution fusion | flops 5286543360 | bytes 11599872 | tf_op jit(solution)/shard_map/dot_general | solution.py:17
  349.5 10.4 %convolution_convert_fusion = bf16[1536,1120]{1,0:T(8,128)(2,1)} fusion(bf16[1536,1536]{0,1:T(8,128)(2,1)} %fusion.75, bf16[1536,1120]{0,1:T(8,128)(2,1)} %get-tuple-element.61), kind=kOutput, calls=%fused_computation.1 | convolution fusion | flops 5286543360 | bytes 11599872 | tf_op jit(solution)/shard_map/dot_general | solution.py:17
  362.4 11.3 %fusion.87 = f32[1536,1536]{1,0:T(8,128)} fusion(bf16[1536,1120]{0,1:T(8,128)(2,1)} %copy-done.53, bf16[1536,1120]{1,0:T(8,128)(2,1)} %all-gather.11.cloned.1.call-done), kind=kOutput, calls=%fused_computation.194 | convolution fusion | flops 5284823040 | bytes 16318464 | tf_op jit(solution)/shard_map/dot_general | solution.py:27
  385.9 12.0 %all-to-all-done.3 = bf16[4,96,1120]{2,1,0:T(8,128)(2,1)} async-done(((bf16[4,96,1120]{2,1,0:T(8,128)(2,1)}), bf16[4,96,1120]{2,1,0:T(8,128)(2,1)}, u32[]{:S(2)}, u32[]{:S(2)}) %all-to-all-start.3) | async-done | bytes 860192 | tf_op jit(solution)/shard_map/all_to_all | solution.py:114
  397.9 8.8 %collective-permute-done.19 = bf16[384,1536]{1,0:T(8,128)(2,1)} collective-permute-done((bf16[384,1536]{1,0:T(8,128)(2,1)S(1)}, bf16[384,1536]{1,0:T(8,128)(2,1)}, u32[]{:S(2)}, u32[]{:S(2)}) %collective-permute-start.19) | collective-permute-done | bytes 1179680 | tf_op jit(solution)/shard_map/ppermute | solution.py:58
  420.1 8.6 %attend_back.1 = (bf16[384,768]{1,0:T(8,128)(2,1)}, bf16[6144,256]{1,0:T(8,128)(2,1)}) custom-call(s32[2]{0:T(128)} %pad_add_fusion.bounds_ref, bf16[384,768]{1,0:T(8,128)(2,1)} %get-tuple-element.67.rotated_ref, f32[384,768]{1,0:T(8,128)} %fusion.20.grad_ref, f32[384,768]{1,0:T(8,128)} %get-tuple-element.55.attended_ref, ...), custom_call_target="tpu_custom_call" | custom-call | flops 294912 | bytes 294912 | tf_op jit(solution)/shard_map/attend_back/pallas_call | solution.py:314
  441.4 6.8 %collective-permute-start.22 = (bf16[4,1,1,384,256]{4,3,2,1,0:T(8,128)(2,1)}, bf16[4,1,1,384,256]{4,3,2,1,0:T(8,128)(2,1)}, u32[]{:S(2)}, u32[]{:S(2)}) collective-permute-start(bf16[4,1,1,384,256]{4,3,2,1,0:T(8,128)(2,1)} %constant_dynamic-slice_fusion.6), channel_id=1, source_target_pairs={{0,4},{4,0},{1,5},{5,1},{2,6},{6,2},{3,7},{7,3},{8,12},{12,8},{9,1... | collective-permute-start | bytes 2359304 | tf_op jit(solution)/shard_map/ppermute | solution.py:58
  457.9 8.5 %collective-permute-done.22 = bf16[4,1,1,384,256]{4,3,2,1,0:T(8,128)(2,1)} collective-permute-done((bf16[4,1,1,384,256]{4,3,2,1,0:T(8,128)(2,1)}, bf16[4,1,1,384,256]{4,3,2,1,0:T(8,128)(2,1)}, u32[]{:S(2)}, u32[]{:S(2)}) %collective-permute-start.22) | collective-permute-done | bytes 786464 | tf_op jit(solution)/shard_map/ppermute | solution.py:58
  473.9 6.9 %collective-permute-start.26 = (bf16[2,1,384,256]{3,2,1,0:T(8,128)(2,1)}, bf16[2,1,384,256]{3,2,1,0:T(8,128)(2,1)}, u32[]{:S(2)}, u32[]{:S(2)}) collective-permute-start(bf16[2,1,384,256]{3,2,1,0:T(8,128)(2,1)} %constant_dynamic-slice_fusion.5), channel_id=1, source_target_pairs={{0,8},{8,0},{16,24},{24,16},{1,9},{9,1},{17,25},{25,17},{2,10},{10... | collective-permute-start | bytes 1179656 | tf_op jit(solution)/shard_map/ppermute | solution.py:153
  488.5 18.4 %collective-permute-done.26 = bf16[2,1,384,256]{3,2,1,0:T(8,128)(2,1)} collective-permute-done((bf16[2,1,384,256]{3,2,1,0:T(8,128)(2,1)}, bf16[2,1,384,256]{3,2,1,0:T(8,128)(2,1)}, u32[]{:S(2)}, u32[]{:S(2)}) %collective-permute-start.26) | collective-permute-done | bytes 393248 | tf_op jit(solution)/shard_map/ppermute | solution.py:153
  512.9 6.8 %collective-permute-done.27 = bf16[1,1,384,256]{3,2,1,0:T(8,128)(2,1)} collective-permute-done((bf16[1,1,384,256]{3,2,1,0:T(8,128)(2,1)}, bf16[1,1,384,256]{3,2,1,0:T(8,128)(2,1)}, u32[]{:S(2)}, u32[]{:S(2)}) %collective-permute-start.27) | collective-permute-done | bytes 196640 | tf_op jit(solution)/shard_map/ppermute | solution.py:153
  542.2 13.2 %collective-permute-done.30 = bf16[4,1,1,96,1536]{4,3,2,1,0:T(8,128)(2,1)} collective-permute-done((bf16[4,1,1,96,1536]{4,3,2,1,0:T(8,128)(2,1)}, bf16[4,1,1,96,1536]{4,3,2,1,0:T(8,128)(2,1)}, u32[]{:S(2)}, u32[]{:S(2)}) %collective-permute-start.30) | collective-permute-done | bytes 1179680 | tf_op jit(solution)/shard_map/ppermute | solution.py:58
  591.2 10.4 %collective-permute-done.24 = bf16[384,1536]{1,0:T(8,128)(2,1)} collective-permute-done((bf16[384,1536]{1,0:T(8,128)(2,1)}, bf16[384,1536]{1,0:T(8,128)(2,1)}, u32[]{:S(2)}, u32[]{:S(2)}) %collective-permute-start.24) | collective-permute-done | bytes 1179680 | tf_op jit(solution)/shard_map/ppermute | solution.py:58
  612.5 8.5 %all-to-all-done.5 = bf16[4,96,1120]{2,1,0:T(8,128)(2,1)S(1)} async-done(((bf16[4,96,1120]{2,1,0:T(8,128)(2,1)}), bf16[4,96,1120]{2,1,0:T(8,128)(2,1)S(1)}, u32[]{:S(2)}, u32[]{:S(2)}) %all-to-all-start.5) | async-done | bytes 860192 | tf_op jit(solution)/shard_map/all_to_all | solution.py:114
  (357 shorter events, 229.5 us)
Async XLA Ops:
  7.2 61.0 %all-gather.5.cloned.1.call-start = ((), (), s32[]{:S(2)}) async-start(), calls=%async_computation.10 | async-start | bytes 1474560 | tf_op jit(solution)/shard_map/all_gather | solution.py:104
  9.0 213.1 %all-gather.7.cloned.1.call-start = ((), (), s32[]{:S(2)}) async-start(), calls=%async_computation.11 | async-start | bytes 4423680 | tf_op jit(solution)/shard_map/all_gather | solution.py:104
  64.6 37.9 %all-to-all-start.1 = ((bf16[4,96,1120]{2,1,0:T(8,128)(2,1)}), bf16[4,96,1120]{2,1,0:T(8,128)(2,1)S(1)}, u32[]{:S(2)}, u32[]{:S(2)}) async-start(bf16[4,96,1120]{2,1,0:T(8,128)(2,1)} %bitcast.105), calls=%async_computation.1 | async-start | bytes 1769472 | tf_op jit(solution)/shard_map/all_to_all | solution.py:99
  68.1 173.6 %all-gather.9.cloned.1.call-start = ((), (), s32[]{:S(2)}) async-start(), calls=%async_computation.12 | async-start | bytes 4423680 | tf_op jit(solution)/shard_map/all_gather | solution.py:104
  68.2 55.4 %collective-permute-start.4 = (bf16[4,1,1,96,1536]{4,3,2,1,0:T(8,128)(2,1)}, bf16[4,1,1,96,1536]{4,3,2,1,0:T(8,128)(2,1)}, u32[]{:S(2)}, u32[]{:S(2)}) collective-permute-start(bf16[4,1,1,96,1536]{4,3,2,1,0:T(8,128)(2,1)} %bitcast.140), channel_id=1, source_target_pairs={{0,4},{4,0},{1,5},{5,1},{2,6},{6,2},{3,7},{7,3},{8,12},{12,8},{9,1... | collective-permute-start | bytes 3538952 | tf_op jit(solution)/shard_map/ppermute | solution.py:58
  102.5 21.1 %collective-permute-start.7 = (bf16[4,1,1,384,256]{4,3,2,1,0:T(8,128)(2,1)}, bf16[4,1,1,384,256]{4,3,2,1,0:T(8,128)(2,1)}, u32[]{:S(2)}, u32[]{:S(2)}) collective-permute-start(bf16[4,1,1,384,256]{4,3,2,1,0:T(8,128)(2,1)} %bitcast.22), channel_id=1, source_target_pairs={{0,4},{4,0},{1,5},{5,1},{2,6},{6,2},{3,7},{7,3},{8,12},{12,8},{9,1... | collective-permute-start | bytes 2359304 | tf_op jit(solution)/shard_map/ppermute | solution.py:58
  103.5 25.0 %collective-permute-start.3 = (bf16[4,1,1,96,1536]{4,3,2,1,0:T(8,128)(2,1)}, bf16[4,1,1,96,1536]{4,3,2,1,0:T(8,128)(2,1)}, u32[]{:S(2)}, u32[]{:S(2)}) collective-permute-start(bf16[4,1,1,96,1536]{4,3,2,1,0:T(8,128)(2,1)} %bitcast.141), channel_id=1, source_target_pairs={{0,2},{2,0},{1,3},{3,1},{4,6},{6,4},{5,7},{7,5},{8,10},{10,8},{9,1... | collective-permute-start | bytes 3538952 | tf_op jit(solution)/shard_map/ppermute | solution.py:58
  103.6 22.5 %collective-permute-start.6 = (bf16[4,1,1,384,256]{4,3,2,1,0:T(8,128)(2,1)}, bf16[4,1,1,384,256]{4,3,2,1,0:T(8,128)(2,1)}, u32[]{:S(2)}, u32[]{:S(2)}) collective-permute-start(bf16[4,1,1,384,256]{4,3,2,1,0:T(8,128)(2,1)} %bitcast.22), channel_id=1, source_target_pairs={{0,2},{2,0},{1,3},{3,1},{4,6},{6,4},{5,7},{7,5},{8,10},{10,8},{9,1... | collective-permute-start | bytes 2359304 | tf_op jit(solution)/shard_map/ppermute | solution.py:58
  107.6 24.4 %collective-permute-start.9 = (bf16[1536,256]{1,0:T(8,128)(2,1)}, bf16[1536,256]{1,0:T(8,128)(2,1)}, u32[]{:S(2)}, u32[]{:S(2)}) collective-permute-start(bf16[1536,256]{1,0:T(8,128)(2,1)} %slice.228), channel_id=1, source_target_pairs={{0,1},{1,0},{2,3},{3,2},{4,5},{5,4},{6,7},{7,6},{8,9},{9,8},{10,11... | collective-permute-start | bytes 2359304 | tf_op jit(solution)/shard_map/ppermute | solution.py:58
  111.0 21.5 %all-to-all-start.2 = ((bf16[4,96,1120]{2,1,0:T(8,128)(2,1)}), bf16[4,96,1120]{2,1,0:T(8,128)(2,1)}, u32[]{:S(2)}, u32[]{:S(2)}) async-start(bf16[4,96,1120]{2,1,0:T(8,128)(2,1)} %bitcast.104), calls=%async_computation.2 | async-start | bytes 1769472 | tf_op jit(solution)/shard_map/all_to_all | solution.py:99
  115.2 179.9 %all-gather.11.cloned.1.call-start = ((), (), s32[]{:S(2)}) async-start(), calls=%async_computation.13 | async-start | bytes 4423680 | tf_op jit(solution)/shard_map/all_gather | solution.py:104
  132.4 27.9 %collective-permute-start.12 = (bf16[384,1536]{1,0:T(8,128)(2,1)}, bf16[384,1536]{1,0:T(8,128)(2,1)}, u32[]{:S(2)}, u32[]{:S(2)}) collective-permute-start(bf16[384,1536]{1,0:T(8,128)(2,1)} %param.29), channel_id=1, source_target_pairs={{0,4},{4,0},{1,5},{5,1},{2,6},{6,2},{3,7},{7,3},{8,12},{12,8},{9,1... | collective-permute-start | bytes 3538952 | tf_op jit(solution)/shard_map/ppermute | solution.py:58
  135.9 30.6 %collective-permute-start.11 = (bf16[384,1536]{1,0:T(8,128)(2,1)}, bf16[384,1536]{1,0:T(8,128)(2,1)}, u32[]{:S(2)}, u32[]{:S(2)}) collective-permute-start(bf16[384,1536]{1,0:T(8,128)(2,1)} %param.29), channel_id=1, source_target_pairs={{0,2},{2,0},{1,3},{3,1},{4,6},{6,4},{5,7},{7,5},{8,10},{10,8},{9,1... | collective-permute-start | bytes 3538952 | tf_op jit(solution)/shard_map/ppermute | solution.py:58
  163.5 28.6 %collective-permute-start.10 = (bf16[384,1536]{1,0:T(8,128)(2,1)S(1)}, bf16[384,1536]{1,0:T(8,128)(2,1)}, u32[]{:S(2)}, u32[]{:S(2)}) collective-permute-start(bf16[384,1536]{1,0:T(8,128)(2,1)S(1)} %convolution_convert_fusion.6), channel_id=1, source_target_pairs={{0,1},{1,0},{2,3},{3,2},{4,5},{5,4},{6,7},{7,6},{8,9},{9,8},{10,11... | collective-permute-start | bytes 3538952 | tf_op jit(solution)/shard_map/ppermute | solution.py:58
  194.2 27.7 %collective-permute-start.15 = (bf16[384,1536]{1,0:T(8,128)(2,1)S(1)}, bf16[384,1536]{1,0:T(8,128)(2,1)}, u32[]{:S(2)}, u32[]{:S(2)}) collective-permute-start(bf16[384,1536]{1,0:T(8,128)(2,1)S(1)} %multiply_convert_fusion.3), channel_id=1, source_target_pairs={{0,4},{4,0},{1,5},{5,1},{2,6},{6,2},{3,7},{7,3},{8,12},{12,8},{9,1... | collective-permute-start | bytes 3538952 | tf_op jit(solution)/shard_map/ppermute | solution.py:58
  194.9 27.2 %collective-permute-start.14 = (bf16[384,1536]{1,0:T(8,128)(2,1)S(1)}, bf16[384,1536]{1,0:T(8,128)(2,1)}, u32[]{:S(2)}, u32[]{:S(2)}) collective-permute-start(bf16[384,1536]{1,0:T(8,128)(2,1)S(1)} %multiply_convert_fusion.3), channel_id=1, source_target_pairs={{0,2},{2,0},{1,3},{3,1},{4,6},{6,4},{5,7},{7,5},{8,10},{10,8},{9,1... | collective-permute-start | bytes 3538952 | tf_op jit(solution)/shard_map/ppermute | solution.py:58
  222.0 140.5 %reduce-scatter.5.cloned.1.call-start = ((), (), s32[]{:S(2)}) async-start(), calls=%async_computation.14 | async-start | bytes 4423680 | tf_op jit(solution)/shard_map/reduce_scatter | solution.py:108
  265.7 192.2 %reduce-scatter.7.cloned.1.call-start = ((), (), s32[]{:S(2)}) async-start(), calls=%async_computation.15 | async-start | bytes 4423680 | tf_op jit(solution)/shard_map/reduce_scatter | solution.py:108
  347.9 28.2 %collective-permute-start.18 = (bf16[384,1536]{1,0:T(8,128)(2,1)S(1)}, bf16[384,1536]{1,0:T(8,128)(2,1)}, u32[]{:S(2)}, u32[]{:S(2)}) collective-permute-start(bf16[384,1536]{1,0:T(8,128)(2,1)S(1)} %fusion.18), channel_id=1, source_target_pairs={{0,4},{4,0},{1,5},{5,1},{2,6},{6,2},{3,7},{7,3},{8,12},{12,8},{9,1... | collective-permute-start | bytes 3538952 | tf_op jit(solution)/shard_map/ppermute | solution.py:58
  379.4 27.3 %collective-permute-start.19 = (bf16[384,1536]{1,0:T(8,128)(2,1)S(1)}, bf16[384,1536]{1,0:T(8,128)(2,1)}, u32[]{:S(2)}, u32[]{:S(2)}) collective-permute-start(bf16[384,1536]{1,0:T(8,128)(2,1)S(1)} %fusion.17), channel_id=1, source_target_pairs={{0,1},{1,0},{2,3},{3,2},{4,5},{5,4},{6,7},{7,6},{8,9},{9,8},{10,11... | collective-permute-start | bytes 3538952 | tf_op jit(solution)/shard_map/ppermute | solution.py:58
  381.0 17.0 %all-to-all-start.3 = ((bf16[4,96,1120]{2,1,0:T(8,128)(2,1)}), bf16[4,96,1120]{2,1,0:T(8,128)(2,1)}, u32[]{:S(2)}, u32[]{:S(2)}) async-start(bf16[4,96,1120]{2,1,0:T(8,128)(2,1)} %bitcast.148), calls=%async_computation.4 | async-start | bytes 1769472 | tf_op jit(solution)/shard_map/all_to_all | solution.py:114
  385.2 136.5 %reduce-scatter.9.cloned.1.call-start = ((), (), s32[]{:S(2)}) async-start(), calls=%async_computation.16 | async-start | bytes 4423680 | tf_op jit(solution)/shard_map/reduce_scatter | solution.py:108
  415.0 35.3 %collective-permute-start.20 = (bf16[768,1536]{1,0:T(8,128)(2,1)}, bf16[768,1536]{1,0:T(8,128)(2,1)}, u32[]{:S(2)}, u32[]{:S(2)}) collective-permute-start(bf16[768,1536]{1,0:T(8,128)(2,1)} %pad_maximum_fusion.3), channel_id=1, source_target_pairs={{0,2},{2,0},{1,3},{3,1},{4,6},{6,4},{5,7},{7,5},{8,10},{10,8},{9,1... | collective-permute-start | bytes 7077896 | tf_op jit(solution)/shard_map/ppermute | solution.py:58
  441.4 25.0 %collective-permute-start.22 = (bf16[4,1,1,384,256]{4,3,2,1,0:T(8,128)(2,1)}, bf16[4,1,1,384,256]{4,3,2,1,0:T(8,128)(2,1)}, u32[]{:S(2)}, u32[]{:S(2)}) collective-permute-start(bf16[4,1,1,384,256]{4,3,2,1,0:T(8,128)(2,1)} %constant_dynamic-slice_fusion.6), channel_id=1, source_target_pairs={{0,4},{4,0},{1,5},{5,1},{2,6},{6,2},{3,7},{7,3},{8,12},{12,8},{9,1... | collective-permute-start | bytes 2359304 | tf_op jit(solution)/shard_map/ppermute | solution.py:58
  472.1 49.6 %collective-permute-start.28 = (bf16[4,2,1,96,1536]{4,3,2,1,0:T(8,128)(2,1)}, bf16[4,2,1,96,1536]{4,3,2,1,0:T(8,128)(2,1)}, u32[]{:S(2)}, u32[]{:S(2)}) collective-permute-start(bf16[4,2,1,96,1536]{4,3,2,1,0:T(8,128)(2,1)} %constant_dynamic-slice_fusion.3), channel_id=1, source_target_pairs={{0,2},{2,0},{1,3},{3,1},{4,6},{6,4},{5,7},{7,5},{8,10},{10,8},{9,1... | collective-permute-start | bytes 7077896 | tf_op jit(solution)/shard_map/ppermute | solution.py:58
  473.9 33.0 %collective-permute-start.26 = (bf16[2,1,384,256]{3,2,1,0:T(8,128)(2,1)}, bf16[2,1,384,256]{3,2,1,0:T(8,128)(2,1)}, u32[]{:S(2)}, u32[]{:S(2)}) collective-permute-start(bf16[2,1,384,256]{3,2,1,0:T(8,128)(2,1)} %constant_dynamic-slice_fusion.5), channel_id=1, source_target_pairs={{0,8},{8,0},{16,24},{24,16},{1,9},{9,1},{17,25},{25,17},{2,10},{10... | collective-permute-start | bytes 1179656 | tf_op jit(solution)/shard_map/ppermute | solution.py:153
  480.8 32.1 %collective-permute-start.25 = (bf16[384,1536]{1,0:T(8,128)(2,1)}, bf16[384,1536]{1,0:T(8,128)(2,1)}, u32[]{:S(2)}, u32[]{:S(2)}) collective-permute-start(bf16[384,1536]{1,0:T(8,128)(2,1)} %convolution_convert_fusion.5), channel_id=1, source_target_pairs={{0,1},{1,0},{2,3},{3,2},{4,5},{5,4},{6,7},{7,6},{8,9},{9,8},{10,11... | collective-permute-start | bytes 3538952 | tf_op jit(solution)/shard_map/ppermute | solution.py:58
  482.3 37.6 %collective-permute-start.23 = (bf16[384,1536]{1,0:T(8,128)(2,1)}, bf16[384,1536]{1,0:T(8,128)(2,1)}, u32[]{:S(2)}, u32[]{:S(2)}) collective-permute-start(bf16[384,1536]{1,0:T(8,128)(2,1)} %fusion.13), channel_id=1, source_target_pairs={{0,4},{4,0},{1,5},{5,1},{2,6},{6,2},{3,7},{7,3},{8,12},{12,8},{9,1... | collective-permute-start | bytes 3538952 | tf_op jit(solution)/shard_map/ppermute | solution.py:58
  484.0 35.9 %all-to-all-start.4 = ((bf16[4,96,1120]{2,1,0:T(8,128)(2,1)}), bf16[4,96,1120]{2,1,0:T(8,128)(2,1)}, u32[]{:S(2)}, u32[]{:S(2)}) async-start(bf16[4,96,1120]{2,1,0:T(8,128)(2,1)} %bitcast.147), calls=%async_computation.6 | async-start | bytes 1769472 | tf_op jit(solution)/shard_map/all_to_all | solution.py:114
  488.3 136.2 %reduce-scatter.11.cloned.1.call-start = ((), (), s32[]{:S(2)}) async-start(), calls=%async_computation.17 | async-start | bytes 1843200 | tf_op jit(solution)/shard_map/reduce_scatter | solution.py:108
  527.3 28.0 %collective-permute-start.30 = (bf16[4,1,1,96,1536]{4,3,2,1,0:T(8,128)(2,1)}, bf16[4,1,1,96,1536]{4,3,2,1,0:T(8,128)(2,1)}, u32[]{:S(2)}, u32[]{:S(2)}) collective-permute-start(bf16[4,1,1,96,1536]{4,3,2,1,0:T(8,128)(2,1)} %constant_dynamic-slice_fusion.1), channel_id=1, source_target_pairs={{0,4},{4,0},{1,5},{5,1},{2,6},{6,2},{3,7},{7,3},{8,12},{12,8},{9,1... | collective-permute-start | bytes 3538952 | tf_op jit(solution)/shard_map/ppermute | solution.py:58
  573.6 28.1 %collective-permute-start.24 = (bf16[384,1536]{1,0:T(8,128)(2,1)}, bf16[384,1536]{1,0:T(8,128)(2,1)}, u32[]{:S(2)}, u32[]{:S(2)}) collective-permute-start(bf16[384,1536]{1,0:T(8,128)(2,1)} %fusion.15), channel_id=1, source_target_pairs={{0,1},{1,0},{2,3},{3,2},{4,5},{5,4},{6,7},{7,6},{8,9},{9,8},{10,11... | collective-permute-start | bytes 3538952 | tf_op jit(solution)/shard_map/ppermute | solution.py:58
  (76 other events, 726.7 us)
Sparse Core Ops, SparseCore 0:
  10.1 35.1 all-gather.4
  50.0 82.9 all-gather.6
  135.2 68.5 all-gather.8
  222.1 72.9 all-gather.10
  297.3 65.0 reduce-scatter.4
  364.6 66.6 reduce-scatter.6
  433.6 75.0 reduce-scatter.8
  578.0 37.1 reduce-scatter.10

commit v12 on v11

--- a/solution.py
+++ b/solution.py
@@ -481,11 +481,11 @@
     key_value_sums = scatter_across(
         key_value_halves, gate_sums, square_grads, grad_query_mine, down_across
     )
-    down_came = other(after(down_across, key_value_sums), "x")
     gate_parts = undeal(after(gate_sums, key_value_sums))
     square_halves = scatter_core(after(square_grads, key_value_sums), features)
-    key_value_grads = halve_z(key_value_sums, rows, (key_value_sums,), (query_came, gate_parts, down_came))
+    key_value_grads = halve_z(key_value_sums, rows, (key_value_sums,), (query_came, gate_parts, square_halves[1]))
     square_sums = scatter_across(square_halves)
+    down_came = other(after(down_across, square_halves[1]), "x")
     key_value_grads = after(key_value_grads, up_sums)
     grad_key_pre = low(
         rotate_halves(key_value_grads[:, :head].reshape(rows, 1, head), cosine_table, -sine_table)
@@ -495,7 +495,7 @@
     grad_project = jnp.concatenate([grad_query_pre, grad_pair], axis=1)
     grad_bias = jnp.sum(grad_project.astype(jnp.float32), axis=0)
     pair_both = in_order(grad_pair, other(grad_pair, "y"))
-    query_came = after(query_came, grad_pair, square_halves[0])
+    query_came = after(query_came, grad_pair)
     grad_normed_one = (
         grad_query_mine.astype(jnp.float32) + query_came.astype(jnp.float32)
     ) + product_right(
@@ -530,7 +530,7 @@
     packed_halves = other_half(
         packed_grads.reshape(-1, 2, 2, features, packed_grads.shape[1]), "c", 2
     )
-    packed_grads = scatter_across(other_half(add_half(packed_halves, square_sums), "x", 1))
+    packed_grads = scatter_across(other_half(add_half(packed_halves, down_came), "x", 1))
     up_parts = undeal(after(up_sums, packed_halves[1]))
     last_grads = scatter_z(jnp.concatenate([square_sums, packed_grads], axis=1)).astype(jnp.float32)
     square_grads = last_grads[:, : 2 * heads_width]

time: 649 us -> 655 us (level)
  waiting for transfers between devices: 210 us -> 181 us
  blocking collectives: 64.3 us -> 80.3 us
  starting transfers between devices: 58.1 us -> 70.8 us
  Pallas kernels: 15.1 us -> 26.6 us
    ppermute x31, waiting for transfers between devices: 132 us -> 112 us  [other(): return lax.ppermute(value, axis, [(0, 1), (1, 0)])]
    all_to_all x0 -> x1, blocking collectives: none -> 16 us  [undeal(): return lax.all_to_all(parts, GROUP, split_axis=0, concat_axis=0, tiled=True)]
    all_to_all x3 -> x2, waiting for transfers between devices: 20.7 us -> 6.03 us  [undeal(): return lax.all_to_all(parts, GROUP, split_axis=0, concat_axis=0, tiled=True)]
    ppermute x2, starting transfers between devices: 6.92 us -> 18.3 us  [halve_z(): lax.ppermute(sent, 'z', [(number, number ^ step) for number in range(high)])]
    pallas_call x1, Pallas kernels: 6.5 us -> 17.5 us  [attend(): pl.pallas_call(attend_kernel, out_shape=(jax.ShapeDtypeStruct((rows, wide...]
    all_gather x4, waiting for transfers between devices: 29.4 us -> 37.6 us  [gather_z(): return lax.all_gather(own, 'z', axis=0, tiled=True)]
    unnamed x129 -> x143, local copies, waits for them, and re-layouts: 19.5 us -> 19.2 us
  transfers between devices with their start and end apart: 46 -> 45, of which waited for: 24 -> 19; matrix products, arithmetic and copies ran while one was open for 37% -> 37% of each run, Pallas kernels for 2% -> 4%
where the time goes in v12:
time: 655 us; the launch traced here: 649 us
  waiting for transfers between devices  181 us (28%)
  matrix products  120 us (18%)
  local copies, waits for them, and re-layouts  82.1 us (13%)
  blocking collectives  80.3 us (12%)
  starting transfers between devices  70.8 us (11%)
  other arithmetic  70.6 us (11%)
  Pallas kernels  26.6 us (4%)
  between operations  17.5 us (3%)
    ppermute x31, waiting for transfers between devices, other(): return lax.ppermute(value, axis, [(0, 1), (1, 0)])  112 us
    dot_general x9, matrix products, product(): return jnp.dot(left, right, preferred_element_type=jnp.float32)  75 us
    all_gather x2, blocking collectives, gather_z(): return lax.all_gather(own, 'z', axis=0, tiled=True)  48.3 us
    dot_general x6, matrix products, product_right(): lax.dot_general(left, right, (((1,), (1,)), ((), ())), preferred_element_...  38.2 us
    all_gather x4, waiting for transfers between devices, gather_z(): return lax.all_gather(own, 'z', axis=0, tiled=True)  37.6 us
    ppermute x31, starting transfers between devices, other(): return lax.ppermute(value, axis, [(0, 1), (1, 0)])  35.2 us
    convert_element_type x15, other arithmetic, low(): return value.astype(jnp.bfloat16)  31.7 us
    ppermute x2, waiting for transfers between devices, halve_z(): lax.ppermute(sent, 'z', [(number, number ^ step) for number in range(high)])  19.5 us
  transfers between devices with their start and end apart: 45, of which 19 were waited for; matrix products, arithmetic and copies ran while one was open for 37% of the time, Pallas kernels for 4%

profile of v12, /device:TPU:0, one launch (start us, length us, event | category | flops | bytes accessed | tf_op | source)
XLA Modules:
  0.0 648.6 jit_solution(17904718547235352394)
XLA Ops:
  13.3 17.9 %all_gather.18 = bf16[384,384]{1,0:T(8,128)(2,1)S(1)} all-gather(bf16[96,384]{1,0:T(8,128)(2,1)S(1)} %pad_maximum_fusion.10), channel_id=1, replica_groups=mesh['z'=4,'x'=2,'c'=2,'y'=2] {'z'}, dimensions={0}, use_global_device_ids=true | all-gather | bytes 368640 | tf_op jit(solution)/shard_map/all_gather | solution.py:104
  33.9 15.9 %all_to_all.30 = bf16[4,96,1120]{2,1,0:T(8,128)(2,1)} all-to-all(bf16[4,96,1120]{2,1,0:T(8,128)(2,1)S(1)} %bitcast.129), channel_id=1, replica_groups=mesh['z'=4,'x'=2,'c'=2,'y'=2] {'x','c'}, dimensions={0} | all-to-all | bytes 1720320 | tf_op jit(solution)/shard_map/all_to_all | solution.py:99
  52.3 6.1 collective-permute-done.1
  72.0 30.4 %all_gather.20 = bf16[1536,256]{1,0:T(8,128)(2,1)} all-gather(bf16[384,256]{1,0:T(8,128)(2,1)S(1)} %pad_maximum_fusion.8), channel_id=1, replica_groups=mesh['z'=4,'x'=2,'c'=2,'y'=2] {'z'}, dimensions={0}, use_global_device_ids=true | all-gather | bytes 983040 | tf_op jit(solution)/shard_map/all_gather | solution.py:104
  115.2 8.3 %collective-permute-done.7 = bf16[4,1,1,384,256]{4,3,2,1,0:T(8,128)(2,1)} collective-permute-done((bf16[4,1,1,384,256]{4,3,2,1,0:T(8,128)(2,1)}, bf16[4,1,1,384,256]{4,3,2,1,0:T(8,128)(2,1)}, u32[]{:S(2)}, u32[]{:S(2)}) %collective-permute-start.7) | collective-permute-done | bytes 786464 | tf_op jit(solution)/shard_map/ppermute | solution.py:58
  142.1 17.5 %attend.1 = (bf16[384,768]{1,0:T(8,128)(2,1)}, f32[384,768]{1,0:T(8,128)}, f32[8,384]{1,0:T(8,128)}) custom-call(s32[2]{0:T(128)} %pad_add_fusion.bounds_ref, f32[384,768]{1,0:T(8,128)} %fusion.32.query_ref, f32[384,128]{1,0:T(8,128)} %get-tuple-element.127.cosine_ref, f32[384,128]{1,0:T(8,128)} %get-tuple-element.128.sine_ref, ...), custom_call_target="tpu_custom_call" | custom-call | flops 4076863488 | bytes 20971520 | tf_op jit(solution)/shard_map/attend/pallas_call | solution.py:295
  173.1 19.9 %collective-permute-done.10 = bf16[384,1536]{1,0:T(8,128)(2,1)S(1)} collective-permute-done((bf16[384,1536]{1,0:T(8,128)(2,1)S(1)}, bf16[384,1536]{1,0:T(8,128)(2,1)S(1)}, u32[]{:S(2)}, u32[]{:S(2)}) %collective-permute-start.10) | collective-permute-done | bytes 1179680 | tf_op jit(solution)/shard_map/ppermute | solution.py:58
  200.1 25.4 %collective-permute-done.15 = bf16[384,1536]{1,0:T(8,128)(2,1)S(1)} collective-permute-done((bf16[384,1536]{1,0:T(8,128)(2,1)S(1)}, bf16[384,1536]{1,0:T(8,128)(2,1)S(1)}, u32[]{:S(2)}, u32[]{:S(2)}) %collective-permute-start.15) | collective-permute-done | bytes 1179680 | tf_op jit(solution)/shard_map/ppermute | solution.py:58
  228.5 11.3 %fusion.76 = f32[1536,1120]{0,1:T(8,128)} fusion(bf16[1536,1120]{1,0:T(8,128)(2,1)} %all-gather.7.cloned.1.call-done, bf16[384,1536]{1,0:T(8,128)(2,1)} %collective-permute-done.16, bf16[384,1536]{1,0:T(8,128)(2,1)S(1)} %collective-permute-done.15, bf16[384,1536]{1,0:T(8,128)(2,1)S(1)} %collective-permute-done.14, ...), kind=kOutput, calls=%fused_computation.182 | convolution fusion | flops 5303697408 | bytes 15040512 | tf_op jit(solution)/shard_map/dot_general | solution.py:17
  243.6 13.6 %multiply_convert_fusion.2 = (bf16[1536,1120]{0,1:T(8,128)(2,1)S(1)}, f32[1536,1120]{0,1:T(8,128)}) fusion(f32[1536,1120]{0,1:T(8,128)} %fusion.76, bf16[1536,1120]{1,0:T(8,128)(2,1)} %all-gather.9.cloned.1.call-done, bf16[384,1536]{1,0:T(8,128)(2,1)} %collective-permute-done.16, bf16[384,1536]{1,0:T(8,128)(2,1)S(1)} %collective-permute-done.15, ...), kind=kOutput, calls=%fused_computation.6 | convolution fusion | flops 5314019328 | bytes 25362432 | tf_op jit(solution)/shard_map/dot_general | solution.py:17
  258.9 9.4 %convolution_convert_fusion.2 = bf16[1536,1120]{1,0:T(8,128)(2,1)} fusion(bf16[1536,1536]{0,1:T(8,128)(2,1)} %bitcast.151, bf16[1536,1120]{0,1:T(8,128)(2,1)S(1)} %get-tuple-element.62), kind=kOutput, calls=%fused_computation.3 | convolution fusion | flops 5286543360 | bytes 11599872 | tf_op jit(solution)/shard_map/dot_general | solution.py:17
  268.8 37.5 %all-gather.11.cloned.1.call-done = bf16[1536,1120]{1,0:T(8,128)(2,1)} async-done(((bf16[384,1120]{1,0:T(8,128)(2,1)}), bf16[1536,1120]{1,0:T(8,128)(2,1)}) %all-gather.11.cloned.1.call-update) | async-done | bytes 3440656 | tf_op jit(solution)/shard_map/all_gather | solution.py:104
  306.3 15.0 %multiply_convert_fusion = (bf16[1536,1120]{0,1:T(8,128)(2,1)S(1)}, bf16[1536,1120]{0,1:T(8,128)(2,1)}) fusion(f32[1536,1120]{0,1:T(8,128)} %fusion.76, f32[1536,1120]{0,1:T(8,128)} %get-tuple-element.123, bf16[1536,1536]{1,0:T(8,128)(2,1)} %copy-done.40, bf16[1536,1120]{1,0:T(8,128)(2,1)} %all-gather.11.cloned.1.call-done), kind=kOutput, calls=%fused_computation.4 | convolution fusion | flops 5307187200 | bytes 28803072 | tf_op jit(solution)/shard_map/dot_general | solution.py:17
  321.4 8.9 %fusion.86 = f32[1536,1536]{1,0:T(8,128)} fusion(bf16[1536,1120]{0,1:T(8,128)(2,1)S(1)} %get-tuple-element.60, bf16[1536,1120]{1,0:T(8,128)(2,1)S(1)} %copy-done.56), kind=kOutput, calls=%fused_computation.192 | convolution fusion | flops 5284823040 | bytes 16318464 | tf_op jit(solution)/shard_map/dot_general | solution.py:27
  330.3 10.2 %fusion.85 = (bf16[1536,1536]{1,0:T(8,128)(2,1)S(1)}, f32[1536,1536]{1,0:T(8,128)S(1)}) fusion(f32[1536,1536]{1,0:T(8,128)} %fusion.86, bf16[1536,1120]{0,1:T(8,128)(2,1)} %get-tuple-element.61, bf16[1536,1120]{1,0:T(8,128)(2,1)S(1)} %copy-done.57), kind=kOutput, calls=%fused_computation.191 | convolution fusion | flops 5289541632 | bytes 30474240 | tf_op jit(solution)/shard_map/dot_general | solution.py:27
  349.9 7.9 %convolution_convert_fusion.1 = bf16[1536,1120]{1,0:T(8,128)(2,1)} fusion(bf16[1536,1536]{0,1:T(8,128)(2,1)S(1)} %bitcast.117, bf16[1536,1120]{0,1:T(8,128)(2,1)S(1)} %copy-done.62), kind=kOutput, calls=%fused_computation.2 | convolution fusion | flops 5286543360 | bytes 11599872 | tf_op jit(solution)/shard_map/dot_general | solution.py:17
  357.9 10.6 %convolution_convert_fusion = bf16[1536,1120]{1,0:T(8,128)(2,1)} fusion(bf16[1536,1536]{0,1:T(8,128)(2,1)} %fusion.75, bf16[1536,1120]{0,1:T(8,128)(2,1)} %get-tuple-element.61), kind=kOutput, calls=%fused_computation.1 | convolution fusion | flops 5286543360 | bytes 11599872 | tf_op jit(solution)/shard_map/dot_general | solution.py:17
  368.5 5.1 reduce-scatter.5.cloned.1.call-done
  373.6 9.4 %fusion.87 = f32[1536,1536]{1,0:T(8,128)S(1)} fusion(bf16[1536,1120]{0,1:T(8,128)(2,1)} %copy-done.60, bf16[1536,1120]{1,0:T(8,128)(2,1)} %all-gather.11.cloned.1.call-done), kind=kOutput, calls=%fused_computation.193 | convolution fusion | flops 5284823040 | bytes 16318464 | tf_op jit(solution)/shard_map/dot_general | solution.py:27
  383.1 6.4 fusion.17
  391.1 16.0 %all_to_all.31 = bf16[4,96,1120]{2,1,0:T(8,128)(2,1)} all-to-all(bf16[4,96,1120]{2,1,0:T(8,128)(2,1)S(1)} %bitcast.148), channel_id=1, replica_groups=mesh['z'=4,'x'=2,'c'=2,'y'=2] {'x','c'}, dimensions={0} | all-to-all | bytes 1720320 | tf_op jit(solution)/shard_map/all_to_all | solution.py:114
  407.1 9.8 %collective-permute-done.19 = bf16[384,1536]{1,0:T(8,128)(2,1)S(1)} collective-permute-done((bf16[384,1536]{1,0:T(8,128)(2,1)S(1)}, bf16[384,1536]{1,0:T(8,128)(2,1)S(1)}, u32[]{:S(2)}, u32[]{:S(2)}) %collective-permute-start.19) | collective-permute-done | bytes 1179680 | tf_op jit(solution)/shard_map/ppermute | solution.py:58
  425.3 9.0 %attend_back.1 = (bf16[384,768]{1,0:T(8,128)(2,1)}, bf16[6144,256]{1,0:T(8,128)(2,1)}) custom-call(s32[2]{0:T(128)} %pad_add_fusion.bounds_ref, bf16[384,768]{1,0:T(8,128)(2,1)} %get-tuple-element.67.rotated_ref, f32[384,768]{1,0:T(8,128)} %fusion.20.grad_ref, f32[384,768]{1,0:T(8,128)} %get-tuple-element.55.attended_ref, ...), custom_call_target="tpu_custom_call" | custom-call | flops 294912 | bytes 294912 | tf_op jit(solution)/shard_map/attend_back/pallas_call | solution.py:314
  449.7 6.7 %collective-permute-start.22 = (bf16[4,1,1,384,256]{4,3,2,1,0:T(8,128)(2,1)}, bf16[4,1,1,384,256]{4,3,2,1,0:T(8,128)(2,1)}, u32[]{:S(2)}, u32[]{:S(2)}) collective-permute-start(bf16[4,1,1,384,256]{4,3,2,1,0:T(8,128)(2,1)} %constant_dynamic-slice_fusion.5), channel_id=1, source_target_pairs={{0,4},{4,0},{1,5},{5,1},{2,6},{6,2},{3,7},{7,3},{8,12},{12,8},{9,1... | collective-permute-start | bytes 2359304 | tf_op jit(solution)/shard_map/ppermute | solution.py:58
  466.6 8.0 %collective-permute-done.22 = bf16[4,1,1,384,256]{4,3,2,1,0:T(8,128)(2,1)} collective-permute-done((bf16[4,1,1,384,256]{4,3,2,1,0:T(8,128)(2,1)}, bf16[4,1,1,384,256]{4,3,2,1,0:T(8,128)(2,1)}, u32[]{:S(2)}, u32[]{:S(2)}) %collective-permute-start.22) | collective-permute-done | bytes 786464 | tf_op jit(solution)/shard_map/ppermute | solution.py:58
  484.1 9.1 %collective-permute-start.28 = (bf16[2,1,384,256]{3,2,1,0:T(8,128)(2,1)}, bf16[2,1,384,256]{3,2,1,0:T(8,128)(2,1)}, u32[]{:S(2)}, u32[]{:S(2)}) collective-permute-start(bf16[2,1,384,256]{3,2,1,0:T(8,128)(2,1)} %constant_dynamic-slice_fusion.2), channel_id=1, source_target_pairs={{0,8},{8,0},{16,24},{24,16},{1,9},{9,1},{17,25},{25,17},{2,10},{10... | collective-permute-start | bytes 1179656 | tf_op jit(solution)/shard_map/ppermute | solution.py:153
  505.1 14.1 %collective-permute-done.28 = bf16[2,1,384,256]{3,2,1,0:T(8,128)(2,1)} collective-permute-done((bf16[2,1,384,256]{3,2,1,0:T(8,128)(2,1)}, bf16[2,1,384,256]{3,2,1,0:T(8,128)(2,1)}, u32[]{:S(2)}, u32[]{:S(2)}) %collective-permute-start.28) | collective-permute-done | bytes 393248 | tf_op jit(solution)/shard_map/ppermute | solution.py:153
  521.9 9.1 %collective-permute-start.29 = (bf16[1,1,384,256]{3,2,1,0:T(8,128)(2,1)}, bf16[1,1,384,256]{3,2,1,0:T(8,128)(2,1)}, u32[]{:S(2)}, u32[]{:S(2)}) collective-permute-start(bf16[1,1,384,256]{3,2,1,0:T(8,128)(2,1)} %constant_dynamic-slice_fusion.1), channel_id=1, source_target_pairs={{0,16},{8,24},{16,0},{24,8},{1,17},{9,25},{17,1},{25,9},{2,18},{10... | collective-permute-start | bytes 589832 | tf_op jit(solution)/shard_map/ppermute | solution.py:153
  534.3 5.4 collective-permute-done.29
  570.0 8.3 %collective-permute-done.25 = bf16[384,1536]{1,0:T(8,128)(2,1)} collective-permute-done((bf16[384,1536]{1,0:T(8,128)(2,1)}, bf16[384,1536]{1,0:T(8,128)(2,1)}, u32[]{:S(2)}, u32[]{:S(2)}) %collective-permute-start.25) | collective-permute-done | bytes 1179680 | tf_op jit(solution)/shard_map/ppermute | solution.py:58
  605.7 6.0 all-to-all-done.5
  618.4 13.8 %collective-permute-done.26 = bf16[384,1536]{1,0:T(8,128)(2,1)} collective-permute-done((bf16[384,1536]{1,0:T(8,128)(2,1)}, bf16[384,1536]{1,0:T(8,128)(2,1)}, u32[]{:S(2)}, u32[]{:S(2)}) %collective-permute-start.26) | collective-permute-done | bytes 1179680 | tf_op jit(solution)/shard_map/ppermute | solution.py:58
  (370 shorter events, 228.7 us)
Async XLA Ops:
  7.2 60.9 %all-gather.5.cloned.1.call-start = ((), (), s32[]{:S(2)}) async-start(), calls=%async_computation.10 | async-start | bytes 1474560 | tf_op jit(solution)/shard_map/all_gather | solution.py:104
  9.0 216.7 %all-gather.7.cloned.1.call-start = ((), (), s32[]{:S(2)}) async-start(), calls=%async_computation.11 | async-start | bytes 4423680 | tf_op jit(solution)/shard_map/all_gather | solution.py:104
  64.5 37.9 %all-to-all-start.1 = ((bf16[4,96,1120]{2,1,0:T(8,128)(2,1)}), bf16[4,96,1120]{2,1,0:T(8,128)(2,1)S(1)}, u32[]{:S(2)}, u32[]{:S(2)}) async-start(bf16[4,96,1120]{2,1,0:T(8,128)(2,1)} %bitcast.105), calls=%async_computation.1 | async-start | bytes 1769472 | tf_op jit(solution)/shard_map/all_to_all | solution.py:99
  68.0 175.6 %all-gather.9.cloned.1.call-start = ((), (), s32[]{:S(2)}) async-start(), calls=%async_computation.12 | async-start | bytes 4423680 | tf_op jit(solution)/shard_map/all_gather | solution.py:104
  68.1 55.4 %collective-permute-start.4 = (bf16[4,1,1,96,1536]{4,3,2,1,0:T(8,128)(2,1)}, bf16[4,1,1,96,1536]{4,3,2,1,0:T(8,128)(2,1)}, u32[]{:S(2)}, u32[]{:S(2)}) collective-permute-start(bf16[4,1,1,96,1536]{4,3,2,1,0:T(8,128)(2,1)} %bitcast.140), channel_id=1, source_target_pairs={{0,4},{4,0},{1,5},{5,1},{2,6},{6,2},{3,7},{7,3},{8,12},{12,8},{9,1... | collective-permute-start | bytes 3538952 | tf_op jit(solution)/shard_map/ppermute | solution.py:58
  102.4 21.1 %collective-permute-start.7 = (bf16[4,1,1,384,256]{4,3,2,1,0:T(8,128)(2,1)}, bf16[4,1,1,384,256]{4,3,2,1,0:T(8,128)(2,1)}, u32[]{:S(2)}, u32[]{:S(2)}) collective-permute-start(bf16[4,1,1,384,256]{4,3,2,1,0:T(8,128)(2,1)} %bitcast.22), channel_id=1, source_target_pairs={{0,4},{4,0},{1,5},{5,1},{2,6},{6,2},{3,7},{7,3},{8,12},{12,8},{9,1... | collective-permute-start | bytes 2359304 | tf_op jit(solution)/shard_map/ppermute | solution.py:58
  103.5 25.0 %collective-permute-start.3 = (bf16[4,1,1,96,1536]{4,3,2,1,0:T(8,128)(2,1)}, bf16[4,1,1,96,1536]{4,3,2,1,0:T(8,128)(2,1)}, u32[]{:S(2)}, u32[]{:S(2)}) collective-permute-start(bf16[4,1,1,96,1536]{4,3,2,1,0:T(8,128)(2,1)} %bitcast.141), channel_id=1, source_target_pairs={{0,2},{2,0},{1,3},{3,1},{4,6},{6,4},{5,7},{7,5},{8,10},{10,8},{9,1... | collective-permute-start | bytes 3538952 | tf_op jit(solution)/shard_map/ppermute | solution.py:58
  103.6 22.5 %collective-permute-start.6 = (bf16[4,1,1,384,256]{4,3,2,1,0:T(8,128)(2,1)}, bf16[4,1,1,384,256]{4,3,2,1,0:T(8,128)(2,1)}, u32[]{:S(2)}, u32[]{:S(2)}) collective-permute-start(bf16[4,1,1,384,256]{4,3,2,1,0:T(8,128)(2,1)} %bitcast.22), channel_id=1, source_target_pairs={{0,2},{2,0},{1,3},{3,1},{4,6},{6,4},{5,7},{7,5},{8,10},{10,8},{9,1... | collective-permute-start | bytes 2359304 | tf_op jit(solution)/shard_map/ppermute | solution.py:58
  107.6 24.4 %collective-permute-start.9 = (bf16[1536,256]{1,0:T(8,128)(2,1)}, bf16[1536,256]{1,0:T(8,128)(2,1)}, u32[]{:S(2)}, u32[]{:S(2)}) collective-permute-start(bf16[1536,256]{1,0:T(8,128)(2,1)} %slice.228), channel_id=1, source_target_pairs={{0,1},{1,0},{2,3},{3,2},{4,5},{5,4},{6,7},{7,6},{8,9},{9,8},{10,11... | collective-permute-start | bytes 2359304 | tf_op jit(solution)/shard_map/ppermute | solution.py:58
  110.9 21.5 %all-to-all-start.2 = ((bf16[4,96,1120]{2,1,0:T(8,128)(2,1)}), bf16[4,96,1120]{2,1,0:T(8,128)(2,1)}, u32[]{:S(2)}, u32[]{:S(2)}) async-start(bf16[4,96,1120]{2,1,0:T(8,128)(2,1)} %bitcast.104), calls=%async_computation.2 | async-start | bytes 1769472 | tf_op jit(solution)/shard_map/all_to_all | solution.py:99
  115.1 191.2 %all-gather.11.cloned.1.call-start = ((), (), s32[]{:S(2)}) async-start(), calls=%async_computation.13 | async-start | bytes 4423680 | tf_op jit(solution)/shard_map/all_gather | solution.py:104
  132.4 27.9 %collective-permute-start.12 = (bf16[384,1536]{1,0:T(8,128)(2,1)}, bf16[384,1536]{1,0:T(8,128)(2,1)}, u32[]{:S(2)}, u32[]{:S(2)}) collective-permute-start(bf16[384,1536]{1,0:T(8,128)(2,1)} %param.29), channel_id=1, source_target_pairs={{0,4},{4,0},{1,5},{5,1},{2,6},{6,2},{3,7},{7,3},{8,12},{12,8},{9,1... | collective-permute-start | bytes 3538952 | tf_op jit(solution)/shard_map/ppermute | solution.py:58
  135.8 32.3 %collective-permute-start.11 = (bf16[384,1536]{1,0:T(8,128)(2,1)}, bf16[384,1536]{1,0:T(8,128)(2,1)}, u32[]{:S(2)}, u32[]{:S(2)}) collective-permute-start(bf16[384,1536]{1,0:T(8,128)(2,1)} %param.29), channel_id=1, source_target_pairs={{0,2},{2,0},{1,3},{3,1},{4,6},{6,4},{5,7},{7,5},{8,10},{10,8},{9,1... | collective-permute-start | bytes 3538952 | tf_op jit(solution)/shard_map/ppermute | solution.py:58
  165.1 27.9 %collective-permute-start.10 = (bf16[384,1536]{1,0:T(8,128)(2,1)S(1)}, bf16[384,1536]{1,0:T(8,128)(2,1)S(1)}, u32[]{:S(2)}, u32[]{:S(2)}) collective-permute-start(bf16[384,1536]{1,0:T(8,128)(2,1)S(1)} %convolution_convert_fusion.6), channel_id=1, source_target_pairs={{0,1},{1,0},{2,3},{3,2},{4,5},{5,4},{6,7},{7,6},{8,9},{9,8},{10,11... | collective-permute-start | bytes 3538952 | tf_op jit(solution)/shard_map/ppermute | solution.py:58
  195.5 30.1 %collective-permute-start.15 = (bf16[384,1536]{1,0:T(8,128)(2,1)S(1)}, bf16[384,1536]{1,0:T(8,128)(2,1)S(1)}, u32[]{:S(2)}, u32[]{:S(2)}) collective-permute-start(bf16[384,1536]{1,0:T(8,128)(2,1)S(1)} %multiply_convert_fusion.3), channel_id=1, source_target_pairs={{0,4},{4,0},{1,5},{5,1},{2,6},{6,2},{3,7},{7,3},{8,12},{12,8},{9,1... | collective-permute-start | bytes 3538952 | tf_op jit(solution)/shard_map/ppermute | solution.py:58
  200.1 25.5 %collective-permute-start.14 = (bf16[384,1536]{1,0:T(8,128)(2,1)S(1)}, bf16[384,1536]{1,0:T(8,128)(2,1)S(1)}, u32[]{:S(2)}, u32[]{:S(2)}) collective-permute-start(bf16[384,1536]{1,0:T(8,128)(2,1)S(1)} %multiply_convert_fusion.3), channel_id=1, source_target_pairs={{0,2},{2,0},{1,3},{3,1},{4,6},{6,4},{5,7},{7,5},{8,10},{10,8},{9,1... | collective-permute-start | bytes 3538952 | tf_op jit(solution)/shard_map/ppermute | solution.py:58
  225.6 148.0 %reduce-scatter.5.cloned.1.call-start = ((), (), s32[]{:S(2)}) async-start(), calls=%async_computation.14 | async-start | bytes 4423680 | tf_op jit(solution)/shard_map/reduce_scatter | solution.py:108
  268.3 198.3 %reduce-scatter.7.cloned.1.call-start = ((), (), s32[]{:S(2)}) async-start(), calls=%async_computation.15 | async-start | bytes 4423680 | tf_op jit(solution)/shard_map/reduce_scatter | solution.py:108
  348.5 34.6 %collective-permute-start.18 = (bf16[384,1536]{1,0:T(8,128)(2,1)S(1)}, bf16[384,1536]{1,0:T(8,128)(2,1)S(1)}, u32[]{:S(2)}, u32[]{:S(2)}) collective-permute-start(bf16[384,1536]{1,0:T(8,128)(2,1)S(1)} %fusion.18), channel_id=1, source_target_pairs={{0,4},{4,0},{1,5},{5,1},{2,6},{6,2},{3,7},{7,3},{8,12},{12,8},{9,1... | collective-permute-start | bytes 3538952 | tf_op jit(solution)/shard_map/ppermute | solution.py:58
  357.9 183.6 %reduce-scatter.9.cloned.1.call-start = ((), (), s32[]{:S(2)}) async-start(), calls=%async_computation.16 | async-start | bytes 4423680 | tf_op jit(solution)/shard_map/reduce_scatter | solution.py:108
  389.5 27.4 %collective-permute-start.19 = (bf16[384,1536]{1,0:T(8,128)(2,1)S(1)}, bf16[384,1536]{1,0:T(8,128)(2,1)S(1)}, u32[]{:S(2)}, u32[]{:S(2)}) collective-permute-start(bf16[384,1536]{1,0:T(8,128)(2,1)S(1)} %fusion.17), channel_id=1, source_target_pairs={{0,1},{1,0},{2,3},{3,2},{4,5},{5,4},{6,7},{7,6},{8,9},{9,8},{10,11... | collective-permute-start | bytes 3538952 | tf_op jit(solution)/shard_map/ppermute | solution.py:58
  419.3 39.2 %collective-permute-start.20 = (bf16[768,1536]{1,0:T(8,128)(2,1)}, bf16[768,1536]{1,0:T(8,128)(2,1)}, u32[]{:S(2)}, u32[]{:S(2)}) collective-permute-start(bf16[768,1536]{1,0:T(8,128)(2,1)} %pad_maximum_fusion.3), channel_id=1, source_target_pairs={{0,2},{2,0},{1,3},{3,1},{4,6},{6,4},{5,7},{7,5},{8,10},{10,8},{9,1... | collective-permute-start | bytes 7077896 | tf_op jit(solution)/shard_map/ppermute | solution.py:58
  449.7 24.9 %collective-permute-start.22 = (bf16[4,1,1,384,256]{4,3,2,1,0:T(8,128)(2,1)}, bf16[4,1,1,384,256]{4,3,2,1,0:T(8,128)(2,1)}, u32[]{:S(2)}, u32[]{:S(2)}) collective-permute-start(bf16[4,1,1,384,256]{4,3,2,1,0:T(8,128)(2,1)} %constant_dynamic-slice_fusion.5), channel_id=1, source_target_pairs={{0,4},{4,0},{1,5},{5,1},{2,6},{6,2},{3,7},{7,3},{8,12},{12,8},{9,1... | collective-permute-start | bytes 2359304 | tf_op jit(solution)/shard_map/ppermute | solution.py:58
  481.0 53.3 %collective-permute-start.27 = (bf16[384,1536]{1,0:T(8,128)(2,1)}, bf16[384,1536]{1,0:T(8,128)(2,1)}, u32[]{:S(2)}, u32[]{:S(2)}) collective-permute-start(bf16[384,1536]{1,0:T(8,128)(2,1)} %convolution_convert_fusion.5), channel_id=1, source_target_pairs={{0,1},{1,0},{2,3},{3,2},{4,5},{5,4},{6,7},{7,6},{8,9},{9,8},{10,11... | collective-permute-start | bytes 3538952 | tf_op jit(solution)/shard_map/ppermute | solution.py:58
  484.1 35.1 %collective-permute-start.28 = (bf16[2,1,384,256]{3,2,1,0:T(8,128)(2,1)}, bf16[2,1,384,256]{3,2,1,0:T(8,128)(2,1)}, u32[]{:S(2)}, u32[]{:S(2)}) collective-permute-start(bf16[2,1,384,256]{3,2,1,0:T(8,128)(2,1)} %constant_dynamic-slice_fusion.2), channel_id=1, source_target_pairs={{0,8},{8,0},{16,24},{24,16},{1,9},{9,1},{17,25},{25,17},{2,10},{10... | collective-permute-start | bytes 1179656 | tf_op jit(solution)/shard_map/ppermute | solution.py:153
  498.9 40.9 %collective-permute-start.24 = (bf16[4,1,1,96,1536]{4,3,2,1,0:T(8,128)(2,1)}, bf16[4,1,1,96,1536]{4,3,2,1,0:T(8,128)(2,1)}, u32[]{:S(2)}, u32[]{:S(2)}) collective-permute-start(bf16[4,1,1,96,1536]{4,3,2,1,0:T(8,128)(2,1)} %constant_dynamic-slice_fusion.3), channel_id=1, source_target_pairs={{0,4},{4,0},{1,5},{5,1},{2,6},{6,2},{3,7},{7,3},{8,12},{12,8},{9,1... | collective-permute-start | bytes 3538952 | tf_op jit(solution)/shard_map/ppermute | solution.py:58
  500.6 39.1 %all-to-all-start.4 = ((bf16[4,96,1120]{2,1,0:T(8,128)(2,1)}), bf16[4,96,1120]{2,1,0:T(8,128)(2,1)}, u32[]{:S(2)}, u32[]{:S(2)}) async-start(bf16[4,96,1120]{2,1,0:T(8,128)(2,1)} %bitcast.147), calls=%async_computation.6 | async-start | bytes 1769472 | tf_op jit(solution)/shard_map/all_to_all | solution.py:114
  504.9 130.5 %reduce-scatter.11.cloned.1.call-start = ((), (), s32[]{:S(2)}) async-start(), calls=%async_computation.17 | async-start | bytes 1843200 | tf_op jit(solution)/shard_map/reduce_scatter | solution.py:108
  521.9 17.8 %collective-permute-start.29 = (bf16[1,1,384,256]{3,2,1,0:T(8,128)(2,1)}, bf16[1,1,384,256]{3,2,1,0:T(8,128)(2,1)}, u32[]{:S(2)}, u32[]{:S(2)}) collective-permute-start(bf16[1,1,384,256]{3,2,1,0:T(8,128)(2,1)} %constant_dynamic-slice_fusion.1), channel_id=1, source_target_pairs={{0,16},{8,24},{16,0},{24,8},{1,17},{9,25},{17,1},{25,9},{2,18},{10... | collective-permute-start | bytes 589832 | tf_op jit(solution)/shard_map/ppermute | solution.py:153
  551.6 26.7 %collective-permute-start.25 = (bf16[384,1536]{1,0:T(8,128)(2,1)}, bf16[384,1536]{1,0:T(8,128)(2,1)}, u32[]{:S(2)}, u32[]{:S(2)}) collective-permute-start(bf16[384,1536]{1,0:T(8,128)(2,1)} %fusion.13), channel_id=1, source_target_pairs={{0,4},{4,0},{1,5},{5,1},{2,6},{6,2},{3,7},{7,3},{8,12},{12,8},{9,1... | collective-permute-start | bytes 3538952 | tf_op jit(solution)/shard_map/ppermute | solution.py:58
  594.6 17.2 %all-to-all-start.5 = ((bf16[4,96,1120]{2,1,0:T(8,128)(2,1)}), bf16[4,96,1120]{2,1,0:T(8,128)(2,1)}, u32[]{:S(2)}, u32[]{:S(2)}) async-start(bf16[4,96,1120]{2,1,0:T(8,128)(2,1)} %bitcast.146), calls=%async_computation.9 | async-start | bytes 1769472 | tf_op jit(solution)/shard_map/all_to_all | solution.py:114
  603.6 28.7 %collective-permute-start.26 = (bf16[384,1536]{1,0:T(8,128)(2,1)}, bf16[384,1536]{1,0:T(8,128)(2,1)}, u32[]{:S(2)}, u32[]{:S(2)}) collective-permute-start(bf16[384,1536]{1,0:T(8,128)(2,1)} %fusion.15), channel_id=1, source_target_pairs={{0,1},{1,0},{2,3},{3,2},{4,5},{5,4},{6,7},{7,6},{8,9},{9,8},{10,11... | collective-permute-start | bytes 3538952 | tf_op jit(solution)/shard_map/ppermute | solution.py:58
  (82 other events, 763.8 us)
Sparse Core Ops, SparseCore 0:
  10.1 35.1 all-gather.4
  50.0 82.9 all-gather.6
  135.1 68.5 all-gather.8
  225.7 80.5 all-gather.10
  308.5 65.0 reduce-scatter.4
  375.8 66.6 reduce-scatter.6
  444.8 87.6 reduce-scatter.8
  588.0 37.4 reduce-scatter.10
